TPU v7x, 32 devices: a whole 2x2x4 slice. The times are simulated.
32 devices in a mesh: dp: 2 (over core), row: 4 (over z), col: 4 (over y, x).
Axes of the slice: x: 2, y: 2, z: 4, core: 2. Of those that a mesh axis runs over, the one named last changes fastest.
Arguments:
- inputs: bfloat16 [512, 12288], P('dp', 'col'), may hold values from -6 to 6
- weight_tiles: bfloat16 [4, 4, 432, 4096], P('row', 'col', 'dp'), may hold values from -0.109375 to 0.109375
- tile_rows: int32 [4, 4, 432], P('row', 'col'), may hold values from 0 to 191, as said below
- tile_cols: int32 [4, 4, 432], P('row', 'col'), may hold values from 0 to 47, as said below
- tile_counts: int32 [4, 4], P('row', 'col'), may hold values from 54 to 432, as said below
- act_grad: bfloat16 [512, 49152], P('dp', ('row', 'col')), may hold values from -6 to 6
Outputs:
- activation: bfloat16 [512, 49152], P('dp', ('row', 'col'))
- input_grad: bfloat16 [512, 12288], P(('dp', 'row'), 'col')
- tile_grads: bfloat16 [4, 4, 432, 4096], P('row', 'col', 'dp')
Inputs may be any that keep to these rules, and one draw needn't show every extreme that they name: `tile_rows`: block row of a slot within its region; within each region the slots name distinct blocks. `tile_cols`: block column of a slot within its region. `tile_counts`: live slots of a region are its first ones; some region has all 432 slots live.
All inputs are finite; a program needn't handle non-finite values.
Results may differ from a plain program's by a relative error of at most 0.015.
Values may be sent and summed in bfloat16 or wider, within the bound.
No kernel may reach another device: no remote copies, remote signals or barrier semaphores. Data moves between devices by JAX's collectives and lax.ppermute only.
A program may use at most 128 MiB of HBM per device.

v0:
```python
import functools

import jax
import jax.numpy as jnp
from jax import lax
from jax.experimental import pallas as pl
from jax.experimental.pallas import tpu as pltpu
from jax.sharding import PartitionSpec as P

COEFF = 0.7978845608028654
CUBIC = 0.044715
BLOCK = 64
HALF = 32
CHUNKS = 2
ADD_UNROLL = 54
OUTER_UNROLL = 27
TURN_UNROLL = 27
PLAIN_UNROLL = 8
MIB = 1024 * 1024
VMEM = pl.BlockSpec(memory_space=pltpu.VMEM)
SMEM = pl.BlockSpec(memory_space=pltpu.SMEM)
ANY = pl.BlockSpec(memory_space=pl.ANY)
NT = (((1,), (1,)), ((), ()))


def widest_divisor(total, most):
    return max(divisor for divisor in range(1, most + 1) if total % divisor == 0)


def unpack(packed):
    return jnp.concatenate([packed[:, :BLOCK], packed[:, BLOCK:]], axis=0)


def pack(square):
    return jnp.concatenate([square[:HALF], square[HALF:]], axis=1)


def matmul(left, right):
    return jnp.dot(left, right, preferred_element_type=jnp.float32)


def matmul_nt(left, right):
    return lax.dot_general(left, right, NT, preferred_element_type=jnp.float32)


def call(kernel, name, out_shape, in_specs, out_specs, operands, mib, flops, scratch=(), **more):
    moved = sum(operand.size * operand.dtype.itemsize for operand in operands)
    moved += sum(leaf.size * leaf.dtype.itemsize for leaf in jax.tree.leaves(out_shape))
    return pl.pallas_call(
        kernel,
        out_shape=out_shape,
        in_specs=in_specs,
        out_specs=out_specs,
        scratch_shapes=list(scratch),
        name=name,
        compiler_params=pltpu.CompilerParams(vmem_limit_bytes=mib * MIB),
        cost_estimate=pl.CostEstimate(flops=flops, bytes_accessed=moved, transcendentals=0),
        **more,
    )(*operands)


def plain_loop(total, body):
    unroll = widest_divisor(total, PLAIN_UNROLL)

    @pl.loop(0, total // unroll)
    def _(group):
        for lane in range(unroll):
            body(group * unroll + lane)


def half_counts(facts_ref, half_slots):
    count, dp = facts_ref[0], facts_ref[2]
    own = dp * half_slots
    other = half_slots - own
    return count, ((own, 0), (other, 1))


def add_products(facts_ref, target_ref, source_ref, tile_refs, table, total, width):
    spare = total.shape[0] - 1
    half_slots = tile_refs[0].shape[0]
    unroll = widest_divisor(half_slots, ADD_UNROLL)
    count, halves = half_counts(facts_ref, half_slots)

    def clear(block):
        total[block] = jnp.zeros(total.shape[1:], jnp.float32)

    plain_loop(spare, clear)

    for first, which in halves:
        live = jnp.clip(count - first, 0, half_slots)

        @pl.loop(0, (live + unroll - 1) // unroll)
        def _(group):
            products = []
            places = []
            for lane in range(unroll):
                index = group * unroll + lane
                slot = first + index
                places.append(jnp.where(slot < count, target_ref[slot], spare))
                products.append(matmul(unpack(tile_refs[which][index]), table[source_ref[slot]]))
            for place, product in zip(places, products):
                total[place] += product


def forward_kernel(share_blocks, facts_ref, row_ref, col_ref, own_ref, other_ref, table_ref, *refs):
    along_x, along_y, own_a, own_b, relay_x, relay_y, total = refs
    half_blocks = share_blocks // 2
    add_products(facts_ref, row_ref, col_ref, (own_ref, other_ref), table_ref, total, table_ref.shape[2])
    me = facts_ref[1]
    for out_ref, share, half in (
        (along_x.at[0], 3, 0),
        (along_x.at[1], 1, 0),
        (along_y.at[0], 3, 1),
        (along_y.at[1], 2, 1),
        (own_a, 0, 0),
        (own_b, 0, 1),
        (relay_x, 1, 1),
        (relay_y, 2, 0),
    ):
        first = (me ^ share) * share_blocks + half * half_blocks

        def write(block, out_ref=out_ref, first=first):
            out_ref[block] = total[first + block].astype(out_ref.dtype)

        plain_loop(half_blocks, write)


def forward(facts, rows, cols, own, other, table, share_blocks, shares):
    blocks = share_blocks * shares
    width = table.shape[2]
    half = (share_blocks // 2, BLOCK, width)
    piece = jax.ShapeDtypeStruct(half, jnp.bfloat16)
    two = jax.ShapeDtypeStruct((2, *half), jnp.bfloat16)
    return call(
        functools.partial(forward_kernel, share_blocks),
        "forward",
        [two] * 2 + [piece] * 4,
        [SMEM] * 3 + [VMEM] * 3,
        [VMEM] * 6,
        (facts, rows, cols, own, other, table),
        20,
        2 * rows.shape[0] * BLOCK * BLOCK * width,
        [pltpu.VMEM((blocks + 1, BLOCK, width), jnp.float32)],
    )


def load_pieces(facts_ref, piece_refs, table, sem, share_blocks):
    half_blocks = share_blocks // 2
    me = facts_ref[1]
    places = ((0, 0, share_blocks), (1, 0, share_blocks), (2, 0, share_blocks))
    places += ((3, 0, half_blocks), (3, half_blocks, half_blocks))
    copies = []
    for number, (piece_ref, (share, start, length)) in enumerate(zip(piece_refs, places)):
        first = (me ^ share) * share_blocks + start
        copies.append(pltpu.make_async_copy(piece_ref, table.at[pl.ds(first, length)], sem.at[number]))
    for copy in copies:
        copy.start()
    return copies


def backward_kernel(share_blocks, facts_ref, row_ref, col_ref, own_ref, other_ref, *refs):
    *piece_refs, out_ref, total, table, sem = refs
    for copy in load_pieces(facts_ref, piece_refs, table, sem, share_blocks):
        copy.wait()
    add_products(facts_ref, col_ref, row_ref, (own_ref, other_ref), table, total, table.shape[2])
    pairs = out_ref.shape[1] // (2 * BLOCK)
    for pair in range(pairs):
        both = jnp.concatenate([total[2 * pair], total[2 * pair + 1]], axis=0)
        out_ref[:, pair * 2 * BLOCK : (pair + 1) * 2 * BLOCK] = both.T.astype(out_ref.dtype)


def backward(facts, rows, cols, own, other, pieces, share_blocks, in_blocks):
    width = pieces[0].shape[2]
    blocks = 4 * share_blocks
    return call(
        functools.partial(backward_kernel, share_blocks),
        "backward",
        jax.ShapeDtypeStruct((width, in_blocks * BLOCK), jnp.bfloat16),
        [SMEM] * 3 + [VMEM] * 2 + [ANY] * len(pieces),
        VMEM,
        (facts, rows, cols, own, other, *pieces),
        20,
        2 * rows.shape[0] * BLOCK * BLOCK * width,
        [
            pltpu.VMEM((in_blocks + 1, BLOCK, width), jnp.float32),
            pltpu.VMEM((blocks, BLOCK, width), jnp.bfloat16),
            pltpu.SemaphoreType.DMA((len(pieces),)),
        ],
    )


def outer_kernel(share_blocks, mine, facts_ref, row_ref, col_ref, *refs):
    if mine:
        added_ref, *refs = refs
    *operand_refs, out_ref, table, sem = refs
    chunks = table.shape[0]
    input_refs, piece_refs = operand_refs[:chunks], operand_refs[chunks:]
    pieces = len(piece_refs) // chunks
    copies = []
    for chunk in range(chunks):
        copies += load_pieces(
            facts_ref, piece_refs[chunk * pieces : (chunk + 1) * pieces], table.at[chunk], sem.at[chunk], share_blocks
        )
    for copy in copies:
        copy.wait()
    half_slots = out_ref.shape[0]
    unroll = widest_divisor(half_slots, OUTER_UNROLL)
    count, halves = half_counts(facts_ref, half_slots)
    first_slot = halves[0][0] if mine else halves[1][0]

    @pl.loop(0, half_slots // unroll)
    def _(group):
        first = group * unroll

        @pl.when(first_slot + first < count)
        def _():
            for lane in range(unroll):
                index = first + lane
                slot = first_slot + index
                row, col = row_ref[slot], col_ref[slot]
                product = matmul_nt(table[0, row], input_refs[0][col])
                for chunk in range(1, chunks):
                    product += matmul_nt(table[chunk, row], input_refs[chunk][col])
                packed = pack(product)
                if mine:
                    packed += added_ref[index].astype(jnp.float32)
                out_ref[index] = jnp.where(slot < count, packed, 0.0).astype(out_ref.dtype)

        @pl.when(first_slot + first >= count)
        def _():
            for lane in range(unroll):
                out_ref[first + lane] = jnp.zeros(out_ref.shape[1:], out_ref.dtype)


def outer(facts, rows, cols, inputs, pieces, share_blocks, half_slots, added=None):
    chunks = len(inputs)
    width = inputs[0].shape[2]
    flat = [piece for chunk in pieces for piece in chunk]
    mine = added is not None
    blocks = 4 * share_blocks
    return call(
        functools.partial(outer_kernel, share_blocks, mine),
        "outer_own" if mine else "outer_other",
        jax.ShapeDtypeStruct((half_slots, HALF, 2 * BLOCK), jnp.bfloat16),
        [SMEM] * 3 + [VMEM] * (int(mine) + chunks) + [ANY] * len(flat),
        VMEM,
        (facts, rows, cols, *([added] if mine else []), *inputs, *flat),
        20,
        2 * half_slots * BLOCK * BLOCK * width * chunks,
        [
            pltpu.VMEM((chunks, blocks, BLOCK, width), jnp.bfloat16),
            pltpu.SemaphoreType.DMA((chunks, len(pieces[0]))),
        ],
    )


def transpose_kernel(unroll, own_ref, other_ref, own_out, other_out):
    row = lax.broadcasted_iota(jnp.int32, (BLOCK, BLOCK), 0)
    col = lax.broadcasted_iota(jnp.int32, (BLOCK, BLOCK), 1)
    unit = (row == col).astype(jnp.bfloat16)

    @pl.loop(0, own_ref.shape[0] // unroll)
    def _(group):
        for lane in range(unroll):
            index = group * unroll + lane
            for source, target in ((own_ref, own_out), (other_ref, other_out)):
                target[index] = pack(matmul_nt(unit, unpack(source[index]))).astype(jnp.bfloat16)


def transpose_tiles(own, other):
    shape = jax.ShapeDtypeStruct(own.shape, own.dtype)
    return call(
        functools.partial(transpose_kernel, widest_divisor(own.shape[0], TURN_UNROLL)),
        "transpose_tiles",
        [shape, shape],
        [VMEM] * 2,
        [VMEM] * 2,
        (own, other),
        12,
        2 * own.size * BLOCK * 2,
    )


def unit_order():
    row = lax.broadcasted_iota(jnp.int32, (2 * BLOCK, 2 * BLOCK), 0)
    col = lax.broadcasted_iota(jnp.int32, (2 * BLOCK, 2 * BLOCK), 1)
    kept = (row & BLOCK) + 2 * (row & (HALF - 1)) + ((row >> 5) & 1)
    return (kept == col).astype(jnp.bfloat16)


def token_rows_kernel(reorder, values_ref, select_ref, *out_refs):
    row = lax.broadcasted_iota(jnp.int32, (2 * BLOCK, 2 * BLOCK), 0)
    col = lax.broadcasted_iota(jnp.int32, (2 * BLOCK, 2 * BLOCK), 1)
    order = unit_order() if reorder else (row == col).astype(jnp.bfloat16)
    for pair in range(out_refs[0].shape[0] // 2):
        lanes = values_ref[:, pair * 2 * BLOCK : (pair + 1) * 2 * BLOCK]
        turned = matmul_nt(order, lanes).astype(jnp.bfloat16)
        for chunk, out_ref in enumerate(out_refs):
            picked = matmul(turned, select_ref[chunk]).astype(jnp.bfloat16)
            out_ref[2 * pair] = picked[:BLOCK]
            out_ref[2 * pair + 1] = picked[BLOCK:]


def token_rows(values, select, reorder):
    chunks, tokens, width = select.shape
    blocks = values.shape[1] // BLOCK
    shape = jax.ShapeDtypeStruct((blocks, BLOCK, width), jnp.bfloat16)
    return call(
        functools.partial(token_rows_kernel, reorder),
        "units_to_rows" if reorder else "features_to_rows",
        [shape] * chunks,
        [VMEM] * 2,
        [VMEM] * chunks,
        (values, select),
        12,
        2 * values.size * 2 * BLOCK * 3,
    )


def rows_to_units_kernel(select_ref, *refs):
    *act_refs, out_ref = refs
    order = unit_order()
    for pair in range(act_refs[0].shape[0] // 2):
        turned = 0.0
        for chunk, act_ref in enumerate(act_refs):
            both = jnp.concatenate([act_ref[2 * pair], act_ref[2 * pair + 1]], axis=0)
            turned = turned + matmul_nt(select_ref[chunk], both)
        out_ref[:, pair * 2 * BLOCK : (pair + 1) * 2 * BLOCK] = matmul(
            turned.astype(jnp.bfloat16), order
        ).astype(out_ref.dtype)


def rows_to_units(select, acts):
    chunks, tokens, width = select.shape
    units = acts[0].shape[0] * BLOCK
    return call(
        rows_to_units_kernel,
        "rows_to_units",
        jax.ShapeDtypeStruct((tokens, units), jnp.bfloat16),
        [VMEM] * (1 + len(acts)),
        VMEM,
        (select, *acts),
        12,
        2 * tokens * units * 2 * BLOCK * 3,
    )


def gelu_kernel(upstream_ref, own_a, near_a, last_a, own_b, near_b, last_b, grad_out, act_out):
    half_blocks = own_a.shape[0]
    for half, (own, near, last) in enumerate(((own_a, near_a, last_a), (own_b, near_b, last_b))):

        def one(block, half=half, own=own, near=near, last=last):
            pre = own[block].astype(jnp.float32) + near[1, block].astype(jnp.float32)
            pre = pre + last[block].astype(jnp.float32)
            square = pre * pre
            inner = jnp.tanh(COEFF * (pre + CUBIC * square * pre))
            front = 0.5 * (1.0 + inner)
            place = half * half_blocks + block
            act_out[place] = (front * pre).astype(act_out.dtype)
            slope = front + 0.5 * pre * (1.0 - inner * inner) * COEFF * (1.0 + 3.0 * CUBIC * square)
            grad_out[place] = (upstream_ref[place].astype(jnp.float32) * slope).astype(grad_out.dtype)

        plain_loop(half_blocks, one)


def gelu(upstream, parts):
    shape = jax.ShapeDtypeStruct(upstream.shape, jnp.bfloat16)
    return call(
        gelu_kernel,
        "gelu",
        [shape] * 2,
        [VMEM] * 7,
        [VMEM] * 2,
        (upstream, *parts),
        12,
        upstream.size * 20,
    )


def token_select(tokens, rows):
    width = tokens // CHUNKS
    part = width // rows
    chunk = jnp.arange(CHUNKS)[:, None, None]
    token = jnp.arange(tokens)[None, :, None]
    lane = jnp.arange(width)[None, None, :]
    kept = (lane // part) * part * CHUNKS + chunk * part + lane % part
    return (kept == token).astype(jnp.bfloat16)


def local(inputs, weight_tiles, tile_rows, tile_cols, tile_counts, act_grad):
    tokens = inputs.shape[0]
    in_blocks = inputs.shape[1] // BLOCK
    shares = lax.axis_size("col")
    row_devices = lax.axis_size("row")
    dp_devices = lax.axis_size("dp")
    share = act_grad.shape[1]
    share_blocks = share // BLOCK
    slots = tile_rows.shape[2]
    half_slots = weight_tiles.shape[2]
    width = tokens // CHUNKS
    part = width // row_devices
    assert shares == 4 and dp_devices == 2 and share_blocks % 2 == 0
    rows = tile_rows.reshape(slots)
    cols = tile_cols.reshape(slots)
    facts = jnp.stack([tile_counts.reshape(()), lax.axis_index("col"), lax.axis_index("dp")]).astype(jnp.int32)

    def across(values, bit):
        return lax.ppermute(values, "col", [(place, place ^ bit) for place in range(shares)])

    def other_core(values):
        return lax.ppermute(values, "dp", [(0, 1), (1, 0)])

    stored = weight_tiles.reshape(half_slots, 4096)
    other = other_core(stored).reshape(half_slots, HALF, 2 * BLOCK)
    own = stored.reshape(half_slots, HALF, 2 * BLOCK)
    select = token_select(tokens, row_devices)
    tables = token_rows(inputs, select, False)

    partials = [forward(facts, rows, cols, own, other, table, share_blocks, shares) for table in tables]
    own_t, other_t = transpose_tiles(own, other)
    upstream = token_rows(act_grad, select, True)

    grads, acts = [], []
    for chunk in range(CHUNKS):
        along_x, along_y, own_a, own_b, relay_x, relay_y = partials[chunk]
        from_x, from_y = across(along_x, 1), across(along_y, 2)
        last_a = across(relay_y + from_x[0], 2)
        last_b = across(relay_x + from_y[0], 1)
        grad, act = gelu(upstream[chunk], (own_a, from_x, last_a, own_b, from_y, last_b))
        acts.append(act)
        grad_x, grad_y = across(grad, 1), across(grad, 2)
        far_a = across(grad_x[: share_blocks // 2], 2)
        far_b = across(grad_y[share_blocks // 2 :], 1)
        grads.append((grad, grad_x, grad_y, far_a, far_b))

    activation = rows_to_units(select, acts)
    input_parts = []
    me_row = lax.axis_index("row")
    for chunk in range(CHUNKS):
        partial = backward(facts, rows, cols, own_t, other_t, grads[chunk], share_blocks, in_blocks)
        if row_devices == 4:
            pieces = partial.reshape(row_devices, part, in_blocks * BLOCK)
            total = lax.dynamic_index_in_dim(pieces, me_row, 0, keepdims=False).astype(jnp.float32)
            for shift in (2, 1, 3):
                piece = lax.dynamic_index_in_dim(pieces, (me_row + shift) % row_devices, 0, keepdims=False)
                moved = lax.ppermute(
                    piece, "row", [(place, (place + shift) % row_devices) for place in range(row_devices)]
                )
                total = total + moved.astype(jnp.float32)
            input_parts.append(total.astype(jnp.bfloat16))
        else:
            input_parts.append(lax.psum_scatter(partial, "row", scatter_dimension=0, tiled=True))
    input_grad = jnp.concatenate(input_parts, axis=0)

    for_other = outer(facts, rows, cols, tables, grads, share_blocks, half_slots)
    tile_sum = outer(facts, rows, cols, tables, grads, share_blocks, half_slots, other_core(for_other))
    tile_grads = tile_sum.reshape(1, 1, half_slots, 4096)
    return (activation, input_grad, tile_grads)


def solution(mesh):
    return jax.shard_map(
        local,
        mesh=mesh,
        in_specs=(
            P("dp", "col"),
            P("row", "col", "dp", None),
            P("row", "col", None),
            P("row", "col", None),
            P("row", "col"),
            P("dp", ("row", "col")),
        ),
        out_specs=(P("dp", ("row", "col")), P(("dp", "row"), "col"), P("row", "col", "dp", None)),
        check_vma=False,
    )
```

profile of v0, /device:TPU:0, one launch (start us, length us, event | category | flops | bytes accessed | tf_op | source)
XLA Modules:
  0.0 171.7 jit_solution(13852590435855524475)
XLA Ops:
  0.6 0.5 collective-permute-start
  1.8 2.0 %copy.9 = bf16[27,8,32,128]{3,2,1,0:T(8,128)(2,1)S(1)} copy(bf16[27,8,32,128]{3,1,2,0:T(8,128)(2,1)} %bitcast.72) | data formatting | bytes 3538944
  3.8 0.1 add_add_fusion
  3.9 4.1 %features_to_rows.1 = (bf16[48,64,128]{2,1,0:T(8,128)(2,1)S(1)}, bf16[48,64,128]{2,1,0:T(8,128)(2,1)S(1)}) custom-call(bf16[256,3072]{1,0:T(8,128)(2,1)S(1)} %copy-done.18, bf16[2,256,128]{2,1,0:T(8,128)(2,1)S(1)} %fusion.10.select_ref), custom_call_target="tpu_custom_call" | custom-call | flops 603979776 | bytes 3276800 | tf_op jit(solution)/shard_map/features_to_rows/pallas_call | solution.py:49
  8.0 0.1 pad_add_fusion.facts_ref
  8.1 0.0 collective-permute-done
  8.1 2.3 %copy.10 = bf16[27,8,32,128]{3,2,1,0:T(8,128)(2,1)S(1)} copy(bf16[27,8,32,128]{3,1,2,0:T(8,128)(2,1)} %bitcast.26) | data formatting | bytes 3538944
  10.5 4.2 %forward.3 = (bf16[2,24,64,128]{3,2,1,0:T(8,128)(2,1)S(1)}, bf16[2,24,64,128]{3,2,1,0:T(8,128)(2,1)S(1)}, bf16[24,64,128]{2,1,0:T(8,128)(2,1)S(1)}, bf16[24,64,1...) custom-call(s32[3]{0:T(128)S(1)} %pad_add_fusion.facts_ref, ...), custom_call_target="tpu_custom_call" | custom-call | flops 452984832 | bytes 7474572 | tf_op jit(solution)/shard_map/forward/pallas_call | solution.py:49
  14.7 4.2 %collective-permute-start.5 = (bf16[2,24,64,128]{3,2,1,0:T(8,128)(2,1)S(1)}, bf16[2,24,64,128]{3,2,1,0:T(8,128)(2,1)S(1)}, u32[]{:S(2)}, u32[]{:S(2)}) collective-permute-start(bf16[2,24,64,128]{3,2,1,0:T(8,128)(2,1)S(1)} %get-tuple-element.37), channel_id=1, source_target_pairs={{0,1},{1,0},{2,3},{3,2},{4,5},{5,4},{6,7},{7,6},{8,9},{9,8},{10,11... | collective-permute-start | bytes 2359304 | tf_op jit(solution)/shard_map/ppermute | solution.py:408
  18.9 1.0 collective-permute-start.7
  19.9 4.4 %forward.2 = (bf16[2,24,64,128]{3,2,1,0:T(8,128)(2,1)S(1)}, bf16[2,24,64,128]{3,2,1,0:T(8,128)(2,1)S(1)}, bf16[24,64,128]{2,1,0:T(8,128)(2,1)S(1)}, bf16[24,64,1...) custom-call(s32[3]{0:T(128)S(1)} %pad_add_fusion.facts_ref, ...), custom_call_target="tpu_custom_call" | custom-call | flops 452984832 | bytes 7474572 | tf_op jit(solution)/shard_map/forward/pallas_call | solution.py:49
  24.4 2.2 %collective-permute-start.1 = (bf16[2,24,64,128]{3,2,1,0:T(8,128)(2,1)S(1)}, bf16[2,24,64,128]{3,2,1,0:T(8,128)(2,1)S(1)}, u32[]{:S(2)}, u32[]{:S(2)}) collective-permute-start(bf16[2,24,64,128]{3,2,1,0:T(8,128)(2,1)S(1)} %get-tuple-element.28), channel_id=1, source_target_pairs={{0,1},{1,0},{2,3},{3,2},{4,5},{5,4},{6,7},{7,6},{8,9},{9,8},{10,11... | collective-permute-start | bytes 2359304 | tf_op jit(solution)/shard_map/ppermute | solution.py:408
  26.6 0.0 collective-permute-start.3
  26.7 4.1 %units_to_rows.1 = (bf16[48,64,128]{2,1,0:T(8,128)(2,1)S(1)}, bf16[48,64,128]{2,1,0:T(8,128)(2,1)S(1)}) custom-call(bf16[256,3072]{1,0:T(8,128)(2,1)S(1)} %copy-done.19, bf16[2,256,128]{2,1,0:T(8,128)(2,1)S(1)} %fusion.10.select_ref), custom_call_target="tpu_custom_call" | custom-call | flops 603979776 | bytes 3276800 | tf_op jit(solution)/shard_map/units_to_rows/pallas_call | solution.py:49
  30.7 6.6 %collective-permute-done.5.near_a = bf16[2,24,64,128]{3,2,1,0:T(8,128)(2,1)S(1)} collective-permute-done((bf16[2,24,64,128]{3,2,1,0:T(8,128)(2,1)S(1)}, bf16[2,24,64,128]{3,2,1,0:T(8,128)(2,1)S(1)}, u32[]{:S(2)}, u32[]{:S(2)}) %collective-permute-start.5) | collective-permute-done | bytes 786464 | tf_op jit(solution)/shard_map/ppermute | solution.py:408
  37.4 1.5 collective-permute-start.6
  38.9 0.4 collective-permute-done.7.near_b
  39.3 1.1 collective-permute-start.8
  40.5 13.7 %collective-permute-done.1.near_a = bf16[2,24,64,128]{3,2,1,0:T(8,128)(2,1)S(1)} collective-permute-done((bf16[2,24,64,128]{3,2,1,0:T(8,128)(2,1)S(1)}, bf16[2,24,64,128]{3,2,1,0:T(8,128)(2,1)S(1)}, u32[]{:S(2)}, u32[]{:S(2)}) %collective-permute-start.1) | collective-permute-done | bytes 786464 | tf_op jit(solution)/shard_map/ppermute | solution.py:408
  54.2 1.5 collective-permute-start.2
  55.7 0.4 collective-permute-done.3.near_b
  56.2 1.1 collective-permute-start.4
  57.3 7.2 %collective-permute-done.6.last_a = bf16[24,64,128]{2,1,0:T(8,128)(2,1)S(1)} collective-permute-done((bf16[24,64,128]{2,1,0:T(8,128)(2,1)S(1)}, bf16[24,64,128]{2,1,0:T(8,128)(2,1)S(1)}, u32[]{:S(2)}, u32[]{:S(2)}) %collective-permute-start.6) | collective-permute-done | bytes 393248 | tf_op jit(solution)/shard_map/ppermute | solution.py:408
  64.6 0.0 collective-permute-done.8.last_b
  64.6 1.4 gelu.3
  66.0 0.1 collective-permute-start.16
  66.1 1.5 collective-permute-start.17
  67.5 5.5 %collective-permute-done.2.last_a = bf16[24,64,128]{2,1,0:T(8,128)(2,1)S(1)} collective-permute-done((bf16[24,64,128]{2,1,0:T(8,128)(2,1)S(1)}, bf16[24,64,128]{2,1,0:T(8,128)(2,1)S(1)}, u32[]{:S(2)}, u32[]{:S(2)}) %collective-permute-start.2) | collective-permute-done | bytes 393248 | tf_op jit(solution)/shard_map/ppermute | solution.py:408
  73.0 0.0 collective-permute-done.4.last_b
  73.0 2.2 %gelu.2 = (bf16[48,64,128]{2,1,0:T(8,128)(2,1)}, bf16[48,64,128]{2,1,0:T(8,128)(2,1)S(1)}) custom-call(bf16[48,64,128]{2,1,0:T(8,128)(2,1)S(1)} %get-tuple-element.25.upstream_ref, bf16[24,64,128]{2,1,0:T(8,128)(2,1)S(1)} %get-tuple-element.27.own_a, bf16[2,24,64,128]{3,2,1,0:T(8,128)(2,1)S(1)} %collective-permute-done.1.near_a, ...), custom_call_target="tpu_custom_call" | custom-call | flops 7864320 | bytes 5505024 | tf_op jit(solution)/shard_map/gelu/pallas_call | solution.py:49
  75.3 0.0 collective-permute-start.9
  75.3 1.5 collective-permute-start.10
  76.8 11.1 %collective-permute-done.16.refs_1_.refs_8_.refs_9_ = bf16[48,64,128]{2,1,0:T(8,128)(2,1)S(1)} collective-permute-done((bf16[48,64,128]{2,1,0:T(8,128)(2,1)S(1)}, bf16[48,64,128]{2,1,0:T(8,128)(2,1)S(1)}, u32[]{:S(2)}, u32[]{:S(2)}) %collective-permute-start.16) | collective-permute-done | bytes 786464 | tf_op jit(solution)/shard_map/ppermute | solution.py:408
  87.9 0.8 slice.38
  88.6 0.9 copy-done
  89.5 1.4 collective-permute-start.18
  91.0 0.8 slice.39
  91.8 0.9 copy-done.2
  92.7 1.5 collective-permute-start.19
  94.2 5.8 %transpose_tiles.1 = (bf16[216,32,128]{2,1,0:T(8,128)(2,1)S(1)}, bf16[216,32,128]{2,1,0:T(8,128)(2,1)S(1)}) custom-call(bf16[216,32,128]{2,1,0:T(8,128)(2,1)S(1)} %bitcast.51, bf16[216,32,128]{2,1,0:T(8,128)(2,1)S(1)} %bitcast.54), custom_call_target="tpu_custom_call" | custom-call | flops 226492416 | bytes 7077888 | tf_op jit(solution)/shard_map/transpose_tiles/pallas_call | solution.py:49
  100.1 5.7 %rows_to_units.1 = bf16[256,3072]{1,0:T(8,128)(2,1)} custom-call(bf16[2,256,128]{2,1,0:T(8,128)(2,1)S(1)} %copy-done.15, bf16[48,64,128]{2,1,0:T(8,128)(2,1)S(1)} %copy-done.13, bf16[48,64,128]{2,1,0:T(8,128)(2,1)S(1)} %copy-done.11), custom_call_target="tpu_custom_call" | custom-call | flops 603979776 | bytes 3276800 | tf_op jit(solution)/shard_map/rows_to_units/pallas_call | solution.py:49
  105.7 0.0 collective-permute-done.9.refs_1_.refs_3_.refs_4_
  105.7 1.0 slice.36
  106.8 1.1 collective-permute-start.11
  107.9 1.0 slice.37
  108.9 1.1 collective-permute-start.12
  110.0 5.3 %collective-permute-done.18.refs_3_.refs_10_.refs_11_ = bf16[24,64,128]{2,1,0:T(8,128)(2,1)} collective-permute-done((bf16[24,64,128]{2,1,0:T(8,128)(2,1)}, bf16[24,64,128]{2,1,0:T(8,128)(2,1)}, u32[]{:S(2)}, u32[]{:S(2)}) %collective-permute-start.18) | collective-permute-done | bytes 393248 | tf_op jit(solution)/shard_map/ppermute | solution.py:408
  115.2 0.0 collective-permute-done.19.refs_4_.refs_11_.refs_12_
  115.3 5.1 %backward.3 = bf16[128,3072]{1,0:T(8,128)(2,1)S(1)} custom-call(s32[3]{0:T(128)S(1)} %pad_add_fusion.facts_ref, s32[432]{0:T(512)S(1)} %bitcast.61, s32[432]{0:T(512)S(1)} %bitcast.67, bf16[216,32,128]{2,1,0:T(8,128)(2,1)S(1)} %get-tuple-element.43.own_ref, bf16[216,32,128]{2,1,0:T(8,128)(2,1)S(1)} %get-tuple-element.44.other_ref, ...), custom_call_target="tpu_custom_call" | custom-call | flops 452984832 | bytes 7474572 | tf_op jit(solution)/shard_map/backward/pallas_call | solution.py:49
  120.4 4.6 %collective-permute-start.22 = (bf16[32,3072]{1,0:T(8,128)(2,1)S(1)}, bf16[32,3072]{1,0:T(8,128)(2,1)S(1)}, u32[]{:S(2)}, u32[]{:S(2)}) collective-permute-start(bf16[32,3072]{1,0:T(8,128)(2,1)S(1)} %get-tuple-element.51), channel_id=1, source_target_pairs={{0,12},{4,0},{8,4},{12,8},{1,13},{5,1},{9,5},{13,9},{2,14},{6,2},{... | collective-permute-start | bytes 589832 | tf_op jit(solution)/shard_map/ppermute | solution.py:446
  125.1 0.6 collective-permute-start.20
  125.7 4.3 %outer_other.1 = bf16[216,32,128]{2,1,0:T(8,128)(2,1)S(1)} custom-call(s32[3]{0:T(128)S(1)} %pad_add_fusion.facts_ref, s32[432]{0:T(512)S(1)} %bitcast.62, s32[432]{0:T(512)S(1)} %bitcast.68, bf16[48,64,128]{2,1,0:T(8,128)(2,1)S(1)} %copy-done.7, bf16[48,64,128]{2,1,0:T(8,128)(2,1)S(1)} %copy-done.9, ...), custom_call_target="tpu_custom_call" | custom-call | flops 452984832 | bytes 9637260 | tf_op jit(solution)/shard_map/outer_other/pallas_call | solution.py:49
  130.0 1.9 %collective-permute-start.23 = (bf16[216,32,128]{2,1,0:T(8,128)(2,1)S(1)}, bf16[216,32,128]{2,1,0:T(8,128)(2,1)S(1)}, u32[]{:S(2)}, u32[]{:S(2)}) collective-permute-start(bf16[216,32,128]{2,1,0:T(8,128)(2,1)S(1)} %outer_other.1), channel_id=1, source_target_pairs={{0,16},{16,0},{1,17},{17,1},{2,18},{18,2},{3,19},{19,3},{4,20},{20... | collective-permute-start | bytes 5308424 | tf_op jit(solution)/shard_map/ppermute | solution.py:411
  131.9 5.4 %backward.2 = bf16[128,3072]{1,0:T(8,128)(2,1)S(1)} custom-call(s32[3]{0:T(128)S(1)} %pad_add_fusion.facts_ref, s32[432]{0:T(512)S(1)} %bitcast.63, s32[432]{0:T(512)S(1)} %bitcast.69, bf16[216,32,128]{2,1,0:T(8,128)(2,1)S(1)} %get-tuple-element.43.own_ref, bf16[216,32,128]{2,1,0:T(8,128)(2,1)S(1)} %get-tuple-element.44.other_ref, ...), custom_call_target="tpu_custom_call" | custom-call | flops 452984832 | bytes 7474572 | tf_op jit(solution)/shard_map/backward/pallas_call | solution.py:49
  137.4 6.7 %collective-permute-start.15 = (bf16[32,3072]{1,0:T(8,128)(2,1)S(1)}, bf16[32,3072]{1,0:T(8,128)(2,1)S(1)}, u32[]{:S(2)}, u32[]{:S(2)}) collective-permute-start(bf16[32,3072]{1,0:T(8,128)(2,1)S(1)} %get-tuple-element.48), channel_id=1, source_target_pairs={{0,12},{4,0},{8,4},{12,8},{1,13},{5,1},{9,5},{13,9},{2,14},{6,2},{... | collective-permute-start | bytes 589832 | tf_op jit(solution)/shard_map/ppermute | solution.py:446
  144.1 0.6 collective-permute-start.13
  144.7 0.1 fusion.6
  144.8 4.5 %collective-permute-done.15 = bf16[32,3072]{1,0:T(8,128)(2,1)S(1)} collective-permute-done((bf16[32,3072]{1,0:T(8,128)(2,1)S(1)}, bf16[32,3072]{1,0:T(8,128)(2,1)S(1)}, u32[]{:S(2)}, u32[]{:S(2)}) %collective-permute-start.15) | collective-permute-done | bytes 196640 | tf_op jit(solution)/shard_map/ppermute | solution.py:446
  149.3 4.8 %collective-permute-done.14 = bf16[32,3072]{1,0:T(8,128)(2,1)S(1)} collective-permute-done((bf16[32,3072]{1,0:T(8,128)(2,1)S(1)}, bf16[32,3072]{1,0:T(8,128)(2,1)S(1)}, u32[]{:S(2)}, u32[]{:S(2)}) %collective-permute-start.14) | collective-permute-done | bytes 196640 | tf_op jit(solution)/shard_map/ppermute | solution.py:446
  154.2 6.4 %collective-permute-done.13 = bf16[32,3072]{1,0:T(8,128)(2,1)S(1)} collective-permute-done((bf16[32,3072]{1,0:T(8,128)(2,1)S(1)}, bf16[32,3072]{1,0:T(8,128)(2,1)S(1)}, u32[]{:S(2)}, u32[]{:S(2)}) %collective-permute-start.13) | collective-permute-done | bytes 196640 | tf_op jit(solution)/shard_map/ppermute | solution.py:446
  160.5 0.1 fusion.9
  160.6 0.8 pad_maximum_fusion
  161.4 8.2 %outer_own.1 = bf16[216,32,128]{2,1,0:T(8,128)(2,1)S(1)} custom-call(s32[3]{0:T(128)S(1)} %pad_add_fusion.facts_ref, s32[432]{0:T(512)S(1)} %bitcast.64, s32[432]{0:T(512)S(1)} %bitcast.70, bf16[216,32,128]{2,1,0:T(8,128)(2,1)S(1)} %collective-permute-done.23.refs_0_, bf16[48,64,128]{2,1,0:T(8,128)(2,1)S(1)} %copy-done.7, ...), custom_call_target="tpu_custom_call" | custom-call | flops 452984832 | bytes 11406732 | tf_op jit(solution)/shard_map/outer_own/pallas_call | solution.py:49
  169.6 2.2 %reshape.142 = bf16[1,1,216,4096]{3,2,1,0:T(8,128)(2,1)} reshape(bf16[216,32,128]{2,1,0:T(8,128)(2,1)S(1)} %outer_own.1) | data formatting | bytes 3538944 | tf_op jit(solution)/shard_map/reshape | solution.py:457
  (57 shorter events, 0.4 us)
Async XLA Ops:
  0.6 7.5 %collective-permute-start = (bf16[216,4096]{1,0:T(8,128)(2,1)}, bf16[216,4096]{1,0:T(8,128)(2,1)}, u32[]{:S(2)}, u32[]{:S(2)}) collective-permute-start(bf16[216,4096]{1,0:T(8,128)(2,1)} %bitcast.71), channel_id=1, source_target_pairs={{0,16},{16,0},{1,17},{17,1},{2,18},{18,2},{3,19},{19,3},{4,20},{20... | collective-permute-start | bytes 5308424 | tf_op jit(solution)/shard_map/ppermute | solution.py:411
  1.8 2.1 %copy-start.18 = (bf16[256,3072]{1,0:T(8,128)(2,1)S(1)}, bf16[256,3072]{1,0:T(8,128)(2,1)}, u32[]{:S(2)}) copy-start(bf16[256,3072]{1,0:T(8,128)(2,1)} %values_ref.3) | copy-start | bytes 4718596
  3.9 22.7 %copy-start.14 = (bf16[2,256,128]{2,1,0:T(8,128)(2,1)}, bf16[2,256,128]{2,1,0:T(8,128)(2,1)S(1)}, u32[]{:S(2)}) copy-start(bf16[2,256,128]{2,1,0:T(8,128)(2,1)S(1)} %fusion.10.select_ref) | copy-start | bytes 393220
  8.0 2.5 %copy-start.8 = (bf16[48,64,128]{2,1,0:T(8,128)(2,1)}, bf16[48,64,128]{2,1,0:T(8,128)(2,1)S(1)}, u32[]{:S(2)}) copy-start(bf16[48,64,128]{2,1,0:T(8,128)(2,1)S(1)} %get-tuple-element.35.table_ref.refs_1_.refs_2_) | copy-start | bytes 2359300
  8.0 11.9 %copy-start.6 = (bf16[48,64,128]{2,1,0:T(8,128)(2,1)}, bf16[48,64,128]{2,1,0:T(8,128)(2,1)S(1)}, u32[]{:S(2)}) copy-start(bf16[48,64,128]{2,1,0:T(8,128)(2,1)S(1)} %get-tuple-element.26.table_ref.refs_0_.refs_1_) | copy-start | bytes 2359300
  8.1 2.4 %copy-start.16 = (s32[1,1,432]{2,1,0:T(1,128)S(1)}, s32[1,1,432]{2,1,0:T(1,128)}, u32[]{:S(2)}) copy-start(s32[1,1,432]{2,1,0:T(1,128)} %param.8) | copy-start | bytes 5188
  8.1 2.4 %copy-start.17 = (s32[1,1,432]{2,1,0:T(1,128)S(1)}, s32[1,1,432]{2,1,0:T(1,128)}, u32[]{:S(2)}) copy-start(s32[1,1,432]{2,1,0:T(1,128)} %param.9) | copy-start | bytes 5188
  14.7 22.6 %collective-permute-start.5 = (bf16[2,24,64,128]{3,2,1,0:T(8,128)(2,1)S(1)}, bf16[2,24,64,128]{3,2,1,0:T(8,128)(2,1)S(1)}, u32[]{:S(2)}, u32[]{:S(2)}) collective-permute-start(bf16[2,24,64,128]{3,2,1,0:T(8,128)(2,1)S(1)} %get-tuple-element.37), channel_id=1, source_target_pairs={{0,1},{1,0},{2,3},{3,2},{4,5},{5,4},{6,7},{7,6},{8,9},{9,8},{10,11... | collective-permute-start | bytes 2359304 | tf_op jit(solution)/shard_map/ppermute | solution.py:408
  18.9 20.4 %collective-permute-start.7 = (bf16[2,24,64,128]{3,2,1,0:T(8,128)(2,1)S(1)}, bf16[2,24,64,128]{3,2,1,0:T(8,128)(2,1)S(1)}, u32[]{:S(2)}, u32[]{:S(2)}) collective-permute-start(bf16[2,24,64,128]{3,2,1,0:T(8,128)(2,1)S(1)} %get-tuple-element.40), channel_id=1, source_target_pairs={{0,2},{1,3},{2,0},{3,1},{4,6},{5,7},{6,4},{7,5},{8,10},{9,11},{10,... | collective-permute-start | bytes 2359304 | tf_op jit(solution)/shard_map/ppermute | solution.py:408
  19.9 6.7 %copy-start.19 = (bf16[256,3072]{1,0:T(8,128)(2,1)S(1)}, bf16[256,3072]{1,0:T(8,128)(2,1)}, u32[]{:S(2)}) copy-start(bf16[256,3072]{1,0:T(8,128)(2,1)} %values_ref.2) | copy-start | bytes 4718596
  24.4 29.8 %collective-permute-start.1 = (bf16[2,24,64,128]{3,2,1,0:T(8,128)(2,1)S(1)}, bf16[2,24,64,128]{3,2,1,0:T(8,128)(2,1)S(1)}, u32[]{:S(2)}, u32[]{:S(2)}) collective-permute-start(bf16[2,24,64,128]{3,2,1,0:T(8,128)(2,1)S(1)} %get-tuple-element.28), channel_id=1, source_target_pairs={{0,1},{1,0},{2,3},{3,2},{4,5},{5,4},{6,7},{7,6},{8,9},{9,8},{10,11... | collective-permute-start | bytes 2359304 | tf_op jit(solution)/shard_map/ppermute | solution.py:408
  26.6 29.5 %collective-permute-start.3 = (bf16[2,24,64,128]{3,2,1,0:T(8,128)(2,1)S(1)}, bf16[2,24,64,128]{3,2,1,0:T(8,128)(2,1)S(1)}, u32[]{:S(2)}, u32[]{:S(2)}) collective-permute-start(bf16[2,24,64,128]{3,2,1,0:T(8,128)(2,1)S(1)} %get-tuple-element.31), channel_id=1, source_target_pairs={{0,2},{1,3},{2,0},{3,1},{4,6},{5,7},{6,4},{7,5},{8,10},{9,11},{10,... | collective-permute-start | bytes 2359304 | tf_op jit(solution)/shard_map/ppermute | solution.py:408
  37.4 27.2 %collective-permute-start.6 = (bf16[24,64,128]{2,1,0:T(8,128)(2,1)S(1)}, bf16[24,64,128]{2,1,0:T(8,128)(2,1)S(1)}, u32[]{:S(2)}, u32[]{:S(2)}) collective-permute-start(bf16[24,64,128]{2,1,0:T(8,128)(2,1)S(1)} %fusion.1), channel_id=1, source_target_pairs={{0,2},{1,3},{2,0},{3,1},{4,6},{5,7},{6,4},{7,5},{8,10},{9,11},{10,... | collective-permute-start | bytes 1179656 | tf_op jit(solution)/shard_map/ppermute | solution.py:408
  39.3 25.2 %collective-permute-start.8 = (bf16[24,64,128]{2,1,0:T(8,128)(2,1)S(1)}, bf16[24,64,128]{2,1,0:T(8,128)(2,1)S(1)}, u32[]{:S(2)}, u32[]{:S(2)}) collective-permute-start(bf16[24,64,128]{2,1,0:T(8,128)(2,1)S(1)} %fusion), channel_id=1, source_target_pairs={{0,1},{1,0},{2,3},{3,2},{4,5},{5,4},{6,7},{7,6},{8,9},{9,8},{10,11... | collective-permute-start | bytes 1179656 | tf_op jit(solution)/shard_map/ppermute | solution.py:408
  54.2 18.8 %collective-permute-start.2 = (bf16[24,64,128]{2,1,0:T(8,128)(2,1)S(1)}, bf16[24,64,128]{2,1,0:T(8,128)(2,1)S(1)}, u32[]{:S(2)}, u32[]{:S(2)}) collective-permute-start(bf16[24,64,128]{2,1,0:T(8,128)(2,1)S(1)} %fusion.3), channel_id=1, source_target_pairs={{0,2},{1,3},{2,0},{3,1},{4,6},{5,7},{6,4},{7,5},{8,10},{9,11},{10,... | collective-permute-start | bytes 1179656 | tf_op jit(solution)/shard_map/ppermute | solution.py:408
  56.2 16.8 %collective-permute-start.4 = (bf16[24,64,128]{2,1,0:T(8,128)(2,1)S(1)}, bf16[24,64,128]{2,1,0:T(8,128)(2,1)S(1)}, u32[]{:S(2)}, u32[]{:S(2)}) collective-permute-start(bf16[24,64,128]{2,1,0:T(8,128)(2,1)S(1)} %fusion.2), channel_id=1, source_target_pairs={{0,1},{1,0},{2,3},{3,2},{4,5},{5,4},{6,7},{7,6},{8,9},{9,8},{10,11... | collective-permute-start | bytes 1179656 | tf_op jit(solution)/shard_map/ppermute | solution.py:408
  65.9 9.3 %copy-start.4 = (bf16[48,64,128]{2,1,0:T(8,128)(2,1)}, bf16[48,64,128]{2,1,0:T(8,128)(2,1)S(1)}, u32[]{:S(2)}) copy-start(bf16[48,64,128]{2,1,0:T(8,128)(2,1)S(1)} %get-tuple-element.46.refs_0_.refs_7_.refs_8_) | copy-start | bytes 2359300
  66.0 9.3 %copy-start.10 = (bf16[48,64,128]{2,1,0:T(8,128)(2,1)}, bf16[48,64,128]{2,1,0:T(8,128)(2,1)S(1)}, u32[]{:S(2)}) copy-start(bf16[48,64,128]{2,1,0:T(8,128)(2,1)S(1)} %get-tuple-element.42.refs_1_) | copy-start | bytes 2359300
  66.0 21.9 %collective-permute-start.16 = (bf16[48,64,128]{2,1,0:T(8,128)(2,1)S(1)}, bf16[48,64,128]{2,1,0:T(8,128)(2,1)S(1)}, u32[]{:S(2)}, u32[]{:S(2)}) collective-permute-start(bf16[48,64,128]{2,1,0:T(8,128)(2,1)S(1)} %get-tuple-element.46.refs_0_.refs_7_.refs_8_), channel_id=1, source_target_pairs={{0,1},{1,0},{2,3},{3,2},{4,5},{5,4},{6,7},{7,6},{8,9},{9,8},{10,11... | collective-permute-start | bytes 2359304 | tf_op jit(solution)/shard_map/ppermute | solution.py:408
  66.1 24.9 %collective-permute-start.17 = (bf16[48,64,128]{2,1,0:T(8,128)(2,1)S(1)}, bf16[48,64,128]{2,1,0:T(8,128)(2,1)S(1)}, u32[]{:S(2)}, u32[]{:S(2)}) collective-permute-start(bf16[48,64,128]{2,1,0:T(8,128)(2,1)S(1)} %get-tuple-element.46.refs_0_.refs_7_.refs_8_), channel_id=1, source_target_pairs={{0,2},{1,3},{2,0},{3,1},{4,6},{5,7},{6,4},{7,5},{8,10},{9,11},{10,... | collective-permute-start | bytes 2359304 | tf_op jit(solution)/shard_map/ppermute | solution.py:408
  75.2 16.6 %copy-start.12 = (bf16[48,64,128]{2,1,0:T(8,128)(2,1)}, bf16[48,64,128]{2,1,0:T(8,128)(2,1)S(1)}, u32[]{:S(2)}) copy-start(bf16[48,64,128]{2,1,0:T(8,128)(2,1)S(1)} %get-tuple-element.33.refs_0_) | copy-start | bytes 2359300
  75.3 30.5 %collective-permute-start.9 = (bf16[48,64,128]{2,1,0:T(8,128)(2,1)}, bf16[48,64,128]{2,1,0:T(8,128)(2,1)}, u32[]{:S(2)}, u32[]{:S(2)}) collective-permute-start(bf16[48,64,128]{2,1,0:T(8,128)(2,1)} %get-tuple-element.45.refs_0_.refs_2_.refs_3_), channel_id=1, source_target_pairs={{0,1},{1,0},{2,3},{3,2},{4,5},{5,4},{6,7},{7,6},{8,9},{9,8},{10,11... | collective-permute-start | bytes 2359304 | tf_op jit(solution)/shard_map/ppermute | solution.py:408
  75.3 32.6 %collective-permute-start.10 = (bf16[48,64,128]{2,1,0:T(8,128)(2,1)}, bf16[48,64,128]{2,1,0:T(8,128)(2,1)}, u32[]{:S(2)}, u32[]{:S(2)}) collective-permute-start(bf16[48,64,128]{2,1,0:T(8,128)(2,1)} %get-tuple-element.45.refs_0_.refs_2_.refs_3_), channel_id=1, source_target_pairs={{0,2},{1,3},{2,0},{3,1},{4,6},{5,7},{6,4},{7,5},{8,10},{9,11},{10,... | collective-permute-start | bytes 2359304 | tf_op jit(solution)/shard_map/ppermute | solution.py:408
  88.6 0.9 copy-start
  89.5 25.7 %collective-permute-start.18 = (bf16[24,64,128]{2,1,0:T(8,128)(2,1)}, bf16[24,64,128]{2,1,0:T(8,128)(2,1)}, u32[]{:S(2)}, u32[]{:S(2)}) collective-permute-start(bf16[24,64,128]{2,1,0:T(8,128)(2,1)} %slice.38), channel_id=1, source_target_pairs={{0,2},{1,3},{2,0},{3,1},{4,6},{5,7},{6,4},{7,5},{8,10},{9,11},{10,... | collective-permute-start | bytes 1179656 | tf_op jit(solution)/shard_map/ppermute | solution.py:408
  91.8 0.9 copy-start.2
  92.7 22.6 %collective-permute-start.19 = (bf16[24,64,128]{2,1,0:T(8,128)(2,1)}, bf16[24,64,128]{2,1,0:T(8,128)(2,1)}, u32[]{:S(2)}, u32[]{:S(2)}) collective-permute-start(bf16[24,64,128]{2,1,0:T(8,128)(2,1)} %slice.39), channel_id=1, source_target_pairs={{0,1},{1,0},{2,3},{3,2},{4,5},{5,4},{6,7},{7,6},{8,9},{9,8},{10,11... | collective-permute-start | bytes 1179656 | tf_op jit(solution)/shard_map/ppermute | solution.py:408
  94.2 5.8 %copy-start.11 = (bf16[48,64,128]{2,1,0:T(8,128)(2,1)S(1)}, bf16[48,64,128]{2,1,0:T(8,128)(2,1)}, u32[]{:S(2)}) copy-start(bf16[48,64,128]{2,1,0:T(8,128)(2,1)} %copy-done.10) | copy-start | bytes 2359300
  94.2 5.8 %copy-start.13 = (bf16[48,64,128]{2,1,0:T(8,128)(2,1)S(1)}, bf16[48,64,128]{2,1,0:T(8,128)(2,1)}, u32[]{:S(2)}) copy-start(bf16[48,64,128]{2,1,0:T(8,128)(2,1)} %copy-done.12) | copy-start | bytes 2359300
  94.2 5.8 %copy-start.15 = (bf16[2,256,128]{2,1,0:T(8,128)(2,1)S(1)}, bf16[2,256,128]{2,1,0:T(8,128)(2,1)}, u32[]{:S(2)}) copy-start(bf16[2,256,128]{2,1,0:T(8,128)(2,1)} %copy-done.14) | copy-start | bytes 393220
  100.0 15.2 %copy-start.1 = (bf16[48,64,128]{2,1,0:T(8,128)(2,1)S(1)}, bf16[48,64,128]{2,1,0:T(8,128)(2,1)}, u32[]{:S(2)}) copy-start(bf16[48,64,128]{2,1,0:T(8,128)(2,1)} %copy-done) | copy-start | bytes 2359300
  100.0 15.2 %copy-start.3 = (bf16[48,64,128]{2,1,0:T(8,128)(2,1)S(1)}, bf16[48,64,128]{2,1,0:T(8,128)(2,1)}, u32[]{:S(2)}) copy-start(bf16[48,64,128]{2,1,0:T(8,128)(2,1)} %copy-done.2) | copy-start | bytes 2359300
  100.1 15.2 %copy-start.5 = (bf16[48,64,128]{2,1,0:T(8,128)(2,1)S(1)}, bf16[48,64,128]{2,1,0:T(8,128)(2,1)}, u32[]{:S(2)}) copy-start(bf16[48,64,128]{2,1,0:T(8,128)(2,1)} %copy-done.4) | copy-start | bytes 2359300
  106.8 18.9 %collective-permute-start.11 = (bf16[24,64,128]{2,1,0:T(8,128)(2,1)S(1)}, bf16[24,64,128]{2,1,0:T(8,128)(2,1)S(1)}, u32[]{:S(2)}, u32[]{:S(2)}) collective-permute-start(bf16[24,64,128]{2,1,0:T(8,128)(2,1)S(1)} %slice.36), channel_id=1, source_target_pairs={{0,2},{1,3},{2,0},{3,1},{4,6},{5,7},{6,4},{7,5},{8,10},{9,11},{10,... | collective-permute-start | bytes 1179656 | tf_op jit(solution)/shard_map/ppermute | solution.py:408
  108.9 16.8 %collective-permute-start.12 = (bf16[24,64,128]{2,1,0:T(8,128)(2,1)S(1)}, bf16[24,64,128]{2,1,0:T(8,128)(2,1)S(1)}, u32[]{:S(2)}, u32[]{:S(2)}) collective-permute-start(bf16[24,64,128]{2,1,0:T(8,128)(2,1)S(1)} %slice.37), channel_id=1, source_target_pairs={{0,1},{1,0},{2,3},{3,2},{4,5},{5,4},{6,7},{7,6},{8,9},{9,8},{10,11... | collective-permute-start | bytes 1179656 | tf_op jit(solution)/shard_map/ppermute | solution.py:408
  115.3 10.5 %copy-start.7 = (bf16[48,64,128]{2,1,0:T(8,128)(2,1)S(1)}, bf16[48,64,128]{2,1,0:T(8,128)(2,1)}, u32[]{:S(2)}) copy-start(bf16[48,64,128]{2,1,0:T(8,128)(2,1)} %copy-done.6) | copy-start | bytes 2359300
  115.3 10.5 %copy-start.9 = (bf16[48,64,128]{2,1,0:T(8,128)(2,1)S(1)}, bf16[48,64,128]{2,1,0:T(8,128)(2,1)}, u32[]{:S(2)}) copy-start(bf16[48,64,128]{2,1,0:T(8,128)(2,1)} %copy-done.8) | copy-start | bytes 2359300
  120.4 23.7 %collective-permute-start.22 = (bf16[32,3072]{1,0:T(8,128)(2,1)S(1)}, bf16[32,3072]{1,0:T(8,128)(2,1)S(1)}, u32[]{:S(2)}, u32[]{:S(2)}) collective-permute-start(bf16[32,3072]{1,0:T(8,128)(2,1)S(1)} %get-tuple-element.51), channel_id=1, source_target_pairs={{0,12},{4,0},{8,4},{12,8},{1,13},{5,1},{9,5},{13,9},{2,14},{6,2},{... | collective-permute-start | bytes 589832 | tf_op jit(solution)/shard_map/ppermute | solution.py:446
  125.1 19.0 %collective-permute-start.21 = (bf16[32,3072]{1,0:T(8,128)(2,1)S(1)}, bf16[32,3072]{1,0:T(8,128)(2,1)S(1)}, u32[]{:S(2)}, u32[]{:S(2)}) collective-permute-start(bf16[32,3072]{1,0:T(8,128)(2,1)S(1)} %get-tuple-element.52), channel_id=1, source_target_pairs={{0,4},{4,8},{8,12},{12,0},{1,5},{5,9},{9,13},{13,1},{2,6},{6,10},{... | collective-permute-start | bytes 589832 | tf_op jit(solution)/shard_map/ppermute | solution.py:446
  125.1 19.7 %collective-permute-start.20 = (bf16[32,3072]{1,0:T(8,128)(2,1)S(1)}, bf16[32,3072]{1,0:T(8,128)(2,1)S(1)}, u32[]{:S(2)}, u32[]{:S(2)}) collective-permute-start(bf16[32,3072]{1,0:T(8,128)(2,1)S(1)} %get-tuple-element.50), channel_id=1, source_target_pairs={{0,8},{4,12},{8,0},{12,4},{1,9},{5,13},{9,1},{13,5},{2,10},{6,14},... | collective-permute-start | bytes 589832 | tf_op jit(solution)/shard_map/ppermute | solution.py:446
  130.0 31.4 %collective-permute-start.23 = (bf16[216,32,128]{2,1,0:T(8,128)(2,1)S(1)}, bf16[216,32,128]{2,1,0:T(8,128)(2,1)S(1)}, u32[]{:S(2)}, u32[]{:S(2)}) collective-permute-start(bf16[216,32,128]{2,1,0:T(8,128)(2,1)S(1)} %outer_other.1), channel_id=1, source_target_pairs={{0,16},{16,0},{1,17},{17,1},{2,18},{18,2},{3,19},{19,3},{4,20},{20... | collective-permute-start | bytes 5308424 | tf_op jit(solution)/shard_map/ppermute | solution.py:411
  137.4 12.0 %collective-permute-start.15 = (bf16[32,3072]{1,0:T(8,128)(2,1)S(1)}, bf16[32,3072]{1,0:T(8,128)(2,1)S(1)}, u32[]{:S(2)}, u32[]{:S(2)}) collective-permute-start(bf16[32,3072]{1,0:T(8,128)(2,1)S(1)} %get-tuple-element.48), channel_id=1, source_target_pairs={{0,12},{4,0},{8,4},{12,8},{1,13},{5,1},{9,5},{13,9},{2,14},{6,2},{... | collective-permute-start | bytes 589832 | tf_op jit(solution)/shard_map/ppermute | solution.py:446
  144.1 10.1 %collective-permute-start.14 = (bf16[32,3072]{1,0:T(8,128)(2,1)S(1)}, bf16[32,3072]{1,0:T(8,128)(2,1)S(1)}, u32[]{:S(2)}, u32[]{:S(2)}) collective-permute-start(bf16[32,3072]{1,0:T(8,128)(2,1)S(1)} %get-tuple-element.49), channel_id=1, source_target_pairs={{0,4},{4,8},{8,12},{12,0},{1,5},{5,9},{9,13},{13,1},{2,6},{6,10},{... | collective-permute-start | bytes 589832 | tf_op jit(solution)/shard_map/ppermute | solution.py:446
  144.1 16.4 %collective-permute-start.13 = (bf16[32,3072]{1,0:T(8,128)(2,1)S(1)}, bf16[32,3072]{1,0:T(8,128)(2,1)S(1)}, u32[]{:S(2)}, u32[]{:S(2)}) collective-permute-start(bf16[32,3072]{1,0:T(8,128)(2,1)S(1)} %get-tuple-element.47), channel_id=1, source_target_pairs={{0,8},{4,12},{8,0},{12,4},{1,9},{5,13},{9,1},{13,5},{2,10},{6,14},... | collective-permute-start | bytes 589832 | tf_op jit(solution)/shard_map/ppermute | solution.py:446
where the time goes:
time: 171 us; the launch traced here: 172 us
  waiting for transfers between devices  65.9 us (39%)
  Pallas kernels  54.9 us (32%)
  starting transfers between devices  36 us (21%)
  local copies, waits for them, and re-layouts  12 us (7%)
    pallas_call x12, Pallas kernels, call(): pl.pallas_call(kernel, out_shape=out_shape, in_specs=in_specs, out_specs=...  54.9 us
    ppermute x16, waiting for transfers between devices, across(): lax.ppermute(values, 'col', [(place, place ^ bit) for place in range(shar...  50.2 us
    ppermute x16, starting transfers between devices, across(): lax.ppermute(values, 'col', [(place, place ^ bit) for place in range(shar...  21 us
    ppermute x6, waiting for transfers between devices, local(): lax.ppermute(piece, 'row', [(place, (place + shift) % row_devices) for pl...  15.7 us
    ppermute x6, starting transfers between devices, local(): lax.ppermute(piece, 'row', [(place, (place + shift) % row_devices) for pl...  12.6 us
    unnamed x42, local copies, waits for them, and re-layouts  6.15 us
  transfers between devices with their start and end apart: 24, of which 11 were waited for; matrix products, arithmetic and copies ran while one was open for 4% of the time, Pallas kernels for 25%

commit v1 on v0

--- a/solution.py
+++ b/solution.py
@@ -16,6 +16,7 @@
 OUTER_UNROLL = 27
 TURN_UNROLL = 27
 PLAIN_UNROLL = 8
+FLOPS_PER_US = 1_150_000_000
 MIB = 1024 * 1024
 VMEM = pl.BlockSpec(memory_space=pltpu.VMEM)
 SMEM = pl.BlockSpec(memory_space=pltpu.SMEM)
@@ -43,7 +44,7 @@
     return lax.dot_general(left, right, NT, preferred_element_type=jnp.float32)
 
 
-def call(kernel, name, out_shape, in_specs, out_specs, operands, mib, flops, scratch=(), **more):
+def call(kernel, name, out_shape, in_specs, out_specs, operands, mib, microseconds, scratch=(), **more):
     moved = sum(operand.size * operand.dtype.itemsize for operand in operands)
     moved += sum(leaf.size * leaf.dtype.itemsize for leaf in jax.tree.leaves(out_shape))
     return pl.pallas_call(
@@ -54,7 +55,7 @@
         scratch_shapes=list(scratch),
         name=name,
         compiler_params=pltpu.CompilerParams(vmem_limit_bytes=mib * MIB),
-        cost_estimate=pl.CostEstimate(flops=flops, bytes_accessed=moved, transcendentals=0),
+        cost_estimate=pl.CostEstimate(flops=microseconds * FLOPS_PER_US, bytes_accessed=moved, transcendentals=0),
         **more,
     )(*operands)
 
@@ -139,7 +140,7 @@
         [VMEM] * 6,
         (facts, rows, cols, own, other, table),
         20,
-        2 * rows.shape[0] * BLOCK * BLOCK * width,
+        7,
         [pltpu.VMEM((blocks + 1, BLOCK, width), jnp.float32)],
     )
 
@@ -180,7 +181,7 @@
         VMEM,
         (facts, rows, cols, own, other, *pieces),
         20,
-        2 * rows.shape[0] * BLOCK * BLOCK * width,
+        7,
         [
             pltpu.VMEM((in_blocks + 1, BLOCK, width), jnp.float32),
             pltpu.VMEM((blocks, BLOCK, width), jnp.bfloat16),
@@ -189,19 +190,10 @@
     )
 
 
-def outer_kernel(share_blocks, mine, facts_ref, row_ref, col_ref, *refs):
-    if mine:
-        added_ref, *refs = refs
-    *operand_refs, out_ref, table, sem = refs
-    chunks = table.shape[0]
-    input_refs, piece_refs = operand_refs[:chunks], operand_refs[chunks:]
-    pieces = len(piece_refs) // chunks
-    copies = []
-    for chunk in range(chunks):
-        copies += load_pieces(
-            facts_ref, piece_refs[chunk * pieces : (chunk + 1) * pieces], table.at[chunk], sem.at[chunk], share_blocks
-        )
-    for copy in copies:
+def outer_kernel(share_blocks, mine, adds, facts_ref, row_ref, col_ref, *refs):
+    added_refs, (input_ref, *piece_refs) = refs[:adds], refs[adds:-3]
+    out_ref, table, sem = refs[-3:]
+    for copy in load_pieces(facts_ref, piece_refs, table, sem, share_blocks):
         copy.wait()
     half_slots = out_ref.shape[0]
     unroll = widest_divisor(half_slots, OUTER_UNROLL)
@@ -217,12 +209,8 @@
             for lane in range(unroll):
                 index = first + lane
                 slot = first_slot + index
-                row, col = row_ref[slot], col_ref[slot]
-                product = matmul_nt(table[0, row], input_refs[0][col])
-                for chunk in range(1, chunks):
-                    product += matmul_nt(table[chunk, row], input_refs[chunk][col])
-                packed = pack(product)
-                if mine:
+                packed = pack(matmul_nt(table[row_ref[slot]], input_ref[col_ref[slot]]))
+                for added_ref in added_refs:
                     packed += added_ref[index].astype(jnp.float32)
                 out_ref[index] = jnp.where(slot < count, packed, 0.0).astype(out_ref.dtype)
 
@@ -232,24 +220,20 @@
                 out_ref[first + lane] = jnp.zeros(out_ref.shape[1:], out_ref.dtype)
 
 
-def outer(facts, rows, cols, inputs, pieces, share_blocks, half_slots, added=None):
-    chunks = len(inputs)
-    width = inputs[0].shape[2]
-    flat = [piece for chunk in pieces for piece in chunk]
-    mine = added is not None
+def outer(facts, rows, cols, inputs, pieces, share_blocks, half_slots, mine, added):
     blocks = 4 * share_blocks
     return call(
-        functools.partial(outer_kernel, share_blocks, mine),
+        functools.partial(outer_kernel, share_blocks, mine, len(added)),
         "outer_own" if mine else "outer_other",
         jax.ShapeDtypeStruct((half_slots, HALF, 2 * BLOCK), jnp.bfloat16),
-        [SMEM] * 3 + [VMEM] * (int(mine) + chunks) + [ANY] * len(flat),
+        [SMEM] * 3 + [VMEM] * (len(added) + 1) + [ANY] * len(pieces),
         VMEM,
-        (facts, rows, cols, *([added] if mine else []), *inputs, *flat),
+        (facts, rows, cols, *added, inputs, *pieces),
         20,
-        2 * half_slots * BLOCK * BLOCK * width * chunks,
+        5,
         [
-            pltpu.VMEM((chunks, blocks, BLOCK, width), jnp.bfloat16),
-            pltpu.SemaphoreType.DMA((chunks, len(pieces[0]))),
+            pltpu.VMEM((blocks, BLOCK, inputs.shape[2]), jnp.bfloat16),
+            pltpu.SemaphoreType.DMA((len(pieces),)),
         ],
     )
 
@@ -277,7 +261,7 @@
         [VMEM] * 2,
         (own, other),
         12,
-        2 * own.size * BLOCK * 2,
+        7,
     )
 
 
@@ -313,7 +297,7 @@
         [VMEM] * chunks,
         (values, select),
         12,
-        2 * values.size * 2 * BLOCK * 3,
+        5,
     )
 
 
@@ -341,7 +325,7 @@
         VMEM,
         (select, *acts),
         12,
-        2 * tokens * units * 2 * BLOCK * 3,
+        6,
     )
 
 
@@ -373,8 +357,12 @@
         [VMEM] * 2,
         (upstream, *parts),
         12,
-        upstream.size * 20,
-    )
+        2,
+    )
+
+
+def after(value, earlier):
+    return lax.optimization_barrier((value, earlier))[0]
 
 
 def token_select(tokens, rows):
@@ -410,15 +398,15 @@
     def other_core(values):
         return lax.ppermute(values, "dp", [(0, 1), (1, 0)])
 
-    stored = weight_tiles.reshape(half_slots, 4096)
-    other = other_core(stored).reshape(half_slots, HALF, 2 * BLOCK)
-    own = stored.reshape(half_slots, HALF, 2 * BLOCK)
+    own = weight_tiles.reshape(half_slots, HALF, 2 * BLOCK)
+    other = other_core(own)
     select = token_select(tokens, row_devices)
     tables = token_rows(inputs, select, False)
 
     partials = [forward(facts, rows, cols, own, other, table, share_blocks, shares) for table in tables]
-    own_t, other_t = transpose_tiles(own, other)
-    upstream = token_rows(act_grad, select, True)
+    upstream = list(token_rows(act_grad, after(select, partials[1][2]), True))
+    own_t, other_t = transpose_tiles(after(own, upstream[1]), after(other, upstream[1]))
+    upstream[0] = after(upstream[0], own_t)
 
     grads, acts = [], []
     for chunk in range(CHUNKS):
@@ -428,33 +416,54 @@
         last_b = across(relay_x + from_y[0], 1)
         grad, act = gelu(upstream[chunk], (own_a, from_x, last_a, own_b, from_y, last_b))
         acts.append(act)
-        grad_x, grad_y = across(grad, 1), across(grad, 2)
+        grads.append([grad, across(grad, 1), across(grad, 2)])
+
+    activation = rows_to_units(select, acts)
+    grads[0][1] = after(grads[0][1], activation)
+    for chunk in range(CHUNKS):
+        grad, grad_x, grad_y = grads[chunk]
         far_a = across(grad_x[: share_blocks // 2], 2)
         far_b = across(grad_y[share_blocks // 2 :], 1)
-        grads.append((grad, grad_x, grad_y, far_a, far_b))
-
-    activation = rows_to_units(select, acts)
-    input_parts = []
+        grads[chunk] += [far_a, far_b]
+
     me_row = lax.axis_index("row")
-    for chunk in range(CHUNKS):
-        partial = backward(facts, rows, cols, own_t, other_t, grads[chunk], share_blocks, in_blocks)
-        if row_devices == 4:
-            pieces = partial.reshape(row_devices, part, in_blocks * BLOCK)
-            total = lax.dynamic_index_in_dim(pieces, me_row, 0, keepdims=False).astype(jnp.float32)
-            for shift in (2, 1, 3):
-                piece = lax.dynamic_index_in_dim(pieces, (me_row + shift) % row_devices, 0, keepdims=False)
-                moved = lax.ppermute(
-                    piece, "row", [(place, (place + shift) % row_devices) for place in range(row_devices)]
-                )
-                total = total + moved.astype(jnp.float32)
-            input_parts.append(total.astype(jnp.bfloat16))
-        else:
-            input_parts.append(lax.psum_scatter(partial, "row", scatter_dimension=0, tiled=True))
-    input_grad = jnp.concatenate(input_parts, axis=0)
-
-    for_other = outer(facts, rows, cols, tables, grads, share_blocks, half_slots)
-    tile_sum = outer(facts, rows, cols, tables, grads, share_blocks, half_slots, other_core(for_other))
-    tile_grads = tile_sum.reshape(1, 1, half_slots, 4096)
+
+    def to_rows(partial):
+        pieces = partial.reshape(row_devices, part, in_blocks * BLOCK)
+        mine = lax.dynamic_index_in_dim(pieces, me_row, 0, keepdims=False)
+        if row_devices != 4:
+            return [lax.psum_scatter(partial, "row", scatter_dimension=0, tiled=True)]
+        moved = []
+        for shift in (2, 1, 3):
+            piece = lax.dynamic_index_in_dim(pieces, (me_row + shift) % row_devices, 0, keepdims=False)
+            pairs = [(place, (place + shift) % row_devices) for place in range(row_devices)]
+            moved.append(lax.ppermute(piece, "row", pairs))
+        return [mine] + moved
+
+    def add_up(parts, earlier):
+        parts = [after(parts[0], earlier)] + parts[1:]
+        return sum(part.astype(jnp.float32) for part in parts).astype(jnp.bfloat16)
+
+    def input_sums(chunk):
+        return backward(facts, rows, cols, own_t, other_t, grads[chunk], share_blocks, in_blocks)
+
+    def tile_part(chunk, earlier, mine, added):
+        table = after(tables[chunk], earlier)
+        return outer(facts, rows, cols, table, grads[chunk], share_blocks, half_slots, mine, added)
+
+    first = input_sums(0)
+    row_parts = to_rows(first)
+    other_first = tile_part(0, first, False, [])
+    grads[1][3] = after(grads[1][3], other_first)
+    second = input_sums(1)
+    first_sum = add_up(row_parts, second)
+    row_parts = to_rows(second)
+    other_second = tile_part(1, first_sum, False, [])
+    own_first = tile_part(0, other_second, True, [other_core(other_first)])
+    own_second = tile_part(1, other_second, True, [own_first, other_core(other_second)])
+    second_sum = add_up(row_parts, own_second)
+    input_grad = jnp.concatenate([first_sum, second_sum], axis=0)
+    tile_grads = own_second.reshape(1, 1, half_slots, 4096)
     return (activation, input_grad, tile_grads)
 
 

time: 171 us -> 172 us (level); the launches traced: 172 us -> 170 us
  starting transfers between devices: 36 us -> 27.9 us
  waiting for transfers between devices: 65.9 us -> 74 us
  Pallas kernels: 54.9 us -> 51.6 us
  other arithmetic: 1.34 us -> 3.13 us
    ppermute x16, waiting for transfers between devices: 50.2 us -> 58.7 us  [across(): lax.ppermute(values, 'col', [(place, place ^ bit) for place in range(shar...]
    ppermute x16, starting transfers between devices: 21 us -> 16 us  [across(): lax.ppermute(values, 'col', [(place, place ^ bit) for place in range(shar...]
    pallas_call x12 -> x14, Pallas kernels: 54.9 us -> 51.6 us  [call(): pl.pallas_call(kernel, out_shape=out_shape, in_specs=in_specs, out_specs=...]
    convert_element_type x2, other arithmetic: 0.2 us -> 1.99 us  [add_up(): sum((part.astype(jnp.float32) for part in parts)).astype(jnp.bfloat16)]
    unnamed x42 -> x35, local copies, waits for them, and re-layouts: 6.15 us -> 7.3 us
  transfers between devices with their start and end apart: 24 -> 25, of which waited for: 11 -> 12; matrix products, arithmetic and copies ran while one was open for 4% -> 3% of each run, Pallas kernels for 25% -> 28%
where the time goes in v1:
time: 172 us; the launch traced here: 170 us
  waiting for transfers between devices  74 us (43%)
  Pallas kernels  51.6 us (30%)
  starting transfers between devices  27.9 us (16%)
  local copies, waits for them, and re-layouts  12 us (7%)
  other arithmetic  3.13 us (2%)
    ppermute x16, waiting for transfers between devices, across(): lax.ppermute(values, 'col', [(place, place ^ bit) for place in range(shar...  58.7 us
    pallas_call x14, Pallas kernels, call(): pl.pallas_call(kernel, out_shape=out_shape, in_specs=in_specs, out_specs=...  51.6 us
    ppermute x16, starting transfers between devices, across(): lax.ppermute(values, 'col', [(place, place ^ bit) for place in range(shar...  16 us
    ppermute x6, waiting for transfers between devices, to_rows(): moved.append(lax.ppermute(piece, 'row', pairs))  15.3 us
    ppermute x6, starting transfers between devices, to_rows(): moved.append(lax.ppermute(piece, 'row', pairs))  11.1 us
    unnamed x35, local copies, waits for them, and re-layouts  7.3 us
  transfers between devices with their start and end apart: 25, of which 12 were waited for; matrix products, arithmetic and copies ran while one was open for 3% of the time, Pallas kernels for 28%

profile of v1, /device:TPU:0, one launch (start us, length us, event | category | flops | bytes accessed | tf_op | source)
XLA Modules:
  0.0 170.2 jit_solution(9750543043576487799)
XLA Ops:
  0.6 2.0 %copy.9 = bf16[27,8,32,128]{3,2,1,0:T(8,128)(2,1)S(1)} copy(bf16[27,8,32,128]{3,1,2,0:T(8,128)(2,1)} %bitcast.66) | data formatting | bytes 3538944
  2.6 0.5 collective-permute-start
  3.8 0.1 pad_add_fusion.facts_ref
  3.9 0.1 add_add_fusion
  4.0 4.1 %features_to_rows.1 = (bf16[48,64,128]{2,1,0:T(8,128)(2,1)S(1)}, bf16[48,64,128]{2,1,0:T(8,128)(2,1)S(1)}) custom-call(bf16[256,3072]{1,0:T(8,128)(2,1)S(1)} %copy-done, bf16[2,256,128]{2,1,0:T(8,128)(2,1)S(1)} %fusion.4.select_ref), custom_call_target="tpu_custom_call" | custom-call | flops 5750000128 | bytes 3276800 | tf_op jit(solution)/shard_map/features_to_rows/pallas_call | solution.py:50
  8.2 4.0 %forward.3 = (bf16[2,24,64,128]{3,2,1,0:T(8,128)(2,1)S(1)}, bf16[2,24,64,128]{3,2,1,0:T(8,128)(2,1)S(1)}, bf16[24,64,128]{2,1,0:T(8,128)(2,1)S(1)}, bf16[24,64,1...) custom-call(s32[3]{0:T(128)S(1)} %pad_add_fusion.facts_ref, ...), custom_call_target="tpu_custom_call" | custom-call | flops 8049999872 | bytes 7474572 | tf_op jit(solution)/shard_map/forward/pallas_call | solution.py:50
  12.2 5.9 %collective-permute-start.1 = (bf16[2,24,64,128]{3,2,1,0:T(8,128)(2,1)S(1)}, bf16[2,24,64,128]{3,2,1,0:T(8,128)(2,1)S(1)}, u32[]{:S(2)}, u32[]{:S(2)}) collective-permute-start(bf16[2,24,64,128]{3,2,1,0:T(8,128)(2,1)S(1)} %get-tuple-element.48), channel_id=1, source_target_pairs={{0,1},{1,0},{2,3},{3,2},{4,5},{5,4},{6,7},{7,6},{8,9},{9,8},{10,11... | collective-permute-start | bytes 2359304 | tf_op jit(solution)/shard_map/ppermute | solution.py:396
  18.1 0.4 collective-permute-start.3
  18.5 3.8 %forward.2 = (bf16[2,24,64,128]{3,2,1,0:T(8,128)(2,1)S(1)}, bf16[2,24,64,128]{3,2,1,0:T(8,128)(2,1)S(1)}, bf16[24,64,128]{2,1,0:T(8,128)(2,1)S(1)}, bf16[24,64,1...) custom-call(s32[3]{0:T(128)S(1)} %pad_add_fusion.facts_ref, ...), custom_call_target="tpu_custom_call" | custom-call | flops 8049999872 | bytes 7474572 | tf_op jit(solution)/shard_map/forward/pallas_call | solution.py:50
  22.3 3.5 %collective-permute-start.5 = (bf16[2,24,64,128]{3,2,1,0:T(8,128)(2,1)S(1)}, bf16[2,24,64,128]{3,2,1,0:T(8,128)(2,1)S(1)}, u32[]{:S(2)}, u32[]{:S(2)}) collective-permute-start(bf16[2,24,64,128]{3,2,1,0:T(8,128)(2,1)S(1)} %get-tuple-element.54), channel_id=1, source_target_pairs={{0,1},{1,0},{2,3},{3,2},{4,5},{5,4},{6,7},{7,6},{8,9},{9,8},{10,11... | collective-permute-start | bytes 2359304 | tf_op jit(solution)/shard_map/ppermute | solution.py:396
  25.8 0.5 collective-permute-start.7
  26.3 4.1 %units_to_rows.1 = (bf16[48,64,128]{2,1,0:T(8,128)(2,1)S(1)}, bf16[48,64,128]{2,1,0:T(8,128)(2,1)S(1)}) custom-call(bf16[256,3072]{1,0:T(8,128)(2,1)S(1)} %copy-done.1, bf16[2,256,128]{2,1,0:T(8,128)(2,1)S(1)} %fusion.4.select_ref), custom_call_target="tpu_custom_call" | custom-call | flops 5750000128 | bytes 3276800 | tf_op jit(solution)/shard_map/units_to_rows/pallas_call | solution.py:50
  30.4 6.1 %collective-permute-done.1.near_a = bf16[2,24,64,128]{3,2,1,0:T(8,128)(2,1)S(1)} collective-permute-done((bf16[2,24,64,128]{3,2,1,0:T(8,128)(2,1)S(1)}, bf16[2,24,64,128]{3,2,1,0:T(8,128)(2,1)S(1)}, u32[]{:S(2)}, u32[]{:S(2)}) %collective-permute-start.1) | collective-permute-done | bytes 786464 | tf_op jit(solution)/shard_map/ppermute | solution.py:396
  36.5 0.5 collective-permute-start.2
  37.0 1.4 collective-permute-done.3.near_b
  38.5 0.6 collective-permute-start.4
  39.1 14.2 %collective-permute-done.5.near_a = bf16[2,24,64,128]{3,2,1,0:T(8,128)(2,1)S(1)} collective-permute-done((bf16[2,24,64,128]{3,2,1,0:T(8,128)(2,1)S(1)}, bf16[2,24,64,128]{3,2,1,0:T(8,128)(2,1)S(1)}, u32[]{:S(2)}, u32[]{:S(2)}) %collective-permute-start.5) | collective-permute-done | bytes 786464 | tf_op jit(solution)/shard_map/ppermute | solution.py:396
  53.4 0.5 collective-permute-start.6
  53.9 1.4 collective-permute-done.7.near_b
  55.4 0.6 collective-permute-start.8
  55.9 7.3 %transpose_tiles.1 = (bf16[216,32,128]{2,1,0:T(8,128)(2,1)S(1)}, bf16[216,32,128]{2,1,0:T(8,128)(2,1)S(1)}) custom-call(bf16[216,32,128]{2,1,0:T(8,128)(2,1)S(1)} %bitcast.47, bf16[216,32,128]{2,1,0:T(8,128)(2,1)} %collective-permute-done.other_ref), custom_call_target="tpu_custom_call" | custom-call | flops 8049999872 | bytes 7077888 | tf_op jit(solution)/shard_map/transpose_tiles/pallas_call | solution.py:50
  63.2 1.2 copy-done.11
  64.4 1.4 gelu.2
  65.8 1.7 collective-permute-start.10
  67.5 0.4 collective-permute-start.9
  67.9 4.3 %collective-permute-done.6.last_a = bf16[24,64,128]{2,1,0:T(8,128)(2,1)S(1)} collective-permute-done((bf16[24,64,128]{2,1,0:T(8,128)(2,1)S(1)}, bf16[24,64,128]{2,1,0:T(8,128)(2,1)S(1)}, u32[]{:S(2)}, u32[]{:S(2)}) %collective-permute-start.6) | collective-permute-done | bytes 393248 | tf_op jit(solution)/shard_map/ppermute | solution.py:396
  72.2 2.2 %gelu.3 = (bf16[48,64,128]{2,1,0:T(8,128)(2,1)}, bf16[48,64,128]{2,1,0:T(8,128)(2,1)S(1)}) custom-call(bf16[48,64,128]{2,1,0:T(8,128)(2,1)S(1)} %get-tuple-element.41.upstream_ref, bf16[24,64,128]{2,1,0:T(8,128)(2,1)S(1)} %get-tuple-element.38.own_a, bf16[2,24,64,128]{3,2,1,0:T(8,128)(2,1)S(1)} %collective-permute-done.5.near_a, ...), custom_call_target="tpu_custom_call" | custom-call | flops 2300000000 | bytes 5505024 | tf_op jit(solution)/shard_map/gelu/pallas_call | solution.py:50
  74.4 0.4 collective-permute-start.14
  74.9 0.0 collective-permute-start.13
  74.9 5.7 %rows_to_units.1 = bf16[256,3072]{1,0:T(8,128)(2,1)} custom-call(bf16[2,256,128]{2,1,0:T(8,128)(2,1)S(1)} %fusion.4.select_ref, bf16[48,64,128]{2,1,0:T(8,128)(2,1)S(1)} %get-tuple-element.53.refs_0_, bf16[48,64,128]{2,1,0:T(8,128)(2,1)S(1)} %get-tuple-element.59.refs_1_), custom_call_target="tpu_custom_call" | custom-call | flops 6899999744 | bytes 3276800 | tf_op jit(solution)/shard_map/rows_to_units/pallas_call | solution.py:50
  80.6 8.4 %collective-permute-done.10.refs_2_.refs_3_.refs_4_ = bf16[48,64,128]{2,1,0:T(8,128)(2,1)S(1)} collective-permute-done((bf16[48,64,128]{2,1,0:T(8,128)(2,1)S(1)}, bf16[48,64,128]{2,1,0:T(8,128)(2,1)S(1)}, u32[]{:S(2)}, u32[]{:S(2)}) %collective-permute-start.10) | collective-permute-done | bytes 786464 | tf_op jit(solution)/shard_map/ppermute | solution.py:396
  89.0 0.8 slice.36
  89.8 0.0 collective-permute-start.12
  89.9 0.8 slice.28
  90.6 0.4 collective-permute-start.11
  91.1 14.8 %collective-permute-done.14.refs_2_.refs_3_.refs_5_ = bf16[48,64,128]{2,1,0:T(8,128)(2,1)S(1)} collective-permute-done((bf16[48,64,128]{2,1,0:T(8,128)(2,1)}, bf16[48,64,128]{2,1,0:T(8,128)(2,1)S(1)}, u32[]{:S(2)}, u32[]{:S(2)}) %collective-permute-start.14) | collective-permute-done | bytes 786464 | tf_op jit(solution)/shard_map/ppermute | solution.py:396
  105.9 0.1 collective-permute-start.16
  106.0 0.5 collective-permute-start.15
  106.5 6.8 %collective-permute-done.12.refs_4_.refs_5_.refs_6_ = bf16[24,64,128]{2,1,0:T(8,128)(2,1)} collective-permute-done((bf16[24,64,128]{2,1,0:T(8,128)(2,1)}, bf16[24,64,128]{2,1,0:T(8,128)(2,1)}, u32[]{:S(2)}, u32[]{:S(2)}) %collective-permute-start.12) | collective-permute-done | bytes 393248 | tf_op jit(solution)/shard_map/ppermute | solution.py:396
  113.4 1.0 collective-permute-done.11.refs_3_.refs_4_.refs_5_
  114.4 1.1 copy-done.3
  115.5 1.5 copy-done.12
  117.0 1.5 copy-done.14
  118.5 3.4 %backward.2 = bf16[128,3072]{1,0:T(8,128)(2,1)S(1)} custom-call(s32[3]{0:T(128)S(1)} %pad_add_fusion.facts_ref, s32[432]{0:T(512)S(1)} %bitcast.52, s32[432]{0:T(512)S(1)} %bitcast.60, bf16[216,32,128]{2,1,0:T(8,128)(2,1)S(1)} %copy-done.12, bf16[216,32,128]{2,1,0:T(8,128)(2,1)S(1)} %copy-done.14, bf16[48,64,128]{2,1,0:T(8,128)(2,1)S(1)} %copy-done.3, ...), custom_call_target="tpu_custom_call" | custom-call | flops 8049999872 | bytes 7474572 | tf_op jit(solution)/shard_map/backward/pallas_call | solution.py:50
  121.9 0.1 dynamic-slice_bitcast_fusion.7
  122.0 3.7 %collective-permute-start.19 = (bf16[32,3072]{1,0:T(8,128)(2,1)S(1)}, bf16[32,3072]{1,0:T(8,128)(2,1)S(1)}, u32[]{:S(2)}, u32[]{:S(2)}) collective-permute-start(bf16[32,3072]{1,0:T(8,128)(2,1)S(1)} %get-tuple-element.72), channel_id=1, source_target_pairs={{0,12},{4,0},{8,4},{12,8},{1,13},{5,1},{9,5},{13,9},{2,14},{6,2},{... | collective-permute-start | bytes 589832 | tf_op jit(solution)/shard_map/ppermute | solution.py:440
  125.7 1.6 collective-permute-start.17
  127.3 2.3 %outer_other.2 = bf16[216,32,128]{2,1,0:T(8,128)(2,1)S(1)} custom-call(s32[3]{0:T(128)S(1)} %pad_add_fusion.facts_ref, s32[432]{0:T(512)S(1)} %bitcast.53, s32[432]{0:T(512)S(1)} %bitcast.61, bf16[48,64,128]{2,1,0:T(8,128)(2,1)S(1)} %copy-done.10, bf16[48,64,128]{2,1,0:T(8,128)(2,1)S(1)} %copy-done.4, ...), custom_call_target="tpu_custom_call" | custom-call | flops 5750000128 | bytes 5705100 | tf_op jit(solution)/shard_map/outer_other/pallas_call | solution.py:50
  129.6 0.2 collective-permute-start.20
  129.8 3.3 %backward.3 = bf16[128,3072]{1,0:T(8,128)(2,1)S(1)} custom-call(s32[3]{0:T(128)S(1)} %pad_add_fusion.facts_ref, s32[432]{0:T(512)S(1)} %bitcast.54, s32[432]{0:T(512)S(1)} %bitcast.62, bf16[216,32,128]{2,1,0:T(8,128)(2,1)S(1)} %copy-done.12, bf16[216,32,128]{2,1,0:T(8,128)(2,1)S(1)} %copy-done.15, ...), custom_call_target="tpu_custom_call" | custom-call | flops 8049999872 | bytes 7474572 | tf_op jit(solution)/shard_map/backward/pallas_call | solution.py:50
  133.1 3.7 %collective-permute-done.18 = bf16[32,3072]{1,0:T(8,128)(2,1)S(1)} collective-permute-done((bf16[32,3072]{1,0:T(8,128)(2,1)S(1)}, bf16[32,3072]{1,0:T(8,128)(2,1)S(1)}, u32[]{:S(2)}, u32[]{:S(2)}) %collective-permute-start.18) | collective-permute-done | bytes 196640 | tf_op jit(solution)/shard_map/ppermute | solution.py:440
  136.8 5.8 %collective-permute-done.17 = bf16[32,3072]{1,0:T(8,128)(2,1)S(1)} collective-permute-done((bf16[32,3072]{1,0:T(8,128)(2,1)S(1)}, bf16[32,3072]{1,0:T(8,128)(2,1)S(1)}, u32[]{:S(2)}, u32[]{:S(2)}) %collective-permute-start.17) | collective-permute-done | bytes 196640 | tf_op jit(solution)/shard_map/ppermute | solution.py:440
  142.6 0.8 add_convert_fusion.1
  143.4 2.2 %outer_other.3 = bf16[216,32,128]{2,1,0:T(8,128)(2,1)S(1)} custom-call(s32[3]{0:T(128)S(1)} %pad_add_fusion.facts_ref, s32[432]{0:T(512)S(1)} %bitcast.55, s32[432]{0:T(512)S(1)} %bitcast.63, bf16[48,64,128]{2,1,0:T(8,128)(2,1)S(1)} %copy-done.8, bf16[48,64,128]{2,1,0:T(8,128)(2,1)} %get-tuple-element.63.refs_0_.refs_1_.refs_3_, ...), custom_call_target="tpu_custom_call" | custom-call | flops 5750000128 | bytes 5705100 | tf_op jit(solution)/shard_map/outer_other/pallas_call | solution.py:50
  145.6 0.1 collective-permute-start.21
  145.7 0.8 dynamic-slice_bitcast_fusion.3
  146.5 5.2 %collective-permute-start.24 = (bf16[32,3072]{1,0:T(8,128)(2,1)}, bf16[32,3072]{1,0:T(8,128)(2,1)}, u32[]{:S(2)}, u32[]{:S(2)}) collective-permute-start(bf16[32,3072]{1,0:T(8,128)(2,1)} %get-tuple-element.76), channel_id=1, source_target_pairs={{0,12},{4,0},{8,4},{12,8},{1,13},{5,1},{9,5},{13,9},{2,14},{6,2},{... | collective-permute-start | bytes 589832 | tf_op jit(solution)/shard_map/ppermute | solution.py:440
  151.7 0.6 collective-permute-start.22
  152.3 4.0 %outer_own.2.refs_0_ = bf16[216,32,128]{2,1,0:T(8,128)(2,1)S(1)} custom-call(s32[3]{0:T(128)S(1)} %pad_add_fusion.facts_ref, s32[432]{0:T(512)S(1)} %bitcast.56, s32[432]{0:T(512)S(1)} %bitcast.64, bf16[216,32,128]{2,1,0:T(8,128)(2,1)S(1)} %collective-permute-done.20.refs_0_, bf16[48,64,128]{2,1,0:T(8,128)(2,1)S(1)} %copy-done.10, ...), custom_call_target="tpu_custom_call" | custom-call | flops 5750000128 | bytes 7474572 | tf_op jit(solution)/shard_map/outer_own/pallas_call | solution.py:50
  156.3 3.8 %outer_own.3 = bf16[216,32,128]{2,1,0:T(8,128)(2,1)S(1)} custom-call(s32[3]{0:T(128)S(1)} %pad_add_fusion.facts_ref, s32[432]{0:T(512)S(1)} %bitcast.57, s32[432]{0:T(512)S(1)} %bitcast.65, bf16[216,32,128]{2,1,0:T(8,128)(2,1)S(1)} %outer_own.2.refs_0_, bf16[216,32,128]{2,1,0:T(8,128)(2,1)S(1)} %collective-permute-done.21.refs_1_, ...), custom_call_target="tpu_custom_call" | custom-call | flops 5750000128 | bytes 9244044 | tf_op jit(solution)/shard_map/outer_own/pallas_call | solution.py:50
  160.2 2.2 %reshape.134 = bf16[1,1,216,4096]{3,2,1,0:T(8,128)(2,1)} reshape(bf16[216,32,128]{2,1,0:T(8,128)(2,1)S(1)} %outer_own.3) | data formatting | bytes 3538944 | tf_op jit(solution)/shard_map/reshape | solution.py:466
  162.3 5.8 %collective-permute-done.22 = bf16[32,3072]{1,0:T(8,128)(2,1)} collective-permute-done((bf16[32,3072]{1,0:T(8,128)(2,1)}, bf16[32,3072]{1,0:T(8,128)(2,1)}, u32[]{:S(2)}, u32[]{:S(2)}) %collective-permute-start.22) | collective-permute-done | bytes 196640 | tf_op jit(solution)/shard_map/ppermute | solution.py:440
  168.2 1.2 add_convert_fusion
  169.4 0.8 pad_maximum_fusion
  (54 shorter events, 0.4 us)
Async XLA Ops:
  0.6 3.4 %copy-start = (bf16[256,3072]{1,0:T(8,128)(2,1)S(1)}, bf16[256,3072]{1,0:T(8,128)(2,1)}, u32[]{:S(2)}) copy-start(bf16[256,3072]{1,0:T(8,128)(2,1)} %values_ref.2) | copy-start | bytes 4718596
  2.6 5.5 %collective-permute-start = (bf16[216,32,128]{2,1,0:T(8,128)(2,1)S(1)}, bf16[216,32,128]{2,1,0:T(8,128)(2,1)}, u32[]{:S(2)}, u32[]{:S(2)}) collective-permute-start(bf16[216,32,128]{2,1,0:T(8,128)(2,1)S(1)} %bitcast.44), channel_id=1, source_target_pairs={{0,16},{16,0},{1,17},{17,1},{2,18},{18,2},{3,19},{19,3},{4,20},{20... | collective-permute-start | bytes 5308424 | tf_op jit(solution)/shard_map/ppermute | solution.py:399
  4.0 4.1 %copy-start.5 = (s32[1,1,432]{2,1,0:T(1,128)S(1)}, s32[1,1,432]{2,1,0:T(1,128)}, u32[]{:S(2)}) copy-start(s32[1,1,432]{2,1,0:T(1,128)} %param.8) | copy-start | bytes 5188
  4.0 4.1 %copy-start.6 = (s32[1,1,432]{2,1,0:T(1,128)S(1)}, s32[1,1,432]{2,1,0:T(1,128)}, u32[]{:S(2)}) copy-start(s32[1,1,432]{2,1,0:T(1,128)} %param.9) | copy-start | bytes 5188
  8.1 4.1 %copy-start.9 = (bf16[48,64,128]{2,1,0:T(8,128)(2,1)}, bf16[48,64,128]{2,1,0:T(8,128)(2,1)S(1)}, u32[]{:S(2)}) copy-start(bf16[48,64,128]{2,1,0:T(8,128)(2,1)S(1)} %get-tuple-element.68.table_ref.refs_0_.refs_1_) | copy-start | bytes 2359300
  8.1 10.4 %copy-start.7 = (bf16[48,64,128]{2,1,0:T(8,128)(2,1)}, bf16[48,64,128]{2,1,0:T(8,128)(2,1)S(1)}, u32[]{:S(2)}) copy-start(bf16[48,64,128]{2,1,0:T(8,128)(2,1)S(1)} %get-tuple-element.69.table_ref.refs_0_.refs_2_) | copy-start | bytes 2359300
  12.2 24.3 %collective-permute-start.1 = (bf16[2,24,64,128]{3,2,1,0:T(8,128)(2,1)S(1)}, bf16[2,24,64,128]{3,2,1,0:T(8,128)(2,1)S(1)}, u32[]{:S(2)}, u32[]{:S(2)}) collective-permute-start(bf16[2,24,64,128]{3,2,1,0:T(8,128)(2,1)S(1)} %get-tuple-element.48), channel_id=1, source_target_pairs={{0,1},{1,0},{2,3},{3,2},{4,5},{5,4},{6,7},{7,6},{8,9},{9,8},{10,11... | collective-permute-start | bytes 2359304 | tf_op jit(solution)/shard_map/ppermute | solution.py:396
  18.1 20.4 %collective-permute-start.3 = (bf16[2,24,64,128]{3,2,1,0:T(8,128)(2,1)S(1)}, bf16[2,24,64,128]{3,2,1,0:T(8,128)(2,1)S(1)}, u32[]{:S(2)}, u32[]{:S(2)}) collective-permute-start(bf16[2,24,64,128]{3,2,1,0:T(8,128)(2,1)S(1)} %get-tuple-element.51), channel_id=1, source_target_pairs={{0,2},{1,3},{2,0},{3,1},{4,6},{5,7},{6,4},{7,5},{8,10},{9,11},{10,... | collective-permute-start | bytes 2359304 | tf_op jit(solution)/shard_map/ppermute | solution.py:396
  18.5 7.8 %copy-start.1 = (bf16[256,3072]{1,0:T(8,128)(2,1)S(1)}, bf16[256,3072]{1,0:T(8,128)(2,1)}, u32[]{:S(2)}) copy-start(bf16[256,3072]{1,0:T(8,128)(2,1)} %values_ref.3) | copy-start | bytes 4718596
  22.3 31.0 %collective-permute-start.5 = (bf16[2,24,64,128]{3,2,1,0:T(8,128)(2,1)S(1)}, bf16[2,24,64,128]{3,2,1,0:T(8,128)(2,1)S(1)}, u32[]{:S(2)}, u32[]{:S(2)}) collective-permute-start(bf16[2,24,64,128]{3,2,1,0:T(8,128)(2,1)S(1)} %get-tuple-element.54), channel_id=1, source_target_pairs={{0,1},{1,0},{2,3},{3,2},{4,5},{5,4},{6,7},{7,6},{8,9},{9,8},{10,11... | collective-permute-start | bytes 2359304 | tf_op jit(solution)/shard_map/ppermute | solution.py:396
  25.8 29.5 %collective-permute-start.7 = (bf16[2,24,64,128]{3,2,1,0:T(8,128)(2,1)S(1)}, bf16[2,24,64,128]{3,2,1,0:T(8,128)(2,1)S(1)}, u32[]{:S(2)}, u32[]{:S(2)}) collective-permute-start(bf16[2,24,64,128]{3,2,1,0:T(8,128)(2,1)S(1)} %get-tuple-element.57), channel_id=1, source_target_pairs={{0,2},{1,3},{2,0},{3,1},{4,6},{5,7},{6,4},{7,5},{8,10},{9,11},{10,... | collective-permute-start | bytes 2359304 | tf_op jit(solution)/shard_map/ppermute | solution.py:396
  36.5 27.9 %collective-permute-start.2 = (bf16[24,64,128]{2,1,0:T(8,128)(2,1)S(1)}, bf16[24,64,128]{2,1,0:T(8,128)(2,1)S(1)}, u32[]{:S(2)}, u32[]{:S(2)}) collective-permute-start(bf16[24,64,128]{2,1,0:T(8,128)(2,1)S(1)} %fusion.3), channel_id=1, source_target_pairs={{0,2},{1,3},{2,0},{3,1},{4,6},{5,7},{6,4},{7,5},{8,10},{9,11},{10,... | collective-permute-start | bytes 1179656 | tf_op jit(solution)/shard_map/ppermute | solution.py:396
  38.5 25.9 %collective-permute-start.4 = (bf16[24,64,128]{2,1,0:T(8,128)(2,1)S(1)}, bf16[24,64,128]{2,1,0:T(8,128)(2,1)S(1)}, u32[]{:S(2)}, u32[]{:S(2)}) collective-permute-start(bf16[24,64,128]{2,1,0:T(8,128)(2,1)S(1)} %fusion.2), channel_id=1, source_target_pairs={{0,1},{1,0},{2,3},{3,2},{4,5},{5,4},{6,7},{7,6},{8,9},{9,8},{10,11... | collective-permute-start | bytes 1179656 | tf_op jit(solution)/shard_map/ppermute | solution.py:396
  53.4 18.8 %collective-permute-start.6 = (bf16[24,64,128]{2,1,0:T(8,128)(2,1)S(1)}, bf16[24,64,128]{2,1,0:T(8,128)(2,1)S(1)}, u32[]{:S(2)}, u32[]{:S(2)}) collective-permute-start(bf16[24,64,128]{2,1,0:T(8,128)(2,1)S(1)} %fusion.1), channel_id=1, source_target_pairs={{0,2},{1,3},{2,0},{3,1},{4,6},{5,7},{6,4},{7,5},{8,10},{9,11},{10,... | collective-permute-start | bytes 1179656 | tf_op jit(solution)/shard_map/ppermute | solution.py:396
  55.4 16.8 %collective-permute-start.8 = (bf16[24,64,128]{2,1,0:T(8,128)(2,1)S(1)}, bf16[24,64,128]{2,1,0:T(8,128)(2,1)S(1)}, u32[]{:S(2)}, u32[]{:S(2)}) collective-permute-start(bf16[24,64,128]{2,1,0:T(8,128)(2,1)S(1)} %fusion), channel_id=1, source_target_pairs={{0,1},{1,0},{2,3},{3,2},{4,5},{5,4},{6,7},{7,6},{8,9},{9,8},{10,11... | collective-permute-start | bytes 1179656 | tf_op jit(solution)/shard_map/ppermute | solution.py:396
  63.2 1.2 copy-start.11
  64.4 1.4 copy-start.13
  65.8 8.6 %copy-start.2 = (bf16[48,64,128]{2,1,0:T(8,128)(2,1)}, bf16[48,64,128]{2,1,0:T(8,128)(2,1)S(1)}, u32[]{:S(2)}) copy-start(bf16[48,64,128]{2,1,0:T(8,128)(2,1)S(1)} %get-tuple-element.61.refs_0_.refs_1_.refs_2_) | copy-start | bytes 2359300
  65.8 23.2 %collective-permute-start.10 = (bf16[48,64,128]{2,1,0:T(8,128)(2,1)S(1)}, bf16[48,64,128]{2,1,0:T(8,128)(2,1)S(1)}, u32[]{:S(2)}, u32[]{:S(2)}) collective-permute-start(bf16[48,64,128]{2,1,0:T(8,128)(2,1)S(1)} %get-tuple-element.61.refs_0_.refs_1_.refs_2_), channel_id=1, source_target_pairs={{0,2},{1,3},{2,0},{3,1},{4,6},{5,7},{6,4},{7,5},{8,10},{9,11},{10,... | collective-permute-start | bytes 2359304 | tf_op jit(solution)/shard_map/ppermute | solution.py:396
  67.5 22.4 %collective-permute-start.9 = (bf16[48,64,128]{2,1,0:T(8,128)(2,1)S(1)}, bf16[48,64,128]{2,1,0:T(8,128)(2,1)S(1)}, u32[]{:S(2)}, u32[]{:S(2)}) collective-permute-start(bf16[48,64,128]{2,1,0:T(8,128)(2,1)S(1)} %get-tuple-element.61.refs_0_.refs_1_.refs_2_), channel_id=1, source_target_pairs={{0,1},{1,0},{2,3},{3,2},{4,5},{5,4},{6,7},{7,6},{8,9},{9,8},{10,11... | collective-permute-start | bytes 2359304 | tf_op jit(solution)/shard_map/ppermute | solution.py:396
  74.4 31.5 %collective-permute-start.14 = (bf16[48,64,128]{2,1,0:T(8,128)(2,1)}, bf16[48,64,128]{2,1,0:T(8,128)(2,1)S(1)}, u32[]{:S(2)}, u32[]{:S(2)}) collective-permute-start(bf16[48,64,128]{2,1,0:T(8,128)(2,1)} %get-tuple-element.63.refs_0_.refs_1_.refs_3_), channel_id=1, source_target_pairs={{0,2},{1,3},{2,0},{3,1},{4,6},{5,7},{6,4},{7,5},{8,10},{9,11},{10,... | collective-permute-start | bytes 2359304 | tf_op jit(solution)/shard_map/ppermute | solution.py:396
  74.9 31.2 %collective-permute-start.13 = (bf16[48,64,128]{2,1,0:T(8,128)(2,1)}, bf16[48,64,128]{2,1,0:T(8,128)(2,1)S(1)}, u32[]{:S(2)}, u32[]{:S(2)}) collective-permute-start(bf16[48,64,128]{2,1,0:T(8,128)(2,1)} %get-tuple-element.63.refs_0_.refs_1_.refs_3_), channel_id=1, source_target_pairs={{0,1},{1,0},{2,3},{3,2},{4,5},{5,4},{6,7},{7,6},{8,9},{9,8},{10,11... | collective-permute-start | bytes 2359304 | tf_op jit(solution)/shard_map/ppermute | solution.py:396
  89.8 23.5 %collective-permute-start.12 = (bf16[24,64,128]{2,1,0:T(8,128)(2,1)}, bf16[24,64,128]{2,1,0:T(8,128)(2,1)}, u32[]{:S(2)}, u32[]{:S(2)}) collective-permute-start(bf16[24,64,128]{2,1,0:T(8,128)(2,1)} %slice.36), channel_id=1, source_target_pairs={{0,1},{1,0},{2,3},{3,2},{4,5},{5,4},{6,7},{7,6},{8,9},{9,8},{10,11... | collective-permute-start | bytes 1179656 | tf_op jit(solution)/shard_map/ppermute | solution.py:396
  90.6 23.8 %collective-permute-start.11 = (bf16[24,64,128]{2,1,0:T(8,128)(2,1)}, bf16[24,64,128]{2,1,0:T(8,128)(2,1)}, u32[]{:S(2)}, u32[]{:S(2)}) collective-permute-start(bf16[24,64,128]{2,1,0:T(8,128)(2,1)} %slice.28), channel_id=1, source_target_pairs={{0,2},{1,3},{2,0},{3,1},{4,6},{5,7},{6,4},{7,5},{8,10},{9,11},{10,... | collective-permute-start | bytes 1179656 | tf_op jit(solution)/shard_map/ppermute | solution.py:396
  105.9 23.9 %collective-permute-start.16 = (bf16[24,64,128]{2,1,0:T(8,128)(2,1)S(1)}, bf16[24,64,128]{2,1,0:T(8,128)(2,1)S(1)}, u32[]{:S(2)}, u32[]{:S(2)}) collective-permute-start(bf16[24,64,128]{2,1,0:T(8,128)(2,1)S(1)} %slice.38), channel_id=1, source_target_pairs={{0,1},{1,0},{2,3},{3,2},{4,5},{5,4},{6,7},{7,6},{8,9},{9,8},{10,11... | collective-permute-start | bytes 1179656 | tf_op jit(solution)/shard_map/ppermute | solution.py:396
  106.0 23.6 %collective-permute-start.15 = (bf16[24,64,128]{2,1,0:T(8,128)(2,1)S(1)}, bf16[24,64,128]{2,1,0:T(8,128)(2,1)S(1)}, u32[]{:S(2)}, u32[]{:S(2)}) collective-permute-start(bf16[24,64,128]{2,1,0:T(8,128)(2,1)S(1)} %slice.37), channel_id=1, source_target_pairs={{0,2},{1,3},{2,0},{3,1},{4,6},{5,7},{6,4},{7,5},{8,10},{9,11},{10,... | collective-permute-start | bytes 1179656 | tf_op jit(solution)/shard_map/ppermute | solution.py:396
  114.4 1.1 copy-start.3
  115.5 1.5 copy-start.12
  117.0 1.5 copy-start.14
  118.5 8.8 %copy-start.4 = (bf16[48,64,128]{2,1,0:T(8,128)(2,1)S(1)}, bf16[48,64,128]{2,1,0:T(8,128)(2,1)}, u32[]{:S(2)}) copy-start(bf16[48,64,128]{2,1,0:T(8,128)(2,1)} %copy-done.2) | copy-start | bytes 2359300
  118.5 8.8 %copy-start.10 = (bf16[48,64,128]{2,1,0:T(8,128)(2,1)S(1)}, bf16[48,64,128]{2,1,0:T(8,128)(2,1)}, u32[]{:S(2)}) copy-start(bf16[48,64,128]{2,1,0:T(8,128)(2,1)} %copy-done.9) | copy-start | bytes 2359300
  122.0 11.1 %collective-permute-start.19 = (bf16[32,3072]{1,0:T(8,128)(2,1)S(1)}, bf16[32,3072]{1,0:T(8,128)(2,1)S(1)}, u32[]{:S(2)}, u32[]{:S(2)}) collective-permute-start(bf16[32,3072]{1,0:T(8,128)(2,1)S(1)} %get-tuple-element.72), channel_id=1, source_target_pairs={{0,12},{4,0},{8,4},{12,8},{1,13},{5,1},{9,5},{13,9},{2,14},{6,2},{... | collective-permute-start | bytes 589832 | tf_op jit(solution)/shard_map/ppermute | solution.py:440
  125.7 11.2 %collective-permute-start.18 = (bf16[32,3072]{1,0:T(8,128)(2,1)S(1)}, bf16[32,3072]{1,0:T(8,128)(2,1)S(1)}, u32[]{:S(2)}, u32[]{:S(2)}) collective-permute-start(bf16[32,3072]{1,0:T(8,128)(2,1)S(1)} %get-tuple-element.73), channel_id=1, source_target_pairs={{0,4},{4,8},{8,12},{12,0},{1,5},{5,9},{9,13},{13,1},{2,6},{6,10},{... | collective-permute-start | bytes 589832 | tf_op jit(solution)/shard_map/ppermute | solution.py:440
  125.7 4.2 %copy-start.15 = (bf16[216,32,128]{2,1,0:T(8,128)(2,1)S(1)}, bf16[216,32,128]{2,1,0:T(8,128)(2,1)}, u32[]{:S(2)}) copy-start(bf16[216,32,128]{2,1,0:T(8,128)(2,1)} %copy-done.13) | copy-start | bytes 5308420
  125.7 16.9 %collective-permute-start.17 = (bf16[32,3072]{1,0:T(8,128)(2,1)S(1)}, bf16[32,3072]{1,0:T(8,128)(2,1)S(1)}, u32[]{:S(2)}, u32[]{:S(2)}) collective-permute-start(bf16[32,3072]{1,0:T(8,128)(2,1)S(1)} %get-tuple-element.74), channel_id=1, source_target_pairs={{0,8},{4,12},{8,0},{12,4},{1,9},{5,13},{9,1},{13,5},{2,10},{6,14},... | collective-permute-start | bytes 589832 | tf_op jit(solution)/shard_map/ppermute | solution.py:440
  129.6 13.8 %copy-start.8 = (bf16[48,64,128]{2,1,0:T(8,128)(2,1)S(1)}, bf16[48,64,128]{2,1,0:T(8,128)(2,1)}, u32[]{:S(2)}) copy-start(bf16[48,64,128]{2,1,0:T(8,128)(2,1)} %copy-done.7) | copy-start | bytes 2359300
  129.6 22.7 %collective-permute-start.20 = (bf16[216,32,128]{2,1,0:T(8,128)(2,1)S(1)}, bf16[216,32,128]{2,1,0:T(8,128)(2,1)S(1)}, u32[]{:S(2)}, u32[]{:S(2)}) collective-permute-start(bf16[216,32,128]{2,1,0:T(8,128)(2,1)S(1)} %outer_other.2), channel_id=1, source_target_pairs={{0,16},{16,0},{1,17},{17,1},{2,18},{18,2},{3,19},{19,3},{4,20},{20... | collective-permute-start | bytes 5308424 | tf_op jit(solution)/shard_map/ppermute | solution.py:399
  145.6 10.7 %collective-permute-start.21 = (bf16[216,32,128]{2,1,0:T(8,128)(2,1)S(1)}, bf16[216,32,128]{2,1,0:T(8,128)(2,1)S(1)}, u32[]{:S(2)}, u32[]{:S(2)}) collective-permute-start(bf16[216,32,128]{2,1,0:T(8,128)(2,1)S(1)} %outer_other.3), channel_id=1, source_target_pairs={{0,16},{16,0},{1,17},{17,1},{2,18},{18,2},{3,19},{19,3},{4,20},{20... | collective-permute-start | bytes 5308424 | tf_op jit(solution)/shard_map/ppermute | solution.py:399
  146.5 15.8 %collective-permute-start.24 = (bf16[32,3072]{1,0:T(8,128)(2,1)}, bf16[32,3072]{1,0:T(8,128)(2,1)}, u32[]{:S(2)}, u32[]{:S(2)}) collective-permute-start(bf16[32,3072]{1,0:T(8,128)(2,1)} %get-tuple-element.76), channel_id=1, source_target_pairs={{0,12},{4,0},{8,4},{12,8},{1,13},{5,1},{9,5},{13,9},{2,14},{6,2},{... | collective-permute-start | bytes 589832 | tf_op jit(solution)/shard_map/ppermute | solution.py:440
  151.7 10.6 %collective-permute-start.23 = (bf16[32,3072]{1,0:T(8,128)(2,1)}, bf16[32,3072]{1,0:T(8,128)(2,1)}, u32[]{:S(2)}, u32[]{:S(2)}) collective-permute-start(bf16[32,3072]{1,0:T(8,128)(2,1)} %get-tuple-element.77), channel_id=1, source_target_pairs={{0,4},{4,8},{8,12},{12,0},{1,5},{5,9},{9,13},{13,1},{2,6},{6,10},{... | collective-permute-start | bytes 589832 | tf_op jit(solution)/shard_map/ppermute | solution.py:440
  151.7 16.4 %collective-permute-start.22 = (bf16[32,3072]{1,0:T(8,128)(2,1)}, bf16[32,3072]{1,0:T(8,128)(2,1)}, u32[]{:S(2)}, u32[]{:S(2)}) collective-permute-start(bf16[32,3072]{1,0:T(8,128)(2,1)} %get-tuple-element.78), channel_id=1, source_target_pairs={{0,8},{4,12},{8,0},{12,4},{1,9},{5,13},{9,1},{13,5},{2,10},{6,14},... | collective-permute-start | bytes 589832 | tf_op jit(solution)/shard_map/ppermute | solution.py:440
  160.1 9.2 %copy-start.16 = (bf16[32,3072]{1,0:T(8,128)(2,1)S(1)}, bf16[32,3072]{1,0:T(8,128)(2,1)}, u32[]{:S(2)}) copy-start(bf16[32,3072]{1,0:T(8,128)(2,1)} %add_convert_fusion.1) | copy-start | bytes 589828

commit v2 on v1

--- a/solution.py
+++ b/solution.py
@@ -55,7 +55,9 @@
         scratch_shapes=list(scratch),
         name=name,
         compiler_params=pltpu.CompilerParams(vmem_limit_bytes=mib * MIB),
-        cost_estimate=pl.CostEstimate(flops=microseconds * FLOPS_PER_US, bytes_accessed=moved, transcendentals=0),
+        cost_estimate=pl.CostEstimate(
+            flops=microseconds * FLOPS_PER_US, bytes_accessed=moved if microseconds else 0, transcendentals=0
+        ),
         **more,
     )(*operands)
 
@@ -409,17 +411,20 @@
     upstream[0] = after(upstream[0], own_t)
 
     grads, acts = [], []
+    from_x = from_y = None
     for chunk in range(CHUNKS):
         along_x, along_y, own_a, own_b, relay_x, relay_y = partials[chunk]
+        if chunk:
+            along_x, along_y = after(along_x, from_x), after(along_y, from_y)
         from_x, from_y = across(along_x, 1), across(along_y, 2)
-        last_a = across(relay_y + from_x[0], 2)
-        last_b = across(relay_x + from_y[0], 1)
+        sum_y, sum_x = relay_y + from_x[0], relay_x + from_y[0]
+        if chunk:
+            sum_y, sum_x = after(sum_y, grads[0][1]), after(sum_x, grads[0][2])
+        last_a, last_b = across(sum_y, 2), across(sum_x, 1)
         grad, act = gelu(upstream[chunk], (own_a, from_x, last_a, own_b, from_y, last_b))
         acts.append(act)
         grads.append([grad, across(grad, 1), across(grad, 2)])
 
-    activation = rows_to_units(select, acts)
-    grads[0][1] = after(grads[0][1], activation)
     for chunk in range(CHUNKS):
         grad, grad_x, grad_y = grads[chunk]
         far_a = across(grad_x[: share_blocks // 2], 2)
@@ -428,20 +433,22 @@
 
     me_row = lax.axis_index("row")
 
+    def take(values, index):
+        return lax.dynamic_index_in_dim(values, index, 0, keepdims=False)
+
     def to_rows(partial):
-        pieces = partial.reshape(row_devices, part, in_blocks * BLOCK)
-        mine = lax.dynamic_index_in_dim(pieces, me_row, 0, keepdims=False)
         if row_devices != 4:
-            return [lax.psum_scatter(partial, "row", scatter_dimension=0, tiled=True)]
-        moved = []
-        for shift in (2, 1, 3):
-            piece = lax.dynamic_index_in_dim(pieces, (me_row + shift) % row_devices, 0, keepdims=False)
-            pairs = [(place, (place + shift) % row_devices) for place in range(row_devices)]
-            moved.append(lax.ppermute(piece, "row", pairs))
-        return [mine] + moved
+            return [lax.psum_scatter(partial, "row", scatter_dimension=0, tiled=True)], partial, partial
+        low, high = me_row & 1, me_row >> 1
+        pieces = partial.reshape(2, 2, part, in_blocks * BLOCK)
+        sent, kept = (lax.dynamic_index_in_dim(pieces, bit, 1, keepdims=False) for bit in (1 - low, low))
+        moved = lax.ppermute(sent, "row", [(place, place ^ 1) for place in range(4)])
+        both = take(kept, 1 - high).astype(jnp.float32) + take(moved, 1 - high).astype(jnp.float32)
+        last = lax.ppermute(both.astype(jnp.bfloat16), "row", [(place, place ^ 2) for place in range(4)])
+        return [last, take(kept, high), take(moved, high)], both, sent
 
     def add_up(parts, earlier):
-        parts = [after(parts[0], earlier)] + parts[1:]
+        parts = [*parts[:-1], after(parts[-1], earlier)]
         return sum(part.astype(jnp.float32) for part in parts).astype(jnp.bfloat16)
 
     def input_sums(chunk):
@@ -452,15 +459,16 @@
         return outer(facts, rows, cols, table, grads[chunk], share_blocks, half_slots, mine, added)
 
     first = input_sums(0)
-    row_parts = to_rows(first)
-    other_first = tile_part(0, first, False, [])
-    grads[1][3] = after(grads[1][3], other_first)
+    row_parts, halfway, sent = to_rows(first)
+    activation = rows_to_units(after(select, first), acts)
+    other_first = tile_part(0, activation, False, [])
+    *first_parts, grads[1][4] = lax.optimization_barrier((*row_parts, after(grads[1][4], other_first)))
     second = input_sums(1)
-    first_sum = add_up(row_parts, second)
-    row_parts = to_rows(second)
-    other_second = tile_part(1, first_sum, False, [])
-    own_first = tile_part(0, other_second, True, [other_core(other_first)])
+    row_parts, halfway, sent = to_rows(second)
+    own_first = tile_part(0, sent, True, [other_core(other_first)])
+    other_second = tile_part(1, after(halfway, own_first), False, [])
     own_second = tile_part(1, other_second, True, [own_first, other_core(other_second)])
+    first_sum = add_up(first_parts, other_second)
     second_sum = add_up(row_parts, own_second)
     input_grad = jnp.concatenate([first_sum, second_sum], axis=0)
     tile_grads = own_second.reshape(1, 1, half_slots, 4096)

time: 172 us -> 175 us (1.017)
  starting transfers between devices: 27.9 us -> 39.6 us
  waiting for transfers between devices: 74 us -> 63.6 us
  other arithmetic: 3.13 us -> 5.24 us
  Pallas kernels: 51.6 us -> 49.6 us
    ppermute x16, starting transfers between devices: 16 us -> 33 us  [across(): lax.ppermute(values, 'col', [(place, place ^ bit) for place in range(shar...]
    ppermute x6 -> x4, waiting for transfers between devices: 15.3 us -> 8.45 us  [the longest x2 7.35 us: to_rows(): lax.ppermute(sent, 'row', [(place, place ^ 1) for place in range(4)])]
    ppermute x6 -> x4, starting transfers between devices: 11.1 us -> 5.01 us  [the longest x2 2.75 us: to_rows(): lax.ppermute(both.astype(jnp.bfloat16), 'row', [(place, place ^ 2) for pl...]
    ppermute x16, waiting for transfers between devices: 58.7 us -> 55.2 us  [across(): lax.ppermute(values, 'col', [(place, place ^ bit) for place in range(shar...]
    pallas_call x14, Pallas kernels: 51.6 us -> 49.6 us  [call(): pl.pallas_call(kernel, out_shape=out_shape, in_specs=in_specs, out_specs=...]
    unnamed x35 -> x49, local copies, waits for them, and re-layouts: 7.3 us -> 8.79 us
  transfers between devices with their start and end apart: 25 -> 23, of which waited for: 12 -> 10; matrix products, arithmetic and copies ran while one was open for 3% -> 5% of each run, Pallas kernels for 28% -> 26%
where the time goes in v2:
time: 175 us; the launch traced here: 173 us
  waiting for transfers between devices  63.6 us (36%)
  Pallas kernels  49.6 us (28%)
  starting transfers between devices  39.6 us (23%)
  local copies, waits for them, and re-layouts  13.4 us (8%)
  other arithmetic  5.24 us (3%)
    ppermute x16, waiting for transfers between devices, across(): lax.ppermute(values, 'col', [(place, place ^ bit) for place in range(shar...  55.2 us
    pallas_call x14, Pallas kernels, call(): pl.pallas_call(kernel, out_shape=out_shape, in_specs=in_specs, out_specs=...  49.6 us
    ppermute x16, starting transfers between devices, across(): lax.ppermute(values, 'col', [(place, place ^ bit) for place in range(shar...  33 us
    unnamed x49, local copies, waits for them, and re-layouts  8.79 us
    ppermute x2, waiting for transfers between devices, to_rows(): lax.ppermute(sent, 'row', [(place, place ^ 1) for place in range(4)])  7.35 us
  transfers between devices with their start and end apart: 23, of which 10 were waited for; matrix products, arithmetic and copies ran while one was open for 5% of the time, Pallas kernels for 26%

profile of v2, /device:TPU:0, one launch (start us, length us, event | category | flops | bytes accessed | tf_op | source)
XLA Modules:
  0.0 173.2 jit_solution(7060469706149116681)
XLA Ops:
  0.6 2.0 %copy.9 = bf16[27,8,32,128]{3,2,1,0:T(8,128)(2,1)S(1)} copy(bf16[27,8,32,128]{3,1,2,0:T(8,128)(2,1)} %bitcast.79) | data formatting | bytes 3538944
  2.6 0.5 collective-permute-start
  3.8 0.1 pad_add_fusion.facts_ref
  3.9 0.1 add_add_fusion
  4.0 4.1 %features_to_rows.1 = (bf16[48,64,128]{2,1,0:T(8,128)(2,1)S(1)}, bf16[48,64,128]{2,1,0:T(8,128)(2,1)S(1)}) custom-call(bf16[256,3072]{1,0:T(8,128)(2,1)S(1)} %copy-done, bf16[2,256,128]{2,1,0:T(8,128)(2,1)S(1)} %fusion.8.select_ref), custom_call_target="tpu_custom_call" | custom-call | flops 5750000128 | bytes 3276800 | tf_op jit(solution)/shard_map/features_to_rows/pallas_call | solution.py:50
  8.2 4.0 %forward.3 = (bf16[2,24,64,128]{3,2,1,0:T(8,128)(2,1)S(1)}, bf16[2,24,64,128]{3,2,1,0:T(8,128)(2,1)S(1)}, bf16[24,64,128]{2,1,0:T(8,128)(2,1)S(1)}, bf16[24,64,1...) custom-call(s32[3]{0:T(128)S(1)} %pad_add_fusion.facts_ref, ...), custom_call_target="tpu_custom_call" | custom-call | flops 8049999872 | bytes 7474572 | tf_op jit(solution)/shard_map/forward/pallas_call | solution.py:50
  12.2 3.6 %collective-permute-start.1 = (bf16[2,24,64,128]{3,2,1,0:T(8,128)(2,1)S(1)}, bf16[2,24,64,128]{3,2,1,0:T(8,128)(2,1)S(1)}, u32[]{:S(2)}, u32[]{:S(2)}) collective-permute-start(bf16[2,24,64,128]{3,2,1,0:T(8,128)(2,1)S(1)} %get-tuple-element.56), channel_id=1, source_target_pairs={{0,1},{1,0},{2,3},{3,2},{4,5},{5,4},{6,7},{7,6},{8,9},{9,8},{10,11... | collective-permute-start | bytes 2359304 | tf_op jit(solution)/shard_map/ppermute | solution.py:398
  15.8 3.7 %forward.2 = (bf16[2,24,64,128]{3,2,1,0:T(8,128)(2,1)S(1)}, bf16[2,24,64,128]{3,2,1,0:T(8,128)(2,1)S(1)}, bf16[24,64,128]{2,1,0:T(8,128)(2,1)S(1)}, bf16[24,64,1...) custom-call(s32[3]{0:T(128)S(1)} %pad_add_fusion.facts_ref, ...), custom_call_target="tpu_custom_call" | custom-call | flops 8049999872 | bytes 7474572 | tf_op jit(solution)/shard_map/forward/pallas_call | solution.py:50
  19.5 0.7 copy-done.10
  20.2 0.8 copy-done.12
  21.0 6.4 %collective-permute-start.3 = (bf16[2,24,64,128]{3,2,1,0:T(8,128)(2,1)S(1)}, bf16[2,24,64,128]{3,2,1,0:T(8,128)(2,1)S(1)}, u32[]{:S(2)}, u32[]{:S(2)}) collective-permute-start(bf16[2,24,64,128]{3,2,1,0:T(8,128)(2,1)S(1)} %get-tuple-element.59), channel_id=1, source_target_pairs={{0,2},{1,3},{2,0},{3,1},{4,6},{5,7},{6,4},{7,5},{8,10},{9,11},{10,... | collective-permute-start | bytes 2359304 | tf_op jit(solution)/shard_map/ppermute | solution.py:398
  27.4 4.1 %units_to_rows.1 = (bf16[48,64,128]{2,1,0:T(8,128)(2,1)S(1)}, bf16[48,64,128]{2,1,0:T(8,128)(2,1)S(1)}) custom-call(bf16[256,3072]{1,0:T(8,128)(2,1)S(1)} %copy-done.1, bf16[2,256,128]{2,1,0:T(8,128)(2,1)S(1)} %fusion.8.select_ref), custom_call_target="tpu_custom_call" | custom-call | flops 5750000128 | bytes 3276800 | tf_op jit(solution)/shard_map/units_to_rows/pallas_call | solution.py:50
  31.5 0.9 copy-done.6
  32.5 1.6 collective-permute-done.1.near_a
  34.1 4.0 %collective-permute-start.2 = (bf16[24,64,128]{2,1,0:T(8,128)(2,1)S(1)}, bf16[24,64,128]{2,1,0:T(8,128)(2,1)S(1)}, u32[]{:S(2)}, u32[]{:S(2)}) collective-permute-start(bf16[24,64,128]{2,1,0:T(8,128)(2,1)S(1)} %fusion.3), channel_id=1, source_target_pairs={{0,2},{1,3},{2,0},{3,1},{4,6},{5,7},{6,4},{7,5},{8,10},{9,11},{10,... | collective-permute-start | bytes 1179656 | tf_op jit(solution)/shard_map/ppermute | solution.py:398
  38.1 7.7 %collective-permute-done.3.near_b = bf16[2,24,64,128]{3,2,1,0:T(8,128)(2,1)S(1)} collective-permute-done((bf16[2,24,64,128]{3,2,1,0:T(8,128)(2,1)S(1)}, bf16[2,24,64,128]{3,2,1,0:T(8,128)(2,1)S(1)}, u32[]{:S(2)}, u32[]{:S(2)}) %collective-permute-start.3) | collective-permute-done | bytes 786464 | tf_op jit(solution)/shard_map/ppermute | solution.py:398
  45.8 0.6 collective-permute-start.4
  46.4 1.5 collective-permute-start.9
  47.9 2.1 %collective-permute-start.11 = (bf16[2,24,64,128]{3,2,1,0:T(8,128)(2,1)S(1)}, bf16[2,24,64,128]{3,2,1,0:T(8,128)(2,1)S(1)}, u32[]{:S(2)}, u32[]{:S(2)}) collective-permute-start(bf16[2,24,64,128]{3,2,1,0:T(8,128)(2,1)S(1)} %get-tuple-element.70), channel_id=1, source_target_pairs={{0,2},{1,3},{2,0},{3,1},{4,6},{5,7},{6,4},{7,5},{8,10},{9,11},{10,... | collective-permute-start | bytes 2359304 | tf_op jit(solution)/shard_map/ppermute | solution.py:398
  50.0 7.3 %transpose_tiles.1 = (bf16[216,32,128]{2,1,0:T(8,128)(2,1)S(1)}, bf16[216,32,128]{2,1,0:T(8,128)(2,1)S(1)}) custom-call(bf16[216,32,128]{2,1,0:T(8,128)(2,1)S(1)} %bitcast.56, bf16[216,32,128]{2,1,0:T(8,128)(2,1)} %collective-permute-done.other_ref), custom_call_target="tpu_custom_call" | custom-call | flops 8049999872 | bytes 7077888 | tf_op jit(solution)/shard_map/transpose_tiles/pallas_call | solution.py:50
  57.3 1.2 copy-done.18
  58.5 1.4 gelu.2
  59.9 0.6 collective-permute-start.5
  60.4 1.5 collective-permute-start.6
  61.9 12.8 %collective-permute-done.9.near_a = bf16[2,24,64,128]{3,2,1,0:T(8,128)(2,1)S(1)} collective-permute-done((bf16[2,24,64,128]{3,2,1,0:T(8,128)(2,1)S(1)}, bf16[2,24,64,128]{3,2,1,0:T(8,128)(2,1)S(1)}, u32[]{:S(2)}, u32[]{:S(2)}) %collective-permute-start.9) | collective-permute-done | bytes 786464 | tf_op jit(solution)/shard_map/ppermute | solution.py:398
  74.8 0.8 fusion.1
  75.6 0.8 fusion
  76.4 13.4 %collective-permute-done.5.refs_1_.refs_2_.refs_3_ = bf16[48,64,128]{2,1,0:T(8,128)(2,1)S(1)} collective-permute-done((bf16[48,64,128]{2,1,0:T(8,128)(2,1)S(1)}, bf16[48,64,128]{2,1,0:T(8,128)(2,1)S(1)}, u32[]{:S(2)}, u32[]{:S(2)}) %collective-permute-start.5) | collective-permute-done | bytes 786464 | tf_op jit(solution)/shard_map/ppermute | solution.py:398
  89.9 1.4 collective-permute-start.10
  91.3 0.5 collective-permute-start.12
  91.9 0.8 slice.34
  92.6 0.6 collective-permute-start.7
  93.2 0.8 slice.35
  94.1 1.5 collective-permute-start.8
  95.5 6.7 %collective-permute-done.10.last_a = bf16[24,64,128]{2,1,0:T(8,128)(2,1)} collective-permute-done((bf16[24,64,128]{2,1,0:T(8,128)(2,1)}, bf16[24,64,128]{2,1,0:T(8,128)(2,1)}, u32[]{:S(2)}, u32[]{:S(2)}) %collective-permute-start.10) | collective-permute-done | bytes 393248 | tf_op jit(solution)/shard_map/ppermute | solution.py:398
  102.2 1.4 collective-permute-done.12.last_b
  103.7 1.1 copy-done.7
  104.8 1.0 copy-done.11
  105.8 1.0 copy-done.13
  106.8 2.6 %gelu.3 = (bf16[48,64,128]{2,1,0:T(8,128)(2,1)S(1)}, bf16[48,64,128]{2,1,0:T(8,128)(2,1)S(1)}) custom-call(bf16[48,64,128]{2,1,0:T(8,128)(2,1)S(1)} %copy-done.7, bf16[24,64,128]{2,1,0:T(8,128)(2,1)S(1)} %copy-done.11, bf16[2,24,64,128]{3,2,1,0:T(8,128)(2,1)S(1)} %collective-permute-done.9.near_a, bf16[24,64,128]{2,1,0:T(8,128)(2,1)} %collective-permute-done.10.last_a, ...), custom_call_target="tpu_custom_call" | custom-call | flops 2300000000 | bytes 5505024 | tf_op jit(solution)/shard_map/gelu/pallas_call | solution.py:50
  109.4 0.6 collective-permute-start.17
  110.0 0.6 collective-permute-start.15
  110.6 0.8 collective-permute-done.8.refs_4_.refs_5_.refs_6_
  111.4 3.7 %backward.2 = bf16[128,3072]{1,0:T(8,128)(2,1)S(1)} custom-call(s32[3]{0:T(128)S(1)} %pad_add_fusion.facts_ref, s32[432]{0:T(512)S(1)} %bitcast.65, s32[432]{0:T(512)S(1)} %bitcast.73, bf16[216,32,128]{2,1,0:T(8,128)(2,1)S(1)} %copy-done.19, bf16[216,32,128]{2,1,0:T(8,128)(2,1)S(1)} %copy-done.21, bf16[48,64,128]{2,1,0:T(8,128)(2,1)S(1)} %copy-done.3, ...), custom_call_target="tpu_custom_call" | custom-call | flops 8049999872 | bytes 7474572 | tf_op jit(solution)/shard_map/backward/pallas_call | solution.py:50
  115.2 2.2 %collective-permute-start.13 = (bf16[2,32,3072]{2,1,0:T(8,128)(2,1)S(1)}, bf16[2,32,3072]{2,1,0:T(8,128)(2,1)S(1)}, u32[]{:S(2)}, u32[]{:S(2)}) collective-permute-start(bf16[2,32,3072]{2,1,0:T(8,128)(2,1)S(1)} %dynamic-slice_bitcast_fusion.1), channel_id=1, source_target_pairs={{0,4},{4,0},{8,12},{12,8},{1,5},{5,1},{9,13},{13,9},{2,6},{6,2},{1... | collective-permute-start | bytes 1179656 | tf_op jit(solution)/shard_map/ppermute | solution.py:445
  117.4 5.7 %rows_to_units.1 = bf16[256,3072]{1,0:T(8,128)(2,1)} custom-call(bf16[2,256,128]{2,1,0:T(8,128)(2,1)S(1)} %fusion.8.select_ref, bf16[48,64,128]{2,1,0:T(8,128)(2,1)S(1)} %copy-done.9, bf16[48,64,128]{2,1,0:T(8,128)(2,1)S(1)} %get-tuple-element.73.refs_1_), custom_call_target="tpu_custom_call" | custom-call | flops 6899999744 | bytes 3276800 | tf_op jit(solution)/shard_map/rows_to_units/pallas_call | solution.py:50
  123.0 2.3 %outer_other.2 = bf16[216,32,128]{2,1,0:T(8,128)(2,1)S(1)} custom-call(s32[3]{0:T(128)S(1)} %pad_add_fusion.facts_ref, s32[432]{0:T(512)S(1)} %bitcast.66, s32[432]{0:T(512)S(1)} %bitcast.74, bf16[48,64,128]{2,1,0:T(8,128)(2,1)S(1)} %copy-done.17, bf16[48,64,128]{2,1,0:T(8,128)(2,1)S(1)} %copy-done.3, ...), custom_call_target="tpu_custom_call" | custom-call | flops 5750000128 | bytes 5705100 | tf_op jit(solution)/shard_map/outer_other/pallas_call | solution.py:50
  125.5 7.1 %collective-permute-start.18 = (bf16[24,64,128]{2,1,0:T(8,128)(2,1)S(1)}, bf16[24,64,128]{2,1,0:T(8,128)(2,1)S(1)}, u32[]{:S(2)}, u32[]{:S(2)}) collective-permute-start(bf16[24,64,128]{2,1,0:T(8,128)(2,1)S(1)} %slice.39), channel_id=1, source_target_pairs={{0,2},{1,3},{2,0},{3,1},{4,6},{5,7},{6,4},{7,5},{8,10},{9,11},{10,... | collective-permute-start | bytes 1179656 | tf_op jit(solution)/shard_map/ppermute | solution.py:398
  132.6 0.4 collective-permute-start.16
  133.2 10.7 %collective-permute-done.16.refs_5_.refs_4_.refs_7_ = bf16[24,64,128]{2,1,0:T(8,128)(2,1)S(1)} collective-permute-done((bf16[24,64,128]{2,1,0:T(8,128)(2,1)S(1)}, bf16[24,64,128]{2,1,0:T(8,128)(2,1)S(1)}, u32[]{:S(2)}, u32[]{:S(2)}) %collective-permute-start.16) | collective-permute-done | bytes 393248 | tf_op jit(solution)/shard_map/ppermute | solution.py:398
  143.9 1.1 collective-permute-done.14
  145.0 2.8 %backward.3 = bf16[128,3072]{1,0:T(8,128)(2,1)S(1)} custom-call(s32[3]{0:T(128)S(1)} %pad_add_fusion.facts_ref, s32[432]{0:T(512)S(1)} %bitcast.67, s32[432]{0:T(512)S(1)} %bitcast.75, bf16[216,32,128]{2,1,0:T(8,128)(2,1)S(1)} %copy-done.19, bf16[216,32,128]{2,1,0:T(8,128)(2,1)S(1)} %copy-done.21, ...), custom_call_target="tpu_custom_call" | custom-call | flops 8049999872 | bytes 7474572 | tf_op jit(solution)/shard_map/backward/pallas_call | solution.py:50
  147.9 1.6 outer_other.3
  149.6 1.0 collective-permute-start.22
  150.6 0.8 add_convert_fusion
  151.3 7.3 %collective-permute-done.19 = bf16[2,32,3072]{2,1,0:T(8,128)(2,1)S(1)} collective-permute-done((bf16[2,32,3072]{2,1,0:T(8,128)(2,1)S(1)}, bf16[2,32,3072]{2,1,0:T(8,128)(2,1)S(1)}, u32[]{:S(2)}, u32[]{:S(2)}) %collective-permute-start.19) | collective-permute-done | bytes 393248 | tf_op jit(solution)/shard_map/ppermute | solution.py:445
  158.7 0.7 fusion.6
  159.4 2.7 %collective-permute-start.20 = (bf16[32,3072]{1,0:T(8,128)(2,1)}, bf16[32,3072]{1,0:T(8,128)(2,1)}, u32[]{:S(2)}, u32[]{:S(2)}) collective-permute-start(bf16[32,3072]{1,0:T(8,128)(2,1)} %fusion.6), channel_id=1, source_target_pairs={{0,8},{4,12},{8,0},{12,4},{1,9},{5,13},{9,1},{13,5},{2,10},{6,14},... | collective-permute-start | bytes 589832 | tf_op jit(solution)/shard_map/ppermute | solution.py:447
  162.1 0.7 dynamic-slice_bitcast_fusion.2
  162.8 3.6 %outer_own.2.refs_0_ = bf16[216,32,128]{2,1,0:T(8,128)(2,1)S(1)} custom-call(s32[3]{0:T(128)S(1)} %pad_add_fusion.facts_ref, s32[432]{0:T(512)S(1)} %bitcast.69, s32[432]{0:T(512)S(1)} %bitcast.77, bf16[216,32,128]{2,1,0:T(8,128)(2,1)S(1)} %collective-permute-done.21.refs_0_, bf16[48,64,128]{2,1,0:T(8,128)(2,1)S(1)} %copy-done.17, ...), custom_call_target="tpu_custom_call" | custom-call | flops 5750000128 | bytes 7474572 | tf_op jit(solution)/shard_map/outer_own/pallas_call | solution.py:50
  166.4 2.9 %outer_own.3 = bf16[216,32,128]{2,1,0:T(8,128)(2,1)S(1)} custom-call(s32[3]{0:T(128)S(1)} %pad_add_fusion.facts_ref, s32[432]{0:T(512)S(1)} %bitcast.70, s32[432]{0:T(512)S(1)} %bitcast.78, bf16[216,32,128]{2,1,0:T(8,128)(2,1)S(1)} %outer_own.2.refs_0_, bf16[216,32,128]{2,1,0:T(8,128)(2,1)S(1)} %collective-permute-done.22.refs_1_, ...), custom_call_target="tpu_custom_call" | custom-call | flops 5750000128 | bytes 9244044 | tf_op jit(solution)/shard_map/outer_own/pallas_call | solution.py:50
  169.2 2.2 %reshape.152 = bf16[1,1,216,4096]{3,2,1,0:T(8,128)(2,1)} reshape(bf16[216,32,128]{2,1,0:T(8,128)(2,1)S(1)} %outer_own.3) | data formatting | bytes 3538944 | tf_op jit(solution)/shard_map/reshape | solution.py:474
  171.4 1.0 fusion.5
  172.4 0.8 pad_maximum_fusion
  (69 shorter events, 0.7 us)
Async XLA Ops:
  0.6 3.4 %copy-start = (bf16[256,3072]{1,0:T(8,128)(2,1)S(1)}, bf16[256,3072]{1,0:T(8,128)(2,1)}, u32[]{:S(2)}) copy-start(bf16[256,3072]{1,0:T(8,128)(2,1)} %values_ref.2) | copy-start | bytes 4718596
  2.6 5.5 %collective-permute-start = (bf16[216,32,128]{2,1,0:T(8,128)(2,1)S(1)}, bf16[216,32,128]{2,1,0:T(8,128)(2,1)}, u32[]{:S(2)}, u32[]{:S(2)}) collective-permute-start(bf16[216,32,128]{2,1,0:T(8,128)(2,1)S(1)} %bitcast.53), channel_id=1, source_target_pairs={{0,16},{16,0},{1,17},{17,1},{2,18},{18,2},{3,19},{19,3},{4,20},{20... | collective-permute-start | bytes 5308424 | tf_op jit(solution)/shard_map/ppermute | solution.py:401
  4.0 4.1 %copy-start.4 = (s32[1,1,432]{2,1,0:T(1,128)S(1)}, s32[1,1,432]{2,1,0:T(1,128)}, u32[]{:S(2)}) copy-start(s32[1,1,432]{2,1,0:T(1,128)} %param.8) | copy-start | bytes 5188
  4.0 4.1 %copy-start.5 = (s32[1,1,432]{2,1,0:T(1,128)S(1)}, s32[1,1,432]{2,1,0:T(1,128)}, u32[]{:S(2)}) copy-start(s32[1,1,432]{2,1,0:T(1,128)} %param.9) | copy-start | bytes 5188
  8.1 4.1 %copy-start.16 = (bf16[48,64,128]{2,1,0:T(8,128)(2,1)}, bf16[48,64,128]{2,1,0:T(8,128)(2,1)S(1)}, u32[]{:S(2)}) copy-start(bf16[48,64,128]{2,1,0:T(8,128)(2,1)S(1)} %get-tuple-element.82.table_ref.refs_0_.refs_1_) | copy-start | bytes 2359300
  8.1 7.7 %copy-start.14 = (bf16[48,64,128]{2,1,0:T(8,128)(2,1)}, bf16[48,64,128]{2,1,0:T(8,128)(2,1)S(1)}, u32[]{:S(2)}) copy-start(bf16[48,64,128]{2,1,0:T(8,128)(2,1)S(1)} %get-tuple-element.83.table_ref.refs_0_.refs_2_) | copy-start | bytes 2359300
  12.2 21.8 %collective-permute-start.1 = (bf16[2,24,64,128]{3,2,1,0:T(8,128)(2,1)S(1)}, bf16[2,24,64,128]{3,2,1,0:T(8,128)(2,1)S(1)}, u32[]{:S(2)}, u32[]{:S(2)}) collective-permute-start(bf16[2,24,64,128]{3,2,1,0:T(8,128)(2,1)S(1)} %get-tuple-element.56), channel_id=1, source_target_pairs={{0,1},{1,0},{2,3},{3,2},{4,5},{5,4},{6,7},{7,6},{8,9},{9,8},{10,11... | collective-permute-start | bytes 2359304 | tf_op jit(solution)/shard_map/ppermute | solution.py:398
  15.8 11.6 %copy-start.1 = (bf16[256,3072]{1,0:T(8,128)(2,1)S(1)}, bf16[256,3072]{1,0:T(8,128)(2,1)}, u32[]{:S(2)}) copy-start(bf16[256,3072]{1,0:T(8,128)(2,1)} %values_ref.3) | copy-start | bytes 4718596
  19.5 0.7 copy-start.10
  20.2 0.8 copy-start.12
  21.0 24.8 %collective-permute-start.3 = (bf16[2,24,64,128]{3,2,1,0:T(8,128)(2,1)S(1)}, bf16[2,24,64,128]{3,2,1,0:T(8,128)(2,1)S(1)}, u32[]{:S(2)}, u32[]{:S(2)}) collective-permute-start(bf16[2,24,64,128]{3,2,1,0:T(8,128)(2,1)S(1)} %get-tuple-element.59), channel_id=1, source_target_pairs={{0,2},{1,3},{2,0},{3,1},{4,6},{5,7},{6,4},{7,5},{8,10},{9,11},{10,... | collective-permute-start | bytes 2359304 | tf_op jit(solution)/shard_map/ppermute | solution.py:398
  31.5 0.9 copy-start.6
  34.1 24.4 %collective-permute-start.2 = (bf16[24,64,128]{2,1,0:T(8,128)(2,1)S(1)}, bf16[24,64,128]{2,1,0:T(8,128)(2,1)S(1)}, u32[]{:S(2)}, u32[]{:S(2)}) collective-permute-start(bf16[24,64,128]{2,1,0:T(8,128)(2,1)S(1)} %fusion.3), channel_id=1, source_target_pairs={{0,2},{1,3},{2,0},{3,1},{4,6},{5,7},{6,4},{7,5},{8,10},{9,11},{10,... | collective-permute-start | bytes 1179656 | tf_op jit(solution)/shard_map/ppermute | solution.py:398
  45.8 12.7 %collective-permute-start.4 = (bf16[24,64,128]{2,1,0:T(8,128)(2,1)S(1)}, bf16[24,64,128]{2,1,0:T(8,128)(2,1)S(1)}, u32[]{:S(2)}, u32[]{:S(2)}) collective-permute-start(bf16[24,64,128]{2,1,0:T(8,128)(2,1)S(1)} %fusion.2), channel_id=1, source_target_pairs={{0,1},{1,0},{2,3},{3,2},{4,5},{5,4},{6,7},{7,6},{8,9},{9,8},{10,11... | collective-permute-start | bytes 1179656 | tf_op jit(solution)/shard_map/ppermute | solution.py:398
  46.4 28.4 %collective-permute-start.9 = (bf16[2,24,64,128]{3,2,1,0:T(8,128)(2,1)S(1)}, bf16[2,24,64,128]{3,2,1,0:T(8,128)(2,1)S(1)}, u32[]{:S(2)}, u32[]{:S(2)}) collective-permute-start(bf16[2,24,64,128]{3,2,1,0:T(8,128)(2,1)S(1)} %get-tuple-element.65), channel_id=1, source_target_pairs={{0,1},{1,0},{2,3},{3,2},{4,5},{5,4},{6,7},{7,6},{8,9},{9,8},{10,11... | collective-permute-start | bytes 2359304 | tf_op jit(solution)/shard_map/ppermute | solution.py:398
  47.9 27.7 %collective-permute-start.11 = (bf16[2,24,64,128]{3,2,1,0:T(8,128)(2,1)S(1)}, bf16[2,24,64,128]{3,2,1,0:T(8,128)(2,1)S(1)}, u32[]{:S(2)}, u32[]{:S(2)}) collective-permute-start(bf16[2,24,64,128]{3,2,1,0:T(8,128)(2,1)S(1)} %get-tuple-element.70), channel_id=1, source_target_pairs={{0,2},{1,3},{2,0},{3,1},{4,6},{5,7},{6,4},{7,5},{8,10},{9,11},{10,... | collective-permute-start | bytes 2359304 | tf_op jit(solution)/shard_map/ppermute | solution.py:398
  57.2 1.2 copy-start.18
  58.5 1.4 copy-start.20
  59.8 34.2 %copy-start.2 = (bf16[48,64,128]{2,1,0:T(8,128)(2,1)}, bf16[48,64,128]{2,1,0:T(8,128)(2,1)S(1)}, u32[]{:S(2)}) copy-start(bf16[48,64,128]{2,1,0:T(8,128)(2,1)S(1)} %get-tuple-element.61.refs_0_.refs_1_.refs_2_) | copy-start | bytes 2359300
  59.9 34.2 %copy-start.8 = (bf16[48,64,128]{2,1,0:T(8,128)(2,1)}, bf16[48,64,128]{2,1,0:T(8,128)(2,1)S(1)}, u32[]{:S(2)}) copy-start(bf16[48,64,128]{2,1,0:T(8,128)(2,1)S(1)} %get-tuple-element.63.refs_0_) | copy-start | bytes 2359300
  59.9 30.0 %collective-permute-start.5 = (bf16[48,64,128]{2,1,0:T(8,128)(2,1)S(1)}, bf16[48,64,128]{2,1,0:T(8,128)(2,1)S(1)}, u32[]{:S(2)}, u32[]{:S(2)}) collective-permute-start(bf16[48,64,128]{2,1,0:T(8,128)(2,1)S(1)} %get-tuple-element.61.refs_0_.refs_1_.refs_2_), channel_id=1, source_target_pairs={{0,1},{1,0},{2,3},{3,2},{4,5},{5,4},{6,7},{7,6},{8,9},{9,8},{10,11... | collective-permute-start | bytes 2359304 | tf_op jit(solution)/shard_map/ppermute | solution.py:398
  60.4 30.9 %collective-permute-start.6 = (bf16[48,64,128]{2,1,0:T(8,128)(2,1)S(1)}, bf16[48,64,128]{2,1,0:T(8,128)(2,1)S(1)}, u32[]{:S(2)}, u32[]{:S(2)}) collective-permute-start(bf16[48,64,128]{2,1,0:T(8,128)(2,1)S(1)} %get-tuple-element.61.refs_0_.refs_1_.refs_2_), channel_id=1, source_target_pairs={{0,2},{1,3},{2,0},{3,1},{4,6},{5,7},{6,4},{7,5},{8,10},{9,11},{10,... | collective-permute-start | bytes 2359304 | tf_op jit(solution)/shard_map/ppermute | solution.py:398
  89.9 12.4 %collective-permute-start.10 = (bf16[24,64,128]{2,1,0:T(8,128)(2,1)}, bf16[24,64,128]{2,1,0:T(8,128)(2,1)}, u32[]{:S(2)}, u32[]{:S(2)}) collective-permute-start(bf16[24,64,128]{2,1,0:T(8,128)(2,1)} %fusion.1), channel_id=1, source_target_pairs={{0,2},{1,3},{2,0},{3,1},{4,6},{5,7},{6,4},{7,5},{8,10},{9,11},{10,... | collective-permute-start | bytes 1179656 | tf_op jit(solution)/shard_map/ppermute | solution.py:398
  91.3 12.4 %collective-permute-start.12 = (bf16[24,64,128]{2,1,0:T(8,128)(2,1)}, bf16[24,64,128]{2,1,0:T(8,128)(2,1)}, u32[]{:S(2)}, u32[]{:S(2)}) collective-permute-start(bf16[24,64,128]{2,1,0:T(8,128)(2,1)} %fusion), channel_id=1, source_target_pairs={{0,1},{1,0},{2,3},{3,2},{4,5},{5,4},{6,7},{7,6},{8,9},{9,8},{10,11... | collective-permute-start | bytes 1179656 | tf_op jit(solution)/shard_map/ppermute | solution.py:398
  92.6 18.0 %collective-permute-start.7 = (bf16[24,64,128]{2,1,0:T(8,128)(2,1)}, bf16[24,64,128]{2,1,0:T(8,128)(2,1)}, u32[]{:S(2)}, u32[]{:S(2)}) collective-permute-start(bf16[24,64,128]{2,1,0:T(8,128)(2,1)} %slice.34), channel_id=1, source_target_pairs={{0,2},{1,3},{2,0},{3,1},{4,6},{5,7},{6,4},{7,5},{8,10},{9,11},{10,... | collective-permute-start | bytes 1179656 | tf_op jit(solution)/shard_map/ppermute | solution.py:398
  94.1 17.4 %collective-permute-start.8 = (bf16[24,64,128]{2,1,0:T(8,128)(2,1)}, bf16[24,64,128]{2,1,0:T(8,128)(2,1)}, u32[]{:S(2)}, u32[]{:S(2)}) collective-permute-start(bf16[24,64,128]{2,1,0:T(8,128)(2,1)} %slice.35), channel_id=1, source_target_pairs={{0,1},{1,0},{2,3},{3,2},{4,5},{5,4},{6,7},{7,6},{8,9},{9,8},{10,11... | collective-permute-start | bytes 1179656 | tf_op jit(solution)/shard_map/ppermute | solution.py:398
  103.7 1.1 copy-start.7
  104.8 1.0 copy-start.11
  105.8 1.0 copy-start.13
  106.8 4.6 %copy-start.3 = (bf16[48,64,128]{2,1,0:T(8,128)(2,1)S(1)}, bf16[48,64,128]{2,1,0:T(8,128)(2,1)}, u32[]{:S(2)}) copy-start(bf16[48,64,128]{2,1,0:T(8,128)(2,1)} %copy-done.2) | copy-start | bytes 2359300
  106.8 4.6 %copy-start.19 = (bf16[216,32,128]{2,1,0:T(8,128)(2,1)S(1)}, bf16[216,32,128]{2,1,0:T(8,128)(2,1)}, u32[]{:S(2)}) copy-start(bf16[216,32,128]{2,1,0:T(8,128)(2,1)} %copy-done.18) | copy-start | bytes 5308420
  106.8 4.6 %copy-start.21 = (bf16[216,32,128]{2,1,0:T(8,128)(2,1)S(1)}, bf16[216,32,128]{2,1,0:T(8,128)(2,1)}, u32[]{:S(2)}) copy-start(bf16[216,32,128]{2,1,0:T(8,128)(2,1)} %copy-done.20) | copy-start | bytes 5308420
  109.4 16.1 %collective-permute-start.17 = (bf16[48,64,128]{2,1,0:T(8,128)(2,1)S(1)}, bf16[48,64,128]{2,1,0:T(8,128)(2,1)S(1)}, u32[]{:S(2)}, u32[]{:S(2)}) collective-permute-start(bf16[48,64,128]{2,1,0:T(8,128)(2,1)S(1)} %get-tuple-element.74.refs_1_.refs_0_.refs_3_), channel_id=1, source_target_pairs={{0,1},{1,0},{2,3},{3,2},{4,5},{5,4},{6,7},{7,6},{8,9},{9,8},{10,11... | collective-permute-start | bytes 2359304 | tf_op jit(solution)/shard_map/ppermute | solution.py:398
  110.0 22.6 %collective-permute-start.15 = (bf16[48,64,128]{2,1,0:T(8,128)(2,1)S(1)}, bf16[48,64,128]{2,1,0:T(8,128)(2,1)S(1)}, u32[]{:S(2)}, u32[]{:S(2)}) collective-permute-start(bf16[48,64,128]{2,1,0:T(8,128)(2,1)S(1)} %get-tuple-element.74.refs_1_.refs_0_.refs_3_), channel_id=1, source_target_pairs={{0,2},{1,3},{2,0},{3,1},{4,6},{5,7},{6,4},{7,5},{8,10},{9,11},{10,... | collective-permute-start | bytes 2359304 | tf_op jit(solution)/shard_map/ppermute | solution.py:398
  111.4 5.9 %copy-start.9 = (bf16[48,64,128]{2,1,0:T(8,128)(2,1)S(1)}, bf16[48,64,128]{2,1,0:T(8,128)(2,1)}, u32[]{:S(2)}) copy-start(bf16[48,64,128]{2,1,0:T(8,128)(2,1)} %copy-done.8) | copy-start | bytes 2359300
  115.2 17.9 %collective-permute-start.13 = (bf16[2,32,3072]{2,1,0:T(8,128)(2,1)S(1)}, bf16[2,32,3072]{2,1,0:T(8,128)(2,1)S(1)}, u32[]{:S(2)}, u32[]{:S(2)}) collective-permute-start(bf16[2,32,3072]{2,1,0:T(8,128)(2,1)S(1)} %dynamic-slice_bitcast_fusion.1), channel_id=1, source_target_pairs={{0,4},{4,0},{8,12},{12,8},{1,5},{5,1},{9,13},{13,9},{2,6},{6,2},{1... | collective-permute-start | bytes 1179656 | tf_op jit(solution)/shard_map/ppermute | solution.py:445
  117.4 5.7 %copy-start.17 = (bf16[48,64,128]{2,1,0:T(8,128)(2,1)S(1)}, bf16[48,64,128]{2,1,0:T(8,128)(2,1)}, u32[]{:S(2)}) copy-start(bf16[48,64,128]{2,1,0:T(8,128)(2,1)} %copy-done.16) | copy-start | bytes 2359300
  125.4 37.4 %collective-permute-start.21 = (bf16[216,32,128]{2,1,0:T(8,128)(2,1)S(1)}, bf16[216,32,128]{2,1,0:T(8,128)(2,1)S(1)}, u32[]{:S(2)}, u32[]{:S(2)}) collective-permute-start(bf16[216,32,128]{2,1,0:T(8,128)(2,1)S(1)} %outer_other.2), channel_id=1, source_target_pairs={{0,16},{16,0},{1,17},{17,1},{2,18},{18,2},{3,19},{19,3},{4,20},{20... | collective-permute-start | bytes 5308424 | tf_op jit(solution)/shard_map/ppermute | solution.py:401
  125.5 19.5 %collective-permute-start.18 = (bf16[24,64,128]{2,1,0:T(8,128)(2,1)S(1)}, bf16[24,64,128]{2,1,0:T(8,128)(2,1)S(1)}, u32[]{:S(2)}, u32[]{:S(2)}) collective-permute-start(bf16[24,64,128]{2,1,0:T(8,128)(2,1)S(1)} %slice.39), channel_id=1, source_target_pairs={{0,2},{1,3},{2,0},{3,1},{4,6},{5,7},{6,4},{7,5},{8,10},{9,11},{10,... | collective-permute-start | bytes 1179656 | tf_op jit(solution)/shard_map/ppermute | solution.py:398
  132.6 11.3 %collective-permute-start.16 = (bf16[24,64,128]{2,1,0:T(8,128)(2,1)S(1)}, bf16[24,64,128]{2,1,0:T(8,128)(2,1)S(1)}, u32[]{:S(2)}, u32[]{:S(2)}) collective-permute-start(bf16[24,64,128]{2,1,0:T(8,128)(2,1)S(1)} %slice.38), channel_id=1, source_target_pairs={{0,1},{1,0},{2,3},{3,2},{4,5},{5,4},{6,7},{7,6},{8,9},{9,8},{10,11... | collective-permute-start | bytes 1179656 | tf_op jit(solution)/shard_map/ppermute | solution.py:398
  133.1 11.9 %collective-permute-start.14 = (bf16[32,3072]{1,0:T(8,128)(2,1)S(1)}, bf16[32,3072]{1,0:T(8,128)(2,1)S(1)}, u32[]{:S(2)}, u32[]{:S(2)}) collective-permute-start(bf16[32,3072]{1,0:T(8,128)(2,1)S(1)} %fusion.7), channel_id=1, source_target_pairs={{0,8},{4,12},{8,0},{12,4},{1,9},{5,13},{9,1},{13,5},{2,10},{6,14},... | collective-permute-start | bytes 589832 | tf_op jit(solution)/shard_map/ppermute | solution.py:447
  133.2 14.7 %copy-start.15 = (bf16[48,64,128]{2,1,0:T(8,128)(2,1)S(1)}, bf16[48,64,128]{2,1,0:T(8,128)(2,1)}, u32[]{:S(2)}) copy-start(bf16[48,64,128]{2,1,0:T(8,128)(2,1)} %copy-done.14) | copy-start | bytes 2359300
  147.8 10.8 %collective-permute-start.19 = (bf16[2,32,3072]{2,1,0:T(8,128)(2,1)S(1)}, bf16[2,32,3072]{2,1,0:T(8,128)(2,1)S(1)}, u32[]{:S(2)}, u32[]{:S(2)}) collective-permute-start(bf16[2,32,3072]{2,1,0:T(8,128)(2,1)S(1)} %dynamic-slice_bitcast_fusion), channel_id=1, source_target_pairs={{0,4},{4,0},{8,12},{12,8},{1,5},{5,1},{9,13},{13,9},{2,6},{6,2},{1... | collective-permute-start | bytes 1179656 | tf_op jit(solution)/shard_map/ppermute | solution.py:445
  149.6 16.8 %collective-permute-start.22 = (bf16[216,32,128]{2,1,0:T(8,128)(2,1)S(1)}, bf16[216,32,128]{2,1,0:T(8,128)(2,1)S(1)}, u32[]{:S(2)}, u32[]{:S(2)}) collective-permute-start(bf16[216,32,128]{2,1,0:T(8,128)(2,1)S(1)} %outer_other.3), channel_id=1, source_target_pairs={{0,16},{16,0},{1,17},{17,1},{2,18},{18,2},{3,19},{19,3},{4,20},{20... | collective-permute-start | bytes 5308424 | tf_op jit(solution)/shard_map/ppermute | solution.py:401
  159.4 12.0 %collective-permute-start.20 = (bf16[32,3072]{1,0:T(8,128)(2,1)}, bf16[32,3072]{1,0:T(8,128)(2,1)}, u32[]{:S(2)}, u32[]{:S(2)}) collective-permute-start(bf16[32,3072]{1,0:T(8,128)(2,1)} %fusion.6), channel_id=1, source_target_pairs={{0,8},{4,12},{8,0},{12,4},{1,9},{5,13},{9,1},{13,5},{2,10},{6,14},... | collective-permute-start | bytes 589832 | tf_op jit(solution)/shard_map/ppermute | solution.py:447
  169.2 2.2 %copy-start.22 = (bf16[32,3072]{1,0:T(8,128)(2,1)S(1)}, bf16[32,3072]{1,0:T(8,128)(2,1)}, u32[]{:S(2)}) copy-start(bf16[32,3072]{1,0:T(8,128)(2,1)} %dynamic-slice_bitcast_fusion.2) | copy-start | bytes 589828
  169.2 3.2 %copy-start.23 = (bf16[32,3072]{1,0:T(8,128)(2,1)S(1)}, bf16[32,3072]{1,0:T(8,128)(2,1)}, u32[]{:S(2)}) copy-start(bf16[32,3072]{1,0:T(8,128)(2,1)} %add_convert_fusion) | copy-start | bytes 589828

commit v3 on v2

--- a/solution.py
+++ b/solution.py
@@ -408,22 +408,21 @@
     partials = [forward(facts, rows, cols, own, other, table, share_blocks, shares) for table in tables]
     upstream = list(token_rows(act_grad, after(select, partials[1][2]), True))
     own_t, other_t = transpose_tiles(after(own, upstream[1]), after(other, upstream[1]))
-    upstream[0] = after(upstream[0], own_t)
 
     grads, acts = [], []
-    from_x = from_y = None
     for chunk in range(CHUNKS):
         along_x, along_y, own_a, own_b, relay_x, relay_y = partials[chunk]
-        if chunk:
-            along_x, along_y = after(along_x, from_x), after(along_y, from_y)
         from_x, from_y = across(along_x, 1), across(along_y, 2)
         sum_y, sum_x = relay_y + from_x[0], relay_x + from_y[0]
         if chunk:
-            sum_y, sum_x = after(sum_y, grads[0][1]), after(sum_x, grads[0][2])
+            sum_y = after(sum_y, own_t)
         last_a, last_b = across(sum_y, 2), across(sum_x, 1)
         grad, act = gelu(upstream[chunk], (own_a, from_x, last_a, own_b, from_y, last_b))
         acts.append(act)
-        grads.append([grad, across(grad, 1), across(grad, 2)])
+        sent_x = sent_y = grad
+        if chunk:
+            sent_x, sent_y = after(grad, grads[0][1]), after(grad, grads[0][2])
+        grads.append([grad, across(sent_x, 1), across(sent_y, 2)])
 
     for chunk in range(CHUNKS):
         grad, grad_x, grad_y = grads[chunk]
@@ -460,7 +459,7 @@
 
     first = input_sums(0)
     row_parts, halfway, sent = to_rows(first)
-    activation = rows_to_units(after(select, first), acts)
+    activation = rows_to_units(after(select, sent), acts)
     other_first = tile_part(0, activation, False, [])
     *first_parts, grads[1][4] = lax.optimization_barrier((*row_parts, after(grads[1][4], other_first)))
     second = input_sums(1)

time: 175 us -> 166 us (0.949)
  starting transfers between devices: 39.6 us -> 15.8 us
  Pallas kernels: 49.6 us -> 68.7 us
  waiting for transfers between devices: 63.6 us -> 57.1 us
  local copies, waits for them, and re-layouts: 13.4 us -> 15.4 us
    pallas_call x14, Pallas kernels: 49.6 us -> 68.7 us  [call(): pl.pallas_call(kernel, out_shape=out_shape, in_specs=in_specs, out_specs=...]
    ppermute x16, starting transfers between devices: 33 us -> 14.2 us  [across(): lax.ppermute(values, 'col', [(place, place ^ bit) for place in range(shar...]
    ppermute x16, waiting for transfers between devices: 55.2 us -> 51.1 us  [across(): lax.ppermute(values, 'col', [(place, place ^ bit) for place in range(shar...]
    ppermute x2, waiting for transfers between devices: 7.35 us -> 5.11 us  [to_rows(): lax.ppermute(sent, 'row', [(place, place ^ 1) for place in range(4)])]
    ppermute x2, starting transfers between devices: 2.26 us -> 0.14 us  [to_rows(): lax.ppermute(sent, 'row', [(place, place ^ 1) for place in range(4)])]
    unnamed x49 -> x61, local copies, waits for them, and re-layouts: 8.79 us -> 10.8 us
    ppermute x2, starting transfers between devices: 2.75 us -> 0.82 us  [to_rows(): lax.ppermute(both.astype(jnp.bfloat16), 'row', [(place, place ^ 2) for pl...]
  transfers between devices with their start and end apart: 23 -> 23, of which waited for: 10 -> 9; matrix products, arithmetic and copies ran while one was open for 5% -> 5% of each run, Pallas kernels for 26% -> 37%
where the time goes in v3:
time: 166 us; the launch traced here: 164 us
  Pallas kernels  68.7 us (41%)
  waiting for transfers between devices  57.1 us (34%)
  starting transfers between devices  15.8 us (10%)
  local copies, waits for them, and re-layouts  15.4 us (9%)
  other arithmetic  5.36 us (3%)
  between operations  1.8 us (1%)
    pallas_call x14, Pallas kernels, call(): pl.pallas_call(kernel, out_shape=out_shape, in_specs=in_specs, out_specs=...  68.7 us
    ppermute x16, waiting for transfers between devices, across(): lax.ppermute(values, 'col', [(place, place ^ bit) for place in range(shar...  51.1 us
    ppermute x16, starting transfers between devices, across(): lax.ppermute(values, 'col', [(place, place ^ bit) for place in range(shar...  14.2 us
    unnamed x61, local copies, waits for them, and re-layouts  10.8 us
    ppermute x2, waiting for transfers between devices, to_rows(): lax.ppermute(sent, 'row', [(place, place ^ 1) for place in range(4)])  5.11 us
  transfers between devices with their start and end apart: 23, of which 9 were waited for; matrix products, arithmetic and copies ran while one was open for 5% of the time, Pallas kernels for 37%

profile of v3, /device:TPU:0, one launch (start us, length us, event | category | flops | bytes accessed | tf_op | source)
XLA Modules:
  0.0 164.2 jit_solution(11652131314922168055)
XLA Ops:
  0.6 2.0 %copy.9 = bf16[27,8,32,128]{3,2,1,0:T(8,128)(2,1)S(1)} copy(bf16[27,8,32,128]{3,1,2,0:T(8,128)(2,1)} %bitcast.79) | data formatting | bytes 3538944
  2.6 0.5 collective-permute-start
  3.8 0.1 pad_add_fusion.facts_ref
  3.9 0.1 add_add_fusion
  4.0 4.1 %features_to_rows.1 = (bf16[48,64,128]{2,1,0:T(8,128)(2,1)S(1)}, bf16[48,64,128]{2,1,0:T(8,128)(2,1)S(1)}) custom-call(bf16[256,3072]{1,0:T(8,128)(2,1)S(1)} %copy-done.6, bf16[2,256,128]{2,1,0:T(8,128)(2,1)S(1)} %fusion.8.select_ref), custom_call_target="tpu_custom_call" | custom-call | flops 5750000128 | bytes 3276800 | tf_op jit(solution)/shard_map/features_to_rows/pallas_call | solution.py:50
  8.2 7.3 %forward.3 = (bf16[2,24,64,128]{3,2,1,0:T(8,128)(2,1)S(1)}, bf16[2,24,64,128]{3,2,1,0:T(8,128)(2,1)S(1)}, bf16[24,64,128]{2,1,0:T(8,128)(2,1)S(1)}, bf16[24,64,1...) custom-call(s32[3]{0:T(128)S(1)} %pad_add_fusion.facts_ref, ...), custom_call_target="tpu_custom_call" | custom-call | flops 8049999872 | bytes 7474572 | tf_op jit(solution)/shard_map/forward/pallas_call | solution.py:50
  15.5 2.5 %collective-permute-start.1 = (bf16[2,24,64,128]{3,2,1,0:T(8,128)(2,1)S(1)}, bf16[2,24,64,128]{3,2,1,0:T(8,128)(2,1)S(1)}, u32[]{:S(2)}, u32[]{:S(2)}) collective-permute-start(bf16[2,24,64,128]{3,2,1,0:T(8,128)(2,1)S(1)} %get-tuple-element.53), channel_id=1, source_target_pairs={{0,1},{1,0},{2,3},{3,2},{4,5},{5,4},{6,7},{7,6},{8,9},{9,8},{10,11... | collective-permute-start | bytes 2359304 | tf_op jit(solution)/shard_map/ppermute | solution.py:398
  18.0 0.5 collective-permute-start.3
  18.5 6.8 %forward.2 = (bf16[2,24,64,128]{3,2,1,0:T(8,128)(2,1)S(1)}, bf16[2,24,64,128]{3,2,1,0:T(8,128)(2,1)S(1)}, bf16[24,64,128]{2,1,0:T(8,128)(2,1)S(1)}, bf16[24,64,1...) custom-call(s32[3]{0:T(128)S(1)} %pad_add_fusion.facts_ref, ...), custom_call_target="tpu_custom_call" | custom-call | flops 8049999872 | bytes 7474572 | tf_op jit(solution)/shard_map/forward/pallas_call | solution.py:50
  25.4 0.1 collective-permute-start.9
  25.4 0.5 collective-permute-start.11
  25.9 10.5 %collective-permute-done.1.near_a = bf16[2,24,64,128]{3,2,1,0:T(8,128)(2,1)S(1)} collective-permute-done((bf16[2,24,64,128]{3,2,1,0:T(8,128)(2,1)S(1)}, bf16[2,24,64,128]{3,2,1,0:T(8,128)(2,1)S(1)}, u32[]{:S(2)}, u32[]{:S(2)}) %collective-permute-start.1) | collective-permute-done | bytes 786464 | tf_op jit(solution)/shard_map/ppermute | solution.py:398
  36.5 0.6 collective-permute-start.2
  37.0 1.4 collective-permute-done.3.near_b
  38.5 0.6 collective-permute-start.4
  39.1 4.1 %units_to_rows.1 = (bf16[48,64,128]{2,1,0:T(8,128)(2,1)S(1)}, bf16[48,64,128]{2,1,0:T(8,128)(2,1)S(1)}) custom-call(bf16[256,3072]{1,0:T(8,128)(2,1)S(1)} %copy-done.7, bf16[2,256,128]{2,1,0:T(8,128)(2,1)S(1)} %fusion.8.select_ref), custom_call_target="tpu_custom_call" | custom-call | flops 5750000128 | bytes 3276800 | tf_op jit(solution)/shard_map/units_to_rows/pallas_call | solution.py:50
  43.2 0.9 copy-done.14
  44.1 18.9 %collective-permute-done.2.last_a = bf16[24,64,128]{2,1,0:T(8,128)(2,1)S(1)} collective-permute-done((bf16[24,64,128]{2,1,0:T(8,128)(2,1)S(1)}, bf16[24,64,128]{2,1,0:T(8,128)(2,1)S(1)}, u32[]{:S(2)}, u32[]{:S(2)}) %collective-permute-start.2) | collective-permute-done | bytes 393248 | tf_op jit(solution)/shard_map/ppermute | solution.py:398
  63.0 1.4 gelu.2
  64.4 0.5 collective-permute-start.6
  64.9 0.4 collective-permute-start.5
  65.3 7.3 %transpose_tiles.1 = (bf16[216,32,128]{2,1,0:T(8,128)(2,1)S(1)}, bf16[216,32,128]{2,1,0:T(8,128)(2,1)S(1)}) custom-call(bf16[216,32,128]{2,1,0:T(8,128)(2,1)S(1)} %bitcast.56, bf16[216,32,128]{2,1,0:T(8,128)(2,1)} %collective-permute-done.other_ref), custom_call_target="tpu_custom_call" | custom-call | flops 8049999872 | bytes 7077888 | tf_op jit(solution)/shard_map/transpose_tiles/pallas_call | solution.py:50
  72.6 1.2 copy-done.24
  73.8 1.3 copy-done.26
  75.0 0.9 fusion
  75.9 1.7 %collective-permute-start.12 = (bf16[24,64,128]{2,1,0:T(8,128)(2,1)}, bf16[24,64,128]{2,1,0:T(8,128)(2,1)S(1)}, u32[]{:S(2)}, u32[]{:S(2)}) collective-permute-start(bf16[24,64,128]{2,1,0:T(8,128)(2,1)} %fusion), channel_id=1, source_target_pairs={{0,1},{1,0},{2,3},{3,2},{4,5},{5,4},{6,7},{7,6},{8,9},{9,8},{10,11... | collective-permute-start | bytes 1179656 | tf_op jit(solution)/shard_map/ppermute | solution.py:398
  77.6 0.9 fusion.1
  78.5 1.6 collective-permute-start.10
  80.0 4.9 %collective-permute-done.6.refs_2_.refs_3_.refs_4_ = bf16[48,64,128]{2,1,0:T(8,128)(2,1)S(1)} collective-permute-done((bf16[48,64,128]{2,1,0:T(8,128)(2,1)S(1)}, bf16[48,64,128]{2,1,0:T(8,128)(2,1)S(1)}, u32[]{:S(2)}, u32[]{:S(2)}) %collective-permute-start.6) | collective-permute-done | bytes 786464 | tf_op jit(solution)/shard_map/ppermute | solution.py:398
  84.9 0.8 slice.35
  85.7 0.3 collective-permute-start.8
  86.0 0.9 slice.34
  86.9 0.9 collective-permute-start.7
  87.8 6.0 %collective-permute-done.12.last_b = bf16[24,64,128]{2,1,0:T(8,128)(2,1)S(1)} collective-permute-done((bf16[24,64,128]{2,1,0:T(8,128)(2,1)}, bf16[24,64,128]{2,1,0:T(8,128)(2,1)S(1)}, u32[]{:S(2)}, u32[]{:S(2)}) %collective-permute-start.12) | collective-permute-done | bytes 393248 | tf_op jit(solution)/shard_map/ppermute | solution.py:398
  93.8 1.1 copy-done.3
  95.0 1.1 copy-done.5
  96.1 1.1 copy-done.15
  97.2 1.0 copy-done.17
  98.2 1.0 copy-done.19
  99.2 1.4 gelu.3
  100.6 1.6 collective-permute-start.15
  102.2 0.4 collective-permute-start.17
  102.6 6.1 %backward.2 = bf16[128,3072]{1,0:T(8,128)(2,1)S(1)} custom-call(s32[3]{0:T(128)S(1)} %pad_add_fusion.facts_ref, s32[432]{0:T(512)S(1)} %bitcast.65, s32[432]{0:T(512)S(1)} %bitcast.73, bf16[216,32,128]{2,1,0:T(8,128)(2,1)S(1)} %copy-done.25, bf16[216,32,128]{2,1,0:T(8,128)(2,1)S(1)} %copy-done.27, bf16[48,64,128]{2,1,0:T(8,128)(2,1)S(1)} %copy-done.9, ...), custom_call_target="tpu_custom_call" | custom-call | flops 8049999872 | bytes 7474572 | tf_op jit(solution)/shard_map/backward/pallas_call | solution.py:50
  108.8 0.1 collective-permute-start.13
  108.9 5.7 %rows_to_units.1 = bf16[256,3072]{1,0:T(8,128)(2,1)} custom-call(bf16[2,256,128]{2,1,0:T(8,128)(2,1)S(1)} %fusion.8.select_ref, bf16[48,64,128]{2,1,0:T(8,128)(2,1)S(1)} %copy-done.13, bf16[48,64,128]{2,1,0:T(8,128)(2,1)S(1)} %get-tuple-element.67.refs_1_), custom_call_target="tpu_custom_call" | custom-call | flops 6899999744 | bytes 3276800 | tf_op jit(solution)/shard_map/rows_to_units/pallas_call | solution.py:50
  114.6 4.4 %outer_other.2 = bf16[216,32,128]{2,1,0:T(8,128)(2,1)S(1)} custom-call(s32[3]{0:T(128)S(1)} %pad_add_fusion.facts_ref, s32[432]{0:T(512)S(1)} %bitcast.66, s32[432]{0:T(512)S(1)} %bitcast.74, bf16[48,64,128]{2,1,0:T(8,128)(2,1)S(1)} %copy-done.23, bf16[48,64,128]{2,1,0:T(8,128)(2,1)S(1)} %copy-done.9, ...), custom_call_target="tpu_custom_call" | custom-call | flops 5750000128 | bytes 5705100 | tf_op jit(solution)/shard_map/outer_other/pallas_call | solution.py:50
  119.0 0.1 collective-permute-start.21
  119.1 2.1 %collective-permute-start.16 = (bf16[24,64,128]{2,1,0:T(8,128)(2,1)S(1)}, bf16[24,64,128]{2,1,0:T(8,128)(2,1)S(1)}, u32[]{:S(2)}, u32[]{:S(2)}) collective-permute-start(bf16[24,64,128]{2,1,0:T(8,128)(2,1)S(1)} %slice.38), channel_id=1, source_target_pairs={{0,1},{1,0},{2,3},{3,2},{4,5},{5,4},{6,7},{7,6},{8,9},{9,8},{10,11... | collective-permute-start | bytes 1179656 | tf_op jit(solution)/shard_map/ppermute | solution.py:398
  121.4 0.8 collective-permute-start.14
  122.2 8.7 %collective-permute-done.16.refs_5_.refs_4_.refs_7_ = bf16[24,64,128]{2,1,0:T(8,128)(2,1)S(1)} collective-permute-done((bf16[24,64,128]{2,1,0:T(8,128)(2,1)S(1)}, bf16[24,64,128]{2,1,0:T(8,128)(2,1)S(1)}, u32[]{:S(2)}, u32[]{:S(2)}) %collective-permute-start.16) | collective-permute-done | bytes 393248 | tf_op jit(solution)/shard_map/ppermute | solution.py:398
  131.0 0.9 collective-permute-done.14
  131.8 0.7 collective-permute-done.18.refs_4_.refs_3_.refs_6_
  132.5 6.0 %backward.3 = bf16[128,3072]{1,0:T(8,128)(2,1)S(1)} custom-call(s32[3]{0:T(128)S(1)} %pad_add_fusion.facts_ref, s32[432]{0:T(512)S(1)} %bitcast.67, s32[432]{0:T(512)S(1)} %bitcast.75, bf16[216,32,128]{2,1,0:T(8,128)(2,1)S(1)} %copy-done.25, bf16[216,32,128]{2,1,0:T(8,128)(2,1)S(1)} %copy-done.27, ...), custom_call_target="tpu_custom_call" | custom-call | flops 8049999872 | bytes 7474572 | tf_op jit(solution)/shard_map/backward/pallas_call | solution.py:50
  138.5 0.1 collective-permute-start.19
  138.6 4.4 %outer_other.3 = bf16[216,32,128]{2,1,0:T(8,128)(2,1)S(1)} custom-call(s32[3]{0:T(128)S(1)} %pad_add_fusion.facts_ref, s32[432]{0:T(512)S(1)} %bitcast.68, s32[432]{0:T(512)S(1)} %bitcast.76, bf16[48,64,128]{2,1,0:T(8,128)(2,1)S(1)} %copy-done.21, bf16[48,64,128]{2,1,0:T(8,128)(2,1)S(1)} %get-tuple-element.69.refs_1_.refs_0_.refs_3_, ...), custom_call_target="tpu_custom_call" | custom-call | flops 5750000128 | bytes 5705100 | tf_op jit(solution)/shard_map/outer_other/pallas_call | solution.py:50
  143.1 0.8 add_convert_fusion
  143.9 5.1 %collective-permute-done.19 = bf16[2,32,3072]{2,1,0:T(8,128)(2,1)S(1)} collective-permute-done((bf16[2,32,3072]{2,1,0:T(8,128)(2,1)S(1)}, bf16[2,32,3072]{2,1,0:T(8,128)(2,1)S(1)}, u32[]{:S(2)}, u32[]{:S(2)}) %collective-permute-start.19) | collective-permute-done | bytes 393248 | tf_op jit(solution)/shard_map/ppermute | solution.py:444
  149.0 0.7 fusion.6
  149.7 0.7 dynamic-slice_bitcast_fusion.2
  150.4 4.9 %outer_own.2.refs_0_ = bf16[216,32,128]{2,1,0:T(8,128)(2,1)S(1)} custom-call(s32[3]{0:T(128)S(1)} %pad_add_fusion.facts_ref, s32[432]{0:T(512)S(1)} %bitcast.69, s32[432]{0:T(512)S(1)} %bitcast.77, bf16[216,32,128]{2,1,0:T(8,128)(2,1)S(1)} %collective-permute-done.21.refs_0_, bf16[48,64,128]{2,1,0:T(8,128)(2,1)S(1)} %copy-done.23, ...), custom_call_target="tpu_custom_call" | custom-call | flops 5750000128 | bytes 7474572 | tf_op jit(solution)/shard_map/outer_own/pallas_call | solution.py:50
  155.3 4.9 %outer_own.3 = bf16[216,32,128]{2,1,0:T(8,128)(2,1)S(1)} custom-call(s32[3]{0:T(128)S(1)} %pad_add_fusion.facts_ref, s32[432]{0:T(512)S(1)} %bitcast.70, s32[432]{0:T(512)S(1)} %bitcast.78, bf16[216,32,128]{2,1,0:T(8,128)(2,1)S(1)} %outer_own.2.refs_0_, bf16[216,32,128]{2,1,0:T(8,128)(2,1)S(1)} %collective-permute-done.22.refs_1_, ...), custom_call_target="tpu_custom_call" | custom-call | flops 5750000128 | bytes 9244044 | tf_op jit(solution)/shard_map/outer_own/pallas_call | solution.py:50
  160.2 2.2 %reshape.152 = bf16[1,1,216,4096]{3,2,1,0:T(8,128)(2,1)} reshape(bf16[216,32,128]{2,1,0:T(8,128)(2,1)S(1)} %outer_own.3) | data formatting | bytes 3538944 | tf_op jit(solution)/shard_map/reshape | solution.py:473
  162.4 1.0 fusion.5
  163.4 0.8 pad_maximum_fusion
  (81 shorter events, 0.7 us)
Async XLA Ops:
  0.6 3.4 %copy-start.6 = (bf16[256,3072]{1,0:T(8,128)(2,1)S(1)}, bf16[256,3072]{1,0:T(8,128)(2,1)}, u32[]{:S(2)}) copy-start(bf16[256,3072]{1,0:T(8,128)(2,1)} %values_ref.2) | copy-start | bytes 4718596
  2.6 5.5 %collective-permute-start = (bf16[216,32,128]{2,1,0:T(8,128)(2,1)S(1)}, bf16[216,32,128]{2,1,0:T(8,128)(2,1)}, u32[]{:S(2)}, u32[]{:S(2)}) collective-permute-start(bf16[216,32,128]{2,1,0:T(8,128)(2,1)S(1)} %bitcast.53), channel_id=1, source_target_pairs={{0,16},{16,0},{1,17},{17,1},{2,18},{18,2},{3,19},{19,3},{4,20},{20... | collective-permute-start | bytes 5308424 | tf_op jit(solution)/shard_map/ppermute | solution.py:401
  4.0 4.1 %copy-start.10 = (s32[1,1,432]{2,1,0:T(1,128)S(1)}, s32[1,1,432]{2,1,0:T(1,128)}, u32[]{:S(2)}) copy-start(s32[1,1,432]{2,1,0:T(1,128)} %param.8) | copy-start | bytes 5188
  4.0 4.1 %copy-start.11 = (s32[1,1,432]{2,1,0:T(1,128)S(1)}, s32[1,1,432]{2,1,0:T(1,128)}, u32[]{:S(2)}) copy-start(s32[1,1,432]{2,1,0:T(1,128)} %param.9) | copy-start | bytes 5188
  8.1 7.4 %copy-start.22 = (bf16[48,64,128]{2,1,0:T(8,128)(2,1)}, bf16[48,64,128]{2,1,0:T(8,128)(2,1)S(1)}, u32[]{:S(2)}) copy-start(bf16[48,64,128]{2,1,0:T(8,128)(2,1)S(1)} %get-tuple-element.78.table_ref.refs_0_.refs_1_) | copy-start | bytes 2359300
  8.1 10.4 %copy-start.20 = (bf16[48,64,128]{2,1,0:T(8,128)(2,1)}, bf16[48,64,128]{2,1,0:T(8,128)(2,1)S(1)}, u32[]{:S(2)}) copy-start(bf16[48,64,128]{2,1,0:T(8,128)(2,1)S(1)} %get-tuple-element.79.table_ref.refs_0_.refs_2_) | copy-start | bytes 2359300
  15.5 20.9 %collective-permute-start.1 = (bf16[2,24,64,128]{3,2,1,0:T(8,128)(2,1)S(1)}, bf16[2,24,64,128]{3,2,1,0:T(8,128)(2,1)S(1)}, u32[]{:S(2)}, u32[]{:S(2)}) collective-permute-start(bf16[2,24,64,128]{3,2,1,0:T(8,128)(2,1)S(1)} %get-tuple-element.53), channel_id=1, source_target_pairs={{0,1},{1,0},{2,3},{3,2},{4,5},{5,4},{6,7},{7,6},{8,9},{9,8},{10,11... | collective-permute-start | bytes 2359304 | tf_op jit(solution)/shard_map/ppermute | solution.py:398
  18.0 20.4 %collective-permute-start.3 = (bf16[2,24,64,128]{3,2,1,0:T(8,128)(2,1)S(1)}, bf16[2,24,64,128]{3,2,1,0:T(8,128)(2,1)S(1)}, u32[]{:S(2)}, u32[]{:S(2)}) collective-permute-start(bf16[2,24,64,128]{3,2,1,0:T(8,128)(2,1)S(1)} %get-tuple-element.56), channel_id=1, source_target_pairs={{0,2},{1,3},{2,0},{3,1},{4,6},{5,7},{6,4},{7,5},{8,10},{9,11},{10,... | collective-permute-start | bytes 2359304 | tf_op jit(solution)/shard_map/ppermute | solution.py:398
  25.3 13.1 %copy-start.16 = (bf16[24,64,128]{2,1,0:T(8,128)(2,1)}, bf16[24,64,128]{2,1,0:T(8,128)(2,1)S(1)}, u32[]{:S(2)}) copy-start(bf16[24,64,128]{2,1,0:T(8,128)(2,1)S(1)} %get-tuple-element.43.own_a) | copy-start | bytes 1179652
  25.3 13.1 %copy-start.18 = (bf16[24,64,128]{2,1,0:T(8,128)(2,1)}, bf16[24,64,128]{2,1,0:T(8,128)(2,1)S(1)}, u32[]{:S(2)}) copy-start(bf16[24,64,128]{2,1,0:T(8,128)(2,1)S(1)} %get-tuple-element.64.own_b) | copy-start | bytes 1179652
  25.3 13.8 %copy-start.7 = (bf16[256,3072]{1,0:T(8,128)(2,1)S(1)}, bf16[256,3072]{1,0:T(8,128)(2,1)}, u32[]{:S(2)}) copy-start(bf16[256,3072]{1,0:T(8,128)(2,1)} %values_ref.3) | copy-start | bytes 4718596
  25.4 52.2 %collective-permute-start.9 = (bf16[2,24,64,128]{3,2,1,0:T(8,128)(2,1)S(1)}, bf16[2,24,64,128]{3,2,1,0:T(8,128)(2,1)S(1)}, u32[]{:S(2)}, u32[]{:S(2)}) collective-permute-start(bf16[2,24,64,128]{3,2,1,0:T(8,128)(2,1)S(1)} %get-tuple-element.61), channel_id=1, source_target_pairs={{0,1},{1,0},{2,3},{3,2},{4,5},{5,4},{6,7},{7,6},{8,9},{9,8},{10,11... | collective-permute-start | bytes 2359304 | tf_op jit(solution)/shard_map/ppermute | solution.py:398
  25.4 49.6 %collective-permute-start.11 = (bf16[2,24,64,128]{3,2,1,0:T(8,128)(2,1)S(1)}, bf16[2,24,64,128]{3,2,1,0:T(8,128)(2,1)S(1)}, u32[]{:S(2)}, u32[]{:S(2)}) collective-permute-start(bf16[2,24,64,128]{3,2,1,0:T(8,128)(2,1)S(1)} %get-tuple-element.65), channel_id=1, source_target_pairs={{0,2},{1,3},{2,0},{3,1},{4,6},{5,7},{6,4},{7,5},{8,10},{9,11},{10,... | collective-permute-start | bytes 2359304 | tf_op jit(solution)/shard_map/ppermute | solution.py:398
  36.5 26.5 %collective-permute-start.2 = (bf16[24,64,128]{2,1,0:T(8,128)(2,1)S(1)}, bf16[24,64,128]{2,1,0:T(8,128)(2,1)S(1)}, u32[]{:S(2)}, u32[]{:S(2)}) collective-permute-start(bf16[24,64,128]{2,1,0:T(8,128)(2,1)S(1)} %fusion.3), channel_id=1, source_target_pairs={{0,2},{1,3},{2,0},{3,1},{4,6},{5,7},{6,4},{7,5},{8,10},{9,11},{10,... | collective-permute-start | bytes 1179656 | tf_op jit(solution)/shard_map/ppermute | solution.py:398
  38.5 24.5 %collective-permute-start.4 = (bf16[24,64,128]{2,1,0:T(8,128)(2,1)S(1)}, bf16[24,64,128]{2,1,0:T(8,128)(2,1)S(1)}, u32[]{:S(2)}, u32[]{:S(2)}) collective-permute-start(bf16[24,64,128]{2,1,0:T(8,128)(2,1)S(1)} %fusion.2), channel_id=1, source_target_pairs={{0,1},{1,0},{2,3},{3,2},{4,5},{5,4},{6,7},{7,6},{8,9},{9,8},{10,11... | collective-permute-start | bytes 1179656 | tf_op jit(solution)/shard_map/ppermute | solution.py:398
  43.2 0.9 copy-start.14
  64.3 8.2 %copy-start.8 = (bf16[48,64,128]{2,1,0:T(8,128)(2,1)}, bf16[48,64,128]{2,1,0:T(8,128)(2,1)S(1)}, u32[]{:S(2)}) copy-start(bf16[48,64,128]{2,1,0:T(8,128)(2,1)S(1)} %get-tuple-element.58.refs_0_.refs_1_.refs_2_) | copy-start | bytes 2359300
  64.4 8.2 %copy-start.12 = (bf16[48,64,128]{2,1,0:T(8,128)(2,1)}, bf16[48,64,128]{2,1,0:T(8,128)(2,1)S(1)}, u32[]{:S(2)}) copy-start(bf16[48,64,128]{2,1,0:T(8,128)(2,1)S(1)} %get-tuple-element.60.refs_0_) | copy-start | bytes 2359300
  64.4 20.5 %collective-permute-start.6 = (bf16[48,64,128]{2,1,0:T(8,128)(2,1)S(1)}, bf16[48,64,128]{2,1,0:T(8,128)(2,1)S(1)}, u32[]{:S(2)}, u32[]{:S(2)}) collective-permute-start(bf16[48,64,128]{2,1,0:T(8,128)(2,1)S(1)} %get-tuple-element.58.refs_0_.refs_1_.refs_2_), channel_id=1, source_target_pairs={{0,2},{1,3},{2,0},{3,1},{4,6},{5,7},{6,4},{7,5},{8,10},{9,11},{10,... | collective-permute-start | bytes 2359304 | tf_op jit(solution)/shard_map/ppermute | solution.py:398
  64.9 21.1 %collective-permute-start.5 = (bf16[48,64,128]{2,1,0:T(8,128)(2,1)S(1)}, bf16[48,64,128]{2,1,0:T(8,128)(2,1)S(1)}, u32[]{:S(2)}, u32[]{:S(2)}) collective-permute-start(bf16[48,64,128]{2,1,0:T(8,128)(2,1)S(1)} %get-tuple-element.58.refs_0_.refs_1_.refs_2_), channel_id=1, source_target_pairs={{0,1},{1,0},{2,3},{3,2},{4,5},{5,4},{6,7},{7,6},{8,9},{9,8},{10,11... | collective-permute-start | bytes 2359304 | tf_op jit(solution)/shard_map/ppermute | solution.py:398
  72.6 1.2 copy-start.24
  73.8 1.3 copy-start.26
  75.0 11.9 %copy-start.4 = (bf16[2,24,64,128]{3,2,1,0:T(8,128)(2,1)}, bf16[2,24,64,128]{3,2,1,0:T(8,128)(2,1)S(1)}, u32[]{:S(2)}) copy-start(bf16[2,24,64,128]{3,2,1,0:T(8,128)(2,1)S(1)} %collective-permute-done.11.near_b) | copy-start | bytes 2359300
  75.9 17.9 %collective-permute-start.12 = (bf16[24,64,128]{2,1,0:T(8,128)(2,1)}, bf16[24,64,128]{2,1,0:T(8,128)(2,1)S(1)}, u32[]{:S(2)}, u32[]{:S(2)}) collective-permute-start(bf16[24,64,128]{2,1,0:T(8,128)(2,1)} %fusion), channel_id=1, source_target_pairs={{0,1},{1,0},{2,3},{3,2},{4,5},{5,4},{6,7},{7,6},{8,9},{9,8},{10,11... | collective-permute-start | bytes 1179656 | tf_op jit(solution)/shard_map/ppermute | solution.py:398
  77.6 8.5 %copy-start.2 = (bf16[2,24,64,128]{3,2,1,0:T(8,128)(2,1)}, bf16[2,24,64,128]{3,2,1,0:T(8,128)(2,1)S(1)}, u32[]{:S(2)}) copy-start(bf16[2,24,64,128]{3,2,1,0:T(8,128)(2,1)S(1)} %collective-permute-done.9.near_a) | copy-start | bytes 2359300
  78.5 15.4 %collective-permute-start.10 = (bf16[24,64,128]{2,1,0:T(8,128)(2,1)}, bf16[24,64,128]{2,1,0:T(8,128)(2,1)S(1)}, u32[]{:S(2)}, u32[]{:S(2)}) collective-permute-start(bf16[24,64,128]{2,1,0:T(8,128)(2,1)} %fusion.1), channel_id=1, source_target_pairs={{0,2},{1,3},{2,0},{3,1},{4,6},{5,7},{6,4},{7,5},{8,10},{9,11},{10,... | collective-permute-start | bytes 1179656 | tf_op jit(solution)/shard_map/ppermute | solution.py:398
  85.7 16.9 %collective-permute-start.8 = (bf16[24,64,128]{2,1,0:T(8,128)(2,1)}, bf16[24,64,128]{2,1,0:T(8,128)(2,1)S(1)}, u32[]{:S(2)}, u32[]{:S(2)}) collective-permute-start(bf16[24,64,128]{2,1,0:T(8,128)(2,1)} %slice.35), channel_id=1, source_target_pairs={{0,1},{1,0},{2,3},{3,2},{4,5},{5,4},{6,7},{7,6},{8,9},{9,8},{10,11... | collective-permute-start | bytes 1179656 | tf_op jit(solution)/shard_map/ppermute | solution.py:398
  86.0 28.5 %copy-start = (bf16[48,64,128]{2,1,0:T(8,128)(2,1)}, bf16[48,64,128]{2,1,0:T(8,128)(2,1)S(1)}, u32[]{:S(2)}) copy-start(bf16[48,64,128]{2,1,0:T(8,128)(2,1)S(1)} %collective-permute-done.5.refs_1_.refs_2_.refs_3_) | copy-start | bytes 2359300
  86.9 15.7 %collective-permute-start.7 = (bf16[24,64,128]{2,1,0:T(8,128)(2,1)}, bf16[24,64,128]{2,1,0:T(8,128)(2,1)S(1)}, u32[]{:S(2)}, u32[]{:S(2)}) collective-permute-start(bf16[24,64,128]{2,1,0:T(8,128)(2,1)} %slice.34), channel_id=1, source_target_pairs={{0,2},{1,3},{2,0},{3,1},{4,6},{5,7},{6,4},{7,5},{8,10},{9,11},{10,... | collective-permute-start | bytes 1179656 | tf_op jit(solution)/shard_map/ppermute | solution.py:398
  93.8 1.1 copy-start.3
  95.0 1.1 copy-start.5
  96.1 1.1 copy-start.15
  97.2 1.0 copy-start.17
  98.2 1.0 copy-start.19
  99.2 3.4 %copy-start.9 = (bf16[48,64,128]{2,1,0:T(8,128)(2,1)S(1)}, bf16[48,64,128]{2,1,0:T(8,128)(2,1)}, u32[]{:S(2)}) copy-start(bf16[48,64,128]{2,1,0:T(8,128)(2,1)} %copy-done.8) | copy-start | bytes 2359300
  99.2 3.4 %copy-start.25 = (bf16[216,32,128]{2,1,0:T(8,128)(2,1)S(1)}, bf16[216,32,128]{2,1,0:T(8,128)(2,1)}, u32[]{:S(2)}) copy-start(bf16[216,32,128]{2,1,0:T(8,128)(2,1)} %copy-done.24) | copy-start | bytes 5308420
  99.2 3.4 %copy-start.27 = (bf16[216,32,128]{2,1,0:T(8,128)(2,1)S(1)}, bf16[216,32,128]{2,1,0:T(8,128)(2,1)}, u32[]{:S(2)}) copy-start(bf16[216,32,128]{2,1,0:T(8,128)(2,1)} %copy-done.26) | copy-start | bytes 5308420
  100.6 18.5 %collective-permute-start.15 = (bf16[48,64,128]{2,1,0:T(8,128)(2,1)S(1)}, bf16[48,64,128]{2,1,0:T(8,128)(2,1)S(1)}, u32[]{:S(2)}, u32[]{:S(2)}) collective-permute-start(bf16[48,64,128]{2,1,0:T(8,128)(2,1)S(1)} %get-tuple-element.69.refs_1_.refs_0_.refs_3_), channel_id=1, source_target_pairs={{0,2},{1,3},{2,0},{3,1},{4,6},{5,7},{6,4},{7,5},{8,10},{9,11},{10,... | collective-permute-start | bytes 2359304 | tf_op jit(solution)/shard_map/ppermute | solution.py:398
  102.2 19.0 %collective-permute-start.17 = (bf16[48,64,128]{2,1,0:T(8,128)(2,1)S(1)}, bf16[48,64,128]{2,1,0:T(8,128)(2,1)S(1)}, u32[]{:S(2)}, u32[]{:S(2)}) collective-permute-start(bf16[48,64,128]{2,1,0:T(8,128)(2,1)S(1)} %get-tuple-element.69.refs_1_.refs_0_.refs_3_), channel_id=1, source_target_pairs={{0,1},{1,0},{2,3},{3,2},{4,5},{5,4},{6,7},{7,6},{8,9},{9,8},{10,11... | collective-permute-start | bytes 2359304 | tf_op jit(solution)/shard_map/ppermute | solution.py:398
  102.6 6.3 %copy-start.13 = (bf16[48,64,128]{2,1,0:T(8,128)(2,1)S(1)}, bf16[48,64,128]{2,1,0:T(8,128)(2,1)}, u32[]{:S(2)}) copy-start(bf16[48,64,128]{2,1,0:T(8,128)(2,1)} %copy-done.12) | copy-start | bytes 2359300
  108.8 12.5 %collective-permute-start.13 = (bf16[2,32,3072]{2,1,0:T(8,128)(2,1)S(1)}, bf16[2,32,3072]{2,1,0:T(8,128)(2,1)S(1)}, u32[]{:S(2)}, u32[]{:S(2)}) collective-permute-start(bf16[2,32,3072]{2,1,0:T(8,128)(2,1)S(1)} %dynamic-slice_bitcast_fusion.1), channel_id=1, source_target_pairs={{0,4},{4,0},{8,12},{12,8},{1,5},{5,1},{9,13},{13,9},{2,6},{6,2},{1... | collective-permute-start | bytes 1179656 | tf_op jit(solution)/shard_map/ppermute | solution.py:444
  108.9 5.7 %copy-start.23 = (bf16[48,64,128]{2,1,0:T(8,128)(2,1)S(1)}, bf16[48,64,128]{2,1,0:T(8,128)(2,1)}, u32[]{:S(2)}) copy-start(bf16[48,64,128]{2,1,0:T(8,128)(2,1)} %copy-done.22) | copy-start | bytes 2359300
  119.0 31.4 %collective-permute-start.21 = (bf16[216,32,128]{2,1,0:T(8,128)(2,1)S(1)}, bf16[216,32,128]{2,1,0:T(8,128)(2,1)S(1)}, u32[]{:S(2)}, u32[]{:S(2)}) collective-permute-start(bf16[216,32,128]{2,1,0:T(8,128)(2,1)S(1)} %outer_other.2), channel_id=1, source_target_pairs={{0,16},{16,0},{1,17},{17,1},{2,18},{18,2},{3,19},{19,3},{4,20},{20... | collective-permute-start | bytes 5308424 | tf_op jit(solution)/shard_map/ppermute | solution.py:401
  119.1 11.8 %collective-permute-start.16 = (bf16[24,64,128]{2,1,0:T(8,128)(2,1)S(1)}, bf16[24,64,128]{2,1,0:T(8,128)(2,1)S(1)}, u32[]{:S(2)}, u32[]{:S(2)}) collective-permute-start(bf16[24,64,128]{2,1,0:T(8,128)(2,1)S(1)} %slice.38), channel_id=1, source_target_pairs={{0,1},{1,0},{2,3},{3,2},{4,5},{5,4},{6,7},{7,6},{8,9},{9,8},{10,11... | collective-permute-start | bytes 1179656 | tf_op jit(solution)/shard_map/ppermute | solution.py:398
  121.2 11.3 %collective-permute-start.18 = (bf16[24,64,128]{2,1,0:T(8,128)(2,1)S(1)}, bf16[24,64,128]{2,1,0:T(8,128)(2,1)S(1)}, u32[]{:S(2)}, u32[]{:S(2)}) collective-permute-start(bf16[24,64,128]{2,1,0:T(8,128)(2,1)S(1)} %slice.39), channel_id=1, source_target_pairs={{0,2},{1,3},{2,0},{3,1},{4,6},{5,7},{6,4},{7,5},{8,10},{9,11},{10,... | collective-permute-start | bytes 1179656 | tf_op jit(solution)/shard_map/ppermute | solution.py:398
  121.4 10.4 %collective-permute-start.14 = (bf16[32,3072]{1,0:T(8,128)(2,1)S(1)}, bf16[32,3072]{1,0:T(8,128)(2,1)S(1)}, u32[]{:S(2)}, u32[]{:S(2)}) collective-permute-start(bf16[32,3072]{1,0:T(8,128)(2,1)S(1)} %fusion.7), channel_id=1, source_target_pairs={{0,8},{4,12},{8,0},{12,4},{1,9},{5,13},{9,1},{13,5},{2,10},{6,14},... | collective-permute-start | bytes 589832 | tf_op jit(solution)/shard_map/ppermute | solution.py:446
  122.2 16.4 %copy-start.21 = (bf16[48,64,128]{2,1,0:T(8,128)(2,1)S(1)}, bf16[48,64,128]{2,1,0:T(8,128)(2,1)}, u32[]{:S(2)}) copy-start(bf16[48,64,128]{2,1,0:T(8,128)(2,1)} %copy-done.20) | copy-start | bytes 2359300
  138.5 10.5 %collective-permute-start.19 = (bf16[2,32,3072]{2,1,0:T(8,128)(2,1)S(1)}, bf16[2,32,3072]{2,1,0:T(8,128)(2,1)S(1)}, u32[]{:S(2)}, u32[]{:S(2)}) collective-permute-start(bf16[2,32,3072]{2,1,0:T(8,128)(2,1)S(1)} %dynamic-slice_bitcast_fusion), channel_id=1, source_target_pairs={{0,4},{4,0},{8,12},{12,8},{1,5},{5,1},{9,13},{13,9},{2,6},{6,2},{1... | collective-permute-start | bytes 1179656 | tf_op jit(solution)/shard_map/ppermute | solution.py:444
  143.1 7.4 %copy-start.1 = (bf16[48,64,128]{2,1,0:T(8,128)(2,1)S(1)}, bf16[48,64,128]{2,1,0:T(8,128)(2,1)}, u32[]{:S(2)}) copy-start(bf16[48,64,128]{2,1,0:T(8,128)(2,1)} %copy-done) | copy-start | bytes 2359300
  143.1 12.2 %collective-permute-start.22 = (bf16[216,32,128]{2,1,0:T(8,128)(2,1)S(1)}, bf16[216,32,128]{2,1,0:T(8,128)(2,1)S(1)}, u32[]{:S(2)}, u32[]{:S(2)}) collective-permute-start(bf16[216,32,128]{2,1,0:T(8,128)(2,1)S(1)} %outer_other.3), channel_id=1, source_target_pairs={{0,16},{16,0},{1,17},{17,1},{2,18},{18,2},{3,19},{19,3},{4,20},{20... | collective-permute-start | bytes 5308424 | tf_op jit(solution)/shard_map/ppermute | solution.py:401
  149.7 12.6 %collective-permute-start.20 = (bf16[32,3072]{1,0:T(8,128)(2,1)}, bf16[32,3072]{1,0:T(8,128)(2,1)}, u32[]{:S(2)}, u32[]{:S(2)}) collective-permute-start(bf16[32,3072]{1,0:T(8,128)(2,1)} %fusion.6), channel_id=1, source_target_pairs={{0,8},{4,12},{8,0},{12,4},{1,9},{5,13},{9,1},{13,5},{2,10},{6,14},... | collective-permute-start | bytes 589832 | tf_op jit(solution)/shard_map/ppermute | solution.py:446
  160.2 2.2 %copy-start.28 = (bf16[32,3072]{1,0:T(8,128)(2,1)S(1)}, bf16[32,3072]{1,0:T(8,128)(2,1)}, u32[]{:S(2)}) copy-start(bf16[32,3072]{1,0:T(8,128)(2,1)} %dynamic-slice_bitcast_fusion.2) | copy-start | bytes 589828
  160.2 3.2 %copy-start.29 = (bf16[32,3072]{1,0:T(8,128)(2,1)S(1)}, bf16[32,3072]{1,0:T(8,128)(2,1)}, u32[]{:S(2)}) copy-start(bf16[32,3072]{1,0:T(8,128)(2,1)} %add_convert_fusion) | copy-start | bytes 589828

commit v4 on v3

--- a/solution.py
+++ b/solution.py
@@ -20,7 +20,7 @@
 MIB = 1024 * 1024
 VMEM = pl.BlockSpec(memory_space=pltpu.VMEM)
 SMEM = pl.BlockSpec(memory_space=pltpu.SMEM)
-ANY = pl.BlockSpec(memory_space=pl.ANY)
+HBM = pl.BlockSpec(memory_space=pltpu.HBM)
 NT = (((1,), (1,)), ((), ()))
 
 
@@ -141,8 +141,8 @@
         [SMEM] * 3 + [VMEM] * 3,
         [VMEM] * 6,
         (facts, rows, cols, own, other, table),
-        20,
-        7,
+        16,
+        0,
         [pltpu.VMEM((blocks + 1, BLOCK, width), jnp.float32)],
     )
 
@@ -179,10 +179,10 @@
         functools.partial(backward_kernel, share_blocks),
         "backward",
         jax.ShapeDtypeStruct((width, in_blocks * BLOCK), jnp.bfloat16),
-        [SMEM] * 3 + [VMEM] * 2 + [ANY] * len(pieces),
+        [SMEM] * 3 + [VMEM] * 2 + [HBM] * len(pieces),
         VMEM,
         (facts, rows, cols, own, other, *pieces),
-        20,
+        12,
         7,
         [
             pltpu.VMEM((in_blocks + 1, BLOCK, width), jnp.float32),
@@ -228,10 +228,10 @@
         functools.partial(outer_kernel, share_blocks, mine, len(added)),
         "outer_own" if mine else "outer_other",
         jax.ShapeDtypeStruct((half_slots, HALF, 2 * BLOCK), jnp.bfloat16),
-        [SMEM] * 3 + [VMEM] * (len(added) + 1) + [ANY] * len(pieces),
+        [SMEM] * 3 + [VMEM] * (len(added) + 1) + [HBM] * len(pieces),
         VMEM,
         (facts, rows, cols, *added, inputs, *pieces),
-        20,
+        12,
         5,
         [
             pltpu.VMEM((blocks, BLOCK, inputs.shape[2]), jnp.bfloat16),
@@ -262,8 +262,8 @@
         [VMEM] * 2,
         [VMEM] * 2,
         (own, other),
-        12,
-        7,
+        10,
+        0,
     )
 
 
@@ -298,8 +298,8 @@
         [VMEM] * 2,
         [VMEM] * chunks,
         (values, select),
-        12,
-        5,
+        6,
+        0,
     )
 
 
@@ -326,18 +326,25 @@
         [VMEM] * (1 + len(acts)),
         VMEM,
         (select, *acts),
-        12,
         6,
-    )
-
-
-def gelu_kernel(upstream_ref, own_a, near_a, last_a, own_b, near_b, last_b, grad_out, act_out):
+        0,
+    )
+
+
+def gelu_kernel(upstream_hbm, own_a, near_a, last_a, own_b, near_b, last_b, grad_out, act_out, upstream_ref, held, sem):
     half_blocks = own_a.shape[0]
-    for half, (own, near, last) in enumerate(((own_a, near_a, last_a), (own_b, near_b, last_b))):
-
-        def one(block, half=half, own=own, near=near, last=last):
-            pre = own[block].astype(jnp.float32) + near[1, block].astype(jnp.float32)
-            pre = pre + last[block].astype(jnp.float32)
+    copies = [pltpu.make_async_copy(upstream_hbm, upstream_ref, sem.at[6])]
+    for number, source in enumerate((own_a, near_a.at[1], last_a, own_b, near_b.at[1], last_b)):
+        copies.append(pltpu.make_async_copy(source, held.at[number], sem.at[number]))
+    for copy in copies:
+        copy.start()
+    for copy in copies:
+        copy.wait()
+    for half in range(2):
+
+        def one(block, half=half):
+            pre = held[3 * half, block].astype(jnp.float32) + held[3 * half + 1, block].astype(jnp.float32)
+            pre = pre + held[3 * half + 2, block].astype(jnp.float32)
             square = pre * pre
             inner = jnp.tanh(COEFF * (pre + CUBIC * square * pre))
             front = 0.5 * (1.0 + inner)
@@ -355,11 +362,16 @@
         gelu_kernel,
         "gelu",
         [shape] * 2,
-        [VMEM] * 7,
+        [HBM] * 7,
         [VMEM] * 2,
         (upstream, *parts),
-        12,
-        2,
+        8,
+        0,
+        [
+            pltpu.VMEM(upstream.shape, jnp.bfloat16),
+            pltpu.VMEM((6, *parts[0].shape), jnp.bfloat16),
+            pltpu.SemaphoreType.DMA((7,)),
+        ],
     )
 
 
@@ -409,7 +421,7 @@
     upstream = list(token_rows(act_grad, after(select, partials[1][2]), True))
     own_t, other_t = transpose_tiles(after(own, upstream[1]), after(other, upstream[1]))
 
-    grads, acts = [], []
+    terms, sums = [], []
     for chunk in range(CHUNKS):
         along_x, along_y, own_a, own_b, relay_x, relay_y = partials[chunk]
         from_x, from_y = across(along_x, 1), across(along_y, 2)
@@ -417,7 +429,13 @@
         if chunk:
             sum_y = after(sum_y, own_t)
         last_a, last_b = across(sum_y, 2), across(sum_x, 1)
-        grad, act = gelu(upstream[chunk], (own_a, from_x, last_a, own_b, from_y, last_b))
+        sums += [sum_y, sum_x]
+        terms.append((own_a, from_x, last_a, own_b, from_y, last_b))
+    upstream[0] = after(upstream[0], sums)
+
+    grads, acts = [], []
+    for chunk in range(CHUNKS):
+        grad, act = gelu(upstream[chunk], terms[chunk])
         acts.append(act)
         sent_x = sent_y = grad
         if chunk:

time: 166 us -> 171 us (1.030); the launches traced: 164 us -> 172 us
  starting transfers between devices: 15.8 us -> 35.5 us
  Pallas kernels: 68.7 us -> 59.2 us
  waiting for transfers between devices: 57.1 us -> 54.8 us
    ppermute x16, starting transfers between devices: 14.2 us -> 23.9 us  [across(): lax.ppermute(values, 'col', [(place, place ^ bit) for place in range(shar...]
    pallas_call x14, Pallas kernels: 68.7 us -> 59.2 us  [call(): pl.pallas_call(kernel, out_shape=out_shape, in_specs=in_specs, out_specs=...]
    ppermute x2, starting transfers between devices: 0.14 us -> 4.94 us  [to_rows(): lax.ppermute(sent, 'row', [(place, place ^ 1) for place in range(4)])]
    ppermute x16, waiting for transfers between devices: 51.1 us -> 47.7 us  [across(): lax.ppermute(values, 'col', [(place, place ^ bit) for place in range(shar...]
    ppermute x2, starting transfers between devices: 0.82 us -> 4.23 us  [to_rows(): lax.ppermute(both.astype(jnp.bfloat16), 'row', [(place, place ^ 2) for pl...]
    ppermute x3, starting transfers between devices: 0.66 us -> 2.45 us  [other_core(): return lax.ppermute(values, 'dp', [(0, 1), (1, 0)])]
    unnamed x61 -> x67, local copies, waits for them, and re-layouts: 10.8 us -> 11.7 us
  transfers between devices with their start and end apart: 23 -> 23, of which waited for: 9 -> 9; matrix products, arithmetic and copies ran while one was open for 5% -> 4% of each run, Pallas kernels for 37% -> 30%
where the time goes in v4:
time: 171 us; the launch traced here: 172 us
  Pallas kernels  59.2 us (35%)
  waiting for transfers between devices  54.8 us (32%)
  starting transfers between devices  35.5 us (21%)
  local copies, waits for them, and re-layouts  15.6 us (9%)
  other arithmetic  5.27 us (3%)
  between operations  1.77 us (1%)
    pallas_call x14, Pallas kernels, call(): pl.pallas_call(kernel, out_shape=out_shape, in_specs=in_specs, out_specs=...  59.2 us
    ppermute x16, waiting for transfers between devices, across(): lax.ppermute(values, 'col', [(place, place ^ bit) for place in range(shar...  47.7 us
    ppermute x16, starting transfers between devices, across(): lax.ppermute(values, 'col', [(place, place ^ bit) for place in range(shar...  23.9 us
    unnamed x67, local copies, waits for them, and re-layouts  11.7 us
    ppermute x2, starting transfers between devices, to_rows(): lax.ppermute(sent, 'row', [(place, place ^ 1) for place in range(4)])  4.94 us
    ppermute x2, waiting for transfers between devices, to_rows(): lax.ppermute(sent, 'row', [(place, place ^ 1) for place in range(4)])  4.63 us
    ppermute x2, starting transfers between devices, to_rows(): lax.ppermute(both.astype(jnp.bfloat16), 'row', [(place, place ^ 2) for pl...  4.23 us
  transfers between devices with their start and end apart: 23, of which 9 were waited for; matrix products, arithmetic and copies ran while one was open for 4% of the time, Pallas kernels for 30%

profile of v4, /device:TPU:0, one launch (start us, length us, event | category | flops | bytes accessed | tf_op | source)
XLA Modules:
  0.0 172.2 jit_solution(16774801104484334195)
XLA Ops:
  0.6 1.8 %copy.9 = bf16[27,8,32,128]{3,2,1,0:T(8,128)(2,1)S(1)} copy(bf16[27,8,32,128]{3,1,2,0:T(8,128)(2,1)} %bitcast.79) | data formatting | bytes 3538944
  2.5 0.5 collective-permute-start
  3.8 1.4 copy-done.6
  5.2 4.1 %features_to_rows.1 = (bf16[48,64,128]{2,1,0:T(8,128)(2,1)S(1)}, bf16[48,64,128]{2,1,0:T(8,128)(2,1)S(1)}) custom-call(bf16[256,3072]{1,0:T(8,128)(2,1)S(1)} %copy-done.6, bf16[2,256,128]{2,1,0:T(8,128)(2,1)S(1)} %fusion.8.select_ref), custom_call_target="tpu_custom_call" | custom-call | tf_op jit(solution)/shard_map/features_to_rows/pallas_call | solution.py:50
  9.3 0.1 pad_add_fusion.facts_ref
  9.4 4.2 %forward.3 = (bf16[2,24,64,128]{3,2,1,0:T(8,128)(2,1)S(1)}, bf16[2,24,64,128]{3,2,1,0:T(8,128)(2,1)S(1)}, bf16[24,64,128]{2,1,0:T(8,128)(2,1)S(1)}, bf16[24,64,1...) custom-call(s32[3]{0:T(128)S(1)} %pad_add_fusion.facts_ref, ...), custom_call_target="tpu_custom_call" | custom-call | tf_op jit(solution)/shard_map/forward/pallas_call | solution.py:50
  13.7 4.1 %collective-permute-start.1 = (bf16[2,24,64,128]{3,2,1,0:T(8,128)(2,1)S(1)}, bf16[2,24,64,128]{3,2,1,0:T(8,128)(2,1)S(1)}, u32[]{:S(2)}, u32[]{:S(2)}) collective-permute-start(bf16[2,24,64,128]{3,2,1,0:T(8,128)(2,1)S(1)} %get-tuple-element.54), channel_id=1, source_target_pairs={{0,1},{1,0},{2,3},{3,2},{4,5},{5,4},{6,7},{7,6},{8,9},{9,8},{10,11... | collective-permute-start | bytes 2359304 | tf_op jit(solution)/shard_map/ppermute | solution.py:410
  17.8 1.5 collective-permute-start.2
  19.4 4.3 %forward.2 = (bf16[2,24,64,128]{3,2,1,0:T(8,128)(2,1)S(1)}, bf16[2,24,64,128]{3,2,1,0:T(8,128)(2,1)S(1)}, bf16[24,64,128]{2,1,0:T(8,128)(2,1)S(1)}, bf16[24,64,1...) custom-call(s32[3]{0:T(128)S(1)} %pad_add_fusion.facts_ref, ...), custom_call_target="tpu_custom_call" | custom-call | tf_op jit(solution)/shard_map/forward/pallas_call | solution.py:50
  23.7 1.8 %collective-permute-start.3 = (bf16[2,24,64,128]{3,2,1,0:T(8,128)(2,1)S(1)}, bf16[2,24,64,128]{3,2,1,0:T(8,128)(2,1)S(1)}, u32[]{:S(2)}, u32[]{:S(2)}) collective-permute-start(bf16[2,24,64,128]{3,2,1,0:T(8,128)(2,1)S(1)} %get-tuple-element.58), channel_id=1, source_target_pairs={{0,1},{1,0},{2,3},{3,2},{4,5},{5,4},{6,7},{7,6},{8,9},{9,8},{10,11... | collective-permute-start | bytes 2359304 | tf_op jit(solution)/shard_map/ppermute | solution.py:410
  25.4 0.5 collective-permute-start.4
  25.9 4.1 %units_to_rows.1 = (bf16[48,64,128]{2,1,0:T(8,128)(2,1)S(1)}, bf16[48,64,128]{2,1,0:T(8,128)(2,1)S(1)}) custom-call(bf16[256,3072]{1,0:T(8,128)(2,1)S(1)} %copy-done.7, bf16[2,256,128]{2,1,0:T(8,128)(2,1)S(1)} %fusion.8.select_ref), custom_call_target="tpu_custom_call" | custom-call | tf_op jit(solution)/shard_map/units_to_rows/pallas_call | solution.py:50
  30.0 0.9 copy-done.12
  30.9 5.8 %transpose_tiles.1 = (bf16[216,32,128]{2,1,0:T(8,128)(2,1)S(1)}, bf16[216,32,128]{2,1,0:T(8,128)(2,1)S(1)}) custom-call(bf16[216,32,128]{2,1,0:T(8,128)(2,1)S(1)} %bitcast.56, bf16[216,32,128]{2,1,0:T(8,128)(2,1)S(1)} %collective-permute-done.other_ref), custom_call_target="tpu_custom_call" | custom-call | tf_op jit(solution)/shard_map/transpose_tiles/pallas_call | solution.py:50
  36.7 1.2 copy-done.26
  38.0 1.6 collective-permute-start.5
  39.7 0.4 collective-permute-start.6
  40.1 13.0 %collective-permute-done.3.near_a = bf16[2,24,64,128]{3,2,1,0:T(8,128)(2,1)S(1)} collective-permute-done((bf16[2,24,64,128]{3,2,1,0:T(8,128)(2,1)S(1)}, bf16[2,24,64,128]{3,2,1,0:T(8,128)(2,1)S(1)}, u32[]{:S(2)}, u32[]{:S(2)}) %collective-permute-start.3) | collective-permute-done | bytes 786464 | tf_op jit(solution)/shard_map/ppermute | solution.py:410
  53.1 0.8 fusion.1
  53.9 0.9 copy-done.2
  54.8 0.3 collective-permute-done.4.near_b
  55.1 0.9 fusion
  55.9 6.8 %collective-permute-done.5.last_a = bf16[24,64,128]{2,1,0:T(8,128)(2,1)S(1)} collective-permute-done((bf16[24,64,128]{2,1,0:T(8,128)(2,1)S(1)}, bf16[24,64,128]{2,1,0:T(8,128)(2,1)S(1)}, u32[]{:S(2)}, u32[]{:S(2)}) %collective-permute-start.5) | collective-permute-done | bytes 393248 | tf_op jit(solution)/shard_map/ppermute | solution.py:410
  62.8 2.6 %gelu.2 = (bf16[48,64,128]{2,1,0:T(8,128)(2,1)S(1)}, bf16[48,64,128]{2,1,0:T(8,128)(2,1)S(1)}) custom-call(bf16[48,64,128]{2,1,0:T(8,128)(2,1)S(1)} %get-tuple-element.62.upstream_hbm, bf16[24,64,128]{2,1,0:T(8,128)(2,1)S(1)} %get-tuple-element.63.own_a, bf16[2,24,64,128]{3,2,1,0:T(8,128)(2,1)S(1)} %collective-permute-done.1.near_a, ...), custom_call_target="tpu_custom_call" | custom-call | tf_op jit(solution)/shard_map/gelu/pallas_call | solution.py:50
  65.4 0.4 collective-permute-start.7
  65.9 1.5 collective-permute-start.8
  67.4 0.5 collective-permute-start.11
  67.9 1.7 collective-permute-start.12
  69.6 16.4 %collective-permute-done.7.refs_1_.refs_2_.refs_3_ = bf16[48,64,128]{2,1,0:T(8,128)(2,1)S(1)} collective-permute-done((bf16[48,64,128]{2,1,0:T(8,128)(2,1)S(1)}, bf16[48,64,128]{2,1,0:T(8,128)(2,1)S(1)}, u32[]{:S(2)}, u32[]{:S(2)}) %collective-permute-start.7) | collective-permute-done | bytes 786464 | tf_op jit(solution)/shard_map/ppermute | solution.py:410
  86.0 0.8 slice.36
  86.8 0.9 copy-done.18
  87.7 1.5 collective-permute-start.9
  89.2 0.8 slice.37
  89.9 0.9 copy-done.20
  90.8 0.3 collective-permute-start.10
  91.1 3.7 %collective-permute-done.11.last_a = bf16[24,64,128]{2,1,0:T(8,128)(2,1)} collective-permute-done((bf16[24,64,128]{2,1,0:T(8,128)(2,1)}, bf16[24,64,128]{2,1,0:T(8,128)(2,1)}, u32[]{:S(2)}, u32[]{:S(2)}) %collective-permute-start.11) | collective-permute-done | bytes 393248 | tf_op jit(solution)/shard_map/ppermute | solution.py:410
  94.9 1.0 copy-done.17
  95.9 3.6 %gelu.3 = (bf16[48,64,128]{2,1,0:T(8,128)(2,1)S(1)}, bf16[48,64,128]{2,1,0:T(8,128)(2,1)S(1)}) custom-call(bf16[48,64,128]{2,1,0:T(8,128)(2,1)S(1)} %copy-done.13, bf16[24,64,128]{2,1,0:T(8,128)(2,1)S(1)} %copy-done.15, bf16[2,24,64,128]{3,2,1,0:T(8,128)(2,1)S(1)} %copy-done.3, bf16[24,64,128]{2,1,0:T(8,128)(2,1)} %collective-permute-done.11.last_a, ...), custom_call_target="tpu_custom_call" | custom-call | tf_op jit(solution)/shard_map/gelu/pallas_call | solution.py:50
  99.5 1.7 %collective-permute-start.17 = (bf16[48,64,128]{2,1,0:T(8,128)(2,1)S(1)}, bf16[48,64,128]{2,1,0:T(8,128)(2,1)S(1)}, u32[]{:S(2)}, u32[]{:S(2)}) collective-permute-start(bf16[48,64,128]{2,1,0:T(8,128)(2,1)S(1)} %get-tuple-element.71.refs_1_.refs_0_.refs_3_), channel_id=1, source_target_pairs={{0,1},{1,0},{2,3},{3,2},{4,5},{5,4},{6,7},{7,6},{8,9},{9,8},{10,11... | collective-permute-start | bytes 2359304 | tf_op jit(solution)/shard_map/ppermute | solution.py:410
  101.2 1.5 collective-permute-start.15
  102.7 0.6 collective-permute-done.9.refs_3_.refs_4_.refs_5_
  103.3 1.5 copy-done.27
  104.8 1.1 copy-done.30
  105.9 5.3 %backward.2 = bf16[128,3072]{1,0:T(8,128)(2,1)S(1)} custom-call(s32[3]{0:T(128)S(1)} %pad_add_fusion.facts_ref, s32[432]{0:T(512)S(1)} %bitcast.65, s32[432]{0:T(512)S(1)} %bitcast.73, bf16[216,32,128]{2,1,0:T(8,128)(2,1)S(1)} %copy-done.25, bf16[216,32,128]{2,1,0:T(8,128)(2,1)S(1)} %copy-done.27, bf16[48,64,128]{2,1,0:T(8,128)(2,1)S(1)} %copy-done.30, ...), custom_call_target="tpu_custom_call" | custom-call | flops 8049999872 | bytes 7474572 | tf_op jit(solution)/shard_map/backward/pallas_call | solution.py:50
  111.3 3.3 %collective-permute-start.13 = (bf16[2,32,3072]{2,1,0:T(8,128)(2,1)S(1)}, bf16[2,32,3072]{2,1,0:T(8,128)(2,1)S(1)}, u32[]{:S(2)}, u32[]{:S(2)}) collective-permute-start(bf16[2,32,3072]{2,1,0:T(8,128)(2,1)S(1)} %dynamic-slice_bitcast_fusion.1), channel_id=1, source_target_pairs={{0,4},{4,0},{8,12},{12,8},{1,5},{5,1},{9,13},{13,9},{2,6},{6,2},{1... | collective-permute-start | bytes 1179656 | tf_op jit(solution)/shard_map/ppermute | solution.py:462
  114.6 5.7 %rows_to_units.1 = bf16[256,3072]{1,0:T(8,128)(2,1)} custom-call(bf16[2,256,128]{2,1,0:T(8,128)(2,1)S(1)} %copy-done.1, bf16[48,64,128]{2,1,0:T(8,128)(2,1)S(1)} %get-tuple-element.67.refs_0_, bf16[48,64,128]{2,1,0:T(8,128)(2,1)S(1)} %get-tuple-element.69.refs_1_), custom_call_target="tpu_custom_call" | custom-call | tf_op jit(solution)/shard_map/rows_to_units/pallas_call | solution.py:50
  120.3 2.7 %outer_other.2 = bf16[216,32,128]{2,1,0:T(8,128)(2,1)S(1)} custom-call(s32[3]{0:T(128)S(1)} %pad_add_fusion.facts_ref, s32[432]{0:T(512)S(1)} %bitcast.66, s32[432]{0:T(512)S(1)} %bitcast.74, bf16[48,64,128]{2,1,0:T(8,128)(2,1)S(1)} %copy-done.11, bf16[48,64,128]{2,1,0:T(8,128)(2,1)S(1)} %copy-done.31, bf16[48,64,128]{2,1,0:T(8,128)(2,1)S(1)} %copy-done.19, ...), custom_call_target="tpu_custom_call" | custom-call | flops 5750000128 | bytes 5705100 | tf_op jit(solution)/shard_map/outer_other/pallas_call | solution.py:50
  123.3 4.8 %collective-permute-start.16 = (bf16[24,64,128]{2,1,0:T(8,128)(2,1)S(1)}, bf16[24,64,128]{2,1,0:T(8,128)(2,1)S(1)}, u32[]{:S(2)}, u32[]{:S(2)}) collective-permute-start(bf16[24,64,128]{2,1,0:T(8,128)(2,1)S(1)} %slice.38), channel_id=1, source_target_pairs={{0,1},{1,0},{2,3},{3,2},{4,5},{5,4},{6,7},{7,6},{8,9},{9,8},{10,11... | collective-permute-start | bytes 1179656 | tf_op jit(solution)/shard_map/ppermute | solution.py:410
  128.2 2.7 %collective-permute-start.14 = (bf16[32,3072]{1,0:T(8,128)(2,1)S(1)}, bf16[32,3072]{1,0:T(8,128)(2,1)S(1)}, u32[]{:S(2)}, u32[]{:S(2)}) collective-permute-start(bf16[32,3072]{1,0:T(8,128)(2,1)S(1)} %fusion.7), channel_id=1, source_target_pairs={{0,8},{4,12},{8,0},{12,4},{1,9},{5,13},{9,1},{13,5},{2,10},{6,14},... | collective-permute-start | bytes 589832 | tf_op jit(solution)/shard_map/ppermute | solution.py:464
  130.9 6.7 %collective-permute-done.16.refs_5_.refs_4_.refs_7_ = bf16[24,64,128]{2,1,0:T(8,128)(2,1)S(1)} collective-permute-done((bf16[24,64,128]{2,1,0:T(8,128)(2,1)S(1)}, bf16[24,64,128]{2,1,0:T(8,128)(2,1)S(1)}, u32[]{:S(2)}, u32[]{:S(2)}) %collective-permute-start.16) | collective-permute-done | bytes 393248 | tf_op jit(solution)/shard_map/ppermute | solution.py:410
  137.6 2.5 %collective-permute-done.14 = bf16[32,3072]{1,0:T(8,128)(2,1)S(1)} collective-permute-done((bf16[32,3072]{1,0:T(8,128)(2,1)S(1)}, bf16[32,3072]{1,0:T(8,128)(2,1)S(1)}, u32[]{:S(2)}, u32[]{:S(2)}) %collective-permute-start.14) | collective-permute-done | bytes 196640 | tf_op jit(solution)/shard_map/ppermute | solution.py:464
  140.1 4.4 %backward.3 = bf16[128,3072]{1,0:T(8,128)(2,1)S(1)} custom-call(s32[3]{0:T(128)S(1)} %pad_add_fusion.facts_ref, s32[432]{0:T(512)S(1)} %bitcast.67, s32[432]{0:T(512)S(1)} %bitcast.75, bf16[216,32,128]{2,1,0:T(8,128)(2,1)S(1)} %copy-done.25, bf16[216,32,128]{2,1,0:T(8,128)(2,1)S(1)} %copy-done.28, ...), custom_call_target="tpu_custom_call" | custom-call | flops 8049999872 | bytes 7474572 | tf_op jit(solution)/shard_map/backward/pallas_call | solution.py:50
  144.5 1.6 collective-permute-start.19
  146.1 2.0 %outer_other.3 = bf16[216,32,128]{2,1,0:T(8,128)(2,1)S(1)} custom-call(s32[3]{0:T(128)S(1)} %pad_add_fusion.facts_ref, s32[432]{0:T(512)S(1)} %bitcast.68, s32[432]{0:T(512)S(1)} %bitcast.76, bf16[48,64,128]{2,1,0:T(8,128)(2,1)S(1)} %copy-done.9, bf16[48,64,128]{2,1,0:T(8,128)(2,1)S(1)} %get-tuple-element.71.refs_1_.refs_0_.refs_3_, ...), custom_call_target="tpu_custom_call" | custom-call | flops 5750000128 | bytes 5705100 | tf_op jit(solution)/shard_map/outer_other/pallas_call | solution.py:50
  148.2 1.9 %collective-permute-start.22 = (bf16[216,32,128]{2,1,0:T(8,128)(2,1)S(1)}, bf16[216,32,128]{2,1,0:T(8,128)(2,1)S(1)}, u32[]{:S(2)}, u32[]{:S(2)}) collective-permute-start(bf16[216,32,128]{2,1,0:T(8,128)(2,1)S(1)} %outer_other.3), channel_id=1, source_target_pairs={{0,16},{16,0},{1,17},{17,1},{2,18},{18,2},{3,19},{19,3},{4,20},{20... | collective-permute-start | bytes 5308424 | tf_op jit(solution)/shard_map/ppermute | solution.py:413
  150.0 0.8 add_convert_fusion
  150.8 4.6 %collective-permute-done.19 = bf16[2,32,3072]{2,1,0:T(8,128)(2,1)S(1)} collective-permute-done((bf16[2,32,3072]{2,1,0:T(8,128)(2,1)S(1)}, bf16[2,32,3072]{2,1,0:T(8,128)(2,1)S(1)}, u32[]{:S(2)}, u32[]{:S(2)}) %collective-permute-start.19) | collective-permute-done | bytes 393248 | tf_op jit(solution)/shard_map/ppermute | solution.py:462
  155.4 0.7 fusion.6
  156.1 1.6 collective-permute-start.20
  157.7 5.6 %outer_own.2.refs_0_ = bf16[216,32,128]{2,1,0:T(8,128)(2,1)S(1)} custom-call(s32[3]{0:T(128)S(1)} %pad_add_fusion.facts_ref, s32[432]{0:T(512)S(1)} %bitcast.69, s32[432]{0:T(512)S(1)} %bitcast.77, bf16[216,32,128]{2,1,0:T(8,128)(2,1)S(1)} %collective-permute-done.21.refs_0_, bf16[48,64,128]{2,1,0:T(8,128)(2,1)S(1)} %copy-done.11, ...), custom_call_target="tpu_custom_call" | custom-call | flops 5750000128 | bytes 7474572 | tf_op jit(solution)/shard_map/outer_own/pallas_call | solution.py:50
  163.3 4.9 %outer_own.3 = bf16[216,32,128]{2,1,0:T(8,128)(2,1)S(1)} custom-call(s32[3]{0:T(128)S(1)} %pad_add_fusion.facts_ref, s32[432]{0:T(512)S(1)} %bitcast.70, s32[432]{0:T(512)S(1)} %bitcast.78, bf16[216,32,128]{2,1,0:T(8,128)(2,1)S(1)} %outer_own.2.refs_0_, bf16[216,32,128]{2,1,0:T(8,128)(2,1)S(1)} %collective-permute-done.22.refs_1_, ...), custom_call_target="tpu_custom_call" | custom-call | flops 5750000128 | bytes 9244044 | tf_op jit(solution)/shard_map/outer_own/pallas_call | solution.py:50
  168.2 2.2 %reshape.152 = bf16[1,1,216,4096]{3,2,1,0:T(8,128)(2,1)} reshape(bf16[216,32,128]{2,1,0:T(8,128)(2,1)S(1)} %outer_own.3) | data formatting | bytes 3538944 | tf_op jit(solution)/shard_map/reshape | solution.py:491
  170.4 1.0 fusion.5
  171.4 0.8 pad_maximum_fusion
  (87 shorter events, 0.7 us)
Async XLA Ops:
  2.5 6.9 %copy-start.22 = (s32[1,1,432]{2,1,0:T(1,128)S(1)}, s32[1,1,432]{2,1,0:T(1,128)}, u32[]{:S(2)}) copy-start(s32[1,1,432]{2,1,0:T(1,128)} %param.8) | copy-start | bytes 5188
  2.5 6.9 %copy-start.23 = (s32[1,1,432]{2,1,0:T(1,128)S(1)}, s32[1,1,432]{2,1,0:T(1,128)}, u32[]{:S(2)}) copy-start(s32[1,1,432]{2,1,0:T(1,128)} %param.9) | copy-start | bytes 5188
  2.5 6.9 %collective-permute-start = (bf16[216,32,128]{2,1,0:T(8,128)(2,1)S(1)}, bf16[216,32,128]{2,1,0:T(8,128)(2,1)S(1)}, u32[]{:S(2)}, u32[]{:S(2)}) collective-permute-start(bf16[216,32,128]{2,1,0:T(8,128)(2,1)S(1)} %bitcast.53), channel_id=1, source_target_pairs={{0,16},{16,0},{1,17},{17,1},{2,18},{18,2},{3,19},{19,3},{4,20},{20... | collective-permute-start | bytes 5308424 | tf_op jit(solution)/shard_map/ppermute | solution.py:413
  3.8 1.4 copy-start.6
  5.2 20.7 %copy-start = (bf16[2,256,128]{2,1,0:T(8,128)(2,1)}, bf16[2,256,128]{2,1,0:T(8,128)(2,1)S(1)}, u32[]{:S(2)}) copy-start(bf16[2,256,128]{2,1,0:T(8,128)(2,1)S(1)} %fusion.8.select_ref) | copy-start | bytes 393220
  9.3 4.4 %copy-start.10 = (bf16[48,64,128]{2,1,0:T(8,128)(2,1)}, bf16[48,64,128]{2,1,0:T(8,128)(2,1)S(1)}, u32[]{:S(2)}) copy-start(bf16[48,64,128]{2,1,0:T(8,128)(2,1)S(1)} %get-tuple-element.80.table_ref.refs_0_.refs_1_) | copy-start | bytes 2359300
  9.3 10.0 %copy-start.8 = (bf16[48,64,128]{2,1,0:T(8,128)(2,1)}, bf16[48,64,128]{2,1,0:T(8,128)(2,1)S(1)}, u32[]{:S(2)}) copy-start(bf16[48,64,128]{2,1,0:T(8,128)(2,1)S(1)} %get-tuple-element.81.table_ref.refs_0_.refs_2_) | copy-start | bytes 2359300
  13.7 24.3 %collective-permute-start.1 = (bf16[2,24,64,128]{3,2,1,0:T(8,128)(2,1)S(1)}, bf16[2,24,64,128]{3,2,1,0:T(8,128)(2,1)S(1)}, u32[]{:S(2)}, u32[]{:S(2)}) collective-permute-start(bf16[2,24,64,128]{3,2,1,0:T(8,128)(2,1)S(1)} %get-tuple-element.54), channel_id=1, source_target_pairs={{0,1},{1,0},{2,3},{3,2},{4,5},{5,4},{6,7},{7,6},{8,9},{9,8},{10,11... | collective-permute-start | bytes 2359304 | tf_op jit(solution)/shard_map/ppermute | solution.py:410
  17.8 21.8 %collective-permute-start.2 = (bf16[2,24,64,128]{3,2,1,0:T(8,128)(2,1)S(1)}, bf16[2,24,64,128]{3,2,1,0:T(8,128)(2,1)S(1)}, u32[]{:S(2)}, u32[]{:S(2)}) collective-permute-start(bf16[2,24,64,128]{3,2,1,0:T(8,128)(2,1)S(1)} %get-tuple-element.56), channel_id=1, source_target_pairs={{0,2},{1,3},{2,0},{3,1},{4,6},{5,7},{6,4},{7,5},{8,10},{9,11},{10,... | collective-permute-start | bytes 2359304 | tf_op jit(solution)/shard_map/ppermute | solution.py:410
  19.4 6.6 %copy-start.7 = (bf16[256,3072]{1,0:T(8,128)(2,1)S(1)}, bf16[256,3072]{1,0:T(8,128)(2,1)}, u32[]{:S(2)}) copy-start(bf16[256,3072]{1,0:T(8,128)(2,1)} %values_ref.3) | copy-start | bytes 4718596
  23.6 13.1 %copy-start.14 = (bf16[24,64,128]{2,1,0:T(8,128)(2,1)}, bf16[24,64,128]{2,1,0:T(8,128)(2,1)S(1)}, u32[]{:S(2)}) copy-start(bf16[24,64,128]{2,1,0:T(8,128)(2,1)S(1)} %get-tuple-element.44.own_a) | copy-start | bytes 1179652
  23.6 13.1 %copy-start.16 = (bf16[24,64,128]{2,1,0:T(8,128)(2,1)}, bf16[24,64,128]{2,1,0:T(8,128)(2,1)S(1)}, u32[]{:S(2)}) copy-start(bf16[24,64,128]{2,1,0:T(8,128)(2,1)S(1)} %get-tuple-element.68.own_b) | copy-start | bytes 1179652
  23.7 29.4 %collective-permute-start.3 = (bf16[2,24,64,128]{3,2,1,0:T(8,128)(2,1)S(1)}, bf16[2,24,64,128]{3,2,1,0:T(8,128)(2,1)S(1)}, u32[]{:S(2)}, u32[]{:S(2)}) collective-permute-start(bf16[2,24,64,128]{3,2,1,0:T(8,128)(2,1)S(1)} %get-tuple-element.58), channel_id=1, source_target_pairs={{0,1},{1,0},{2,3},{3,2},{4,5},{5,4},{6,7},{7,6},{8,9},{9,8},{10,11... | collective-permute-start | bytes 2359304 | tf_op jit(solution)/shard_map/ppermute | solution.py:410
  25.4 29.6 %collective-permute-start.4 = (bf16[2,24,64,128]{3,2,1,0:T(8,128)(2,1)S(1)}, bf16[2,24,64,128]{3,2,1,0:T(8,128)(2,1)S(1)}, u32[]{:S(2)}, u32[]{:S(2)}) collective-permute-start(bf16[2,24,64,128]{3,2,1,0:T(8,128)(2,1)S(1)} %get-tuple-element.61), channel_id=1, source_target_pairs={{0,2},{1,3},{2,0},{3,1},{4,6},{5,7},{6,4},{7,5},{8,10},{9,11},{10,... | collective-permute-start | bytes 2359304 | tf_op jit(solution)/shard_map/ppermute | solution.py:410
  30.0 0.9 copy-start.12
  36.7 1.3 copy-start.26
  38.0 15.9 %copy-start.24 = (bf16[216,32,128]{2,1,0:T(8,128)(2,1)}, bf16[216,32,128]{2,1,0:T(8,128)(2,1)S(1)}, u32[]{:S(2)}) copy-start(bf16[216,32,128]{2,1,0:T(8,128)(2,1)S(1)} %get-tuple-element.49.own_ref) | copy-start | bytes 5308420
  38.0 24.8 %collective-permute-start.5 = (bf16[24,64,128]{2,1,0:T(8,128)(2,1)S(1)}, bf16[24,64,128]{2,1,0:T(8,128)(2,1)S(1)}, u32[]{:S(2)}, u32[]{:S(2)}) collective-permute-start(bf16[24,64,128]{2,1,0:T(8,128)(2,1)S(1)} %fusion.3), channel_id=1, source_target_pairs={{0,2},{1,3},{2,0},{3,1},{4,6},{5,7},{6,4},{7,5},{8,10},{9,11},{10,... | collective-permute-start | bytes 1179656 | tf_op jit(solution)/shard_map/ppermute | solution.py:410
  39.7 23.1 %collective-permute-start.6 = (bf16[24,64,128]{2,1,0:T(8,128)(2,1)S(1)}, bf16[24,64,128]{2,1,0:T(8,128)(2,1)S(1)}, u32[]{:S(2)}, u32[]{:S(2)}) collective-permute-start(bf16[24,64,128]{2,1,0:T(8,128)(2,1)S(1)} %fusion.2), channel_id=1, source_target_pairs={{0,1},{1,0},{2,3},{3,2},{4,5},{5,4},{6,7},{7,6},{8,9},{9,8},{10,11... | collective-permute-start | bytes 1179656 | tf_op jit(solution)/shard_map/ppermute | solution.py:410
  53.9 0.9 copy-start.2
  55.1 10.3 %copy-start.4 = (bf16[2,24,64,128]{3,2,1,0:T(8,128)(2,1)}, bf16[2,24,64,128]{3,2,1,0:T(8,128)(2,1)S(1)}, u32[]{:S(2)}) copy-start(bf16[2,24,64,128]{3,2,1,0:T(8,128)(2,1)S(1)} %collective-permute-done.4.near_b) | copy-start | bytes 2359300
  62.8 32.1 %copy-start.13 = (bf16[48,64,128]{2,1,0:T(8,128)(2,1)S(1)}, bf16[48,64,128]{2,1,0:T(8,128)(2,1)}, u32[]{:S(2)}) copy-start(bf16[48,64,128]{2,1,0:T(8,128)(2,1)} %copy-done.12) | copy-start | bytes 2359300
  62.8 32.1 %copy-start.15 = (bf16[24,64,128]{2,1,0:T(8,128)(2,1)S(1)}, bf16[24,64,128]{2,1,0:T(8,128)(2,1)}, u32[]{:S(2)}) copy-start(bf16[24,64,128]{2,1,0:T(8,128)(2,1)} %copy-done.14) | copy-start | bytes 1179652
  65.4 24.5 %copy-start.29 = (bf16[48,64,128]{2,1,0:T(8,128)(2,1)}, bf16[48,64,128]{2,1,0:T(8,128)(2,1)S(1)}, u32[]{:S(2)}) copy-start(bf16[48,64,128]{2,1,0:T(8,128)(2,1)S(1)} %get-tuple-element.65.refs_0_.refs_1_.refs_2_) | copy-start | bytes 2359300
  65.4 29.5 %copy-start.3 = (bf16[2,24,64,128]{3,2,1,0:T(8,128)(2,1)S(1)}, bf16[2,24,64,128]{3,2,1,0:T(8,128)(2,1)}, u32[]{:S(2)}) copy-start(bf16[2,24,64,128]{3,2,1,0:T(8,128)(2,1)} %copy-done.2) | copy-start | bytes 2359300
  65.4 29.5 %copy-start.5 = (bf16[2,24,64,128]{3,2,1,0:T(8,128)(2,1)S(1)}, bf16[2,24,64,128]{3,2,1,0:T(8,128)(2,1)}, u32[]{:S(2)}) copy-start(bf16[2,24,64,128]{3,2,1,0:T(8,128)(2,1)} %copy-done.4) | copy-start | bytes 2359300
  65.4 20.5 %collective-permute-start.7 = (bf16[48,64,128]{2,1,0:T(8,128)(2,1)S(1)}, bf16[48,64,128]{2,1,0:T(8,128)(2,1)S(1)}, u32[]{:S(2)}, u32[]{:S(2)}) collective-permute-start(bf16[48,64,128]{2,1,0:T(8,128)(2,1)S(1)} %get-tuple-element.65.refs_0_.refs_1_.refs_2_), channel_id=1, source_target_pairs={{0,1},{1,0},{2,3},{3,2},{4,5},{5,4},{6,7},{7,6},{8,9},{9,8},{10,11... | collective-permute-start | bytes 2359304 | tf_op jit(solution)/shard_map/ppermute | solution.py:410
  65.9 23.3 %collective-permute-start.8 = (bf16[48,64,128]{2,1,0:T(8,128)(2,1)S(1)}, bf16[48,64,128]{2,1,0:T(8,128)(2,1)S(1)}, u32[]{:S(2)}, u32[]{:S(2)}) collective-permute-start(bf16[48,64,128]{2,1,0:T(8,128)(2,1)S(1)} %get-tuple-element.65.refs_0_.refs_1_.refs_2_), channel_id=1, source_target_pairs={{0,2},{1,3},{2,0},{3,1},{4,6},{5,7},{6,4},{7,5},{8,10},{9,11},{10,... | collective-permute-start | bytes 2359304 | tf_op jit(solution)/shard_map/ppermute | solution.py:410
  67.4 27.5 %collective-permute-start.11 = (bf16[24,64,128]{2,1,0:T(8,128)(2,1)}, bf16[24,64,128]{2,1,0:T(8,128)(2,1)}, u32[]{:S(2)}, u32[]{:S(2)}) collective-permute-start(bf16[24,64,128]{2,1,0:T(8,128)(2,1)} %fusion.1), channel_id=1, source_target_pairs={{0,2},{1,3},{2,0},{3,1},{4,6},{5,7},{6,4},{7,5},{8,10},{9,11},{10,... | collective-permute-start | bytes 1179656 | tf_op jit(solution)/shard_map/ppermute | solution.py:410
  67.9 27.0 %collective-permute-start.12 = (bf16[24,64,128]{2,1,0:T(8,128)(2,1)}, bf16[24,64,128]{2,1,0:T(8,128)(2,1)}, u32[]{:S(2)}, u32[]{:S(2)}) collective-permute-start(bf16[24,64,128]{2,1,0:T(8,128)(2,1)} %fusion), channel_id=1, source_target_pairs={{0,1},{1,0},{2,3},{3,2},{4,5},{5,4},{6,7},{7,6},{8,9},{9,8},{10,11... | collective-permute-start | bytes 1179656 | tf_op jit(solution)/shard_map/ppermute | solution.py:410
  86.8 0.9 copy-start.18
  87.7 15.6 %collective-permute-start.9 = (bf16[24,64,128]{2,1,0:T(8,128)(2,1)}, bf16[24,64,128]{2,1,0:T(8,128)(2,1)}, u32[]{:S(2)}, u32[]{:S(2)}) collective-permute-start(bf16[24,64,128]{2,1,0:T(8,128)(2,1)} %slice.36), channel_id=1, source_target_pairs={{0,2},{1,3},{2,0},{3,1},{4,6},{5,7},{6,4},{7,5},{8,10},{9,11},{10,... | collective-permute-start | bytes 1179656 | tf_op jit(solution)/shard_map/ppermute | solution.py:410
  89.9 0.9 copy-start.20
  90.8 12.5 %collective-permute-start.10 = (bf16[24,64,128]{2,1,0:T(8,128)(2,1)}, bf16[24,64,128]{2,1,0:T(8,128)(2,1)}, u32[]{:S(2)}, u32[]{:S(2)}) collective-permute-start(bf16[24,64,128]{2,1,0:T(8,128)(2,1)} %slice.37), channel_id=1, source_target_pairs={{0,1},{1,0},{2,3},{3,2},{4,5},{5,4},{6,7},{7,6},{8,9},{9,8},{10,11... | collective-permute-start | bytes 1179656 | tf_op jit(solution)/shard_map/ppermute | solution.py:410
  94.9 1.0 copy-start.17
  95.9 7.4 %copy-start.19 = (bf16[48,64,128]{2,1,0:T(8,128)(2,1)S(1)}, bf16[48,64,128]{2,1,0:T(8,128)(2,1)}, u32[]{:S(2)}) copy-start(bf16[48,64,128]{2,1,0:T(8,128)(2,1)} %copy-done.18) | copy-start | bytes 2359300
  95.9 7.4 %copy-start.21 = (bf16[48,64,128]{2,1,0:T(8,128)(2,1)S(1)}, bf16[48,64,128]{2,1,0:T(8,128)(2,1)}, u32[]{:S(2)}) copy-start(bf16[48,64,128]{2,1,0:T(8,128)(2,1)} %copy-done.20) | copy-start | bytes 2359300
  95.9 7.4 %copy-start.25 = (bf16[216,32,128]{2,1,0:T(8,128)(2,1)S(1)}, bf16[216,32,128]{2,1,0:T(8,128)(2,1)}, u32[]{:S(2)}) copy-start(bf16[216,32,128]{2,1,0:T(8,128)(2,1)} %copy-done.24) | copy-start | bytes 5308420
  99.5 23.7 %collective-permute-start.17 = (bf16[48,64,128]{2,1,0:T(8,128)(2,1)S(1)}, bf16[48,64,128]{2,1,0:T(8,128)(2,1)S(1)}, u32[]{:S(2)}, u32[]{:S(2)}) collective-permute-start(bf16[48,64,128]{2,1,0:T(8,128)(2,1)S(1)} %get-tuple-element.71.refs_1_.refs_0_.refs_3_), channel_id=1, source_target_pairs={{0,1},{1,0},{2,3},{3,2},{4,5},{5,4},{6,7},{7,6},{8,9},{9,8},{10,11... | collective-permute-start | bytes 2359304 | tf_op jit(solution)/shard_map/ppermute | solution.py:410
  101.2 22.1 %collective-permute-start.15 = (bf16[48,64,128]{2,1,0:T(8,128)(2,1)S(1)}, bf16[48,64,128]{2,1,0:T(8,128)(2,1)S(1)}, u32[]{:S(2)}, u32[]{:S(2)}) collective-permute-start(bf16[48,64,128]{2,1,0:T(8,128)(2,1)S(1)} %get-tuple-element.71.refs_1_.refs_0_.refs_3_), channel_id=1, source_target_pairs={{0,2},{1,3},{2,0},{3,1},{4,6},{5,7},{6,4},{7,5},{8,10},{9,11},{10,... | collective-permute-start | bytes 2359304 | tf_op jit(solution)/shard_map/ppermute | solution.py:410
  103.3 1.5 copy-start.27
  104.8 1.1 copy-start.30
  105.9 8.7 %copy-start.1 = (bf16[2,256,128]{2,1,0:T(8,128)(2,1)S(1)}, bf16[2,256,128]{2,1,0:T(8,128)(2,1)}, u32[]{:S(2)}) copy-start(bf16[2,256,128]{2,1,0:T(8,128)(2,1)} %copy-done) | copy-start | bytes 393220
  111.3 9.0 %copy-start.11 = (bf16[48,64,128]{2,1,0:T(8,128)(2,1)S(1)}, bf16[48,64,128]{2,1,0:T(8,128)(2,1)}, u32[]{:S(2)}) copy-start(bf16[48,64,128]{2,1,0:T(8,128)(2,1)} %copy-done.10) | copy-start | bytes 2359300
  111.3 9.0 %copy-start.31 = (bf16[48,64,128]{2,1,0:T(8,128)(2,1)S(1)}, bf16[48,64,128]{2,1,0:T(8,128)(2,1)}, u32[]{:S(2)}) copy-start(bf16[48,64,128]{2,1,0:T(8,128)(2,1)} %copy-done.29) | copy-start | bytes 2359300
  111.3 16.8 %collective-permute-start.13 = (bf16[2,32,3072]{2,1,0:T(8,128)(2,1)S(1)}, bf16[2,32,3072]{2,1,0:T(8,128)(2,1)S(1)}, u32[]{:S(2)}, u32[]{:S(2)}) collective-permute-start(bf16[2,32,3072]{2,1,0:T(8,128)(2,1)S(1)} %dynamic-slice_bitcast_fusion.1), channel_id=1, source_target_pairs={{0,4},{4,0},{8,12},{12,8},{1,5},{5,1},{9,13},{13,9},{2,6},{6,2},{1... | collective-permute-start | bytes 1179656 | tf_op jit(solution)/shard_map/ppermute | solution.py:462
  123.0 17.0 %copy-start.28 = (bf16[216,32,128]{2,1,0:T(8,128)(2,1)S(1)}, bf16[216,32,128]{2,1,0:T(8,128)(2,1)}, u32[]{:S(2)}) copy-start(bf16[216,32,128]{2,1,0:T(8,128)(2,1)} %copy-done.26) | copy-start | bytes 5308420
  123.1 34.7 %collective-permute-start.21 = (bf16[216,32,128]{2,1,0:T(8,128)(2,1)S(1)}, bf16[216,32,128]{2,1,0:T(8,128)(2,1)S(1)}, u32[]{:S(2)}, u32[]{:S(2)}) collective-permute-start(bf16[216,32,128]{2,1,0:T(8,128)(2,1)S(1)} %outer_other.2), channel_id=1, source_target_pairs={{0,16},{16,0},{1,17},{17,1},{2,18},{18,2},{3,19},{19,3},{4,20},{20... | collective-permute-start | bytes 5308424 | tf_op jit(solution)/shard_map/ppermute | solution.py:413
  123.2 16.9 %collective-permute-start.18 = (bf16[24,64,128]{2,1,0:T(8,128)(2,1)S(1)}, bf16[24,64,128]{2,1,0:T(8,128)(2,1)S(1)}, u32[]{:S(2)}, u32[]{:S(2)}) collective-permute-start(bf16[24,64,128]{2,1,0:T(8,128)(2,1)S(1)} %slice.39), channel_id=1, source_target_pairs={{0,2},{1,3},{2,0},{3,1},{4,6},{5,7},{6,4},{7,5},{8,10},{9,11},{10,... | collective-permute-start | bytes 1179656 | tf_op jit(solution)/shard_map/ppermute | solution.py:410
  123.3 14.3 %collective-permute-start.16 = (bf16[24,64,128]{2,1,0:T(8,128)(2,1)S(1)}, bf16[24,64,128]{2,1,0:T(8,128)(2,1)S(1)}, u32[]{:S(2)}, u32[]{:S(2)}) collective-permute-start(bf16[24,64,128]{2,1,0:T(8,128)(2,1)S(1)} %slice.38), channel_id=1, source_target_pairs={{0,1},{1,0},{2,3},{3,2},{4,5},{5,4},{6,7},{7,6},{8,9},{9,8},{10,11... | collective-permute-start | bytes 1179656 | tf_op jit(solution)/shard_map/ppermute | solution.py:410
  128.2 11.9 %collective-permute-start.14 = (bf16[32,3072]{1,0:T(8,128)(2,1)S(1)}, bf16[32,3072]{1,0:T(8,128)(2,1)S(1)}, u32[]{:S(2)}, u32[]{:S(2)}) collective-permute-start(bf16[32,3072]{1,0:T(8,128)(2,1)S(1)} %fusion.7), channel_id=1, source_target_pairs={{0,8},{4,12},{8,0},{12,4},{1,9},{5,13},{9,1},{13,5},{2,10},{6,14},... | collective-permute-start | bytes 589832 | tf_op jit(solution)/shard_map/ppermute | solution.py:464
  130.9 15.3 %copy-start.9 = (bf16[48,64,128]{2,1,0:T(8,128)(2,1)S(1)}, bf16[48,64,128]{2,1,0:T(8,128)(2,1)}, u32[]{:S(2)}) copy-start(bf16[48,64,128]{2,1,0:T(8,128)(2,1)} %copy-done.8) | copy-start | bytes 2359300
  144.5 10.9 %collective-permute-start.19 = (bf16[2,32,3072]{2,1,0:T(8,128)(2,1)S(1)}, bf16[2,32,3072]{2,1,0:T(8,128)(2,1)S(1)}, u32[]{:S(2)}, u32[]{:S(2)}) collective-permute-start(bf16[2,32,3072]{2,1,0:T(8,128)(2,1)S(1)} %dynamic-slice_bitcast_fusion), channel_id=1, source_target_pairs={{0,4},{4,0},{8,12},{12,8},{1,5},{5,1},{9,13},{13,9},{2,6},{6,2},{1... | collective-permute-start | bytes 1179656 | tf_op jit(solution)/shard_map/ppermute | solution.py:462
  148.2 15.2 %collective-permute-start.22 = (bf16[216,32,128]{2,1,0:T(8,128)(2,1)S(1)}, bf16[216,32,128]{2,1,0:T(8,128)(2,1)S(1)}, u32[]{:S(2)}, u32[]{:S(2)}) collective-permute-start(bf16[216,32,128]{2,1,0:T(8,128)(2,1)S(1)} %outer_other.3), channel_id=1, source_target_pairs={{0,16},{16,0},{1,17},{17,1},{2,18},{18,2},{3,19},{19,3},{4,20},{20... | collective-permute-start | bytes 5308424 | tf_op jit(solution)/shard_map/ppermute | solution.py:413
  156.1 14.2 %collective-permute-start.20 = (bf16[32,3072]{1,0:T(8,128)(2,1)}, bf16[32,3072]{1,0:T(8,128)(2,1)}, u32[]{:S(2)}, u32[]{:S(2)}) collective-permute-start(bf16[32,3072]{1,0:T(8,128)(2,1)} %fusion.6), channel_id=1, source_target_pairs={{0,8},{4,12},{8,0},{12,4},{1,9},{5,13},{9,1},{13,5},{2,10},{6,14},... | collective-permute-start | bytes 589832 | tf_op jit(solution)/shard_map/ppermute | solution.py:464
  168.2 3.2 %copy-start.32 = (bf16[32,3072]{1,0:T(8,128)(2,1)S(1)}, bf16[32,3072]{1,0:T(8,128)(2,1)}, u32[]{:S(2)}) copy-start(bf16[32,3072]{1,0:T(8,128)(2,1)} %add_convert_fusion) | copy-start | bytes 589828

commit v5 on v4

--- a/solution.py
+++ b/solution.py
@@ -421,7 +421,7 @@
     upstream = list(token_rows(act_grad, after(select, partials[1][2]), True))
     own_t, other_t = transpose_tiles(after(own, upstream[1]), after(other, upstream[1]))
 
-    terms, sums = [], []
+    terms = []
     for chunk in range(CHUNKS):
         along_x, along_y, own_a, own_b, relay_x, relay_y = partials[chunk]
         from_x, from_y = across(along_x, 1), across(along_y, 2)
@@ -429,9 +429,8 @@
         if chunk:
             sum_y = after(sum_y, own_t)
         last_a, last_b = across(sum_y, 2), across(sum_x, 1)
-        sums += [sum_y, sum_x]
         terms.append((own_a, from_x, last_a, own_b, from_y, last_b))
-    upstream[0] = after(upstream[0], sums)
+    upstream[0] = after(upstream[0], terms[1])
 
     grads, acts = [], []
     for chunk in range(CHUNKS):
@@ -442,6 +441,8 @@
             sent_x, sent_y = after(grad, grads[0][1]), after(grad, grads[0][2])
         grads.append([grad, across(sent_x, 1), across(sent_y, 2)])
 
+    activation = rows_to_units(select, acts)
+    grads[0][1] = after(grads[0][1], activation)
     for chunk in range(CHUNKS):
         grad, grad_x, grad_y = grads[chunk]
         far_a = across(grad_x[: share_blocks // 2], 2)
@@ -477,8 +478,7 @@
 
     first = input_sums(0)
     row_parts, halfway, sent = to_rows(first)
-    activation = rows_to_units(after(select, sent), acts)
-    other_first = tile_part(0, activation, False, [])
+    other_first = tile_part(0, (sent, grads[1][1], grads[1][2]), False, [])
     *first_parts, grads[1][4] = lax.optimization_barrier((*row_parts, after(grads[1][4], other_first)))
     second = input_sums(1)
     row_parts, halfway, sent = to_rows(second)

time: 171 us -> 174 us (1.018)
  starting transfers between devices: 35.5 us -> 19.2 us
  waiting for transfers between devices: 54.8 us -> 69.7 us
  Pallas kernels: 59.2 us -> 70.3 us
  local copies, waits for them, and re-layouts: 15.6 us -> 9.82 us
    pallas_call x14, Pallas kernels: 59.2 us -> 70.3 us  [call(): pl.pallas_call(kernel, out_shape=out_shape, in_specs=in_specs, out_specs=...]
    ppermute x2, waiting for transfers between devices: 2.48 us -> 11.2 us  [to_rows(): lax.ppermute(both.astype(jnp.bfloat16), 'row', [(place, place ^ 2) for pl...]
    ppermute x16, starting transfers between devices: 23.9 us -> 17.5 us  [across(): lax.ppermute(values, 'col', [(place, place ^ bit) for place in range(shar...]
    unnamed x67 -> x41, local copies, waits for them, and re-layouts: 11.7 us -> 5.93 us
    ppermute x16, waiting for transfers between devices: 47.7 us -> 53.3 us  [across(): lax.ppermute(values, 'col', [(place, place ^ bit) for place in range(shar...]
    ppermute x2, starting transfers between devices: 4.23 us -> 0.17 us  [to_rows(): lax.ppermute(both.astype(jnp.bfloat16), 'row', [(place, place ^ 2) for pl...]
    ppermute x2, starting transfers between devices: 4.94 us -> 0.89 us  [to_rows(): lax.ppermute(sent, 'row', [(place, place ^ 1) for place in range(4)])]
    ppermute x3, starting transfers between devices: 2.45 us -> 0.66 us  [other_core(): return lax.ppermute(values, 'dp', [(0, 1), (1, 0)])]
  transfers between devices with their start and end apart: 23 -> 23, of which waited for: 9 -> 11; matrix products, arithmetic and copies ran while one was open for 4% -> 3% of each run, Pallas kernels for 30% -> 35%
where the time goes in v5:
time: 174 us; the launch traced here: 175 us
  Pallas kernels  70.3 us (40%)
  waiting for transfers between devices  69.7 us (40%)
  starting transfers between devices  19.2 us (11%)
  local copies, waits for them, and re-layouts  9.82 us (6%)
  other arithmetic  3.7 us (2%)
  between operations  1.74 us (1%)
    pallas_call x14, Pallas kernels, call(): pl.pallas_call(kernel, out_shape=out_shape, in_specs=in_specs, out_specs=...  70.3 us
    ppermute x16, waiting for transfers between devices, across(): lax.ppermute(values, 'col', [(place, place ^ bit) for place in range(shar...  53.3 us
    ppermute x16, starting transfers between devices, across(): lax.ppermute(values, 'col', [(place, place ^ bit) for place in range(shar...  17.5 us
    ppermute x2, waiting for transfers between devices, to_rows(): lax.ppermute(both.astype(jnp.bfloat16), 'row', [(place, place ^ 2) for pl...  11.2 us
    unnamed x41, local copies, waits for them, and re-layouts  5.93 us
    ppermute x2, waiting for transfers between devices, to_rows(): lax.ppermute(sent, 'row', [(place, place ^ 1) for place in range(4)])  5.25 us
  transfers between devices with their start and end apart: 23, of which 11 were waited for; matrix products, arithmetic and copies ran while one was open for 3% of the time, Pallas kernels for 35%

profile of v5, /device:TPU:0, one launch (start us, length us, event | category | flops | bytes accessed | tf_op | source)
XLA Modules:
  0.0 174.5 jit_solution(14231575289231460719)
XLA Ops:
  0.6 1.8 %copy.9 = bf16[27,8,32,128]{3,2,1,0:T(8,128)(2,1)S(1)} copy(bf16[27,8,32,128]{3,1,2,0:T(8,128)(2,1)} %bitcast.79) | data formatting | bytes 3538944
  2.5 0.0 copy-start.6
  2.5 0.0 copy-start.7
  2.5 0.5 collective-permute-start
  3.7 0.1 add_add_fusion
  3.8 1.4 copy-done
  5.2 4.1 %features_to_rows.1 = (bf16[48,64,128]{2,1,0:T(8,128)(2,1)S(1)}, bf16[48,64,128]{2,1,0:T(8,128)(2,1)S(1)}) custom-call(bf16[256,3072]{1,0:T(8,128)(2,1)S(1)} %copy-done, bf16[2,256,128]{2,1,0:T(8,128)(2,1)S(1)} %fusion.8.select_ref), custom_call_target="tpu_custom_call" | custom-call | tf_op jit(solution)/shard_map/features_to_rows/pallas_call | solution.py:50
  9.3 0.1 pad_add_fusion.facts_ref
  9.4 5.8 %forward.2 = (bf16[2,24,64,128]{3,2,1,0:T(8,128)(2,1)S(1)}, bf16[2,24,64,128]{3,2,1,0:T(8,128)(2,1)S(1)}, bf16[24,64,128]{2,1,0:T(8,128)(2,1)S(1)}, bf16[24,64,1...) custom-call(s32[3]{0:T(128)S(1)} %pad_add_fusion.facts_ref, ...), custom_call_target="tpu_custom_call" | custom-call | tf_op jit(solution)/shard_map/forward/pallas_call | solution.py:50
  15.3 2.6 %collective-permute-start.1 = (bf16[2,24,64,128]{3,2,1,0:T(8,128)(2,1)S(1)}, bf16[2,24,64,128]{3,2,1,0:T(8,128)(2,1)S(1)}, u32[]{:S(2)}, u32[]{:S(2)}) collective-permute-start(bf16[2,24,64,128]{3,2,1,0:T(8,128)(2,1)S(1)} %get-tuple-element.47), channel_id=1, source_target_pairs={{0,1},{1,0},{2,3},{3,2},{4,5},{5,4},{6,7},{7,6},{8,9},{9,8},{10,11... | collective-permute-start | bytes 2359304 | tf_op jit(solution)/shard_map/ppermute | solution.py:410
  17.8 0.1 collective-permute-start.3
  18.0 6.1 %forward.3 = (bf16[2,24,64,128]{3,2,1,0:T(8,128)(2,1)S(1)}, bf16[2,24,64,128]{3,2,1,0:T(8,128)(2,1)S(1)}, bf16[24,64,128]{2,1,0:T(8,128)(2,1)S(1)}, bf16[24,64,1...) custom-call(s32[3]{0:T(128)S(1)} %pad_add_fusion.facts_ref, ...), custom_call_target="tpu_custom_call" | custom-call | tf_op jit(solution)/shard_map/forward/pallas_call | solution.py:50
  24.0 2.0 %collective-permute-start.5 = (bf16[2,24,64,128]{3,2,1,0:T(8,128)(2,1)S(1)}, bf16[2,24,64,128]{3,2,1,0:T(8,128)(2,1)S(1)}, u32[]{:S(2)}, u32[]{:S(2)}) collective-permute-start(bf16[2,24,64,128]{3,2,1,0:T(8,128)(2,1)S(1)} %get-tuple-element.60), channel_id=1, source_target_pairs={{0,1},{1,0},{2,3},{3,2},{4,5},{5,4},{6,7},{7,6},{8,9},{9,8},{10,11... | collective-permute-start | bytes 2359304 | tf_op jit(solution)/shard_map/ppermute | solution.py:410
  26.1 0.0 collective-permute-start.7
  26.1 4.1 %units_to_rows.1 = (bf16[48,64,128]{2,1,0:T(8,128)(2,1)S(1)}, bf16[48,64,128]{2,1,0:T(8,128)(2,1)S(1)}) custom-call(bf16[256,3072]{1,0:T(8,128)(2,1)S(1)} %copy-done.1, bf16[2,256,128]{2,1,0:T(8,128)(2,1)S(1)} %fusion.8.select_ref), custom_call_target="tpu_custom_call" | custom-call | tf_op jit(solution)/shard_map/units_to_rows/pallas_call | solution.py:50
  30.2 5.8 %transpose_tiles.1 = (bf16[216,32,128]{2,1,0:T(8,128)(2,1)S(1)}, bf16[216,32,128]{2,1,0:T(8,128)(2,1)S(1)}) custom-call(bf16[216,32,128]{2,1,0:T(8,128)(2,1)S(1)} %bitcast.56, bf16[216,32,128]{2,1,0:T(8,128)(2,1)S(1)} %collective-permute-done.other_ref), custom_call_target="tpu_custom_call" | custom-call | tf_op jit(solution)/shard_map/transpose_tiles/pallas_call | solution.py:50
  36.0 0.2 collective-permute-done.1.near_a
  36.3 2.0 %collective-permute-start.2 = (bf16[24,64,128]{2,1,0:T(8,128)(2,1)S(1)}, bf16[24,64,128]{2,1,0:T(8,128)(2,1)S(1)}, u32[]{:S(2)}, u32[]{:S(2)}) collective-permute-start(bf16[24,64,128]{2,1,0:T(8,128)(2,1)S(1)} %fusion.3), channel_id=1, source_target_pairs={{0,2},{1,3},{2,0},{3,1},{4,6},{5,7},{6,4},{7,5},{8,10},{9,11},{10,... | collective-permute-start | bytes 1179656 | tf_op jit(solution)/shard_map/ppermute | solution.py:410
  38.4 0.1 collective-permute-start.4
  38.5 14.6 %collective-permute-done.5.near_a = bf16[2,24,64,128]{3,2,1,0:T(8,128)(2,1)S(1)} collective-permute-done((bf16[2,24,64,128]{3,2,1,0:T(8,128)(2,1)S(1)}, bf16[2,24,64,128]{3,2,1,0:T(8,128)(2,1)S(1)}, u32[]{:S(2)}, u32[]{:S(2)}) %collective-permute-start.5) | collective-permute-done | bytes 786464 | tf_op jit(solution)/shard_map/ppermute | solution.py:410
  53.2 2.0 %collective-permute-start.6 = (bf16[24,64,128]{2,1,0:T(8,128)(2,1)S(1)}, bf16[24,64,128]{2,1,0:T(8,128)(2,1)S(1)}, u32[]{:S(2)}, u32[]{:S(2)}) collective-permute-start(bf16[24,64,128]{2,1,0:T(8,128)(2,1)S(1)} %fusion.1), channel_id=1, source_target_pairs={{0,2},{1,3},{2,0},{3,1},{4,6},{5,7},{6,4},{7,5},{8,10},{9,11},{10,... | collective-permute-start | bytes 1179656 | tf_op jit(solution)/shard_map/ppermute | solution.py:410
  55.2 0.1 collective-permute-start.8
  55.4 8.1 %collective-permute-done.2.last_a = bf16[24,64,128]{2,1,0:T(8,128)(2,1)S(1)} collective-permute-done((bf16[24,64,128]{2,1,0:T(8,128)(2,1)S(1)}, bf16[24,64,128]{2,1,0:T(8,128)(2,1)S(1)}, u32[]{:S(2)}, u32[]{:S(2)}) %collective-permute-start.2) | collective-permute-done | bytes 393248 | tf_op jit(solution)/shard_map/ppermute | solution.py:410
  63.5 7.7 %collective-permute-done.6.last_a = bf16[24,64,128]{2,1,0:T(8,128)(2,1)S(1)} collective-permute-done((bf16[24,64,128]{2,1,0:T(8,128)(2,1)S(1)}, bf16[24,64,128]{2,1,0:T(8,128)(2,1)S(1)}, u32[]{:S(2)}, u32[]{:S(2)}) %collective-permute-start.6) | collective-permute-done | bytes 393248 | tf_op jit(solution)/shard_map/ppermute | solution.py:410
  71.2 2.6 %gelu.2 = (bf16[48,64,128]{2,1,0:T(8,128)(2,1)S(1)}, bf16[48,64,128]{2,1,0:T(8,128)(2,1)S(1)}) custom-call(bf16[48,64,128]{2,1,0:T(8,128)(2,1)S(1)} %get-tuple-element.57.upstream_hbm, bf16[24,64,128]{2,1,0:T(8,128)(2,1)S(1)} %get-tuple-element.59.own_a, bf16[2,24,64,128]{3,2,1,0:T(8,128)(2,1)S(1)} %collective-permute-done.5.near_a, ...), custom_call_target="tpu_custom_call" | custom-call | tf_op jit(solution)/shard_map/gelu/pallas_call | solution.py:50
  73.8 0.4 collective-permute-start.9
  74.3 1.7 collective-permute-start.10
  76.0 2.6 %gelu.3 = (bf16[48,64,128]{2,1,0:T(8,128)(2,1)S(1)}, bf16[48,64,128]{2,1,0:T(8,128)(2,1)S(1)}) custom-call(bf16[48,64,128]{2,1,0:T(8,128)(2,1)S(1)} %get-tuple-element.49.upstream_hbm, bf16[24,64,128]{2,1,0:T(8,128)(2,1)S(1)} %get-tuple-element.44.own_a, bf16[2,24,64,128]{3,2,1,0:T(8,128)(2,1)S(1)} %collective-permute-done.1.near_a, ...), custom_call_target="tpu_custom_call" | custom-call | tf_op jit(solution)/shard_map/gelu/pallas_call | solution.py:50
  78.6 0.0 copy-start.9
  78.6 5.7 %rows_to_units.1 = bf16[256,3072]{1,0:T(8,128)(2,1)} custom-call(bf16[2,256,128]{2,1,0:T(8,128)(2,1)S(1)} %fusion.8.select_ref, bf16[48,64,128]{2,1,0:T(8,128)(2,1)S(1)} %get-tuple-element.65.refs_0_, bf16[48,64,128]{2,1,0:T(8,128)(2,1)S(1)} %get-tuple-element.66.refs_1_), custom_call_target="tpu_custom_call" | custom-call | tf_op jit(solution)/shard_map/rows_to_units/pallas_call | solution.py:50
  84.3 8.5 %collective-permute-done.9.refs_1_.refs_2_.refs_3_ = bf16[48,64,128]{2,1,0:T(8,128)(2,1)S(1)} collective-permute-done((bf16[48,64,128]{2,1,0:T(8,128)(2,1)S(1)}, bf16[48,64,128]{2,1,0:T(8,128)(2,1)S(1)}, u32[]{:S(2)}, u32[]{:S(2)}) %collective-permute-start.9) | collective-permute-done | bytes 786464 | tf_op jit(solution)/shard_map/ppermute | solution.py:410
  92.7 0.8 slice.28
  93.5 0.7 collective-permute-start.11
  94.2 0.8 slice.36
  95.0 1.3 collective-permute-start.12
  96.4 0.7 collective-permute-start.17
  97.0 1.3 collective-permute-start.15
  98.4 7.5 %collective-permute-done.11.refs_3_.refs_4_.refs_5_ = bf16[24,64,128]{2,1,0:T(8,128)(2,1)} collective-permute-done((bf16[24,64,128]{2,1,0:T(8,128)(2,1)}, bf16[24,64,128]{2,1,0:T(8,128)(2,1)}, u32[]{:S(2)}, u32[]{:S(2)}) %collective-permute-start.11) | collective-permute-done | bytes 393248 | tf_op jit(solution)/shard_map/ppermute | solution.py:410
  105.9 1.5 collective-permute-done.12.refs_4_.refs_5_.refs_6_
  107.4 1.5 copy-done.12
  108.9 1.1 copy-done.15
  110.0 6.6 %backward.2 = bf16[128,3072]{1,0:T(8,128)(2,1)S(1)} custom-call(s32[3]{0:T(128)S(1)} %pad_add_fusion.facts_ref, s32[432]{0:T(512)S(1)} %bitcast.65, s32[432]{0:T(512)S(1)} %bitcast.73, bf16[216,32,128]{2,1,0:T(8,128)(2,1)S(1)} %copy-done.9, bf16[216,32,128]{2,1,0:T(8,128)(2,1)S(1)} %copy-done.12, bf16[48,64,128]{2,1,0:T(8,128)(2,1)S(1)} %copy-done.15, ...), custom_call_target="tpu_custom_call" | custom-call | flops 8049999872 | bytes 7474572 | tf_op jit(solution)/shard_map/backward/pallas_call | solution.py:50
  116.7 0.8 collective-permute-start.13
  117.6 4.1 %collective-permute-done.17.refs_2_.refs_1_.refs_4_ = bf16[48,64,128]{2,1,0:T(8,128)(2,1)S(1)} collective-permute-done((bf16[48,64,128]{2,1,0:T(8,128)(2,1)}, bf16[48,64,128]{2,1,0:T(8,128)(2,1)S(1)}, u32[]{:S(2)}, u32[]{:S(2)}) %collective-permute-start.17) | collective-permute-done | bytes 786464 | tf_op jit(solution)/shard_map/ppermute | solution.py:410
  121.7 1.0 collective-permute-start.18
  122.8 1.1 collective-permute-start.16
  123.9 5.5 %outer_other.2 = bf16[216,32,128]{2,1,0:T(8,128)(2,1)S(1)} custom-call(s32[3]{0:T(128)S(1)} %pad_add_fusion.facts_ref, s32[432]{0:T(512)S(1)} %bitcast.66, s32[432]{0:T(512)S(1)} %bitcast.74, bf16[48,64,128]{2,1,0:T(8,128)(2,1)S(1)} %copy-done.5, bf16[48,64,128]{2,1,0:T(8,128)(2,1)S(1)} %copy-done.16, ...), custom_call_target="tpu_custom_call" | custom-call | flops 5750000128 | bytes 5705100 | tf_op jit(solution)/shard_map/outer_other/pallas_call | solution.py:50
  129.4 0.1 collective-permute-start.21
  129.5 0.1 fusion.7
  129.6 0.2 collective-permute-start.14
  129.8 1.1 collective-permute-done.16.refs_5_.refs_4_.refs_7_
  130.9 11.2 %collective-permute-done.14 = bf16[32,3072]{1,0:T(8,128)(2,1)S(1)} collective-permute-done((bf16[32,3072]{1,0:T(8,128)(2,1)S(1)}, bf16[32,3072]{1,0:T(8,128)(2,1)S(1)}, u32[]{:S(2)}, u32[]{:S(2)}) %collective-permute-start.14) | collective-permute-done | bytes 196640 | tf_op jit(solution)/shard_map/ppermute | solution.py:465
  142.1 6.2 %backward.3 = bf16[128,3072]{1,0:T(8,128)(2,1)S(1)} custom-call(s32[3]{0:T(128)S(1)} %pad_add_fusion.facts_ref, s32[432]{0:T(512)S(1)} %bitcast.67, s32[432]{0:T(512)S(1)} %bitcast.75, bf16[216,32,128]{2,1,0:T(8,128)(2,1)S(1)} %copy-done.10, bf16[216,32,128]{2,1,0:T(8,128)(2,1)S(1)} %copy-done.13, bf16[48,64,128]{2,1,0:T(8,128)(2,1)S(1)} %copy-done.18, ...), custom_call_target="tpu_custom_call" | custom-call | flops 8049999872 | bytes 7474572 | tf_op jit(solution)/shard_map/backward/pallas_call | solution.py:50
  148.3 0.1 collective-permute-start.19
  148.4 4.8 %outer_other.3 = bf16[216,32,128]{2,1,0:T(8,128)(2,1)S(1)} custom-call(s32[3]{0:T(128)S(1)} %pad_add_fusion.facts_ref, s32[432]{0:T(512)S(1)} %bitcast.68, s32[432]{0:T(512)S(1)} %bitcast.76, bf16[48,64,128]{2,1,0:T(8,128)(2,1)S(1)} %copy-done.3, bf16[48,64,128]{2,1,0:T(8,128)(2,1)S(1)} %copy-done.18, ...), custom_call_target="tpu_custom_call" | custom-call | flops 5750000128 | bytes 5705100 | tf_op jit(solution)/shard_map/outer_other/pallas_call | solution.py:50
  153.2 0.1 collective-permute-start.22
  153.3 0.8 add_convert_fusion
  154.1 5.2 %collective-permute-done.19 = bf16[2,32,3072]{2,1,0:T(8,128)(2,1)S(1)} collective-permute-done((bf16[2,32,3072]{2,1,0:T(8,128)(2,1)S(1)}, bf16[2,32,3072]{2,1,0:T(8,128)(2,1)S(1)}, u32[]{:S(2)}, u32[]{:S(2)}) %collective-permute-start.19) | collective-permute-done | bytes 393248 | tf_op jit(solution)/shard_map/ppermute | solution.py:463
  159.3 0.7 fusion.6
  160.1 5.6 %outer_own.2.refs_0_ = bf16[216,32,128]{2,1,0:T(8,128)(2,1)S(1)} custom-call(s32[3]{0:T(128)S(1)} %pad_add_fusion.facts_ref, s32[432]{0:T(512)S(1)} %bitcast.69, s32[432]{0:T(512)S(1)} %bitcast.77, bf16[216,32,128]{2,1,0:T(8,128)(2,1)S(1)} %collective-permute-done.21.refs_0_, bf16[48,64,128]{2,1,0:T(8,128)(2,1)S(1)} %copy-done.5, ...), custom_call_target="tpu_custom_call" | custom-call | flops 5750000128 | bytes 7474572 | tf_op jit(solution)/shard_map/outer_own/pallas_call | solution.py:50
  165.7 4.9 %outer_own.3 = bf16[216,32,128]{2,1,0:T(8,128)(2,1)S(1)} custom-call(s32[3]{0:T(128)S(1)} %pad_add_fusion.facts_ref, s32[432]{0:T(512)S(1)} %bitcast.70, s32[432]{0:T(512)S(1)} %bitcast.78, bf16[216,32,128]{2,1,0:T(8,128)(2,1)S(1)} %outer_own.2.refs_0_, bf16[216,32,128]{2,1,0:T(8,128)(2,1)S(1)} %collective-permute-done.22.refs_1_, ...), custom_call_target="tpu_custom_call" | custom-call | flops 5750000128 | bytes 9244044 | tf_op jit(solution)/shard_map/outer_own/pallas_call | solution.py:50
  170.6 2.2 %reshape.152 = bf16[1,1,216,4096]{3,2,1,0:T(8,128)(2,1)} reshape(bf16[216,32,128]{2,1,0:T(8,128)(2,1)S(1)} %outer_own.3) | data formatting | bytes 3538944 | tf_op jit(solution)/shard_map/reshape | solution.py:491
  172.7 1.0 fusion.5
  173.7 0.8 pad_maximum_fusion
  (61 shorter events, 0.5 us)
Async XLA Ops:
  2.5 6.9 %copy-start.6 = (s32[1,1,432]{2,1,0:T(1,128)S(1)}, s32[1,1,432]{2,1,0:T(1,128)}, u32[]{:S(2)}) copy-start(s32[1,1,432]{2,1,0:T(1,128)} %param.8) | copy-start | bytes 5188
  2.5 6.9 %copy-start.7 = (s32[1,1,432]{2,1,0:T(1,128)S(1)}, s32[1,1,432]{2,1,0:T(1,128)}, u32[]{:S(2)}) copy-start(s32[1,1,432]{2,1,0:T(1,128)} %param.9) | copy-start | bytes 5188
  2.5 6.9 %collective-permute-start = (bf16[216,32,128]{2,1,0:T(8,128)(2,1)S(1)}, bf16[216,32,128]{2,1,0:T(8,128)(2,1)S(1)}, u32[]{:S(2)}, u32[]{:S(2)}) collective-permute-start(bf16[216,32,128]{2,1,0:T(8,128)(2,1)S(1)} %bitcast.53), channel_id=1, source_target_pairs={{0,16},{16,0},{1,17},{17,1},{2,18},{18,2},{3,19},{19,3},{4,20},{20... | collective-permute-start | bytes 5308424 | tf_op jit(solution)/shard_map/ppermute | solution.py:413
  3.8 1.4 copy-start
  9.3 5.9 %copy-start.2 = (bf16[48,64,128]{2,1,0:T(8,128)(2,1)}, bf16[48,64,128]{2,1,0:T(8,128)(2,1)S(1)}, u32[]{:S(2)}) copy-start(bf16[48,64,128]{2,1,0:T(8,128)(2,1)S(1)} %get-tuple-element.81.table_ref.refs_0_.refs_2_) | copy-start | bytes 2359300
  9.3 8.6 %copy-start.4 = (bf16[48,64,128]{2,1,0:T(8,128)(2,1)}, bf16[48,64,128]{2,1,0:T(8,128)(2,1)S(1)}, u32[]{:S(2)}) copy-start(bf16[48,64,128]{2,1,0:T(8,128)(2,1)S(1)} %get-tuple-element.80.table_ref.refs_0_.refs_1_) | copy-start | bytes 2359300
  15.3 21.0 %collective-permute-start.1 = (bf16[2,24,64,128]{3,2,1,0:T(8,128)(2,1)S(1)}, bf16[2,24,64,128]{3,2,1,0:T(8,128)(2,1)S(1)}, u32[]{:S(2)}, u32[]{:S(2)}) collective-permute-start(bf16[2,24,64,128]{3,2,1,0:T(8,128)(2,1)S(1)} %get-tuple-element.47), channel_id=1, source_target_pairs={{0,1},{1,0},{2,3},{3,2},{4,5},{5,4},{6,7},{7,6},{8,9},{9,8},{10,11... | collective-permute-start | bytes 2359304 | tf_op jit(solution)/shard_map/ppermute | solution.py:410
  17.8 20.5 %collective-permute-start.3 = (bf16[2,24,64,128]{3,2,1,0:T(8,128)(2,1)S(1)}, bf16[2,24,64,128]{3,2,1,0:T(8,128)(2,1)S(1)}, u32[]{:S(2)}, u32[]{:S(2)}) collective-permute-start(bf16[2,24,64,128]{3,2,1,0:T(8,128)(2,1)S(1)} %get-tuple-element.55), channel_id=1, source_target_pairs={{0,2},{1,3},{2,0},{3,1},{4,6},{5,7},{6,4},{7,5},{8,10},{9,11},{10,... | collective-permute-start | bytes 2359304 | tf_op jit(solution)/shard_map/ppermute | solution.py:410
  18.0 8.2 %copy-start.1 = (bf16[256,3072]{1,0:T(8,128)(2,1)S(1)}, bf16[256,3072]{1,0:T(8,128)(2,1)}, u32[]{:S(2)}) copy-start(bf16[256,3072]{1,0:T(8,128)(2,1)} %values_ref.3) | copy-start | bytes 4718596
  24.0 29.0 %collective-permute-start.5 = (bf16[2,24,64,128]{3,2,1,0:T(8,128)(2,1)S(1)}, bf16[2,24,64,128]{3,2,1,0:T(8,128)(2,1)S(1)}, u32[]{:S(2)}, u32[]{:S(2)}) collective-permute-start(bf16[2,24,64,128]{3,2,1,0:T(8,128)(2,1)S(1)} %get-tuple-element.60), channel_id=1, source_target_pairs={{0,1},{1,0},{2,3},{3,2},{4,5},{5,4},{6,7},{7,6},{8,9},{9,8},{10,11... | collective-permute-start | bytes 2359304 | tf_op jit(solution)/shard_map/ppermute | solution.py:410
  26.1 29.1 %collective-permute-start.7 = (bf16[2,24,64,128]{3,2,1,0:T(8,128)(2,1)S(1)}, bf16[2,24,64,128]{3,2,1,0:T(8,128)(2,1)S(1)}, u32[]{:S(2)}, u32[]{:S(2)}) collective-permute-start(bf16[2,24,64,128]{3,2,1,0:T(8,128)(2,1)S(1)} %get-tuple-element.63), channel_id=1, source_target_pairs={{0,2},{1,3},{2,0},{3,1},{4,6},{5,7},{6,4},{7,5},{8,10},{9,11},{10,... | collective-permute-start | bytes 2359304 | tf_op jit(solution)/shard_map/ppermute | solution.py:410
  36.0 17.1 %copy-start.8 = (bf16[216,32,128]{2,1,0:T(8,128)(2,1)}, bf16[216,32,128]{2,1,0:T(8,128)(2,1)S(1)}, u32[]{:S(2)}) copy-start(bf16[216,32,128]{2,1,0:T(8,128)(2,1)S(1)} %get-tuple-element.52.own_ref) | copy-start | bytes 5308420
  36.0 17.1 %copy-start.11 = (bf16[216,32,128]{2,1,0:T(8,128)(2,1)}, bf16[216,32,128]{2,1,0:T(8,128)(2,1)S(1)}, u32[]{:S(2)}) copy-start(bf16[216,32,128]{2,1,0:T(8,128)(2,1)S(1)} %get-tuple-element.67.other_ref) | copy-start | bytes 5308420
  36.3 27.2 %collective-permute-start.2 = (bf16[24,64,128]{2,1,0:T(8,128)(2,1)S(1)}, bf16[24,64,128]{2,1,0:T(8,128)(2,1)S(1)}, u32[]{:S(2)}, u32[]{:S(2)}) collective-permute-start(bf16[24,64,128]{2,1,0:T(8,128)(2,1)S(1)} %fusion.3), channel_id=1, source_target_pairs={{0,2},{1,3},{2,0},{3,1},{4,6},{5,7},{6,4},{7,5},{8,10},{9,11},{10,... | collective-permute-start | bytes 1179656 | tf_op jit(solution)/shard_map/ppermute | solution.py:410
  38.4 25.1 %collective-permute-start.4 = (bf16[24,64,128]{2,1,0:T(8,128)(2,1)S(1)}, bf16[24,64,128]{2,1,0:T(8,128)(2,1)S(1)}, u32[]{:S(2)}, u32[]{:S(2)}) collective-permute-start(bf16[24,64,128]{2,1,0:T(8,128)(2,1)S(1)} %fusion.2), channel_id=1, source_target_pairs={{0,1},{1,0},{2,3},{3,2},{4,5},{5,4},{6,7},{7,6},{8,9},{9,8},{10,11... | collective-permute-start | bytes 1179656 | tf_op jit(solution)/shard_map/ppermute | solution.py:410
  53.2 18.1 %collective-permute-start.6 = (bf16[24,64,128]{2,1,0:T(8,128)(2,1)S(1)}, bf16[24,64,128]{2,1,0:T(8,128)(2,1)S(1)}, u32[]{:S(2)}, u32[]{:S(2)}) collective-permute-start(bf16[24,64,128]{2,1,0:T(8,128)(2,1)S(1)} %fusion.1), channel_id=1, source_target_pairs={{0,2},{1,3},{2,0},{3,1},{4,6},{5,7},{6,4},{7,5},{8,10},{9,11},{10,... | collective-permute-start | bytes 1179656 | tf_op jit(solution)/shard_map/ppermute | solution.py:410
  55.2 16.0 %collective-permute-start.8 = (bf16[24,64,128]{2,1,0:T(8,128)(2,1)S(1)}, bf16[24,64,128]{2,1,0:T(8,128)(2,1)S(1)}, u32[]{:S(2)}, u32[]{:S(2)}) collective-permute-start(bf16[24,64,128]{2,1,0:T(8,128)(2,1)S(1)} %fusion), channel_id=1, source_target_pairs={{0,1},{1,0},{2,3},{3,2},{4,5},{5,4},{6,7},{7,6},{8,9},{9,8},{10,11... | collective-permute-start | bytes 1179656 | tf_op jit(solution)/shard_map/ppermute | solution.py:410
  73.8 4.7 %copy-start.14 = (bf16[48,64,128]{2,1,0:T(8,128)(2,1)}, bf16[48,64,128]{2,1,0:T(8,128)(2,1)S(1)}, u32[]{:S(2)}) copy-start(bf16[48,64,128]{2,1,0:T(8,128)(2,1)S(1)} %get-tuple-element.68.refs_0_.refs_1_.refs_2_) | copy-start | bytes 2359300
  73.8 18.9 %collective-permute-start.9 = (bf16[48,64,128]{2,1,0:T(8,128)(2,1)S(1)}, bf16[48,64,128]{2,1,0:T(8,128)(2,1)S(1)}, u32[]{:S(2)}, u32[]{:S(2)}) collective-permute-start(bf16[48,64,128]{2,1,0:T(8,128)(2,1)S(1)} %get-tuple-element.68.refs_0_.refs_1_.refs_2_), channel_id=1, source_target_pairs={{0,1},{1,0},{2,3},{3,2},{4,5},{5,4},{6,7},{7,6},{8,9},{9,8},{10,11... | collective-permute-start | bytes 2359304 | tf_op jit(solution)/shard_map/ppermute | solution.py:410
  74.3 20.0 %collective-permute-start.10 = (bf16[48,64,128]{2,1,0:T(8,128)(2,1)S(1)}, bf16[48,64,128]{2,1,0:T(8,128)(2,1)S(1)}, u32[]{:S(2)}, u32[]{:S(2)}) collective-permute-start(bf16[48,64,128]{2,1,0:T(8,128)(2,1)S(1)} %get-tuple-element.68.refs_0_.refs_1_.refs_2_), channel_id=1, source_target_pairs={{0,2},{1,3},{2,0},{3,1},{4,6},{5,7},{6,4},{7,5},{8,10},{9,11},{10,... | collective-permute-start | bytes 2359304 | tf_op jit(solution)/shard_map/ppermute | solution.py:410
  78.6 5.7 %copy-start.17 = (bf16[48,64,128]{2,1,0:T(8,128)(2,1)}, bf16[48,64,128]{2,1,0:T(8,128)(2,1)S(1)}, u32[]{:S(2)}) copy-start(bf16[48,64,128]{2,1,0:T(8,128)(2,1)S(1)} %get-tuple-element.71.refs_1_.refs_0_.refs_3_) | copy-start | bytes 2359300
  78.6 28.8 %copy-start.9 = (bf16[216,32,128]{2,1,0:T(8,128)(2,1)S(1)}, bf16[216,32,128]{2,1,0:T(8,128)(2,1)}, u32[]{:S(2)}) copy-start(bf16[216,32,128]{2,1,0:T(8,128)(2,1)} %copy-done.8) | copy-start | bytes 5308420
  93.5 12.4 %collective-permute-start.11 = (bf16[24,64,128]{2,1,0:T(8,128)(2,1)}, bf16[24,64,128]{2,1,0:T(8,128)(2,1)}, u32[]{:S(2)}, u32[]{:S(2)}) collective-permute-start(bf16[24,64,128]{2,1,0:T(8,128)(2,1)} %slice.28), channel_id=1, source_target_pairs={{0,2},{1,3},{2,0},{3,1},{4,6},{5,7},{6,4},{7,5},{8,10},{9,11},{10,... | collective-permute-start | bytes 1179656 | tf_op jit(solution)/shard_map/ppermute | solution.py:410
  95.0 12.4 %collective-permute-start.12 = (bf16[24,64,128]{2,1,0:T(8,128)(2,1)}, bf16[24,64,128]{2,1,0:T(8,128)(2,1)}, u32[]{:S(2)}, u32[]{:S(2)}) collective-permute-start(bf16[24,64,128]{2,1,0:T(8,128)(2,1)} %slice.36), channel_id=1, source_target_pairs={{0,1},{1,0},{2,3},{3,2},{4,5},{5,4},{6,7},{7,6},{8,9},{9,8},{10,11... | collective-permute-start | bytes 1179656 | tf_op jit(solution)/shard_map/ppermute | solution.py:410
  96.4 25.3 %collective-permute-start.17 = (bf16[48,64,128]{2,1,0:T(8,128)(2,1)}, bf16[48,64,128]{2,1,0:T(8,128)(2,1)S(1)}, u32[]{:S(2)}, u32[]{:S(2)}) collective-permute-start(bf16[48,64,128]{2,1,0:T(8,128)(2,1)} %copy-done.17), channel_id=1, source_target_pairs={{0,1},{1,0},{2,3},{3,2},{4,5},{5,4},{6,7},{7,6},{8,9},{9,8},{10,11... | collective-permute-start | bytes 2359304 | tf_op jit(solution)/shard_map/ppermute | solution.py:410
  97.0 25.7 %collective-permute-start.15 = (bf16[48,64,128]{2,1,0:T(8,128)(2,1)}, bf16[48,64,128]{2,1,0:T(8,128)(2,1)S(1)}, u32[]{:S(2)}, u32[]{:S(2)}) collective-permute-start(bf16[48,64,128]{2,1,0:T(8,128)(2,1)} %copy-done.17), channel_id=1, source_target_pairs={{0,2},{1,3},{2,0},{3,1},{4,6},{5,7},{6,4},{7,5},{8,10},{9,11},{10,... | collective-permute-start | bytes 2359304 | tf_op jit(solution)/shard_map/ppermute | solution.py:410
  107.4 1.5 copy-start.12
  108.9 1.1 copy-start.15
  116.7 7.2 %copy-start.5 = (bf16[48,64,128]{2,1,0:T(8,128)(2,1)S(1)}, bf16[48,64,128]{2,1,0:T(8,128)(2,1)}, u32[]{:S(2)}) copy-start(bf16[48,64,128]{2,1,0:T(8,128)(2,1)} %copy-done.4) | copy-start | bytes 2359300
  116.7 7.2 %copy-start.16 = (bf16[48,64,128]{2,1,0:T(8,128)(2,1)S(1)}, bf16[48,64,128]{2,1,0:T(8,128)(2,1)}, u32[]{:S(2)}) copy-start(bf16[48,64,128]{2,1,0:T(8,128)(2,1)} %copy-done.14) | copy-start | bytes 2359300
  116.7 12.8 %collective-permute-start.13 = (bf16[2,32,3072]{2,1,0:T(8,128)(2,1)S(1)}, bf16[2,32,3072]{2,1,0:T(8,128)(2,1)S(1)}, u32[]{:S(2)}, u32[]{:S(2)}) collective-permute-start(bf16[2,32,3072]{2,1,0:T(8,128)(2,1)S(1)} %dynamic-slice_bitcast_fusion.1), channel_id=1, source_target_pairs={{0,4},{4,0},{8,12},{12,8},{1,5},{5,1},{9,13},{13,9},{2,6},{6,2},{1... | collective-permute-start | bytes 1179656 | tf_op jit(solution)/shard_map/ppermute | solution.py:463
  121.7 20.4 %collective-permute-start.18 = (bf16[24,64,128]{2,1,0:T(8,128)(2,1)S(1)}, bf16[24,64,128]{2,1,0:T(8,128)(2,1)S(1)}, u32[]{:S(2)}, u32[]{:S(2)}) collective-permute-start(bf16[24,64,128]{2,1,0:T(8,128)(2,1)S(1)} %slice.38), channel_id=1, source_target_pairs={{0,2},{1,3},{2,0},{3,1},{4,6},{5,7},{6,4},{7,5},{8,10},{9,11},{10,... | collective-permute-start | bytes 1179656 | tf_op jit(solution)/shard_map/ppermute | solution.py:410
  122.8 19.3 %copy-start.10 = (bf16[216,32,128]{2,1,0:T(8,128)(2,1)S(1)}, bf16[216,32,128]{2,1,0:T(8,128)(2,1)}, u32[]{:S(2)}) copy-start(bf16[216,32,128]{2,1,0:T(8,128)(2,1)} %copy-done.8) | copy-start | bytes 5308420
  122.8 19.3 %copy-start.13 = (bf16[216,32,128]{2,1,0:T(8,128)(2,1)S(1)}, bf16[216,32,128]{2,1,0:T(8,128)(2,1)}, u32[]{:S(2)}) copy-start(bf16[216,32,128]{2,1,0:T(8,128)(2,1)} %copy-done.11) | copy-start | bytes 5308420
  122.8 19.3 %copy-start.18 = (bf16[48,64,128]{2,1,0:T(8,128)(2,1)S(1)}, bf16[48,64,128]{2,1,0:T(8,128)(2,1)}, u32[]{:S(2)}) copy-start(bf16[48,64,128]{2,1,0:T(8,128)(2,1)} %copy-done.17) | copy-start | bytes 2359300
  122.8 8.1 %collective-permute-start.16 = (bf16[24,64,128]{2,1,0:T(8,128)(2,1)S(1)}, bf16[24,64,128]{2,1,0:T(8,128)(2,1)S(1)}, u32[]{:S(2)}, u32[]{:S(2)}) collective-permute-start(bf16[24,64,128]{2,1,0:T(8,128)(2,1)S(1)} %slice.37), channel_id=1, source_target_pairs={{0,1},{1,0},{2,3},{3,2},{4,5},{5,4},{6,7},{7,6},{8,9},{9,8},{10,11... | collective-permute-start | bytes 1179656 | tf_op jit(solution)/shard_map/ppermute | solution.py:410
  129.4 30.6 %collective-permute-start.21 = (bf16[216,32,128]{2,1,0:T(8,128)(2,1)S(1)}, bf16[216,32,128]{2,1,0:T(8,128)(2,1)S(1)}, u32[]{:S(2)}, u32[]{:S(2)}) collective-permute-start(bf16[216,32,128]{2,1,0:T(8,128)(2,1)S(1)} %outer_other.2), channel_id=1, source_target_pairs={{0,16},{16,0},{1,17},{17,1},{2,18},{18,2},{3,19},{19,3},{4,20},{20... | collective-permute-start | bytes 5308424 | tf_op jit(solution)/shard_map/ppermute | solution.py:413
  129.6 12.5 %collective-permute-start.14 = (bf16[32,3072]{1,0:T(8,128)(2,1)S(1)}, bf16[32,3072]{1,0:T(8,128)(2,1)S(1)}, u32[]{:S(2)}, u32[]{:S(2)}) collective-permute-start(bf16[32,3072]{1,0:T(8,128)(2,1)S(1)} %fusion.7), channel_id=1, source_target_pairs={{0,8},{4,12},{8,0},{12,4},{1,9},{5,13},{9,1},{13,5},{2,10},{6,14},... | collective-permute-start | bytes 589832 | tf_op jit(solution)/shard_map/ppermute | solution.py:465
  129.8 18.6 %copy-start.3 = (bf16[48,64,128]{2,1,0:T(8,128)(2,1)S(1)}, bf16[48,64,128]{2,1,0:T(8,128)(2,1)}, u32[]{:S(2)}) copy-start(bf16[48,64,128]{2,1,0:T(8,128)(2,1)} %copy-done.2) | copy-start | bytes 2359300
  148.3 11.0 %collective-permute-start.19 = (bf16[2,32,3072]{2,1,0:T(8,128)(2,1)S(1)}, bf16[2,32,3072]{2,1,0:T(8,128)(2,1)S(1)}, u32[]{:S(2)}, u32[]{:S(2)}) collective-permute-start(bf16[2,32,3072]{2,1,0:T(8,128)(2,1)S(1)} %dynamic-slice_bitcast_fusion), channel_id=1, source_target_pairs={{0,4},{4,0},{8,12},{12,8},{1,5},{5,1},{9,13},{13,9},{2,6},{6,2},{1... | collective-permute-start | bytes 1179656 | tf_op jit(solution)/shard_map/ppermute | solution.py:463
  153.2 12.4 %collective-permute-start.22 = (bf16[216,32,128]{2,1,0:T(8,128)(2,1)S(1)}, bf16[216,32,128]{2,1,0:T(8,128)(2,1)S(1)}, u32[]{:S(2)}, u32[]{:S(2)}) collective-permute-start(bf16[216,32,128]{2,1,0:T(8,128)(2,1)S(1)} %outer_other.3), channel_id=1, source_target_pairs={{0,16},{16,0},{1,17},{17,1},{2,18},{18,2},{3,19},{19,3},{4,20},{20... | collective-permute-start | bytes 5308424 | tf_op jit(solution)/shard_map/ppermute | solution.py:413
  160.0 12.7 %collective-permute-start.20 = (bf16[32,3072]{1,0:T(8,128)(2,1)}, bf16[32,3072]{1,0:T(8,128)(2,1)}, u32[]{:S(2)}, u32[]{:S(2)}) collective-permute-start(bf16[32,3072]{1,0:T(8,128)(2,1)} %fusion.6), channel_id=1, source_target_pairs={{0,8},{4,12},{8,0},{12,4},{1,9},{5,13},{9,1},{13,5},{2,10},{6,14},... | collective-permute-start | bytes 589832 | tf_op jit(solution)/shard_map/ppermute | solution.py:465
  170.6 3.2 %copy-start.19 = (bf16[32,3072]{1,0:T(8,128)(2,1)S(1)}, bf16[32,3072]{1,0:T(8,128)(2,1)}, u32[]{:S(2)}) copy-start(bf16[32,3072]{1,0:T(8,128)(2,1)} %add_convert_fusion) | copy-start | bytes 589828

commit v6 on v5

--- a/solution.py
+++ b/solution.py
@@ -222,7 +222,7 @@
                 out_ref[first + lane] = jnp.zeros(out_ref.shape[1:], out_ref.dtype)
 
 
-def outer(facts, rows, cols, inputs, pieces, share_blocks, half_slots, mine, added):
+def outer(facts, rows, cols, inputs, pieces, share_blocks, half_slots, mine, added, microseconds):
     blocks = 4 * share_blocks
     return call(
         functools.partial(outer_kernel, share_blocks, mine, len(added)),
@@ -232,7 +232,7 @@
         VMEM,
         (facts, rows, cols, *added, inputs, *pieces),
         12,
-        5,
+        microseconds,
         [
             pltpu.VMEM((blocks, BLOCK, inputs.shape[2]), jnp.bfloat16),
             pltpu.SemaphoreType.DMA((len(pieces),)),
@@ -454,16 +454,19 @@
     def take(values, index):
         return lax.dynamic_index_in_dim(values, index, 0, keepdims=False)
 
-    def to_rows(partial):
+    def to_rows(partial, filler):
         if row_devices != 4:
-            return [lax.psum_scatter(partial, "row", scatter_dimension=0, tiled=True)], partial, partial
+            return [lax.psum_scatter(partial, "row", scatter_dimension=0, tiled=True)], partial, filler(partial)
         low, high = me_row & 1, me_row >> 1
         pieces = partial.reshape(2, 2, part, in_blocks * BLOCK)
         sent, kept = (lax.dynamic_index_in_dim(pieces, bit, 1, keepdims=False) for bit in (1 - low, low))
         moved = lax.ppermute(sent, "row", [(place, place ^ 1) for place in range(4)])
+        filled = filler(sent)
+        moved = after(moved, filled)
         both = take(kept, 1 - high).astype(jnp.float32) + take(moved, 1 - high).astype(jnp.float32)
-        last = lax.ppermute(both.astype(jnp.bfloat16), "row", [(place, place ^ 2) for place in range(4)])
-        return [last, take(kept, high), take(moved, high)], both, sent
+        both = both.astype(jnp.bfloat16)
+        last = lax.ppermute(both, "row", [(place, place ^ 2) for place in range(4)])
+        return [last, take(kept, high), take(moved, high)], both, filled
 
     def add_up(parts, earlier):
         parts = [*parts[:-1], after(parts[-1], earlier)]
@@ -472,21 +475,25 @@
     def input_sums(chunk):
         return backward(facts, rows, cols, own_t, other_t, grads[chunk], share_blocks, in_blocks)
 
-    def tile_part(chunk, earlier, mine, added):
+    def tile_part(chunk, earlier, mine, added, microseconds=20):
         table = after(tables[chunk], earlier)
-        return outer(facts, rows, cols, table, grads[chunk], share_blocks, half_slots, mine, added)
-
-    first = input_sums(0)
-    row_parts, halfway, sent = to_rows(first)
-    other_first = tile_part(0, (sent, grads[1][1], grads[1][2]), False, [])
-    *first_parts, grads[1][4] = lax.optimization_barrier((*row_parts, after(grads[1][4], other_first)))
-    second = input_sums(1)
-    row_parts, halfway, sent = to_rows(second)
-    own_first = tile_part(0, sent, True, [other_core(other_first)])
-    other_second = tile_part(1, after(halfway, own_first), False, [])
-    own_second = tile_part(1, other_second, True, [own_first, other_core(other_second)])
-    first_sum = add_up(first_parts, other_second)
-    second_sum = add_up(row_parts, own_second)
+        return outer(facts, rows, cols, table, grads[chunk], share_blocks, half_slots, mine, added, microseconds)
+
+    def first_filler(sent):
+        return tile_part(0, (sent, grads[1][1], grads[1][2]), False, [], 5)
+
+    first_terms, halfway, other_first = to_rows(input_sums(0), first_filler)
+    grads[1][4] = after(grads[1][4], halfway)
+
+    def second_filler(sent):
+        first_sum = add_up(first_terms, sent)
+        other_second = tile_part(1, first_sum, False, [])
+        own_first = tile_part(0, other_second, True, [other_core(other_first)])
+        return own_first, other_second, first_sum
+
+    second_terms, halfway, (own_first, other_second, first_sum) = to_rows(input_sums(1), second_filler)
+    own_second = tile_part(1, halfway, True, [own_first, other_core(other_second)])
+    second_sum = add_up(second_terms, own_second)
     input_grad = jnp.concatenate([first_sum, second_sum], axis=0)
     tile_grads = own_second.reshape(1, 1, half_slots, 4096)
     return (activation, input_grad, tile_grads)

time: 174 us -> 163 us (0.937)
  Pallas kernels: 70.3 us -> 59.1 us
  waiting for transfers between devices: 69.7 us -> 61.1 us
  starting transfers between devices: 19.2 us -> 26.7 us
    pallas_call x14, Pallas kernels: 70.3 us -> 59.1 us  [call(): pl.pallas_call(kernel, out_shape=out_shape, in_specs=in_specs, out_specs=...]
    ppermute x2, waiting for transfers between devices: 11.2 us -> 5.23 us  [to_rows(): last = lax.ppermute(both, 'row', [(place, place ^ 2) for place in range(4)])]
    ppermute x2, waiting for transfers between devices: 5.25 us -> 0.01 us  [to_rows(): lax.ppermute(sent, 'row', [(place, place ^ 1) for place in range(4)])]
    ppermute x2, starting transfers between devices: 0.17 us -> 5.23 us  [to_rows(): last = lax.ppermute(both, 'row', [(place, place ^ 2) for place in range(4)])]
    ppermute x16, waiting for transfers between devices: 53.3 us -> 55.9 us  [across(): lax.ppermute(values, 'col', [(place, place ^ bit) for place in range(shar...]
    ppermute x3, starting transfers between devices: 0.66 us -> 3.08 us  [other_core(): return lax.ppermute(values, 'dp', [(0, 1), (1, 0)])]
  transfers between devices with their start and end apart: 23 -> 23, of which waited for: 11 -> 13; matrix products, arithmetic and copies ran while one was open for 3% -> 4% of each run, Pallas kernels for 35% -> 32%
where the time goes in v6:
time: 163 us; the launch traced here: 162 us
  waiting for transfers between devices  61.1 us (37%)
  Pallas kernels  59.1 us (36%)
  starting transfers between devices  26.7 us (16%)
  local copies, waits for them, and re-layouts  9.81 us (6%)
  other arithmetic  3.71 us (2%)
  between operations  1.76 us (1%)
    pallas_call x14, Pallas kernels, call(): pl.pallas_call(kernel, out_shape=out_shape, in_specs=in_specs, out_specs=...  59.1 us
    ppermute x16, waiting for transfers between devices, across(): lax.ppermute(values, 'col', [(place, place ^ bit) for place in range(shar...  55.9 us
    ppermute x16, starting transfers between devices, across(): lax.ppermute(values, 'col', [(place, place ^ bit) for place in range(shar...  18.3 us
    unnamed x41, local copies, waits for them, and re-layouts  5.93 us
    ppermute x2, starting transfers between devices, to_rows(): last = lax.ppermute(both, 'row', [(place, place ^ 2) for place in range(4)])  5.23 us
    ppermute x2, waiting for transfers between devices, to_rows(): last = lax.ppermute(both, 'row', [(place, place ^ 2) for place in range(4)])  5.23 us
  transfers between devices with their start and end apart: 23, of which 13 were waited for; matrix products, arithmetic and copies ran while one was open for 4% of the time, Pallas kernels for 32%

profile of v6, /device:TPU:0, one launch (start us, length us, event | category | flops | bytes accessed | tf_op | source)
XLA Modules:
  0.0 162.3 jit_solution(482549531967357680)
XLA Ops:
  0.6 1.8 %copy.9 = bf16[27,8,32,128]{3,2,1,0:T(8,128)(2,1)S(1)} copy(bf16[27,8,32,128]{3,1,2,0:T(8,128)(2,1)} %bitcast.80) | data formatting | bytes 3538944
  2.5 0.5 collective-permute-start
  3.7 0.1 add_add_fusion
  3.8 0.0 copy-start
  3.8 1.4 copy-done
  5.2 4.1 %features_to_rows.1 = (bf16[48,64,128]{2,1,0:T(8,128)(2,1)S(1)}, bf16[48,64,128]{2,1,0:T(8,128)(2,1)S(1)}) custom-call(bf16[256,3072]{1,0:T(8,128)(2,1)S(1)} %copy-done, bf16[2,256,128]{2,1,0:T(8,128)(2,1)S(1)} %fusion.10.select_ref), custom_call_target="tpu_custom_call" | custom-call | tf_op jit(solution)/shard_map/features_to_rows/pallas_call | solution.py:50
  9.3 0.1 pad_add_fusion.facts_ref
  9.4 4.2 %forward.2 = (bf16[2,24,64,128]{3,2,1,0:T(8,128)(2,1)S(1)}, bf16[2,24,64,128]{3,2,1,0:T(8,128)(2,1)S(1)}, bf16[24,64,128]{2,1,0:T(8,128)(2,1)S(1)}, bf16[24,64,1...) custom-call(s32[3]{0:T(128)S(1)} %pad_add_fusion.facts_ref, ...), custom_call_target="tpu_custom_call" | custom-call | tf_op jit(solution)/shard_map/forward/pallas_call | solution.py:50
  13.7 3.1 %collective-permute-start.1 = (bf16[2,24,64,128]{3,2,1,0:T(8,128)(2,1)S(1)}, bf16[2,24,64,128]{3,2,1,0:T(8,128)(2,1)S(1)}, u32[]{:S(2)}, u32[]{:S(2)}) collective-permute-start(bf16[2,24,64,128]{3,2,1,0:T(8,128)(2,1)S(1)} %get-tuple-element.46), channel_id=1, source_target_pairs={{0,1},{1,0},{2,3},{3,2},{4,5},{5,4},{6,7},{7,6},{8,9},{9,8},{10,11... | collective-permute-start | bytes 2359304 | tf_op jit(solution)/shard_map/ppermute | solution.py:410
  16.8 1.5 collective-permute-start.3
  18.3 4.4 %forward.3 = (bf16[2,24,64,128]{3,2,1,0:T(8,128)(2,1)S(1)}, bf16[2,24,64,128]{3,2,1,0:T(8,128)(2,1)S(1)}, bf16[24,64,128]{2,1,0:T(8,128)(2,1)S(1)}, bf16[24,64,1...) custom-call(s32[3]{0:T(128)S(1)} %pad_add_fusion.facts_ref, ...), custom_call_target="tpu_custom_call" | custom-call | tf_op jit(solution)/shard_map/forward/pallas_call | solution.py:50
  22.7 0.1 collective-permute-start.7
  22.8 1.1 collective-permute-start.5
  23.9 4.1 %units_to_rows.1 = (bf16[48,64,128]{2,1,0:T(8,128)(2,1)S(1)}, bf16[48,64,128]{2,1,0:T(8,128)(2,1)S(1)}) custom-call(bf16[256,3072]{1,0:T(8,128)(2,1)S(1)} %copy-done.1, bf16[2,256,128]{2,1,0:T(8,128)(2,1)S(1)} %fusion.10.select_ref), custom_call_target="tpu_custom_call" | custom-call | tf_op jit(solution)/shard_map/units_to_rows/pallas_call | solution.py:50
  28.0 5.8 %transpose_tiles.1 = (bf16[216,32,128]{2,1,0:T(8,128)(2,1)S(1)}, bf16[216,32,128]{2,1,0:T(8,128)(2,1)S(1)}) custom-call(bf16[216,32,128]{2,1,0:T(8,128)(2,1)S(1)} %bitcast.57, bf16[216,32,128]{2,1,0:T(8,128)(2,1)S(1)} %collective-permute-done.other_ref), custom_call_target="tpu_custom_call" | custom-call | tf_op jit(solution)/shard_map/transpose_tiles/pallas_call | solution.py:50
  33.8 1.3 collective-permute-done.1.near_a
  35.2 1.6 collective-permute-start.2
  36.8 0.4 collective-permute-done.3.near_b
  37.2 1.6 %collective-permute-start.4 = (bf16[24,64,128]{2,1,0:T(8,128)(2,1)S(1)}, bf16[24,64,128]{2,1,0:T(8,128)(2,1)S(1)}, u32[]{:S(2)}, u32[]{:S(2)}) collective-permute-start(bf16[24,64,128]{2,1,0:T(8,128)(2,1)S(1)} %fusion.2), channel_id=1, source_target_pairs={{0,1},{1,0},{2,3},{3,2},{4,5},{5,4},{6,7},{7,6},{8,9},{9,8},{10,11... | collective-permute-start | bytes 1179656 | tf_op jit(solution)/shard_map/ppermute | solution.py:410
  38.8 15.2 %collective-permute-done.7.near_b = bf16[2,24,64,128]{3,2,1,0:T(8,128)(2,1)S(1)} collective-permute-done((bf16[2,24,64,128]{3,2,1,0:T(8,128)(2,1)S(1)}, bf16[2,24,64,128]{3,2,1,0:T(8,128)(2,1)S(1)}, u32[]{:S(2)}, u32[]{:S(2)}) %collective-permute-start.7) | collective-permute-done | bytes 786464 | tf_op jit(solution)/shard_map/ppermute | solution.py:410
  54.1 0.1 collective-permute-start.8
  54.2 1.6 collective-permute-start.6
  55.8 6.6 %collective-permute-done.2.last_a = bf16[24,64,128]{2,1,0:T(8,128)(2,1)S(1)} collective-permute-done((bf16[24,64,128]{2,1,0:T(8,128)(2,1)S(1)}, bf16[24,64,128]{2,1,0:T(8,128)(2,1)S(1)}, u32[]{:S(2)}, u32[]{:S(2)}) %collective-permute-start.2) | collective-permute-done | bytes 393248 | tf_op jit(solution)/shard_map/ppermute | solution.py:410
  62.4 6.3 %collective-permute-done.8.last_b = bf16[24,64,128]{2,1,0:T(8,128)(2,1)S(1)} collective-permute-done((bf16[24,64,128]{2,1,0:T(8,128)(2,1)S(1)}, bf16[24,64,128]{2,1,0:T(8,128)(2,1)S(1)}, u32[]{:S(2)}, u32[]{:S(2)}) %collective-permute-start.8) | collective-permute-done | bytes 393248 | tf_op jit(solution)/shard_map/ppermute | solution.py:410
  68.7 1.5 collective-permute-done.6.last_a
  70.1 2.6 %gelu.2 = (bf16[48,64,128]{2,1,0:T(8,128)(2,1)S(1)}, bf16[48,64,128]{2,1,0:T(8,128)(2,1)S(1)}) custom-call(bf16[48,64,128]{2,1,0:T(8,128)(2,1)S(1)} %get-tuple-element.56.upstream_hbm, bf16[24,64,128]{2,1,0:T(8,128)(2,1)S(1)} %get-tuple-element.58.own_a, bf16[2,24,64,128]{3,2,1,0:T(8,128)(2,1)S(1)} %collective-permute-done.5.near_a, ...), custom_call_target="tpu_custom_call" | custom-call | tf_op jit(solution)/shard_map/gelu/pallas_call | solution.py:50
  72.8 0.4 collective-permute-start.9
  73.2 1.5 collective-permute-start.10
  74.7 2.6 %gelu.3 = (bf16[48,64,128]{2,1,0:T(8,128)(2,1)S(1)}, bf16[48,64,128]{2,1,0:T(8,128)(2,1)S(1)}) custom-call(bf16[48,64,128]{2,1,0:T(8,128)(2,1)S(1)} %get-tuple-element.48.upstream_hbm, bf16[24,64,128]{2,1,0:T(8,128)(2,1)S(1)} %get-tuple-element.43.own_a, bf16[2,24,64,128]{3,2,1,0:T(8,128)(2,1)S(1)} %collective-permute-done.1.near_a, ...), custom_call_target="tpu_custom_call" | custom-call | tf_op jit(solution)/shard_map/gelu/pallas_call | solution.py:50
  77.3 5.7 %rows_to_units.1 = bf16[256,3072]{1,0:T(8,128)(2,1)} custom-call(bf16[2,256,128]{2,1,0:T(8,128)(2,1)S(1)} %fusion.10.select_ref, bf16[48,64,128]{2,1,0:T(8,128)(2,1)S(1)} %get-tuple-element.64.refs_0_, bf16[48,64,128]{2,1,0:T(8,128)(2,1)S(1)} %get-tuple-element.65.refs_1_), custom_call_target="tpu_custom_call" | custom-call | tf_op jit(solution)/shard_map/rows_to_units/pallas_call | solution.py:50
  83.0 8.7 %collective-permute-done.9.refs_1_.refs_2_.refs_3_ = bf16[48,64,128]{2,1,0:T(8,128)(2,1)S(1)} collective-permute-done((bf16[48,64,128]{2,1,0:T(8,128)(2,1)S(1)}, bf16[48,64,128]{2,1,0:T(8,128)(2,1)S(1)}, u32[]{:S(2)}, u32[]{:S(2)}) %collective-permute-start.9) | collective-permute-done | bytes 786464 | tf_op jit(solution)/shard_map/ppermute | solution.py:410
  91.7 0.8 slice.28
  92.5 1.5 collective-permute-start.11
  93.9 0.8 slice.36
  94.7 0.7 collective-permute-start.12
  95.4 0.5 collective-permute-start.15
  96.0 1.3 collective-permute-start.14
  97.3 7.5 %collective-permute-done.11.refs_3_.refs_4_.refs_5_ = bf16[24,64,128]{2,1,0:T(8,128)(2,1)} collective-permute-done((bf16[24,64,128]{2,1,0:T(8,128)(2,1)}, bf16[24,64,128]{2,1,0:T(8,128)(2,1)}, u32[]{:S(2)}, u32[]{:S(2)}) %collective-permute-start.11) | collective-permute-done | bytes 393248 | tf_op jit(solution)/shard_map/ppermute | solution.py:410
  104.8 2.3 %collective-permute-done.12.refs_4_.refs_5_.refs_6_ = bf16[24,64,128]{2,1,0:T(8,128)(2,1)} collective-permute-done((bf16[24,64,128]{2,1,0:T(8,128)(2,1)}, bf16[24,64,128]{2,1,0:T(8,128)(2,1)}, u32[]{:S(2)}, u32[]{:S(2)}) %collective-permute-start.12) | collective-permute-done | bytes 393248 | tf_op jit(solution)/shard_map/ppermute | solution.py:410
  107.1 1.5 copy-done.12
  108.6 1.1 copy-done.17
  109.7 5.0 %backward.2 = bf16[128,3072]{1,0:T(8,128)(2,1)S(1)} custom-call(s32[3]{0:T(128)S(1)} %pad_add_fusion.facts_ref, s32[432]{0:T(512)S(1)} %bitcast.66, s32[432]{0:T(512)S(1)} %bitcast.74, bf16[216,32,128]{2,1,0:T(8,128)(2,1)S(1)} %copy-done.9, bf16[216,32,128]{2,1,0:T(8,128)(2,1)S(1)} %copy-done.12, bf16[48,64,128]{2,1,0:T(8,128)(2,1)S(1)} %copy-done.17, ...), custom_call_target="tpu_custom_call" | custom-call | flops 8049999872 | bytes 7474572 | tf_op jit(solution)/shard_map/backward/pallas_call | solution.py:50
  114.8 0.1 collective-permute-start.13
  114.9 4.1 %collective-permute-done.15.refs_2_.refs_3_.refs_5_ = bf16[48,64,128]{2,1,0:T(8,128)(2,1)S(1)} collective-permute-done((bf16[48,64,128]{2,1,0:T(8,128)(2,1)}, bf16[48,64,128]{2,1,0:T(8,128)(2,1)S(1)}, u32[]{:S(2)}, u32[]{:S(2)}) %collective-permute-start.15) | collective-permute-done | bytes 786464 | tf_op jit(solution)/shard_map/ppermute | solution.py:410
  119.0 2.0 %collective-permute-done.14.refs_1_.refs_2_.refs_4_ = bf16[48,64,128]{2,1,0:T(8,128)(2,1)S(1)} collective-permute-done((bf16[48,64,128]{2,1,0:T(8,128)(2,1)}, bf16[48,64,128]{2,1,0:T(8,128)(2,1)S(1)}, u32[]{:S(2)}, u32[]{:S(2)}) %collective-permute-start.14) | collective-permute-done | bytes 786464 | tf_op jit(solution)/shard_map/ppermute | solution.py:410
  121.1 1.1 collective-permute-start.18
  122.2 0.6 collective-permute-start.17
  122.8 3.1 %outer_other.2 = bf16[216,32,128]{2,1,0:T(8,128)(2,1)S(1)} custom-call(s32[3]{0:T(128)S(1)} %pad_add_fusion.facts_ref, s32[432]{0:T(512)S(1)} %bitcast.67, s32[432]{0:T(512)S(1)} %bitcast.75, bf16[48,64,128]{2,1,0:T(8,128)(2,1)S(1)} %copy-done.5, bf16[48,64,128]{2,1,0:T(8,128)(2,1)S(1)} %copy-done.18, ...), custom_call_target="tpu_custom_call" | custom-call | flops 5750000128 | bytes 5705100 | tf_op jit(solution)/shard_map/outer_other/pallas_call | solution.py:50
  126.0 0.1 collective-permute-start.20
  126.1 0.1 fusion.9
  126.1 5.2 %collective-permute-start.16 = (bf16[32,3072]{1,0:T(8,128)(2,1)S(1)}, bf16[32,3072]{1,0:T(8,128)(2,1)S(1)}, u32[]{:S(2)}, u32[]{:S(2)}) collective-permute-start(bf16[32,3072]{1,0:T(8,128)(2,1)S(1)} %fusion.9), channel_id=1, source_target_pairs={{0,8},{4,12},{8,0},{12,4},{1,9},{5,13},{9,1},{13,5},{2,10},{6,14},... | collective-permute-start | bytes 589832 | tf_op jit(solution)/shard_map/ppermute | solution.py:468
  131.4 4.6 %backward.3 = bf16[128,3072]{1,0:T(8,128)(2,1)S(1)} custom-call(s32[3]{0:T(128)S(1)} %pad_add_fusion.facts_ref, s32[432]{0:T(512)S(1)} %bitcast.68, s32[432]{0:T(512)S(1)} %bitcast.76, bf16[216,32,128]{2,1,0:T(8,128)(2,1)S(1)} %copy-done.10, bf16[216,32,128]{2,1,0:T(8,128)(2,1)S(1)} %copy-done.13, bf16[48,64,128]{2,1,0:T(8,128)(2,1)S(1)} %copy-done.15, ...), custom_call_target="tpu_custom_call" | custom-call | flops 8049999872 | bytes 7474572 | tf_op jit(solution)/shard_map/backward/pallas_call | solution.py:50
  136.1 0.1 collective-permute-start.19
  136.1 3.4 %collective-permute-done.16 = bf16[32,3072]{1,0:T(8,128)(2,1)S(1)} collective-permute-done((bf16[32,3072]{1,0:T(8,128)(2,1)S(1)}, bf16[32,3072]{1,0:T(8,128)(2,1)S(1)}, u32[]{:S(2)}, u32[]{:S(2)}) %collective-permute-start.16) | collective-permute-done | bytes 196640 | tf_op jit(solution)/shard_map/ppermute | solution.py:468
  139.6 0.8 fusion.8
  140.4 2.4 %outer_other.3 = bf16[216,32,128]{2,1,0:T(8,128)(2,1)S(1)} custom-call(s32[3]{0:T(128)S(1)} %pad_add_fusion.facts_ref, s32[432]{0:T(512)S(1)} %bitcast.69, s32[432]{0:T(512)S(1)} %bitcast.77, bf16[48,64,128]{2,1,0:T(8,128)(2,1)S(1)} %copy-done.3, bf16[48,64,128]{2,1,0:T(8,128)(2,1)S(1)} %copy-done.15, ...), custom_call_target="tpu_custom_call" | custom-call | flops 23000000512 | bytes 5705100 | tf_op jit(solution)/shard_map/outer_other/pallas_call | solution.py:50
  142.8 2.5 %collective-permute-start.22 = (bf16[216,32,128]{2,1,0:T(8,128)(2,1)S(1)}, bf16[216,32,128]{2,1,0:T(8,128)(2,1)S(1)}, u32[]{:S(2)}, u32[]{:S(2)}) collective-permute-start(bf16[216,32,128]{2,1,0:T(8,128)(2,1)S(1)} %outer_other.3), channel_id=1, source_target_pairs={{0,16},{16,0},{1,17},{17,1},{2,18},{18,2},{3,19},{19,3},{4,20},{20... | collective-permute-start | bytes 5308424 | tf_op jit(solution)/shard_map/ppermute | solution.py:413
  145.3 5.6 %outer_own.2.refs_0_ = bf16[216,32,128]{2,1,0:T(8,128)(2,1)S(1)} custom-call(s32[3]{0:T(128)S(1)} %pad_add_fusion.facts_ref, s32[432]{0:T(512)S(1)} %bitcast.70, s32[432]{0:T(512)S(1)} %bitcast.78, bf16[216,32,128]{2,1,0:T(8,128)(2,1)S(1)} %collective-permute-done.20.refs_0_, bf16[48,64,128]{2,1,0:T(8,128)(2,1)S(1)} %copy-done.5, ...), custom_call_target="tpu_custom_call" | custom-call | flops 23000000512 | bytes 7474572 | tf_op jit(solution)/shard_map/outer_own/pallas_call | solution.py:50
  150.9 0.7 fusion.6
  151.6 4.9 %outer_own.3 = bf16[216,32,128]{2,1,0:T(8,128)(2,1)S(1)} custom-call(s32[3]{0:T(128)S(1)} %pad_add_fusion.facts_ref, s32[432]{0:T(512)S(1)} %bitcast.71, s32[432]{0:T(512)S(1)} %bitcast.79, bf16[216,32,128]{2,1,0:T(8,128)(2,1)S(1)} %outer_own.2.refs_0_, bf16[216,32,128]{2,1,0:T(8,128)(2,1)S(1)} %collective-permute-done.22.refs_1_, ...), custom_call_target="tpu_custom_call" | custom-call | flops 23000000512 | bytes 9244044 | tf_op jit(solution)/shard_map/outer_own/pallas_call | solution.py:50
  156.5 2.2 %reshape.154 = bf16[1,1,216,4096]{3,2,1,0:T(8,128)(2,1)} reshape(bf16[216,32,128]{2,1,0:T(8,128)(2,1)S(1)} %outer_own.3) | data formatting | bytes 3538944 | tf_op jit(solution)/shard_map/reshape | solution.py:498
  158.7 1.8 %collective-permute-done.21 = bf16[32,3072]{1,0:T(8,128)(2,1)} collective-permute-done((bf16[32,3072]{1,0:T(8,128)(2,1)}, bf16[32,3072]{1,0:T(8,128)(2,1)}, u32[]{:S(2)}, u32[]{:S(2)}) %collective-permute-start.21) | collective-permute-done | bytes 196640 | tf_op jit(solution)/shard_map/ppermute | solution.py:468
  160.5 1.0 fusion.5
  161.5 0.8 pad_maximum_fusion
  (60 shorter events, 0.5 us)
Async XLA Ops:
  2.5 6.9 %copy-start.6 = (s32[1,1,432]{2,1,0:T(1,128)S(1)}, s32[1,1,432]{2,1,0:T(1,128)}, u32[]{:S(2)}) copy-start(s32[1,1,432]{2,1,0:T(1,128)} %param.8) | copy-start | bytes 5188
  2.5 6.9 %copy-start.7 = (s32[1,1,432]{2,1,0:T(1,128)S(1)}, s32[1,1,432]{2,1,0:T(1,128)}, u32[]{:S(2)}) copy-start(s32[1,1,432]{2,1,0:T(1,128)} %param.9) | copy-start | bytes 5188
  2.5 6.9 %collective-permute-start = (bf16[216,32,128]{2,1,0:T(8,128)(2,1)S(1)}, bf16[216,32,128]{2,1,0:T(8,128)(2,1)S(1)}, u32[]{:S(2)}, u32[]{:S(2)}) collective-permute-start(bf16[216,32,128]{2,1,0:T(8,128)(2,1)S(1)} %bitcast.54), channel_id=1, source_target_pairs={{0,16},{16,0},{1,17},{17,1},{2,18},{18,2},{3,19},{19,3},{4,20},{20... | collective-permute-start | bytes 5308424 | tf_op jit(solution)/shard_map/ppermute | solution.py:413
  3.8 1.4 copy-start
  9.3 4.3 %copy-start.2 = (bf16[48,64,128]{2,1,0:T(8,128)(2,1)}, bf16[48,64,128]{2,1,0:T(8,128)(2,1)S(1)}, u32[]{:S(2)}) copy-start(bf16[48,64,128]{2,1,0:T(8,128)(2,1)S(1)} %get-tuple-element.79.table_ref.refs_0_.refs_2_) | copy-start | bytes 2359300
  9.3 8.9 %copy-start.4 = (bf16[48,64,128]{2,1,0:T(8,128)(2,1)}, bf16[48,64,128]{2,1,0:T(8,128)(2,1)S(1)}, u32[]{:S(2)}) copy-start(bf16[48,64,128]{2,1,0:T(8,128)(2,1)S(1)} %get-tuple-element.77.table_ref.refs_0_.refs_1_) | copy-start | bytes 2359300
  13.7 21.5 %collective-permute-start.1 = (bf16[2,24,64,128]{3,2,1,0:T(8,128)(2,1)S(1)}, bf16[2,24,64,128]{3,2,1,0:T(8,128)(2,1)S(1)}, u32[]{:S(2)}, u32[]{:S(2)}) collective-permute-start(bf16[2,24,64,128]{3,2,1,0:T(8,128)(2,1)S(1)} %get-tuple-element.46), channel_id=1, source_target_pairs={{0,1},{1,0},{2,3},{3,2},{4,5},{5,4},{6,7},{7,6},{8,9},{9,8},{10,11... | collective-permute-start | bytes 2359304 | tf_op jit(solution)/shard_map/ppermute | solution.py:410
  16.8 20.4 %collective-permute-start.3 = (bf16[2,24,64,128]{3,2,1,0:T(8,128)(2,1)S(1)}, bf16[2,24,64,128]{3,2,1,0:T(8,128)(2,1)S(1)}, u32[]{:S(2)}, u32[]{:S(2)}) collective-permute-start(bf16[2,24,64,128]{3,2,1,0:T(8,128)(2,1)S(1)} %get-tuple-element.54), channel_id=1, source_target_pairs={{0,2},{1,3},{2,0},{3,1},{4,6},{5,7},{6,4},{7,5},{8,10},{9,11},{10,... | collective-permute-start | bytes 2359304 | tf_op jit(solution)/shard_map/ppermute | solution.py:410
  18.3 5.6 %copy-start.1 = (bf16[256,3072]{1,0:T(8,128)(2,1)S(1)}, bf16[256,3072]{1,0:T(8,128)(2,1)}, u32[]{:S(2)}) copy-start(bf16[256,3072]{1,0:T(8,128)(2,1)} %values_ref.3) | copy-start | bytes 4718596
  22.7 31.3 %collective-permute-start.7 = (bf16[2,24,64,128]{3,2,1,0:T(8,128)(2,1)S(1)}, bf16[2,24,64,128]{3,2,1,0:T(8,128)(2,1)S(1)}, u32[]{:S(2)}, u32[]{:S(2)}) collective-permute-start(bf16[2,24,64,128]{3,2,1,0:T(8,128)(2,1)S(1)} %get-tuple-element.62), channel_id=1, source_target_pairs={{0,2},{1,3},{2,0},{3,1},{4,6},{5,7},{6,4},{7,5},{8,10},{9,11},{10,... | collective-permute-start | bytes 2359304 | tf_op jit(solution)/shard_map/ppermute | solution.py:410
  22.8 31.4 %collective-permute-start.5 = (bf16[2,24,64,128]{3,2,1,0:T(8,128)(2,1)S(1)}, bf16[2,24,64,128]{3,2,1,0:T(8,128)(2,1)S(1)}, u32[]{:S(2)}, u32[]{:S(2)}) collective-permute-start(bf16[2,24,64,128]{3,2,1,0:T(8,128)(2,1)S(1)} %get-tuple-element.59), channel_id=1, source_target_pairs={{0,1},{1,0},{2,3},{3,2},{4,5},{5,4},{6,7},{7,6},{8,9},{9,8},{10,11... | collective-permute-start | bytes 2359304 | tf_op jit(solution)/shard_map/ppermute | solution.py:410
  33.8 20.2 %copy-start.8 = (bf16[216,32,128]{2,1,0:T(8,128)(2,1)}, bf16[216,32,128]{2,1,0:T(8,128)(2,1)S(1)}, u32[]{:S(2)}) copy-start(bf16[216,32,128]{2,1,0:T(8,128)(2,1)S(1)} %get-tuple-element.51.own_ref) | copy-start | bytes 5308420
  33.8 20.2 %copy-start.11 = (bf16[216,32,128]{2,1,0:T(8,128)(2,1)}, bf16[216,32,128]{2,1,0:T(8,128)(2,1)S(1)}, u32[]{:S(2)}) copy-start(bf16[216,32,128]{2,1,0:T(8,128)(2,1)S(1)} %get-tuple-element.66.other_ref) | copy-start | bytes 5308420
  35.2 27.2 %collective-permute-start.2 = (bf16[24,64,128]{2,1,0:T(8,128)(2,1)S(1)}, bf16[24,64,128]{2,1,0:T(8,128)(2,1)S(1)}, u32[]{:S(2)}, u32[]{:S(2)}) collective-permute-start(bf16[24,64,128]{2,1,0:T(8,128)(2,1)S(1)} %fusion.3), channel_id=1, source_target_pairs={{0,2},{1,3},{2,0},{3,1},{4,6},{5,7},{6,4},{7,5},{8,10},{9,11},{10,... | collective-permute-start | bytes 1179656 | tf_op jit(solution)/shard_map/ppermute | solution.py:410
  37.2 25.2 %collective-permute-start.4 = (bf16[24,64,128]{2,1,0:T(8,128)(2,1)S(1)}, bf16[24,64,128]{2,1,0:T(8,128)(2,1)S(1)}, u32[]{:S(2)}, u32[]{:S(2)}) collective-permute-start(bf16[24,64,128]{2,1,0:T(8,128)(2,1)S(1)} %fusion.2), channel_id=1, source_target_pairs={{0,1},{1,0},{2,3},{3,2},{4,5},{5,4},{6,7},{7,6},{8,9},{9,8},{10,11... | collective-permute-start | bytes 1179656 | tf_op jit(solution)/shard_map/ppermute | solution.py:410
  54.1 14.6 %collective-permute-start.8 = (bf16[24,64,128]{2,1,0:T(8,128)(2,1)S(1)}, bf16[24,64,128]{2,1,0:T(8,128)(2,1)S(1)}, u32[]{:S(2)}, u32[]{:S(2)}) collective-permute-start(bf16[24,64,128]{2,1,0:T(8,128)(2,1)S(1)} %fusion), channel_id=1, source_target_pairs={{0,1},{1,0},{2,3},{3,2},{4,5},{5,4},{6,7},{7,6},{8,9},{9,8},{10,11... | collective-permute-start | bytes 1179656 | tf_op jit(solution)/shard_map/ppermute | solution.py:410
  54.2 15.9 %collective-permute-start.6 = (bf16[24,64,128]{2,1,0:T(8,128)(2,1)S(1)}, bf16[24,64,128]{2,1,0:T(8,128)(2,1)S(1)}, u32[]{:S(2)}, u32[]{:S(2)}) collective-permute-start(bf16[24,64,128]{2,1,0:T(8,128)(2,1)S(1)} %fusion.1), channel_id=1, source_target_pairs={{0,2},{1,3},{2,0},{3,1},{4,6},{5,7},{6,4},{7,5},{8,10},{9,11},{10,... | collective-permute-start | bytes 1179656 | tf_op jit(solution)/shard_map/ppermute | solution.py:410
  72.7 4.5 %copy-start.16 = (bf16[48,64,128]{2,1,0:T(8,128)(2,1)}, bf16[48,64,128]{2,1,0:T(8,128)(2,1)S(1)}, u32[]{:S(2)}) copy-start(bf16[48,64,128]{2,1,0:T(8,128)(2,1)S(1)} %get-tuple-element.67.refs_0_.refs_1_.refs_2_) | copy-start | bytes 2359300
  72.8 18.9 %collective-permute-start.9 = (bf16[48,64,128]{2,1,0:T(8,128)(2,1)S(1)}, bf16[48,64,128]{2,1,0:T(8,128)(2,1)S(1)}, u32[]{:S(2)}, u32[]{:S(2)}) collective-permute-start(bf16[48,64,128]{2,1,0:T(8,128)(2,1)S(1)} %get-tuple-element.67.refs_0_.refs_1_.refs_2_), channel_id=1, source_target_pairs={{0,1},{1,0},{2,3},{3,2},{4,5},{5,4},{6,7},{7,6},{8,9},{9,8},{10,11... | collective-permute-start | bytes 2359304 | tf_op jit(solution)/shard_map/ppermute | solution.py:410
  73.2 20.8 %collective-permute-start.10 = (bf16[48,64,128]{2,1,0:T(8,128)(2,1)S(1)}, bf16[48,64,128]{2,1,0:T(8,128)(2,1)S(1)}, u32[]{:S(2)}, u32[]{:S(2)}) collective-permute-start(bf16[48,64,128]{2,1,0:T(8,128)(2,1)S(1)} %get-tuple-element.67.refs_0_.refs_1_.refs_2_), channel_id=1, source_target_pairs={{0,2},{1,3},{2,0},{3,1},{4,6},{5,7},{6,4},{7,5},{8,10},{9,11},{10,... | collective-permute-start | bytes 2359304 | tf_op jit(solution)/shard_map/ppermute | solution.py:410
  77.3 5.7 %copy-start.14 = (bf16[48,64,128]{2,1,0:T(8,128)(2,1)}, bf16[48,64,128]{2,1,0:T(8,128)(2,1)S(1)}, u32[]{:S(2)}) copy-start(bf16[48,64,128]{2,1,0:T(8,128)(2,1)S(1)} %get-tuple-element.71.refs_0_.refs_1_.refs_3_) | copy-start | bytes 2359300
  77.3 29.8 %copy-start.9 = (bf16[216,32,128]{2,1,0:T(8,128)(2,1)S(1)}, bf16[216,32,128]{2,1,0:T(8,128)(2,1)}, u32[]{:S(2)}) copy-start(bf16[216,32,128]{2,1,0:T(8,128)(2,1)} %copy-done.8) | copy-start | bytes 5308420
  92.5 12.4 %collective-permute-start.11 = (bf16[24,64,128]{2,1,0:T(8,128)(2,1)}, bf16[24,64,128]{2,1,0:T(8,128)(2,1)}, u32[]{:S(2)}, u32[]{:S(2)}) collective-permute-start(bf16[24,64,128]{2,1,0:T(8,128)(2,1)} %slice.28), channel_id=1, source_target_pairs={{0,2},{1,3},{2,0},{3,1},{4,6},{5,7},{6,4},{7,5},{8,10},{9,11},{10,... | collective-permute-start | bytes 1179656 | tf_op jit(solution)/shard_map/ppermute | solution.py:410
  94.7 12.4 %collective-permute-start.12 = (bf16[24,64,128]{2,1,0:T(8,128)(2,1)}, bf16[24,64,128]{2,1,0:T(8,128)(2,1)}, u32[]{:S(2)}, u32[]{:S(2)}) collective-permute-start(bf16[24,64,128]{2,1,0:T(8,128)(2,1)} %slice.36), channel_id=1, source_target_pairs={{0,1},{1,0},{2,3},{3,2},{4,5},{5,4},{6,7},{7,6},{8,9},{9,8},{10,11... | collective-permute-start | bytes 1179656 | tf_op jit(solution)/shard_map/ppermute | solution.py:410
  95.4 23.6 %collective-permute-start.15 = (bf16[48,64,128]{2,1,0:T(8,128)(2,1)}, bf16[48,64,128]{2,1,0:T(8,128)(2,1)S(1)}, u32[]{:S(2)}, u32[]{:S(2)}) collective-permute-start(bf16[48,64,128]{2,1,0:T(8,128)(2,1)} %copy-done.14), channel_id=1, source_target_pairs={{0,2},{1,3},{2,0},{3,1},{4,6},{5,7},{6,4},{7,5},{8,10},{9,11},{10,... | collective-permute-start | bytes 2359304 | tf_op jit(solution)/shard_map/ppermute | solution.py:410
  96.0 25.1 %collective-permute-start.14 = (bf16[48,64,128]{2,1,0:T(8,128)(2,1)}, bf16[48,64,128]{2,1,0:T(8,128)(2,1)S(1)}, u32[]{:S(2)}, u32[]{:S(2)}) collective-permute-start(bf16[48,64,128]{2,1,0:T(8,128)(2,1)} %copy-done.14), channel_id=1, source_target_pairs={{0,1},{1,0},{2,3},{3,2},{4,5},{5,4},{6,7},{7,6},{8,9},{9,8},{10,11... | collective-permute-start | bytes 2359304 | tf_op jit(solution)/shard_map/ppermute | solution.py:410
  107.1 1.5 copy-start.12
  108.6 1.1 copy-start.17
  114.8 8.1 %copy-start.5 = (bf16[48,64,128]{2,1,0:T(8,128)(2,1)S(1)}, bf16[48,64,128]{2,1,0:T(8,128)(2,1)}, u32[]{:S(2)}) copy-start(bf16[48,64,128]{2,1,0:T(8,128)(2,1)} %copy-done.4) | copy-start | bytes 2359300
  114.8 8.1 %copy-start.18 = (bf16[48,64,128]{2,1,0:T(8,128)(2,1)S(1)}, bf16[48,64,128]{2,1,0:T(8,128)(2,1)}, u32[]{:S(2)}) copy-start(bf16[48,64,128]{2,1,0:T(8,128)(2,1)} %copy-done.16) | copy-start | bytes 2359300
  114.8 11.2 %collective-permute-start.13 = (bf16[2,32,3072]{2,1,0:T(8,128)(2,1)S(1)}, bf16[2,32,3072]{2,1,0:T(8,128)(2,1)S(1)}, u32[]{:S(2)}, u32[]{:S(2)}) collective-permute-start(bf16[2,32,3072]{2,1,0:T(8,128)(2,1)S(1)} %dynamic-slice_bitcast_fusion.1), channel_id=1, source_target_pairs={{0,4},{4,0},{8,12},{12,8},{1,5},{5,1},{9,13},{13,9},{2,6},{6,2},{1... | collective-permute-start | bytes 1179656 | tf_op jit(solution)/shard_map/ppermute | solution.py:463
  121.1 10.3 %collective-permute-start.18 = (bf16[24,64,128]{2,1,0:T(8,128)(2,1)S(1)}, bf16[24,64,128]{2,1,0:T(8,128)(2,1)S(1)}, u32[]{:S(2)}, u32[]{:S(2)}) collective-permute-start(bf16[24,64,128]{2,1,0:T(8,128)(2,1)S(1)} %slice.38), channel_id=1, source_target_pairs={{0,1},{1,0},{2,3},{3,2},{4,5},{5,4},{6,7},{7,6},{8,9},{9,8},{10,11... | collective-permute-start | bytes 1179656 | tf_op jit(solution)/shard_map/ppermute | solution.py:410
  122.2 9.2 %copy-start.10 = (bf16[216,32,128]{2,1,0:T(8,128)(2,1)S(1)}, bf16[216,32,128]{2,1,0:T(8,128)(2,1)}, u32[]{:S(2)}) copy-start(bf16[216,32,128]{2,1,0:T(8,128)(2,1)} %copy-done.8) | copy-start | bytes 5308420
  122.2 9.2 %copy-start.13 = (bf16[216,32,128]{2,1,0:T(8,128)(2,1)S(1)}, bf16[216,32,128]{2,1,0:T(8,128)(2,1)}, u32[]{:S(2)}) copy-start(bf16[216,32,128]{2,1,0:T(8,128)(2,1)} %copy-done.11) | copy-start | bytes 5308420
  122.2 9.2 %copy-start.15 = (bf16[48,64,128]{2,1,0:T(8,128)(2,1)S(1)}, bf16[48,64,128]{2,1,0:T(8,128)(2,1)}, u32[]{:S(2)}) copy-start(bf16[48,64,128]{2,1,0:T(8,128)(2,1)} %copy-done.14) | copy-start | bytes 2359300
  122.2 9.2 %collective-permute-start.17 = (bf16[24,64,128]{2,1,0:T(8,128)(2,1)S(1)}, bf16[24,64,128]{2,1,0:T(8,128)(2,1)S(1)}, u32[]{:S(2)}, u32[]{:S(2)}) collective-permute-start(bf16[24,64,128]{2,1,0:T(8,128)(2,1)S(1)} %slice.37), channel_id=1, source_target_pairs={{0,2},{1,3},{2,0},{3,1},{4,6},{5,7},{6,4},{7,5},{8,10},{9,11},{10,... | collective-permute-start | bytes 1179656 | tf_op jit(solution)/shard_map/ppermute | solution.py:410
  126.0 19.3 %collective-permute-start.20 = (bf16[216,32,128]{2,1,0:T(8,128)(2,1)S(1)}, bf16[216,32,128]{2,1,0:T(8,128)(2,1)S(1)}, u32[]{:S(2)}, u32[]{:S(2)}) collective-permute-start(bf16[216,32,128]{2,1,0:T(8,128)(2,1)S(1)} %outer_other.2), channel_id=1, source_target_pairs={{0,16},{16,0},{1,17},{17,1},{2,18},{18,2},{3,19},{19,3},{4,20},{20... | collective-permute-start | bytes 5308424 | tf_op jit(solution)/shard_map/ppermute | solution.py:413
  126.1 13.4 %collective-permute-start.16 = (bf16[32,3072]{1,0:T(8,128)(2,1)S(1)}, bf16[32,3072]{1,0:T(8,128)(2,1)S(1)}, u32[]{:S(2)}, u32[]{:S(2)}) collective-permute-start(bf16[32,3072]{1,0:T(8,128)(2,1)S(1)} %fusion.9), channel_id=1, source_target_pairs={{0,8},{4,12},{8,0},{12,4},{1,9},{5,13},{9,1},{13,5},{2,10},{6,14},... | collective-permute-start | bytes 589832 | tf_op jit(solution)/shard_map/ppermute | solution.py:468
  131.4 9.0 %copy-start.3 = (bf16[48,64,128]{2,1,0:T(8,128)(2,1)S(1)}, bf16[48,64,128]{2,1,0:T(8,128)(2,1)}, u32[]{:S(2)}) copy-start(bf16[48,64,128]{2,1,0:T(8,128)(2,1)} %copy-done.2) | copy-start | bytes 2359300
  136.1 14.8 %collective-permute-start.19 = (bf16[2,32,3072]{2,1,0:T(8,128)(2,1)S(1)}, bf16[2,32,3072]{2,1,0:T(8,128)(2,1)S(1)}, u32[]{:S(2)}, u32[]{:S(2)}) collective-permute-start(bf16[2,32,3072]{2,1,0:T(8,128)(2,1)S(1)} %dynamic-slice_bitcast_fusion), channel_id=1, source_target_pairs={{0,4},{4,0},{8,12},{12,8},{1,5},{5,1},{9,13},{13,9},{2,6},{6,2},{1... | collective-permute-start | bytes 1179656 | tf_op jit(solution)/shard_map/ppermute | solution.py:463
  142.8 8.8 %collective-permute-start.22 = (bf16[216,32,128]{2,1,0:T(8,128)(2,1)S(1)}, bf16[216,32,128]{2,1,0:T(8,128)(2,1)S(1)}, u32[]{:S(2)}, u32[]{:S(2)}) collective-permute-start(bf16[216,32,128]{2,1,0:T(8,128)(2,1)S(1)} %outer_other.3), channel_id=1, source_target_pairs={{0,16},{16,0},{1,17},{17,1},{2,18},{18,2},{3,19},{19,3},{4,20},{20... | collective-permute-start | bytes 5308424 | tf_op jit(solution)/shard_map/ppermute | solution.py:413
  151.6 8.9 %collective-permute-start.21 = (bf16[32,3072]{1,0:T(8,128)(2,1)}, bf16[32,3072]{1,0:T(8,128)(2,1)}, u32[]{:S(2)}, u32[]{:S(2)}) collective-permute-start(bf16[32,3072]{1,0:T(8,128)(2,1)} %fusion.6), channel_id=1, source_target_pairs={{0,8},{4,12},{8,0},{12,4},{1,9},{5,13},{9,1},{13,5},{2,10},{6,14},... | collective-permute-start | bytes 589832 | tf_op jit(solution)/shard_map/ppermute | solution.py:468
  156.5 5.0 %copy-start.19 = (bf16[32,3072]{1,0:T(8,128)(2,1)S(1)}, bf16[32,3072]{1,0:T(8,128)(2,1)}, u32[]{:S(2)}) copy-start(bf16[32,3072]{1,0:T(8,128)(2,1)} %fusion.8) | copy-start | bytes 589828

commit v7 on v6

--- a/solution.py
+++ b/solution.py
@@ -486,9 +486,9 @@
     grads[1][4] = after(grads[1][4], halfway)
 
     def second_filler(sent):
-        first_sum = add_up(first_terms, sent)
-        other_second = tile_part(1, first_sum, False, [])
-        own_first = tile_part(0, other_second, True, [other_core(other_first)])
+        other_second = tile_part(1, sent, False, [])
+        first_sum = add_up(first_terms, other_second)
+        own_first = tile_part(0, first_sum, True, [other_core(other_first)])
         return own_first, other_second, first_sum
 
     second_terms, halfway, (own_first, other_second, first_sum) = to_rows(input_sums(1), second_filler)

time: 163 us -> 163 us (level); the launches traced: 162 us -> 164 us
  starting transfers between devices: 26.7 us -> 35.1 us
  waiting for transfers between devices: 61.1 us -> 55.3 us
    ppermute x16, waiting for transfers between devices: 55.9 us -> 51.5 us  [across(): lax.ppermute(values, 'col', [(place, place ^ bit) for place in range(shar...]
    ppermute x16, starting transfers between devices: 18.3 us -> 22.3 us  [across(): lax.ppermute(values, 'col', [(place, place ^ bit) for place in range(shar...]
    ppermute x2, starting transfers between devices: 5.23 us -> 8.12 us  [to_rows(): last = lax.ppermute(both, 'row', [(place, place ^ 2) for place in range(4)])]
    ppermute x2, waiting for transfers between devices: 5.23 us -> 2.48 us  [to_rows(): last = lax.ppermute(both, 'row', [(place, place ^ 2) for place in range(4)])]
  transfers between devices with their start and end apart: 23 -> 23, of which waited for: 13 -> 12; matrix products, arithmetic and copies ran while one was open for 4% -> 4% of each run, Pallas kernels for 32% -> 31%
where the time goes in v7:
time: 163 us; the launch traced here: 164 us
  Pallas kernels  58.4 us (36%)
  waiting for transfers between devices  55.3 us (34%)
  starting transfers between devices  35.1 us (22%)
  local copies, waits for them, and re-layouts  9.81 us (6%)
  other arithmetic  3.7 us (2%)
  between operations  1.74 us (1%)
    pallas_call x14, Pallas kernels, call(): pl.pallas_call(kernel, out_shape=out_shape, in_specs=in_specs, out_specs=...  58.4 us
    ppermute x16, waiting for transfers between devices, across(): lax.ppermute(values, 'col', [(place, place ^ bit) for place in range(shar...  51.5 us
    ppermute x16, starting transfers between devices, across(): lax.ppermute(values, 'col', [(place, place ^ bit) for place in range(shar...  22.3 us
    ppermute x2, starting transfers between devices, to_rows(): last = lax.ppermute(both, 'row', [(place, place ^ 2) for place in range(4)])  8.12 us
    unnamed x41, local copies, waits for them, and re-layouts  5.93 us
    ppermute x3, starting transfers between devices, other_core(): return lax.ppermute(values, 'dp', [(0, 1), (1, 0)])  3.66 us
  transfers between devices with their start and end apart: 23, of which 12 were waited for; matrix products, arithmetic and copies ran while one was open for 4% of the time, Pallas kernels for 31%

profile of v7, /device:TPU:0, one launch (start us, length us, event | category | flops | bytes accessed | tf_op | source)
XLA Modules:
  0.0 164.0 jit_solution(3211859965905551015)
XLA Ops:
  0.6 1.8 %copy.9 = bf16[27,8,32,128]{3,2,1,0:T(8,128)(2,1)S(1)} copy(bf16[27,8,32,128]{3,1,2,0:T(8,128)(2,1)} %bitcast.80) | data formatting | bytes 3538944
  2.5 0.0 copy-start.7
  2.5 0.5 collective-permute-start
  3.7 0.1 add_add_fusion
  3.8 0.0 copy-start
  3.8 1.4 copy-done
  5.2 4.1 %features_to_rows.1 = (bf16[48,64,128]{2,1,0:T(8,128)(2,1)S(1)}, bf16[48,64,128]{2,1,0:T(8,128)(2,1)S(1)}) custom-call(bf16[256,3072]{1,0:T(8,128)(2,1)S(1)} %copy-done, bf16[2,256,128]{2,1,0:T(8,128)(2,1)S(1)} %fusion.10.select_ref), custom_call_target="tpu_custom_call" | custom-call | tf_op jit(solution)/shard_map/features_to_rows/pallas_call | solution.py:50
  9.3 0.1 pad_add_fusion.facts_ref
  9.4 4.2 %forward.2 = (bf16[2,24,64,128]{3,2,1,0:T(8,128)(2,1)S(1)}, bf16[2,24,64,128]{3,2,1,0:T(8,128)(2,1)S(1)}, bf16[24,64,128]{2,1,0:T(8,128)(2,1)S(1)}, bf16[24,64,1...) custom-call(s32[3]{0:T(128)S(1)} %pad_add_fusion.facts_ref, ...), custom_call_target="tpu_custom_call" | custom-call | tf_op jit(solution)/shard_map/forward/pallas_call | solution.py:50
  13.7 1.5 collective-permute-start.1
  15.2 2.2 %collective-permute-start.3 = (bf16[2,24,64,128]{3,2,1,0:T(8,128)(2,1)S(1)}, bf16[2,24,64,128]{3,2,1,0:T(8,128)(2,1)S(1)}, u32[]{:S(2)}, u32[]{:S(2)}) collective-permute-start(bf16[2,24,64,128]{3,2,1,0:T(8,128)(2,1)S(1)} %get-tuple-element.54), channel_id=1, source_target_pairs={{0,2},{1,3},{2,0},{3,1},{4,6},{5,7},{6,4},{7,5},{8,10},{9,11},{10,... | collective-permute-start | bytes 2359304 | tf_op jit(solution)/shard_map/ppermute | solution.py:410
  17.4 4.5 %forward.3 = (bf16[2,24,64,128]{3,2,1,0:T(8,128)(2,1)S(1)}, bf16[2,24,64,128]{3,2,1,0:T(8,128)(2,1)S(1)}, bf16[24,64,128]{2,1,0:T(8,128)(2,1)S(1)}, bf16[24,64,1...) custom-call(s32[3]{0:T(128)S(1)} %pad_add_fusion.facts_ref, ...), custom_call_target="tpu_custom_call" | custom-call | tf_op jit(solution)/shard_map/forward/pallas_call | solution.py:50
  21.9 1.1 collective-permute-start.7
  23.0 4.1 %units_to_rows.1 = (bf16[48,64,128]{2,1,0:T(8,128)(2,1)S(1)}, bf16[48,64,128]{2,1,0:T(8,128)(2,1)S(1)}) custom-call(bf16[256,3072]{1,0:T(8,128)(2,1)S(1)} %copy-done.1, bf16[2,256,128]{2,1,0:T(8,128)(2,1)S(1)} %fusion.10.select_ref), custom_call_target="tpu_custom_call" | custom-call | tf_op jit(solution)/shard_map/units_to_rows/pallas_call | solution.py:50
  27.1 5.8 %transpose_tiles.1 = (bf16[216,32,128]{2,1,0:T(8,128)(2,1)S(1)}, bf16[216,32,128]{2,1,0:T(8,128)(2,1)S(1)}) custom-call(bf16[216,32,128]{2,1,0:T(8,128)(2,1)S(1)} %bitcast.57, bf16[216,32,128]{2,1,0:T(8,128)(2,1)S(1)} %collective-permute-done.other_ref), custom_call_target="tpu_custom_call" | custom-call | tf_op jit(solution)/shard_map/transpose_tiles/pallas_call | solution.py:50
  32.9 1.2 collective-permute-done.1.near_a
  34.2 3.6 %collective-permute-start.2 = (bf16[24,64,128]{2,1,0:T(8,128)(2,1)S(1)}, bf16[24,64,128]{2,1,0:T(8,128)(2,1)S(1)}, u32[]{:S(2)}, u32[]{:S(2)}) collective-permute-start(bf16[24,64,128]{2,1,0:T(8,128)(2,1)S(1)} %fusion.3), channel_id=1, source_target_pairs={{0,2},{1,3},{2,0},{3,1},{4,6},{5,7},{6,4},{7,5},{8,10},{9,11},{10,... | collective-permute-start | bytes 1179656 | tf_op jit(solution)/shard_map/ppermute | solution.py:410
  37.8 0.1 collective-permute-start.4
  38.0 14.7 %collective-permute-done.7.near_b = bf16[2,24,64,128]{3,2,1,0:T(8,128)(2,1)S(1)} collective-permute-done((bf16[2,24,64,128]{3,2,1,0:T(8,128)(2,1)S(1)}, bf16[2,24,64,128]{3,2,1,0:T(8,128)(2,1)S(1)}, u32[]{:S(2)}, u32[]{:S(2)}) %collective-permute-start.7) | collective-permute-done | bytes 786464 | tf_op jit(solution)/shard_map/ppermute | solution.py:410
  52.7 1.9 %collective-permute-start.8 = (bf16[24,64,128]{2,1,0:T(8,128)(2,1)S(1)}, bf16[24,64,128]{2,1,0:T(8,128)(2,1)S(1)}, u32[]{:S(2)}, u32[]{:S(2)}) collective-permute-start(bf16[24,64,128]{2,1,0:T(8,128)(2,1)S(1)} %fusion), channel_id=1, source_target_pairs={{0,1},{1,0},{2,3},{3,2},{4,5},{5,4},{6,7},{7,6},{8,9},{9,8},{10,11... | collective-permute-start | bytes 1179656 | tf_op jit(solution)/shard_map/ppermute | solution.py:410
  54.7 2.1 %collective-permute-start.6 = (bf16[24,64,128]{2,1,0:T(8,128)(2,1)S(1)}, bf16[24,64,128]{2,1,0:T(8,128)(2,1)S(1)}, u32[]{:S(2)}, u32[]{:S(2)}) collective-permute-start(bf16[24,64,128]{2,1,0:T(8,128)(2,1)S(1)} %fusion.1), channel_id=1, source_target_pairs={{0,2},{1,3},{2,0},{3,1},{4,6},{5,7},{6,4},{7,5},{8,10},{9,11},{10,... | collective-permute-start | bytes 1179656 | tf_op jit(solution)/shard_map/ppermute | solution.py:410
  56.8 4.3 %collective-permute-done.2.last_a = bf16[24,64,128]{2,1,0:T(8,128)(2,1)S(1)} collective-permute-done((bf16[24,64,128]{2,1,0:T(8,128)(2,1)S(1)}, bf16[24,64,128]{2,1,0:T(8,128)(2,1)S(1)}, u32[]{:S(2)}, u32[]{:S(2)}) %collective-permute-start.2) | collective-permute-done | bytes 393248 | tf_op jit(solution)/shard_map/ppermute | solution.py:410
  61.1 6.0 %collective-permute-done.8.last_b = bf16[24,64,128]{2,1,0:T(8,128)(2,1)S(1)} collective-permute-done((bf16[24,64,128]{2,1,0:T(8,128)(2,1)S(1)}, bf16[24,64,128]{2,1,0:T(8,128)(2,1)S(1)}, u32[]{:S(2)}, u32[]{:S(2)}) %collective-permute-start.8) | collective-permute-done | bytes 393248 | tf_op jit(solution)/shard_map/ppermute | solution.py:410
  67.1 2.2 %collective-permute-done.6.last_a = bf16[24,64,128]{2,1,0:T(8,128)(2,1)S(1)} collective-permute-done((bf16[24,64,128]{2,1,0:T(8,128)(2,1)S(1)}, bf16[24,64,128]{2,1,0:T(8,128)(2,1)S(1)}, u32[]{:S(2)}, u32[]{:S(2)}) %collective-permute-start.6) | collective-permute-done | bytes 393248 | tf_op jit(solution)/shard_map/ppermute | solution.py:410
  69.3 2.6 %gelu.2 = (bf16[48,64,128]{2,1,0:T(8,128)(2,1)S(1)}, bf16[48,64,128]{2,1,0:T(8,128)(2,1)S(1)}) custom-call(bf16[48,64,128]{2,1,0:T(8,128)(2,1)S(1)} %get-tuple-element.56.upstream_hbm, bf16[24,64,128]{2,1,0:T(8,128)(2,1)S(1)} %get-tuple-element.58.own_a, bf16[2,24,64,128]{3,2,1,0:T(8,128)(2,1)S(1)} %collective-permute-done.5.near_a, ...), custom_call_target="tpu_custom_call" | custom-call | tf_op jit(solution)/shard_map/gelu/pallas_call | solution.py:50
  71.9 1.7 %collective-permute-start.9 = (bf16[48,64,128]{2,1,0:T(8,128)(2,1)S(1)}, bf16[48,64,128]{2,1,0:T(8,128)(2,1)S(1)}, u32[]{:S(2)}, u32[]{:S(2)}) collective-permute-start(bf16[48,64,128]{2,1,0:T(8,128)(2,1)S(1)} %get-tuple-element.67.refs_0_.refs_1_.refs_2_), channel_id=1, source_target_pairs={{0,1},{1,0},{2,3},{3,2},{4,5},{5,4},{6,7},{7,6},{8,9},{9,8},{10,11... | collective-permute-start | bytes 2359304 | tf_op jit(solution)/shard_map/ppermute | solution.py:410
  73.7 1.7 %collective-permute-start.10 = (bf16[48,64,128]{2,1,0:T(8,128)(2,1)S(1)}, bf16[48,64,128]{2,1,0:T(8,128)(2,1)S(1)}, u32[]{:S(2)}, u32[]{:S(2)}) collective-permute-start(bf16[48,64,128]{2,1,0:T(8,128)(2,1)S(1)} %get-tuple-element.67.refs_0_.refs_1_.refs_2_), channel_id=1, source_target_pairs={{0,2},{1,3},{2,0},{3,1},{4,6},{5,7},{6,4},{7,5},{8,10},{9,11},{10,... | collective-permute-start | bytes 2359304 | tf_op jit(solution)/shard_map/ppermute | solution.py:410
  75.4 2.6 %gelu.3 = (bf16[48,64,128]{2,1,0:T(8,128)(2,1)S(1)}, bf16[48,64,128]{2,1,0:T(8,128)(2,1)S(1)}) custom-call(bf16[48,64,128]{2,1,0:T(8,128)(2,1)S(1)} %get-tuple-element.48.upstream_hbm, bf16[24,64,128]{2,1,0:T(8,128)(2,1)S(1)} %get-tuple-element.43.own_a, bf16[2,24,64,128]{3,2,1,0:T(8,128)(2,1)S(1)} %collective-permute-done.1.near_a, ...), custom_call_target="tpu_custom_call" | custom-call | tf_op jit(solution)/shard_map/gelu/pallas_call | solution.py:50
  78.0 5.7 %rows_to_units.1 = bf16[256,3072]{1,0:T(8,128)(2,1)} custom-call(bf16[2,256,128]{2,1,0:T(8,128)(2,1)S(1)} %fusion.10.select_ref, bf16[48,64,128]{2,1,0:T(8,128)(2,1)S(1)} %get-tuple-element.64.refs_0_, bf16[48,64,128]{2,1,0:T(8,128)(2,1)S(1)} %get-tuple-element.65.refs_1_), custom_call_target="tpu_custom_call" | custom-call | tf_op jit(solution)/shard_map/rows_to_units/pallas_call | solution.py:50
  83.7 7.7 %collective-permute-done.9.refs_1_.refs_2_.refs_3_ = bf16[48,64,128]{2,1,0:T(8,128)(2,1)S(1)} collective-permute-done((bf16[48,64,128]{2,1,0:T(8,128)(2,1)S(1)}, bf16[48,64,128]{2,1,0:T(8,128)(2,1)S(1)}, u32[]{:S(2)}, u32[]{:S(2)}) %collective-permute-start.9) | collective-permute-done | bytes 786464 | tf_op jit(solution)/shard_map/ppermute | solution.py:410
  91.4 0.8 slice.28
  92.1 1.5 collective-permute-start.11
  93.7 0.8 slice.36
  94.5 1.3 collective-permute-start.12
  95.8 0.6 collective-permute-start.15
  96.4 0.6 collective-permute-start.14
  97.0 7.5 %collective-permute-done.11.refs_3_.refs_4_.refs_5_ = bf16[24,64,128]{2,1,0:T(8,128)(2,1)} collective-permute-done((bf16[24,64,128]{2,1,0:T(8,128)(2,1)}, bf16[24,64,128]{2,1,0:T(8,128)(2,1)}, u32[]{:S(2)}, u32[]{:S(2)}) %collective-permute-start.11) | collective-permute-done | bytes 393248 | tf_op jit(solution)/shard_map/ppermute | solution.py:410
  104.5 2.3 %collective-permute-done.12.refs_4_.refs_5_.refs_6_ = bf16[24,64,128]{2,1,0:T(8,128)(2,1)} collective-permute-done((bf16[24,64,128]{2,1,0:T(8,128)(2,1)}, bf16[24,64,128]{2,1,0:T(8,128)(2,1)}, u32[]{:S(2)}, u32[]{:S(2)}) %collective-permute-start.12) | collective-permute-done | bytes 393248 | tf_op jit(solution)/shard_map/ppermute | solution.py:410
  106.9 1.5 copy-done.12
  108.3 1.1 copy-done.17
  109.5 5.1 %backward.2 = bf16[128,3072]{1,0:T(8,128)(2,1)S(1)} custom-call(s32[3]{0:T(128)S(1)} %pad_add_fusion.facts_ref, s32[432]{0:T(512)S(1)} %bitcast.66, s32[432]{0:T(512)S(1)} %bitcast.74, bf16[216,32,128]{2,1,0:T(8,128)(2,1)S(1)} %copy-done.9, bf16[216,32,128]{2,1,0:T(8,128)(2,1)S(1)} %copy-done.12, bf16[48,64,128]{2,1,0:T(8,128)(2,1)S(1)} %copy-done.17, ...), custom_call_target="tpu_custom_call" | custom-call | flops 8049999872 | bytes 7474572 | tf_op jit(solution)/shard_map/backward/pallas_call | solution.py:50
  114.6 1.0 collective-permute-start.13
  115.6 3.7 %collective-permute-done.15.refs_2_.refs_3_.refs_5_ = bf16[48,64,128]{2,1,0:T(8,128)(2,1)S(1)} collective-permute-done((bf16[48,64,128]{2,1,0:T(8,128)(2,1)}, bf16[48,64,128]{2,1,0:T(8,128)(2,1)S(1)}, u32[]{:S(2)}, u32[]{:S(2)}) %collective-permute-start.15) | collective-permute-done | bytes 786464 | tf_op jit(solution)/shard_map/ppermute | solution.py:410
  119.3 1.8 %collective-permute-done.14.refs_1_.refs_2_.refs_4_ = bf16[48,64,128]{2,1,0:T(8,128)(2,1)S(1)} collective-permute-done((bf16[48,64,128]{2,1,0:T(8,128)(2,1)}, bf16[48,64,128]{2,1,0:T(8,128)(2,1)S(1)}, u32[]{:S(2)}, u32[]{:S(2)}) %collective-permute-start.14) | collective-permute-done | bytes 786464 | tf_op jit(solution)/shard_map/ppermute | solution.py:410
  121.2 1.1 collective-permute-start.18
  122.3 1.0 collective-permute-start.17
  123.3 2.7 %outer_other.2 = bf16[216,32,128]{2,1,0:T(8,128)(2,1)S(1)} custom-call(s32[3]{0:T(128)S(1)} %pad_add_fusion.facts_ref, s32[432]{0:T(512)S(1)} %bitcast.67, s32[432]{0:T(512)S(1)} %bitcast.75, bf16[48,64,128]{2,1,0:T(8,128)(2,1)S(1)} %copy-done.5, bf16[48,64,128]{2,1,0:T(8,128)(2,1)S(1)} %copy-done.18, ...), custom_call_target="tpu_custom_call" | custom-call | flops 5750000128 | bytes 5705100 | tf_op jit(solution)/shard_map/outer_other/pallas_call | solution.py:50
  126.1 0.1 collective-permute-start.20
  126.1 0.1 fusion.9
  126.2 5.5 %collective-permute-start.16 = (bf16[32,3072]{1,0:T(8,128)(2,1)S(1)}, bf16[32,3072]{1,0:T(8,128)(2,1)S(1)}, u32[]{:S(2)}, u32[]{:S(2)}) collective-permute-start(bf16[32,3072]{1,0:T(8,128)(2,1)S(1)} %fusion.9), channel_id=1, source_target_pairs={{0,8},{4,12},{8,0},{12,4},{1,9},{5,13},{9,1},{13,5},{2,10},{6,14},... | collective-permute-start | bytes 589832 | tf_op jit(solution)/shard_map/ppermute | solution.py:468
  131.8 4.6 %backward.3 = bf16[128,3072]{1,0:T(8,128)(2,1)S(1)} custom-call(s32[3]{0:T(128)S(1)} %pad_add_fusion.facts_ref, s32[432]{0:T(512)S(1)} %bitcast.68, s32[432]{0:T(512)S(1)} %bitcast.76, bf16[216,32,128]{2,1,0:T(8,128)(2,1)S(1)} %copy-done.10, bf16[216,32,128]{2,1,0:T(8,128)(2,1)S(1)} %copy-done.13, bf16[48,64,128]{2,1,0:T(8,128)(2,1)S(1)} %copy-done.15, ...), custom_call_target="tpu_custom_call" | custom-call | flops 8049999872 | bytes 7474572 | tf_op jit(solution)/shard_map/backward/pallas_call | solution.py:50
  136.4 0.1 collective-permute-start.19
  136.5 2.0 %outer_other.3 = bf16[216,32,128]{2,1,0:T(8,128)(2,1)S(1)} custom-call(s32[3]{0:T(128)S(1)} %pad_add_fusion.facts_ref, s32[432]{0:T(512)S(1)} %bitcast.69, s32[432]{0:T(512)S(1)} %bitcast.77, bf16[48,64,128]{2,1,0:T(8,128)(2,1)S(1)} %copy-done.3, bf16[48,64,128]{2,1,0:T(8,128)(2,1)S(1)} %copy-done.15, ...), custom_call_target="tpu_custom_call" | custom-call | flops 23000000512 | bytes 5705100 | tf_op jit(solution)/shard_map/outer_other/pallas_call | solution.py:50
  138.5 3.1 %collective-permute-start.22 = (bf16[216,32,128]{2,1,0:T(8,128)(2,1)S(1)}, bf16[216,32,128]{2,1,0:T(8,128)(2,1)S(1)}, u32[]{:S(2)}, u32[]{:S(2)}) collective-permute-start(bf16[216,32,128]{2,1,0:T(8,128)(2,1)S(1)} %outer_other.3), channel_id=1, source_target_pairs={{0,16},{16,0},{1,17},{17,1},{2,18},{18,2},{3,19},{19,3},{4,20},{20... | collective-permute-start | bytes 5308424 | tf_op jit(solution)/shard_map/ppermute | solution.py:413
  141.6 0.8 fusion.8
  142.4 5.6 %outer_own.2.refs_0_ = bf16[216,32,128]{2,1,0:T(8,128)(2,1)S(1)} custom-call(s32[3]{0:T(128)S(1)} %pad_add_fusion.facts_ref, s32[432]{0:T(512)S(1)} %bitcast.70, s32[432]{0:T(512)S(1)} %bitcast.78, bf16[216,32,128]{2,1,0:T(8,128)(2,1)S(1)} %collective-permute-done.20.refs_0_, bf16[48,64,128]{2,1,0:T(8,128)(2,1)S(1)} %copy-done.5, ...), custom_call_target="tpu_custom_call" | custom-call | flops 23000000512 | bytes 7474572 | tf_op jit(solution)/shard_map/outer_own/pallas_call | solution.py:50
  148.0 1.3 collective-permute-done.19
  149.3 0.7 fusion.6
  150.0 2.6 %collective-permute-start.21 = (bf16[32,3072]{1,0:T(8,128)(2,1)}, bf16[32,3072]{1,0:T(8,128)(2,1)}, u32[]{:S(2)}, u32[]{:S(2)}) collective-permute-start(bf16[32,3072]{1,0:T(8,128)(2,1)} %fusion.6), channel_id=1, source_target_pairs={{0,8},{4,12},{8,0},{12,4},{1,9},{5,13},{9,1},{13,5},{2,10},{6,14},... | collective-permute-start | bytes 589832 | tf_op jit(solution)/shard_map/ppermute | solution.py:468
  152.7 4.9 %outer_own.3 = bf16[216,32,128]{2,1,0:T(8,128)(2,1)S(1)} custom-call(s32[3]{0:T(128)S(1)} %pad_add_fusion.facts_ref, s32[432]{0:T(512)S(1)} %bitcast.71, s32[432]{0:T(512)S(1)} %bitcast.79, bf16[216,32,128]{2,1,0:T(8,128)(2,1)S(1)} %outer_own.2.refs_0_, bf16[216,32,128]{2,1,0:T(8,128)(2,1)S(1)} %collective-permute-done.22.refs_1_, ...), custom_call_target="tpu_custom_call" | custom-call | flops 23000000512 | bytes 9244044 | tf_op jit(solution)/shard_map/outer_own/pallas_call | solution.py:50
  157.6 2.2 %reshape.154 = bf16[1,1,216,4096]{3,2,1,0:T(8,128)(2,1)} reshape(bf16[216,32,128]{2,1,0:T(8,128)(2,1)S(1)} %outer_own.3) | data formatting | bytes 3538944 | tf_op jit(solution)/shard_map/reshape | solution.py:498
  159.7 2.5 %collective-permute-done.21 = bf16[32,3072]{1,0:T(8,128)(2,1)} collective-permute-done((bf16[32,3072]{1,0:T(8,128)(2,1)}, bf16[32,3072]{1,0:T(8,128)(2,1)}, u32[]{:S(2)}, u32[]{:S(2)}) %collective-permute-start.21) | collective-permute-done | bytes 196640 | tf_op jit(solution)/shard_map/ppermute | solution.py:468
  162.2 1.0 fusion.5
  163.2 0.8 pad_maximum_fusion
  (60 shorter events, 0.5 us)
Async XLA Ops:
  2.5 6.9 %copy-start.6 = (s32[1,1,432]{2,1,0:T(1,128)S(1)}, s32[1,1,432]{2,1,0:T(1,128)}, u32[]{:S(2)}) copy-start(s32[1,1,432]{2,1,0:T(1,128)} %param.8) | copy-start | bytes 5188
  2.5 6.9 %copy-start.7 = (s32[1,1,432]{2,1,0:T(1,128)S(1)}, s32[1,1,432]{2,1,0:T(1,128)}, u32[]{:S(2)}) copy-start(s32[1,1,432]{2,1,0:T(1,128)} %param.9) | copy-start | bytes 5188
  2.5 6.9 %collective-permute-start = (bf16[216,32,128]{2,1,0:T(8,128)(2,1)S(1)}, bf16[216,32,128]{2,1,0:T(8,128)(2,1)S(1)}, u32[]{:S(2)}, u32[]{:S(2)}) collective-permute-start(bf16[216,32,128]{2,1,0:T(8,128)(2,1)S(1)} %bitcast.54), channel_id=1, source_target_pairs={{0,16},{16,0},{1,17},{17,1},{2,18},{18,2},{3,19},{19,3},{4,20},{20... | collective-permute-start | bytes 5308424 | tf_op jit(solution)/shard_map/ppermute | solution.py:413
  3.8 1.4 copy-start
  9.3 4.4 %copy-start.2 = (bf16[48,64,128]{2,1,0:T(8,128)(2,1)}, bf16[48,64,128]{2,1,0:T(8,128)(2,1)S(1)}, u32[]{:S(2)}) copy-start(bf16[48,64,128]{2,1,0:T(8,128)(2,1)S(1)} %get-tuple-element.79.table_ref.refs_0_.refs_2_) | copy-start | bytes 2359300
  9.3 8.1 %copy-start.4 = (bf16[48,64,128]{2,1,0:T(8,128)(2,1)}, bf16[48,64,128]{2,1,0:T(8,128)(2,1)S(1)}, u32[]{:S(2)}) copy-start(bf16[48,64,128]{2,1,0:T(8,128)(2,1)S(1)} %get-tuple-element.77.table_ref.refs_0_.refs_1_) | copy-start | bytes 2359300
  13.7 20.4 %collective-permute-start.1 = (bf16[2,24,64,128]{3,2,1,0:T(8,128)(2,1)S(1)}, bf16[2,24,64,128]{3,2,1,0:T(8,128)(2,1)S(1)}, u32[]{:S(2)}, u32[]{:S(2)}) collective-permute-start(bf16[2,24,64,128]{3,2,1,0:T(8,128)(2,1)S(1)} %get-tuple-element.46), channel_id=1, source_target_pairs={{0,1},{1,0},{2,3},{3,2},{4,5},{5,4},{6,7},{7,6},{8,9},{9,8},{10,11... | collective-permute-start | bytes 2359304 | tf_op jit(solution)/shard_map/ppermute | solution.py:410
  15.2 22.6 %collective-permute-start.3 = (bf16[2,24,64,128]{3,2,1,0:T(8,128)(2,1)S(1)}, bf16[2,24,64,128]{3,2,1,0:T(8,128)(2,1)S(1)}, u32[]{:S(2)}, u32[]{:S(2)}) collective-permute-start(bf16[2,24,64,128]{3,2,1,0:T(8,128)(2,1)S(1)} %get-tuple-element.54), channel_id=1, source_target_pairs={{0,2},{1,3},{2,0},{3,1},{4,6},{5,7},{6,4},{7,5},{8,10},{9,11},{10,... | collective-permute-start | bytes 2359304 | tf_op jit(solution)/shard_map/ppermute | solution.py:410
  17.4 5.6 %copy-start.1 = (bf16[256,3072]{1,0:T(8,128)(2,1)S(1)}, bf16[256,3072]{1,0:T(8,128)(2,1)}, u32[]{:S(2)}) copy-start(bf16[256,3072]{1,0:T(8,128)(2,1)} %values_ref.3) | copy-start | bytes 4718596
  21.9 30.8 %collective-permute-start.7 = (bf16[2,24,64,128]{3,2,1,0:T(8,128)(2,1)S(1)}, bf16[2,24,64,128]{3,2,1,0:T(8,128)(2,1)S(1)}, u32[]{:S(2)}, u32[]{:S(2)}) collective-permute-start(bf16[2,24,64,128]{3,2,1,0:T(8,128)(2,1)S(1)} %get-tuple-element.62), channel_id=1, source_target_pairs={{0,2},{1,3},{2,0},{3,1},{4,6},{5,7},{6,4},{7,5},{8,10},{9,11},{10,... | collective-permute-start | bytes 2359304 | tf_op jit(solution)/shard_map/ppermute | solution.py:410
  23.0 31.6 %collective-permute-start.5 = (bf16[2,24,64,128]{3,2,1,0:T(8,128)(2,1)S(1)}, bf16[2,24,64,128]{3,2,1,0:T(8,128)(2,1)S(1)}, u32[]{:S(2)}, u32[]{:S(2)}) collective-permute-start(bf16[2,24,64,128]{3,2,1,0:T(8,128)(2,1)S(1)} %get-tuple-element.59), channel_id=1, source_target_pairs={{0,1},{1,0},{2,3},{3,2},{4,5},{5,4},{6,7},{7,6},{8,9},{9,8},{10,11... | collective-permute-start | bytes 2359304 | tf_op jit(solution)/shard_map/ppermute | solution.py:410
  32.9 19.8 %copy-start.8 = (bf16[216,32,128]{2,1,0:T(8,128)(2,1)}, bf16[216,32,128]{2,1,0:T(8,128)(2,1)S(1)}, u32[]{:S(2)}) copy-start(bf16[216,32,128]{2,1,0:T(8,128)(2,1)S(1)} %get-tuple-element.51.own_ref) | copy-start | bytes 5308420
  32.9 19.8 %copy-start.11 = (bf16[216,32,128]{2,1,0:T(8,128)(2,1)}, bf16[216,32,128]{2,1,0:T(8,128)(2,1)S(1)}, u32[]{:S(2)}) copy-start(bf16[216,32,128]{2,1,0:T(8,128)(2,1)S(1)} %get-tuple-element.66.other_ref) | copy-start | bytes 5308420
  34.2 26.9 %collective-permute-start.2 = (bf16[24,64,128]{2,1,0:T(8,128)(2,1)S(1)}, bf16[24,64,128]{2,1,0:T(8,128)(2,1)S(1)}, u32[]{:S(2)}, u32[]{:S(2)}) collective-permute-start(bf16[24,64,128]{2,1,0:T(8,128)(2,1)S(1)} %fusion.3), channel_id=1, source_target_pairs={{0,2},{1,3},{2,0},{3,1},{4,6},{5,7},{6,4},{7,5},{8,10},{9,11},{10,... | collective-permute-start | bytes 1179656 | tf_op jit(solution)/shard_map/ppermute | solution.py:410
  37.8 23.3 %collective-permute-start.4 = (bf16[24,64,128]{2,1,0:T(8,128)(2,1)S(1)}, bf16[24,64,128]{2,1,0:T(8,128)(2,1)S(1)}, u32[]{:S(2)}, u32[]{:S(2)}) collective-permute-start(bf16[24,64,128]{2,1,0:T(8,128)(2,1)S(1)} %fusion.2), channel_id=1, source_target_pairs={{0,1},{1,0},{2,3},{3,2},{4,5},{5,4},{6,7},{7,6},{8,9},{9,8},{10,11... | collective-permute-start | bytes 1179656 | tf_op jit(solution)/shard_map/ppermute | solution.py:410
  52.7 14.4 %collective-permute-start.8 = (bf16[24,64,128]{2,1,0:T(8,128)(2,1)S(1)}, bf16[24,64,128]{2,1,0:T(8,128)(2,1)S(1)}, u32[]{:S(2)}, u32[]{:S(2)}) collective-permute-start(bf16[24,64,128]{2,1,0:T(8,128)(2,1)S(1)} %fusion), channel_id=1, source_target_pairs={{0,1},{1,0},{2,3},{3,2},{4,5},{5,4},{6,7},{7,6},{8,9},{9,8},{10,11... | collective-permute-start | bytes 1179656 | tf_op jit(solution)/shard_map/ppermute | solution.py:410
  54.7 14.6 %collective-permute-start.6 = (bf16[24,64,128]{2,1,0:T(8,128)(2,1)S(1)}, bf16[24,64,128]{2,1,0:T(8,128)(2,1)S(1)}, u32[]{:S(2)}, u32[]{:S(2)}) collective-permute-start(bf16[24,64,128]{2,1,0:T(8,128)(2,1)S(1)} %fusion.1), channel_id=1, source_target_pairs={{0,2},{1,3},{2,0},{3,1},{4,6},{5,7},{6,4},{7,5},{8,10},{9,11},{10,... | collective-permute-start | bytes 1179656 | tf_op jit(solution)/shard_map/ppermute | solution.py:410
  71.9 6.1 %copy-start.16 = (bf16[48,64,128]{2,1,0:T(8,128)(2,1)}, bf16[48,64,128]{2,1,0:T(8,128)(2,1)S(1)}, u32[]{:S(2)}) copy-start(bf16[48,64,128]{2,1,0:T(8,128)(2,1)S(1)} %get-tuple-element.67.refs_0_.refs_1_.refs_2_) | copy-start | bytes 2359300
  71.9 19.4 %collective-permute-start.9 = (bf16[48,64,128]{2,1,0:T(8,128)(2,1)S(1)}, bf16[48,64,128]{2,1,0:T(8,128)(2,1)S(1)}, u32[]{:S(2)}, u32[]{:S(2)}) collective-permute-start(bf16[48,64,128]{2,1,0:T(8,128)(2,1)S(1)} %get-tuple-element.67.refs_0_.refs_1_.refs_2_), channel_id=1, source_target_pairs={{0,1},{1,0},{2,3},{3,2},{4,5},{5,4},{6,7},{7,6},{8,9},{9,8},{10,11... | collective-permute-start | bytes 2359304 | tf_op jit(solution)/shard_map/ppermute | solution.py:410
  73.7 20.0 %collective-permute-start.10 = (bf16[48,64,128]{2,1,0:T(8,128)(2,1)S(1)}, bf16[48,64,128]{2,1,0:T(8,128)(2,1)S(1)}, u32[]{:S(2)}, u32[]{:S(2)}) collective-permute-start(bf16[48,64,128]{2,1,0:T(8,128)(2,1)S(1)} %get-tuple-element.67.refs_0_.refs_1_.refs_2_), channel_id=1, source_target_pairs={{0,2},{1,3},{2,0},{3,1},{4,6},{5,7},{6,4},{7,5},{8,10},{9,11},{10,... | collective-permute-start | bytes 2359304 | tf_op jit(solution)/shard_map/ppermute | solution.py:410
  78.0 5.7 %copy-start.14 = (bf16[48,64,128]{2,1,0:T(8,128)(2,1)}, bf16[48,64,128]{2,1,0:T(8,128)(2,1)S(1)}, u32[]{:S(2)}) copy-start(bf16[48,64,128]{2,1,0:T(8,128)(2,1)S(1)} %get-tuple-element.71.refs_0_.refs_1_.refs_3_) | copy-start | bytes 2359300
  78.0 28.8 %copy-start.9 = (bf16[216,32,128]{2,1,0:T(8,128)(2,1)S(1)}, bf16[216,32,128]{2,1,0:T(8,128)(2,1)}, u32[]{:S(2)}) copy-start(bf16[216,32,128]{2,1,0:T(8,128)(2,1)} %copy-done.8) | copy-start | bytes 5308420
  92.1 12.4 %collective-permute-start.11 = (bf16[24,64,128]{2,1,0:T(8,128)(2,1)}, bf16[24,64,128]{2,1,0:T(8,128)(2,1)}, u32[]{:S(2)}, u32[]{:S(2)}) collective-permute-start(bf16[24,64,128]{2,1,0:T(8,128)(2,1)} %slice.28), channel_id=1, source_target_pairs={{0,2},{1,3},{2,0},{3,1},{4,6},{5,7},{6,4},{7,5},{8,10},{9,11},{10,... | collective-permute-start | bytes 1179656 | tf_op jit(solution)/shard_map/ppermute | solution.py:410
  94.5 12.4 %collective-permute-start.12 = (bf16[24,64,128]{2,1,0:T(8,128)(2,1)}, bf16[24,64,128]{2,1,0:T(8,128)(2,1)}, u32[]{:S(2)}, u32[]{:S(2)}) collective-permute-start(bf16[24,64,128]{2,1,0:T(8,128)(2,1)} %slice.36), channel_id=1, source_target_pairs={{0,1},{1,0},{2,3},{3,2},{4,5},{5,4},{6,7},{7,6},{8,9},{9,8},{10,11... | collective-permute-start | bytes 1179656 | tf_op jit(solution)/shard_map/ppermute | solution.py:410
  95.8 23.5 %collective-permute-start.15 = (bf16[48,64,128]{2,1,0:T(8,128)(2,1)}, bf16[48,64,128]{2,1,0:T(8,128)(2,1)S(1)}, u32[]{:S(2)}, u32[]{:S(2)}) collective-permute-start(bf16[48,64,128]{2,1,0:T(8,128)(2,1)} %copy-done.14), channel_id=1, source_target_pairs={{0,2},{1,3},{2,0},{3,1},{4,6},{5,7},{6,4},{7,5},{8,10},{9,11},{10,... | collective-permute-start | bytes 2359304 | tf_op jit(solution)/shard_map/ppermute | solution.py:410
  96.4 24.7 %collective-permute-start.14 = (bf16[48,64,128]{2,1,0:T(8,128)(2,1)}, bf16[48,64,128]{2,1,0:T(8,128)(2,1)S(1)}, u32[]{:S(2)}, u32[]{:S(2)}) collective-permute-start(bf16[48,64,128]{2,1,0:T(8,128)(2,1)} %copy-done.14), channel_id=1, source_target_pairs={{0,1},{1,0},{2,3},{3,2},{4,5},{5,4},{6,7},{7,6},{8,9},{9,8},{10,11... | collective-permute-start | bytes 2359304 | tf_op jit(solution)/shard_map/ppermute | solution.py:410
  106.8 1.5 copy-start.12
  108.3 1.1 copy-start.17
  114.5 8.8 %copy-start.5 = (bf16[48,64,128]{2,1,0:T(8,128)(2,1)S(1)}, bf16[48,64,128]{2,1,0:T(8,128)(2,1)}, u32[]{:S(2)}) copy-start(bf16[48,64,128]{2,1,0:T(8,128)(2,1)} %copy-done.4) | copy-start | bytes 2359300
  114.5 8.8 %copy-start.18 = (bf16[48,64,128]{2,1,0:T(8,128)(2,1)S(1)}, bf16[48,64,128]{2,1,0:T(8,128)(2,1)}, u32[]{:S(2)}) copy-start(bf16[48,64,128]{2,1,0:T(8,128)(2,1)} %copy-done.16) | copy-start | bytes 2359300
  114.6 11.6 %collective-permute-start.13 = (bf16[2,32,3072]{2,1,0:T(8,128)(2,1)S(1)}, bf16[2,32,3072]{2,1,0:T(8,128)(2,1)S(1)}, u32[]{:S(2)}, u32[]{:S(2)}) collective-permute-start(bf16[2,32,3072]{2,1,0:T(8,128)(2,1)S(1)} %dynamic-slice_bitcast_fusion.1), channel_id=1, source_target_pairs={{0,4},{4,0},{8,12},{12,8},{1,5},{5,1},{9,13},{13,9},{2,6},{6,2},{1... | collective-permute-start | bytes 1179656 | tf_op jit(solution)/shard_map/ppermute | solution.py:463
  121.2 10.6 %collective-permute-start.18 = (bf16[24,64,128]{2,1,0:T(8,128)(2,1)S(1)}, bf16[24,64,128]{2,1,0:T(8,128)(2,1)S(1)}, u32[]{:S(2)}, u32[]{:S(2)}) collective-permute-start(bf16[24,64,128]{2,1,0:T(8,128)(2,1)S(1)} %slice.38), channel_id=1, source_target_pairs={{0,1},{1,0},{2,3},{3,2},{4,5},{5,4},{6,7},{7,6},{8,9},{9,8},{10,11... | collective-permute-start | bytes 1179656 | tf_op jit(solution)/shard_map/ppermute | solution.py:410
  122.3 9.5 %copy-start.10 = (bf16[216,32,128]{2,1,0:T(8,128)(2,1)S(1)}, bf16[216,32,128]{2,1,0:T(8,128)(2,1)}, u32[]{:S(2)}) copy-start(bf16[216,32,128]{2,1,0:T(8,128)(2,1)} %copy-done.8) | copy-start | bytes 5308420
  122.3 9.5 %copy-start.13 = (bf16[216,32,128]{2,1,0:T(8,128)(2,1)S(1)}, bf16[216,32,128]{2,1,0:T(8,128)(2,1)}, u32[]{:S(2)}) copy-start(bf16[216,32,128]{2,1,0:T(8,128)(2,1)} %copy-done.11) | copy-start | bytes 5308420
  122.3 9.5 %copy-start.15 = (bf16[48,64,128]{2,1,0:T(8,128)(2,1)S(1)}, bf16[48,64,128]{2,1,0:T(8,128)(2,1)}, u32[]{:S(2)}) copy-start(bf16[48,64,128]{2,1,0:T(8,128)(2,1)} %copy-done.14) | copy-start | bytes 2359300
  122.3 9.4 %collective-permute-start.17 = (bf16[24,64,128]{2,1,0:T(8,128)(2,1)S(1)}, bf16[24,64,128]{2,1,0:T(8,128)(2,1)S(1)}, u32[]{:S(2)}, u32[]{:S(2)}) collective-permute-start(bf16[24,64,128]{2,1,0:T(8,128)(2,1)S(1)} %slice.37), channel_id=1, source_target_pairs={{0,2},{1,3},{2,0},{3,1},{4,6},{5,7},{6,4},{7,5},{8,10},{9,11},{10,... | collective-permute-start | bytes 1179656 | tf_op jit(solution)/shard_map/ppermute | solution.py:410
  126.1 16.3 %collective-permute-start.20 = (bf16[216,32,128]{2,1,0:T(8,128)(2,1)S(1)}, bf16[216,32,128]{2,1,0:T(8,128)(2,1)S(1)}, u32[]{:S(2)}, u32[]{:S(2)}) collective-permute-start(bf16[216,32,128]{2,1,0:T(8,128)(2,1)S(1)} %outer_other.2), channel_id=1, source_target_pairs={{0,16},{16,0},{1,17},{17,1},{2,18},{18,2},{3,19},{19,3},{4,20},{20... | collective-permute-start | bytes 5308424 | tf_op jit(solution)/shard_map/ppermute | solution.py:413
  126.2 15.4 %collective-permute-start.16 = (bf16[32,3072]{1,0:T(8,128)(2,1)S(1)}, bf16[32,3072]{1,0:T(8,128)(2,1)S(1)}, u32[]{:S(2)}, u32[]{:S(2)}) collective-permute-start(bf16[32,3072]{1,0:T(8,128)(2,1)S(1)} %fusion.9), channel_id=1, source_target_pairs={{0,8},{4,12},{8,0},{12,4},{1,9},{5,13},{9,1},{13,5},{2,10},{6,14},... | collective-permute-start | bytes 589832 | tf_op jit(solution)/shard_map/ppermute | solution.py:468
  131.7 4.8 %copy-start.3 = (bf16[48,64,128]{2,1,0:T(8,128)(2,1)S(1)}, bf16[48,64,128]{2,1,0:T(8,128)(2,1)}, u32[]{:S(2)}) copy-start(bf16[48,64,128]{2,1,0:T(8,128)(2,1)} %copy-done.2) | copy-start | bytes 2359300
  136.4 12.9 %collective-permute-start.19 = (bf16[2,32,3072]{2,1,0:T(8,128)(2,1)S(1)}, bf16[2,32,3072]{2,1,0:T(8,128)(2,1)S(1)}, u32[]{:S(2)}, u32[]{:S(2)}) collective-permute-start(bf16[2,32,3072]{2,1,0:T(8,128)(2,1)S(1)} %dynamic-slice_bitcast_fusion), channel_id=1, source_target_pairs={{0,4},{4,0},{8,12},{12,8},{1,5},{5,1},{9,13},{13,9},{2,6},{6,2},{1... | collective-permute-start | bytes 1179656 | tf_op jit(solution)/shard_map/ppermute | solution.py:463
  138.5 14.1 %collective-permute-start.22 = (bf16[216,32,128]{2,1,0:T(8,128)(2,1)S(1)}, bf16[216,32,128]{2,1,0:T(8,128)(2,1)S(1)}, u32[]{:S(2)}, u32[]{:S(2)}) collective-permute-start(bf16[216,32,128]{2,1,0:T(8,128)(2,1)S(1)} %outer_other.3), channel_id=1, source_target_pairs={{0,16},{16,0},{1,17},{17,1},{2,18},{18,2},{3,19},{19,3},{4,20},{20... | collective-permute-start | bytes 5308424 | tf_op jit(solution)/shard_map/ppermute | solution.py:413
  150.0 12.2 %collective-permute-start.21 = (bf16[32,3072]{1,0:T(8,128)(2,1)}, bf16[32,3072]{1,0:T(8,128)(2,1)}, u32[]{:S(2)}, u32[]{:S(2)}) collective-permute-start(bf16[32,3072]{1,0:T(8,128)(2,1)} %fusion.6), channel_id=1, source_target_pairs={{0,8},{4,12},{8,0},{12,4},{1,9},{5,13},{9,1},{13,5},{2,10},{6,14},... | collective-permute-start | bytes 589832 | tf_op jit(solution)/shard_map/ppermute | solution.py:468
  157.6 5.6 %copy-start.19 = (bf16[32,3072]{1,0:T(8,128)(2,1)S(1)}, bf16[32,3072]{1,0:T(8,128)(2,1)}, u32[]{:S(2)}) copy-start(bf16[32,3072]{1,0:T(8,128)(2,1)} %fusion.8) | copy-start | bytes 589828

commit v8 on v7

--- a/solution.py
+++ b/solution.py
@@ -150,8 +150,7 @@
 def load_pieces(facts_ref, piece_refs, table, sem, share_blocks):
     half_blocks = share_blocks // 2
     me = facts_ref[1]
-    places = ((0, 0, share_blocks), (1, 0, share_blocks), (2, 0, share_blocks))
-    places += ((3, 0, half_blocks), (3, half_blocks, half_blocks))
+    places = [(share, half * half_blocks, half_blocks) for share in range(4) for half in range(2)]
     copies = []
     for number, (piece_ref, (share, start, length)) in enumerate(zip(piece_refs, places)):
         first = (me ^ share) * share_blocks + start
@@ -331,7 +330,7 @@
     )
 
 
-def gelu_kernel(upstream_hbm, own_a, near_a, last_a, own_b, near_b, last_b, grad_out, act_out, upstream_ref, held, sem):
+def gelu_kernel(upstream_hbm, own_a, near_a, last_a, own_b, near_b, last_b, grad_a, grad_b, act_out, upstream_ref, held, sem):
     half_blocks = own_a.shape[0]
     copies = [pltpu.make_async_copy(upstream_hbm, upstream_ref, sem.at[6])]
     for number, source in enumerate((own_a, near_a.at[1], last_a, own_b, near_b.at[1], last_b)):
@@ -340,9 +339,9 @@
         copy.start()
     for copy in copies:
         copy.wait()
-    for half in range(2):
-
-        def one(block, half=half):
+    for half, grad_out in enumerate((grad_a, grad_b)):
+
+        def one(block, half=half, grad_out=grad_out):
             pre = held[3 * half, block].astype(jnp.float32) + held[3 * half + 1, block].astype(jnp.float32)
             pre = pre + held[3 * half + 2, block].astype(jnp.float32)
             square = pre * pre
@@ -351,19 +350,19 @@
             place = half * half_blocks + block
             act_out[place] = (front * pre).astype(act_out.dtype)
             slope = front + 0.5 * pre * (1.0 - inner * inner) * COEFF * (1.0 + 3.0 * CUBIC * square)
-            grad_out[place] = (upstream_ref[place].astype(jnp.float32) * slope).astype(grad_out.dtype)
+            grad_out[block] = (upstream_ref[place].astype(jnp.float32) * slope).astype(grad_out.dtype)
 
         plain_loop(half_blocks, one)
 
 
 def gelu(upstream, parts):
-    shape = jax.ShapeDtypeStruct(upstream.shape, jnp.bfloat16)
+    half = jax.ShapeDtypeStruct(parts[0].shape, jnp.bfloat16)
     return call(
         gelu_kernel,
         "gelu",
-        [shape] * 2,
+        [half, half, jax.ShapeDtypeStruct(upstream.shape, jnp.bfloat16)],
         [HBM] * 7,
-        [VMEM] * 2,
+        [VMEM] * 3,
         (upstream, *parts),
         8,
         0,
@@ -434,20 +433,21 @@
 
     grads, acts = [], []
     for chunk in range(CHUNKS):
-        grad, act = gelu(upstream[chunk], terms[chunk])
+        grad_a, grad_b, act = gelu(upstream[chunk], terms[chunk])
         acts.append(act)
-        sent_x = sent_y = grad
+        x_a, y_b, x_b, y_a = grad_a, grad_b, grad_b, grad_a
         if chunk:
-            sent_x, sent_y = after(grad, grads[0][1]), after(grad, grads[0][2])
-        grads.append([grad, across(sent_x, 1), across(sent_y, 2)])
+            x_a, x_b = after(grad_a, grads[0][3]), after(grad_b, grads[0][3])
+            y_a, y_b = after(grad_a, grads[0][4]), after(grad_b, grads[0][4])
+        x_a, y_b = across(x_a, 1), across(y_b, 2)
+        x_b, y_a = across(x_b, 1), across(y_a, 2)
+        grads.append([grad_a, grad_b, x_a, x_b, y_a, y_b])
 
     activation = rows_to_units(select, acts)
-    grads[0][1] = after(grads[0][1], activation)
     for chunk in range(CHUNKS):
-        grad, grad_x, grad_y = grads[chunk]
-        far_a = across(grad_x[: share_blocks // 2], 2)
-        far_b = across(grad_y[share_blocks // 2 :], 1)
-        grads[chunk] += [far_a, far_b]
+        x_a, y_b = grads[chunk][2], grads[chunk][5]
+        grads[chunk] += [across(x_a, 2), across(y_b, 1)]
+    grads[0][7] = after(grads[0][7], activation)
 
     me_row = lax.axis_index("row")
 
@@ -480,10 +480,10 @@
         return outer(facts, rows, cols, table, grads[chunk], share_blocks, half_slots, mine, added, microseconds)
 
     def first_filler(sent):
-        return tile_part(0, (sent, grads[1][1], grads[1][2]), False, [], 5)
+        return tile_part(0, (sent, grads[1][2:6]), False, [], 5)
 
     first_terms, halfway, other_first = to_rows(input_sums(0), first_filler)
-    grads[1][4] = after(grads[1][4], halfway)
+    grads[1][7] = after(grads[1][7], halfway)
 
     def second_filler(sent):
         other_second = tile_part(1, sent, False, [])

time: 163 us -> 163 us (level)
  the two profiles are of different devices: /device:TPU:0 before, /device:TPU:5 now
where the time goes in v8:
time: 163 us; the launch traced here: 160 us
  Pallas kernels  71.4 us (44%)
  waiting for transfers between devices  48.9 us (30%)
  starting transfers between devices  21.3 us (13%)
  local copies, waits for them, and re-layouts  13.4 us (8%)
  other arithmetic  3.69 us (2%)
  between operations  1.74 us (1%)
    pallas_call x14, Pallas kernels, call(): pl.pallas_call(kernel, out_shape=out_shape, in_specs=in_specs, out_specs=...  71.4 us
    ppermute x20, waiting for transfers between devices, across(): lax.ppermute(values, 'col', [(place, place ^ bit) for place in range(shar...  44.9 us
    ppermute x20, starting transfers between devices, across(): lax.ppermute(values, 'col', [(place, place ^ bit) for place in range(shar...  13.9 us
    unnamed x59, local copies, waits for them, and re-layouts  11.2 us
    ppermute x3, starting transfers between devices, other_core(): return lax.ppermute(values, 'dp', [(0, 1), (1, 0)])  4.85 us
    ppermute x2, waiting for transfers between devices, to_rows(): last = lax.ppermute(both, 'row', [(place, place ^ 2) for place in range(4)])  3.95 us
  transfers between devices with their start and end apart: 27, of which 7 were waited for; matrix products, arithmetic and copies ran while one was open for 3% of the time, Pallas kernels for 39%

profile of v8, /device:TPU:5, one launch (start us, length us, event | category | flops | bytes accessed | tf_op | source)
XLA Modules:
  0.0 160.4 jit_solution(5095581407008844254)
XLA Ops:
  0.6 1.8 %copy.9 = bf16[27,8,32,128]{3,2,1,0:T(8,128)(2,1)S(1)} copy(bf16[27,8,32,128]{3,1,2,0:T(8,128)(2,1)} %bitcast.80) | data formatting | bytes 3538944
  2.5 0.0 copy-start.22
  2.5 0.0 copy-start.23
  2.5 0.7 collective-permute-start
  3.9 0.1 add_add_fusion
  4.0 1.4 copy-done.6
  5.4 4.1 %features_to_rows.1 = (bf16[48,64,128]{2,1,0:T(8,128)(2,1)S(1)}, bf16[48,64,128]{2,1,0:T(8,128)(2,1)S(1)}) custom-call(bf16[256,3072]{1,0:T(8,128)(2,1)S(1)} %copy-done.6, bf16[2,256,128]{2,1,0:T(8,128)(2,1)S(1)} %fusion.10.select_ref), custom_call_target="tpu_custom_call" | custom-call | tf_op jit(solution)/shard_map/features_to_rows/pallas_call | solution.py:50
  9.6 0.1 pad_add_fusion.facts_ref
  9.7 5.3 %forward.2 = (bf16[2,24,64,128]{3,2,1,0:T(8,128)(2,1)S(1)}, bf16[2,24,64,128]{3,2,1,0:T(8,128)(2,1)S(1)}, bf16[24,64,128]{2,1,0:T(8,128)(2,1)S(1)}, bf16[24,64,1...) custom-call(s32[3]{0:T(128)S(1)} %pad_add_fusion.facts_ref, ...), custom_call_target="tpu_custom_call" | custom-call | tf_op jit(solution)/shard_map/forward/pallas_call | solution.py:50
  15.0 0.8 copy-done.14
  15.8 5.6 %forward.3 = (bf16[2,24,64,128]{3,2,1,0:T(8,128)(2,1)S(1)}, bf16[2,24,64,128]{3,2,1,0:T(8,128)(2,1)S(1)}, bf16[24,64,128]{2,1,0:T(8,128)(2,1)S(1)}, bf16[24,64,1...) custom-call(s32[3]{0:T(128)S(1)} %pad_add_fusion.facts_ref, ...), custom_call_target="tpu_custom_call" | custom-call | tf_op jit(solution)/shard_map/forward/pallas_call | solution.py:50
  21.4 0.1 collective-permute-start.7
  21.4 0.7 collective-permute-start.5
  22.2 4.1 %units_to_rows.1 = (bf16[48,64,128]{2,1,0:T(8,128)(2,1)S(1)}, bf16[48,64,128]{2,1,0:T(8,128)(2,1)S(1)}) custom-call(bf16[256,3072]{1,0:T(8,128)(2,1)S(1)} %copy-done.7, bf16[2,256,128]{2,1,0:T(8,128)(2,1)S(1)} %fusion.10.select_ref), custom_call_target="tpu_custom_call" | custom-call | tf_op jit(solution)/shard_map/units_to_rows/pallas_call | solution.py:50
  26.3 0.9 copy-done.12
  27.1 5.8 %transpose_tiles.1 = (bf16[216,32,128]{2,1,0:T(8,128)(2,1)S(1)}, bf16[216,32,128]{2,1,0:T(8,128)(2,1)S(1)}) custom-call(bf16[216,32,128]{2,1,0:T(8,128)(2,1)S(1)} %bitcast.57, bf16[216,32,128]{2,1,0:T(8,128)(2,1)S(1)} %collective-permute-done.other_ref), custom_call_target="tpu_custom_call" | custom-call | tf_op jit(solution)/shard_map/transpose_tiles/pallas_call | solution.py:50
  32.9 1.2 copy-done.24
  34.1 1.3 copy-done.26
  35.4 0.8 collective-permute-start.2
  36.3 1.5 collective-permute-start.4
  37.8 13.9 %collective-permute-done.7.near_b = bf16[2,24,64,128]{3,2,1,0:T(8,128)(2,1)S(1)} collective-permute-done((bf16[2,24,64,128]{3,2,1,0:T(8,128)(2,1)S(1)}, bf16[2,24,64,128]{3,2,1,0:T(8,128)(2,1)S(1)}, u32[]{:S(2)}, u32[]{:S(2)}) %collective-permute-start.7) | collective-permute-done | bytes 786464 | tf_op jit(solution)/shard_map/ppermute | solution.py:409
  51.8 1.2 collective-permute-start.8
  53.1 0.4 collective-permute-start.6
  53.5 6.7 %collective-permute-done.2.last_a = bf16[24,64,128]{2,1,0:T(8,128)(2,1)S(1)} collective-permute-done((bf16[24,64,128]{2,1,0:T(8,128)(2,1)S(1)}, bf16[24,64,128]{2,1,0:T(8,128)(2,1)S(1)}, u32[]{:S(2)}, u32[]{:S(2)}) %collective-permute-start.2) | collective-permute-done | bytes 393248 | tf_op jit(solution)/shard_map/ppermute | solution.py:409
  60.2 0.7 copy-done.18
  60.9 7.7 %collective-permute-done.8.last_b = bf16[24,64,128]{2,1,0:T(8,128)(2,1)S(1)} collective-permute-done((bf16[24,64,128]{2,1,0:T(8,128)(2,1)S(1)}, bf16[24,64,128]{2,1,0:T(8,128)(2,1)S(1)}, u32[]{:S(2)}, u32[]{:S(2)}) %collective-permute-start.8) | collective-permute-done | bytes 393248 | tf_op jit(solution)/shard_map/ppermute | solution.py:409
  68.6 3.3 %gelu.2 = (bf16[24,64,128]{2,1,0:T(8,128)(2,1)}, bf16[24,64,128]{2,1,0:T(8,128)(2,1)}, bf16[48,64,128]{2,1,0:T(8,128)(2,1)S(1)}) custom-call(bf16[48,64,128]{2,1,0:T(8,128)(2,1)S(1)} %get-tuple-element.60.upstream_hbm, bf16[24,64,128]{2,1,0:T(8,128)(2,1)S(1)} %get-tuple-element.62.own_a, bf16[2,24,64,128]{3,2,1,0:T(8,128)(2,1)S(1)} %collective-permute-done.5.near_a, ...), custom_call_target="tpu_custom_call" | custom-call | tf_op jit(solution)/shard_map/gelu/pallas_call | solution.py:50
  72.0 0.3 collective-permute-start.12
  72.3 1.3 collective-permute-start.9
  73.5 1.1 collective-permute-start.11
  74.7 0.3 collective-permute-start.10
  75.0 7.2 %collective-permute-done.12.refs_5_.refs_6_.refs_7_ = bf16[24,64,128]{2,1,0:T(8,128)(2,1)} collective-permute-done((bf16[24,64,128]{2,1,0:T(8,128)(2,1)}, bf16[24,64,128]{2,1,0:T(8,128)(2,1)}, u32[]{:S(2)}, u32[]{:S(2)}) %collective-permute-start.12) | collective-permute-done | bytes 393248 | tf_op jit(solution)/shard_map/ppermute | solution.py:409
  82.2 0.8 collective-permute-start.14
  83.0 0.7 collective-permute-start.13
  83.7 1.0 copy-done.17
  84.7 1.0 copy-done.19
  85.7 1.0 copy-done.21
  86.7 2.6 %gelu.3 = (bf16[24,64,128]{2,1,0:T(8,128)(2,1)S(1)}, bf16[24,64,128]{2,1,0:T(8,128)(2,1)S(1)}, bf16[48,64,128]{2,1,0:T(8,128)(2,1)S(1)}) custom-call(bf16[48,64,128]{2,1,0:T(8,128)(2,1)S(1)} %copy-done.13, bf16[24,64,128]{2,1,0:T(8,128)(2,1)S(1)} %copy-done.15, bf16[2,24,64,128]{3,2,1,0:T(8,128)(2,1)S(1)} %copy-done.3, bf16[24,64,128]{2,1,0:T(8,128)(2,1)S(1)} %copy-done.19, ...), custom_call_target="tpu_custom_call" | custom-call | tf_op jit(solution)/shard_map/gelu/pallas_call | solution.py:50
  89.3 5.7 %rows_to_units.1 = bf16[256,3072]{1,0:T(8,128)(2,1)} custom-call(bf16[2,256,128]{2,1,0:T(8,128)(2,1)S(1)} %copy-done.1, bf16[48,64,128]{2,1,0:T(8,128)(2,1)S(1)} %get-tuple-element.68.refs_0_, bf16[48,64,128]{2,1,0:T(8,128)(2,1)S(1)} %get-tuple-element.69.refs_1_), custom_call_target="tpu_custom_call" | custom-call | tf_op jit(solution)/shard_map/rows_to_units/pallas_call | solution.py:50
  95.0 0.8 collective-permute-start.19
  95.8 0.7 collective-permute-start.18
  96.5 0.5 collective-permute-start.17
  97.0 2.2 %collective-permute-done.14.refs_7_.refs_8_.refs_9_ = bf16[24,64,128]{2,1,0:T(8,128)(2,1)} collective-permute-done((bf16[24,64,128]{2,1,0:T(8,128)(2,1)}, bf16[24,64,128]{2,1,0:T(8,128)(2,1)}, u32[]{:S(2)}, u32[]{:S(2)}) %collective-permute-start.14) | collective-permute-done | bytes 393248 | tf_op jit(solution)/shard_map/ppermute | solution.py:409
  99.2 1.0 collective-permute-start.16
  100.3 6.8 %backward.2 = bf16[128,3072]{1,0:T(8,128)(2,1)S(1)} custom-call(s32[3]{0:T(128)S(1)} %pad_add_fusion.facts_ref, s32[432]{0:T(512)S(1)} %bitcast.66, s32[432]{0:T(512)S(1)} %bitcast.74, bf16[216,32,128]{2,1,0:T(8,128)(2,1)S(1)} %copy-done.25, bf16[216,32,128]{2,1,0:T(8,128)(2,1)S(1)} %copy-done.27, ...), custom_call_target="tpu_custom_call" | custom-call | flops 8049999872 | bytes 7474572 | tf_op jit(solution)/shard_map/backward/pallas_call | solution.py:50
  107.1 1.4 collective-permute-start.15
  108.5 7.1 %collective-permute-done.18.refs_4_.refs_5_.refs_7_ = bf16[24,64,128]{2,1,0:T(8,128)(2,1)S(1)} collective-permute-done((bf16[24,64,128]{2,1,0:T(8,128)(2,1)S(1)}, bf16[24,64,128]{2,1,0:T(8,128)(2,1)S(1)}, u32[]{:S(2)}, u32[]{:S(2)}) %collective-permute-start.18) | collective-permute-done | bytes 393248 | tf_op jit(solution)/shard_map/ppermute | solution.py:409
  115.6 0.8 collective-permute-start.22
  116.4 0.9 collective-permute-start.21
  117.3 6.1 %outer_other.2 = bf16[216,32,128]{2,1,0:T(8,128)(2,1)S(1)} custom-call(s32[3]{0:T(128)S(1)} %pad_add_fusion.facts_ref, s32[432]{0:T(512)S(1)} %bitcast.67, s32[432]{0:T(512)S(1)} %bitcast.75, bf16[48,64,128]{2,1,0:T(8,128)(2,1)S(1)} %copy-done.11, bf16[24,64,128]{2,1,0:T(8,128)(2,1)} %get-tuple-element.71.refs_0_.refs_1_.refs_2_, ...), custom_call_target="tpu_custom_call" | custom-call | flops 5750000128 | bytes 5705100 | tf_op jit(solution)/shard_map/outer_other/pallas_call | solution.py:50
  123.4 2.2 %collective-permute-start.24 = (bf16[216,32,128]{2,1,0:T(8,128)(2,1)S(1)}, bf16[216,32,128]{2,1,0:T(8,128)(2,1)S(1)}, u32[]{:S(2)}, u32[]{:S(2)}) collective-permute-start(bf16[216,32,128]{2,1,0:T(8,128)(2,1)S(1)} %outer_other.2), channel_id=1, source_target_pairs={{0,16},{16,0},{1,17},{17,1},{2,18},{18,2},{3,19},{19,3},{4,20},{20... | collective-permute-start | bytes 5308424 | tf_op jit(solution)/shard_map/ppermute | solution.py:412
  125.7 1.1 collective-permute-start.20
  126.8 6.7 %backward.3 = bf16[128,3072]{1,0:T(8,128)(2,1)S(1)} custom-call(s32[3]{0:T(128)S(1)} %pad_add_fusion.facts_ref, s32[432]{0:T(512)S(1)} %bitcast.68, s32[432]{0:T(512)S(1)} %bitcast.76, bf16[216,32,128]{2,1,0:T(8,128)(2,1)S(1)} %copy-done.25, bf16[216,32,128]{2,1,0:T(8,128)(2,1)S(1)} %copy-done.27, ...), custom_call_target="tpu_custom_call" | custom-call | flops 8049999872 | bytes 7474572 | tf_op jit(solution)/shard_map/backward/pallas_call | solution.py:50
  133.5 0.1 collective-permute-start.23
  133.6 5.8 %outer_other.3 = bf16[216,32,128]{2,1,0:T(8,128)(2,1)S(1)} custom-call(s32[3]{0:T(128)S(1)} %pad_add_fusion.facts_ref, s32[432]{0:T(512)S(1)} %bitcast.69, s32[432]{0:T(512)S(1)} %bitcast.77, bf16[48,64,128]{2,1,0:T(8,128)(2,1)S(1)} %copy-done.9, bf16[24,64,128]{2,1,0:T(8,128)(2,1)S(1)} %get-tuple-element.78.refs_0_.refs_1_.refs_3_, ...), custom_call_target="tpu_custom_call" | custom-call | flops 23000000512 | bytes 5705100 | tf_op jit(solution)/shard_map/outer_other/pallas_call | solution.py:50
  139.4 1.9 %collective-permute-start.26 = (bf16[216,32,128]{2,1,0:T(8,128)(2,1)S(1)}, bf16[216,32,128]{2,1,0:T(8,128)(2,1)S(1)}, u32[]{:S(2)}, u32[]{:S(2)}) collective-permute-start(bf16[216,32,128]{2,1,0:T(8,128)(2,1)S(1)} %outer_other.3), channel_id=1, source_target_pairs={{0,16},{16,0},{1,17},{17,1},{2,18},{18,2},{3,19},{19,3},{4,20},{20... | collective-permute-start | bytes 5308424 | tf_op jit(solution)/shard_map/ppermute | solution.py:412
  141.3 0.8 fusion.8
  142.1 4.9 %outer_own.2.refs_0_ = bf16[216,32,128]{2,1,0:T(8,128)(2,1)S(1)} custom-call(s32[3]{0:T(128)S(1)} %pad_add_fusion.facts_ref, s32[432]{0:T(512)S(1)} %bitcast.70, s32[432]{0:T(512)S(1)} %bitcast.78, bf16[216,32,128]{2,1,0:T(8,128)(2,1)S(1)} %collective-permute-done.24.refs_0_, bf16[48,64,128]{2,1,0:T(8,128)(2,1)S(1)} %copy-done.11, ...), custom_call_target="tpu_custom_call" | custom-call | flops 23000000512 | bytes 7474572 | tf_op jit(solution)/shard_map/outer_own/pallas_call | solution.py:50
  147.0 0.7 fusion.6
  147.8 4.7 %outer_own.3 = bf16[216,32,128]{2,1,0:T(8,128)(2,1)S(1)} custom-call(s32[3]{0:T(128)S(1)} %pad_add_fusion.facts_ref, s32[432]{0:T(512)S(1)} %bitcast.71, s32[432]{0:T(512)S(1)} %bitcast.79, bf16[216,32,128]{2,1,0:T(8,128)(2,1)S(1)} %outer_own.2.refs_0_, bf16[216,32,128]{2,1,0:T(8,128)(2,1)S(1)} %collective-permute-done.26.refs_1_, ...), custom_call_target="tpu_custom_call" | custom-call | flops 23000000512 | bytes 9244044 | tf_op jit(solution)/shard_map/outer_own/pallas_call | solution.py:50
  152.5 2.2 %reshape.154 = bf16[1,1,216,4096]{3,2,1,0:T(8,128)(2,1)} reshape(bf16[216,32,128]{2,1,0:T(8,128)(2,1)S(1)} %outer_own.3) | data formatting | bytes 3538944 | tf_op jit(solution)/shard_map/reshape | solution.py:498
  154.6 4.0 %collective-permute-done.25 = bf16[32,3072]{1,0:T(8,128)(2,1)} collective-permute-done((bf16[32,3072]{1,0:T(8,128)(2,1)}, bf16[32,3072]{1,0:T(8,128)(2,1)}, u32[]{:S(2)}, u32[]{:S(2)}) %collective-permute-start.25) | collective-permute-done | bytes 196640 | tf_op jit(solution)/shard_map/ppermute | solution.py:468
  158.6 1.0 fusion.5
  159.6 0.8 pad_maximum_fusion
  (82 shorter events, 0.5 us)
Async XLA Ops:
  2.5 7.2 %copy-start.22 = (s32[1,1,432]{2,1,0:T(1,128)S(1)}, s32[1,1,432]{2,1,0:T(1,128)}, u32[]{:S(2)}) copy-start(s32[1,1,432]{2,1,0:T(1,128)} %param.8) | copy-start | bytes 5188
  2.5 7.2 %copy-start.23 = (s32[1,1,432]{2,1,0:T(1,128)S(1)}, s32[1,1,432]{2,1,0:T(1,128)}, u32[]{:S(2)}) copy-start(s32[1,1,432]{2,1,0:T(1,128)} %param.9) | copy-start | bytes 5188
  2.5 7.1 %collective-permute-start = (bf16[216,32,128]{2,1,0:T(8,128)(2,1)S(1)}, bf16[216,32,128]{2,1,0:T(8,128)(2,1)S(1)}, u32[]{:S(2)}, u32[]{:S(2)}) collective-permute-start(bf16[216,32,128]{2,1,0:T(8,128)(2,1)S(1)} %bitcast.54), channel_id=1, source_target_pairs={{0,16},{16,0},{1,17},{17,1},{2,18},{18,2},{3,19},{19,3},{4,20},{20... | collective-permute-start | bytes 5308424 | tf_op jit(solution)/shard_map/ppermute | solution.py:412
  4.0 1.4 copy-start.6
  5.4 16.7 %copy-start = (bf16[2,256,128]{2,1,0:T(8,128)(2,1)}, bf16[2,256,128]{2,1,0:T(8,128)(2,1)S(1)}, u32[]{:S(2)}) copy-start(bf16[2,256,128]{2,1,0:T(8,128)(2,1)S(1)} %fusion.10.select_ref) | copy-start | bytes 393220
  9.5 5.4 %copy-start.8 = (bf16[48,64,128]{2,1,0:T(8,128)(2,1)}, bf16[48,64,128]{2,1,0:T(8,128)(2,1)S(1)}, u32[]{:S(2)}) copy-start(bf16[48,64,128]{2,1,0:T(8,128)(2,1)S(1)} %get-tuple-element.87.table_ref.refs_0_.refs_2_) | copy-start | bytes 2359300
  9.6 6.2 %copy-start.10 = (bf16[48,64,128]{2,1,0:T(8,128)(2,1)}, bf16[48,64,128]{2,1,0:T(8,128)(2,1)S(1)}, u32[]{:S(2)}) copy-start(bf16[48,64,128]{2,1,0:T(8,128)(2,1)S(1)} %get-tuple-element.85.table_ref.refs_0_.refs_1_) | copy-start | bytes 2359300
  15.0 0.8 copy-start.14
  15.7 5.6 %copy-start.16 = (bf16[24,64,128]{2,1,0:T(8,128)(2,1)}, bf16[24,64,128]{2,1,0:T(8,128)(2,1)S(1)}, u32[]{:S(2)}) copy-start(bf16[24,64,128]{2,1,0:T(8,128)(2,1)S(1)} %get-tuple-element.57.own_b) | copy-start | bytes 1179652
  15.8 19.6 %collective-permute-start.1 = (bf16[2,24,64,128]{3,2,1,0:T(8,128)(2,1)S(1)}, bf16[2,24,64,128]{3,2,1,0:T(8,128)(2,1)S(1)}, u32[]{:S(2)}, u32[]{:S(2)}) collective-permute-start(bf16[2,24,64,128]{3,2,1,0:T(8,128)(2,1)S(1)} %get-tuple-element.50), channel_id=1, source_target_pairs={{0,1},{1,0},{2,3},{3,2},{4,5},{5,4},{6,7},{7,6},{8,9},{9,8},{10,11... | collective-permute-start | bytes 2359304 | tf_op jit(solution)/shard_map/ppermute | solution.py:409
  15.8 20.5 %collective-permute-start.3 = (bf16[2,24,64,128]{3,2,1,0:T(8,128)(2,1)S(1)}, bf16[2,24,64,128]{3,2,1,0:T(8,128)(2,1)S(1)}, u32[]{:S(2)}, u32[]{:S(2)}) collective-permute-start(bf16[2,24,64,128]{3,2,1,0:T(8,128)(2,1)S(1)} %get-tuple-element.58), channel_id=1, source_target_pairs={{0,2},{1,3},{2,0},{3,1},{4,6},{5,7},{6,4},{7,5},{8,10},{9,11},{10,... | collective-permute-start | bytes 2359304 | tf_op jit(solution)/shard_map/ppermute | solution.py:409
  15.8 6.4 %copy-start.7 = (bf16[256,3072]{1,0:T(8,128)(2,1)S(1)}, bf16[256,3072]{1,0:T(8,128)(2,1)}, u32[]{:S(2)}) copy-start(bf16[256,3072]{1,0:T(8,128)(2,1)} %values_ref.3) | copy-start | bytes 4718596
  21.4 30.4 %collective-permute-start.7 = (bf16[2,24,64,128]{3,2,1,0:T(8,128)(2,1)S(1)}, bf16[2,24,64,128]{3,2,1,0:T(8,128)(2,1)S(1)}, u32[]{:S(2)}, u32[]{:S(2)}) collective-permute-start(bf16[2,24,64,128]{3,2,1,0:T(8,128)(2,1)S(1)} %get-tuple-element.66), channel_id=1, source_target_pairs={{0,2},{1,3},{2,0},{3,1},{4,6},{5,7},{6,4},{7,5},{8,10},{9,11},{10,... | collective-permute-start | bytes 2359304 | tf_op jit(solution)/shard_map/ppermute | solution.py:409
  21.4 31.6 %collective-permute-start.5 = (bf16[2,24,64,128]{3,2,1,0:T(8,128)(2,1)S(1)}, bf16[2,24,64,128]{3,2,1,0:T(8,128)(2,1)S(1)}, u32[]{:S(2)}, u32[]{:S(2)}) collective-permute-start(bf16[2,24,64,128]{3,2,1,0:T(8,128)(2,1)S(1)} %get-tuple-element.63), channel_id=1, source_target_pairs={{0,1},{1,0},{2,3},{3,2},{4,5},{5,4},{6,7},{7,6},{8,9},{9,8},{10,11... | collective-permute-start | bytes 2359304 | tf_op jit(solution)/shard_map/ppermute | solution.py:409
  26.2 0.9 copy-start.12
  32.9 1.2 copy-start.24
  34.1 1.3 copy-start.26
  35.4 16.4 %copy-start.2 = (bf16[2,24,64,128]{3,2,1,0:T(8,128)(2,1)}, bf16[2,24,64,128]{3,2,1,0:T(8,128)(2,1)S(1)}, u32[]{:S(2)}) copy-start(bf16[2,24,64,128]{3,2,1,0:T(8,128)(2,1)S(1)} %collective-permute-done.1.near_a) | copy-start | bytes 2359300
  35.4 24.8 %collective-permute-start.2 = (bf16[24,64,128]{2,1,0:T(8,128)(2,1)S(1)}, bf16[24,64,128]{2,1,0:T(8,128)(2,1)S(1)}, u32[]{:S(2)}, u32[]{:S(2)}) collective-permute-start(bf16[24,64,128]{2,1,0:T(8,128)(2,1)S(1)} %fusion.3), channel_id=1, source_target_pairs={{0,2},{1,3},{2,0},{3,1},{4,6},{5,7},{6,4},{7,5},{8,10},{9,11},{10,... | collective-permute-start | bytes 1179656 | tf_op jit(solution)/shard_map/ppermute | solution.py:409
  36.3 16.8 %copy-start.4 = (bf16[2,24,64,128]{3,2,1,0:T(8,128)(2,1)}, bf16[2,24,64,128]{3,2,1,0:T(8,128)(2,1)S(1)}, u32[]{:S(2)}) copy-start(bf16[2,24,64,128]{3,2,1,0:T(8,128)(2,1)S(1)} %collective-permute-done.3.near_b) | copy-start | bytes 2359300
  36.3 24.6 %collective-permute-start.4 = (bf16[24,64,128]{2,1,0:T(8,128)(2,1)S(1)}, bf16[24,64,128]{2,1,0:T(8,128)(2,1)S(1)}, u32[]{:S(2)}, u32[]{:S(2)}) collective-permute-start(bf16[24,64,128]{2,1,0:T(8,128)(2,1)S(1)} %fusion.2), channel_id=1, source_target_pairs={{0,1},{1,0},{2,3},{3,2},{4,5},{5,4},{6,7},{7,6},{8,9},{9,8},{10,11... | collective-permute-start | bytes 1179656 | tf_op jit(solution)/shard_map/ppermute | solution.py:409
  51.8 16.8 %collective-permute-start.8 = (bf16[24,64,128]{2,1,0:T(8,128)(2,1)S(1)}, bf16[24,64,128]{2,1,0:T(8,128)(2,1)S(1)}, u32[]{:S(2)}, u32[]{:S(2)}) collective-permute-start(bf16[24,64,128]{2,1,0:T(8,128)(2,1)S(1)} %fusion), channel_id=1, source_target_pairs={{0,1},{1,0},{2,3},{3,2},{4,5},{5,4},{6,7},{7,6},{8,9},{9,8},{10,11... | collective-permute-start | bytes 1179656 | tf_op jit(solution)/shard_map/ppermute | solution.py:409
  53.1 15.5 %collective-permute-start.6 = (bf16[24,64,128]{2,1,0:T(8,128)(2,1)S(1)}, bf16[24,64,128]{2,1,0:T(8,128)(2,1)S(1)}, u32[]{:S(2)}, u32[]{:S(2)}) collective-permute-start(bf16[24,64,128]{2,1,0:T(8,128)(2,1)S(1)} %fusion.1), channel_id=1, source_target_pairs={{0,2},{1,3},{2,0},{3,1},{4,6},{5,7},{6,4},{7,5},{8,10},{9,11},{10,... | collective-permute-start | bytes 1179656 | tf_op jit(solution)/shard_map/ppermute | solution.py:409
  60.2 0.7 copy-start.18
  60.9 11.1 %copy-start.20 = (bf16[24,64,128]{2,1,0:T(8,128)(2,1)}, bf16[24,64,128]{2,1,0:T(8,128)(2,1)S(1)}, u32[]{:S(2)}) copy-start(bf16[24,64,128]{2,1,0:T(8,128)(2,1)S(1)} %collective-permute-done.4.last_b) | copy-start | bytes 1179652
  68.6 15.1 %copy-start.3 = (bf16[2,24,64,128]{3,2,1,0:T(8,128)(2,1)S(1)}, bf16[2,24,64,128]{3,2,1,0:T(8,128)(2,1)}, u32[]{:S(2)}) copy-start(bf16[2,24,64,128]{3,2,1,0:T(8,128)(2,1)} %copy-done.2) | copy-start | bytes 2359300
  68.6 15.1 %copy-start.5 = (bf16[2,24,64,128]{3,2,1,0:T(8,128)(2,1)S(1)}, bf16[2,24,64,128]{3,2,1,0:T(8,128)(2,1)}, u32[]{:S(2)}) copy-start(bf16[2,24,64,128]{3,2,1,0:T(8,128)(2,1)} %copy-done.4) | copy-start | bytes 2359300
  68.6 15.1 %copy-start.13 = (bf16[48,64,128]{2,1,0:T(8,128)(2,1)S(1)}, bf16[48,64,128]{2,1,0:T(8,128)(2,1)}, u32[]{:S(2)}) copy-start(bf16[48,64,128]{2,1,0:T(8,128)(2,1)} %copy-done.12) | copy-start | bytes 2359300
  68.6 15.1 %copy-start.15 = (bf16[24,64,128]{2,1,0:T(8,128)(2,1)S(1)}, bf16[24,64,128]{2,1,0:T(8,128)(2,1)}, u32[]{:S(2)}) copy-start(bf16[24,64,128]{2,1,0:T(8,128)(2,1)} %copy-done.14) | copy-start | bytes 1179652
  72.0 10.2 %collective-permute-start.12 = (bf16[24,64,128]{2,1,0:T(8,128)(2,1)}, bf16[24,64,128]{2,1,0:T(8,128)(2,1)}, u32[]{:S(2)}, u32[]{:S(2)}) collective-permute-start(bf16[24,64,128]{2,1,0:T(8,128)(2,1)} %get-tuple-element.72.refs_1_.refs_2_.refs_3_), channel_id=1, source_target_pairs={{0,2},{1,3},{2,0},{3,1},{4,6},{5,7},{6,4},{7,5},{8,10},{9,11},{10,... | collective-permute-start | bytes 1179656 | tf_op jit(solution)/shard_map/ppermute | solution.py:409
  72.3 10.8 %collective-permute-start.9 = (bf16[24,64,128]{2,1,0:T(8,128)(2,1)}, bf16[24,64,128]{2,1,0:T(8,128)(2,1)}, u32[]{:S(2)}, u32[]{:S(2)}) collective-permute-start(bf16[24,64,128]{2,1,0:T(8,128)(2,1)} %get-tuple-element.71.refs_0_.refs_1_.refs_2_), channel_id=1, source_target_pairs={{0,1},{1,0},{2,3},{3,2},{4,5},{5,4},{6,7},{7,6},{8,9},{9,8},{10,11... | collective-permute-start | bytes 1179656 | tf_op jit(solution)/shard_map/ppermute | solution.py:409
  73.5 21.5 %collective-permute-start.11 = (bf16[24,64,128]{2,1,0:T(8,128)(2,1)}, bf16[24,64,128]{2,1,0:T(8,128)(2,1)}, u32[]{:S(2)}, u32[]{:S(2)}) collective-permute-start(bf16[24,64,128]{2,1,0:T(8,128)(2,1)} %get-tuple-element.71.refs_0_.refs_1_.refs_2_), channel_id=1, source_target_pairs={{0,2},{1,3},{2,0},{3,1},{4,6},{5,7},{6,4},{7,5},{8,10},{9,11},{10,... | collective-permute-start | bytes 1179656 | tf_op jit(solution)/shard_map/ppermute | solution.py:409
  74.7 21.8 %collective-permute-start.10 = (bf16[24,64,128]{2,1,0:T(8,128)(2,1)}, bf16[24,64,128]{2,1,0:T(8,128)(2,1)}, u32[]{:S(2)}, u32[]{:S(2)}) collective-permute-start(bf16[24,64,128]{2,1,0:T(8,128)(2,1)} %get-tuple-element.72.refs_1_.refs_2_.refs_3_), channel_id=1, source_target_pairs={{0,1},{1,0},{2,3},{3,2},{4,5},{5,4},{6,7},{7,6},{8,9},{9,8},{10,11... | collective-permute-start | bytes 1179656 | tf_op jit(solution)/shard_map/ppermute | solution.py:409
  82.2 17.0 %collective-permute-start.14 = (bf16[24,64,128]{2,1,0:T(8,128)(2,1)}, bf16[24,64,128]{2,1,0:T(8,128)(2,1)}, u32[]{:S(2)}, u32[]{:S(2)}) collective-permute-start(bf16[24,64,128]{2,1,0:T(8,128)(2,1)} %collective-permute-done.12.refs_5_.refs_6_.refs_7_), channel_id=1, source_target_pairs={{0,1},{1,0},{2,3},{3,2},{4,5},{5,4},{6,7},{7,6},{8,9},{9,8},{10,11... | collective-permute-start | bytes 1179656 | tf_op jit(solution)/shard_map/ppermute | solution.py:409
  83.0 17.2 %collective-permute-start.13 = (bf16[24,64,128]{2,1,0:T(8,128)(2,1)}, bf16[24,64,128]{2,1,0:T(8,128)(2,1)}, u32[]{:S(2)}, u32[]{:S(2)}) collective-permute-start(bf16[24,64,128]{2,1,0:T(8,128)(2,1)} %collective-permute-done.9.refs_2_.refs_3_.refs_4_), channel_id=1, source_target_pairs={{0,2},{1,3},{2,0},{3,1},{4,6},{5,7},{6,4},{7,5},{8,10},{9,11},{10,... | collective-permute-start | bytes 1179656 | tf_op jit(solution)/shard_map/ppermute | solution.py:409
  83.7 1.0 copy-start.17
  84.7 1.0 copy-start.19
  85.7 1.0 copy-start.21
  86.7 2.6 %copy-start.1 = (bf16[2,256,128]{2,1,0:T(8,128)(2,1)S(1)}, bf16[2,256,128]{2,1,0:T(8,128)(2,1)}, u32[]{:S(2)}) copy-start(bf16[2,256,128]{2,1,0:T(8,128)(2,1)} %copy-done) | copy-start | bytes 393220
  86.7 13.5 %copy-start.27 = (bf16[216,32,128]{2,1,0:T(8,128)(2,1)S(1)}, bf16[216,32,128]{2,1,0:T(8,128)(2,1)}, u32[]{:S(2)}) copy-start(bf16[216,32,128]{2,1,0:T(8,128)(2,1)} %copy-done.26) | copy-start | bytes 5308420
  89.3 10.9 %copy-start.25 = (bf16[216,32,128]{2,1,0:T(8,128)(2,1)S(1)}, bf16[216,32,128]{2,1,0:T(8,128)(2,1)}, u32[]{:S(2)}) copy-start(bf16[216,32,128]{2,1,0:T(8,128)(2,1)} %copy-done.24) | copy-start | bytes 5308420
  95.0 13.5 %collective-permute-start.19 = (bf16[24,64,128]{2,1,0:T(8,128)(2,1)S(1)}, bf16[24,64,128]{2,1,0:T(8,128)(2,1)S(1)}, u32[]{:S(2)}, u32[]{:S(2)}) collective-permute-start(bf16[24,64,128]{2,1,0:T(8,128)(2,1)S(1)} %get-tuple-element.79.refs_1_.refs_2_.refs_4_), channel_id=1, source_target_pairs={{0,2},{1,3},{2,0},{3,1},{4,6},{5,7},{6,4},{7,5},{8,10},{9,11},{10,... | collective-permute-start | bytes 1179656 | tf_op jit(solution)/shard_map/ppermute | solution.py:409
  95.8 19.8 %collective-permute-start.18 = (bf16[24,64,128]{2,1,0:T(8,128)(2,1)S(1)}, bf16[24,64,128]{2,1,0:T(8,128)(2,1)S(1)}, u32[]{:S(2)}, u32[]{:S(2)}) collective-permute-start(bf16[24,64,128]{2,1,0:T(8,128)(2,1)S(1)} %get-tuple-element.78.refs_0_.refs_1_.refs_3_), channel_id=1, source_target_pairs={{0,2},{1,3},{2,0},{3,1},{4,6},{5,7},{6,4},{7,5},{8,10},{9,11},{10,... | collective-permute-start | bytes 1179656 | tf_op jit(solution)/shard_map/ppermute | solution.py:409
  96.5 19.1 %collective-permute-start.17 = (bf16[24,64,128]{2,1,0:T(8,128)(2,1)S(1)}, bf16[24,64,128]{2,1,0:T(8,128)(2,1)S(1)}, u32[]{:S(2)}, u32[]{:S(2)}) collective-permute-start(bf16[24,64,128]{2,1,0:T(8,128)(2,1)S(1)} %get-tuple-element.79.refs_1_.refs_2_.refs_4_), channel_id=1, source_target_pairs={{0,1},{1,0},{2,3},{3,2},{4,5},{5,4},{6,7},{7,6},{8,9},{9,8},{10,11... | collective-permute-start | bytes 1179656 | tf_op jit(solution)/shard_map/ppermute | solution.py:409
  99.2 16.4 %collective-permute-start.16 = (bf16[24,64,128]{2,1,0:T(8,128)(2,1)S(1)}, bf16[24,64,128]{2,1,0:T(8,128)(2,1)S(1)}, u32[]{:S(2)}, u32[]{:S(2)}) collective-permute-start(bf16[24,64,128]{2,1,0:T(8,128)(2,1)S(1)} %get-tuple-element.78.refs_0_.refs_1_.refs_3_), channel_id=1, source_target_pairs={{0,1},{1,0},{2,3},{3,2},{4,5},{5,4},{6,7},{7,6},{8,9},{9,8},{10,11... | collective-permute-start | bytes 1179656 | tf_op jit(solution)/shard_map/ppermute | solution.py:409
  100.3 17.1 %copy-start.11 = (bf16[48,64,128]{2,1,0:T(8,128)(2,1)S(1)}, bf16[48,64,128]{2,1,0:T(8,128)(2,1)}, u32[]{:S(2)}) copy-start(bf16[48,64,128]{2,1,0:T(8,128)(2,1)} %copy-done.10) | copy-start | bytes 2359300
  107.1 18.6 %collective-permute-start.15 = (bf16[2,32,3072]{2,1,0:T(8,128)(2,1)S(1)}, bf16[2,32,3072]{2,1,0:T(8,128)(2,1)S(1)}, u32[]{:S(2)}, u32[]{:S(2)}) collective-permute-start(bf16[2,32,3072]{2,1,0:T(8,128)(2,1)S(1)} %dynamic-slice_bitcast_fusion.1), channel_id=1, source_target_pairs={{0,4},{4,0},{8,12},{12,8},{1,5},{5,1},{9,13},{13,9},{2,6},{6,2},{1... | collective-permute-start | bytes 1179656 | tf_op jit(solution)/shard_map/ppermute | solution.py:463
  115.6 11.2 %collective-permute-start.22 = (bf16[24,64,128]{2,1,0:T(8,128)(2,1)S(1)}, bf16[24,64,128]{2,1,0:T(8,128)(2,1)S(1)}, u32[]{:S(2)}, u32[]{:S(2)}) collective-permute-start(bf16[24,64,128]{2,1,0:T(8,128)(2,1)S(1)} %collective-permute-done.19.refs_5_.refs_6_.refs_8_), channel_id=1, source_target_pairs={{0,1},{1,0},{2,3},{3,2},{4,5},{5,4},{6,7},{7,6},{8,9},{9,8},{10,11... | collective-permute-start | bytes 1179656 | tf_op jit(solution)/shard_map/ppermute | solution.py:409
  116.4 10.4 %collective-permute-start.21 = (bf16[24,64,128]{2,1,0:T(8,128)(2,1)S(1)}, bf16[24,64,128]{2,1,0:T(8,128)(2,1)S(1)}, u32[]{:S(2)}, u32[]{:S(2)}) collective-permute-start(bf16[24,64,128]{2,1,0:T(8,128)(2,1)S(1)} %collective-permute-done.16.refs_2_.refs_3_.refs_5_), channel_id=1, source_target_pairs={{0,2},{1,3},{2,0},{3,1},{4,6},{5,7},{6,4},{7,5},{8,10},{9,11},{10,... | collective-permute-start | bytes 1179656 | tf_op jit(solution)/shard_map/ppermute | solution.py:409
  123.4 18.7 %collective-permute-start.24 = (bf16[216,32,128]{2,1,0:T(8,128)(2,1)S(1)}, bf16[216,32,128]{2,1,0:T(8,128)(2,1)S(1)}, u32[]{:S(2)}, u32[]{:S(2)}) collective-permute-start(bf16[216,32,128]{2,1,0:T(8,128)(2,1)S(1)} %outer_other.2), channel_id=1, source_target_pairs={{0,16},{16,0},{1,17},{17,1},{2,18},{18,2},{3,19},{19,3},{4,20},{20... | collective-permute-start | bytes 5308424 | tf_op jit(solution)/shard_map/ppermute | solution.py:412
  125.7 7.9 %copy-start.9 = (bf16[48,64,128]{2,1,0:T(8,128)(2,1)S(1)}, bf16[48,64,128]{2,1,0:T(8,128)(2,1)}, u32[]{:S(2)}) copy-start(bf16[48,64,128]{2,1,0:T(8,128)(2,1)} %copy-done.8) | copy-start | bytes 2359300
  125.7 15.6 %collective-permute-start.20 = (bf16[32,3072]{1,0:T(8,128)(2,1)S(1)}, bf16[32,3072]{1,0:T(8,128)(2,1)S(1)}, u32[]{:S(2)}, u32[]{:S(2)}) collective-permute-start(bf16[32,3072]{1,0:T(8,128)(2,1)S(1)} %fusion.9), channel_id=1, source_target_pairs={{0,8},{4,12},{8,0},{12,4},{1,9},{5,13},{9,1},{13,5},{2,10},{6,14},... | collective-permute-start | bytes 589832 | tf_op jit(solution)/shard_map/ppermute | solution.py:468
  133.5 13.5 %collective-permute-start.23 = (bf16[2,32,3072]{2,1,0:T(8,128)(2,1)S(1)}, bf16[2,32,3072]{2,1,0:T(8,128)(2,1)S(1)}, u32[]{:S(2)}, u32[]{:S(2)}) collective-permute-start(bf16[2,32,3072]{2,1,0:T(8,128)(2,1)S(1)} %dynamic-slice_bitcast_fusion), channel_id=1, source_target_pairs={{0,4},{4,0},{8,12},{12,8},{1,5},{5,1},{9,13},{13,9},{2,6},{6,2},{1... | collective-permute-start | bytes 1179656 | tf_op jit(solution)/shard_map/ppermute | solution.py:463
  139.4 8.4 %collective-permute-start.26 = (bf16[216,32,128]{2,1,0:T(8,128)(2,1)S(1)}, bf16[216,32,128]{2,1,0:T(8,128)(2,1)S(1)}, u32[]{:S(2)}, u32[]{:S(2)}) collective-permute-start(bf16[216,32,128]{2,1,0:T(8,128)(2,1)S(1)} %outer_other.3), channel_id=1, source_target_pairs={{0,16},{16,0},{1,17},{17,1},{2,18},{18,2},{3,19},{19,3},{4,20},{20... | collective-permute-start | bytes 5308424 | tf_op jit(solution)/shard_map/ppermute | solution.py:412
  147.8 10.8 %collective-permute-start.25 = (bf16[32,3072]{1,0:T(8,128)(2,1)}, bf16[32,3072]{1,0:T(8,128)(2,1)}, u32[]{:S(2)}, u32[]{:S(2)}) collective-permute-start(bf16[32,3072]{1,0:T(8,128)(2,1)} %fusion.6), channel_id=1, source_target_pairs={{0,8},{4,12},{8,0},{12,4},{1,9},{5,13},{9,1},{13,5},{2,10},{6,14},... | collective-permute-start | bytes 589832 | tf_op jit(solution)/shard_map/ppermute | solution.py:468
  152.5 7.1 %copy-start.28 = (bf16[32,3072]{1,0:T(8,128)(2,1)S(1)}, bf16[32,3072]{1,0:T(8,128)(2,1)}, u32[]{:S(2)}) copy-start(bf16[32,3072]{1,0:T(8,128)(2,1)} %fusion.8) | copy-start | bytes 589828

commit v9 on v8

--- a/solution.py
+++ b/solution.py
@@ -446,8 +446,9 @@
     activation = rows_to_units(select, acts)
     for chunk in range(CHUNKS):
         x_a, y_b = grads[chunk][2], grads[chunk][5]
+        if chunk == 0:
+            x_a, y_b = after(x_a, activation), after(y_b, activation)
         grads[chunk] += [across(x_a, 2), across(y_b, 1)]
-    grads[0][7] = after(grads[0][7], activation)
 
     me_row = lax.axis_index("row")
 

time: 163 us -> 162 us (level)
  the two profiles are of different devices: /device:TPU:5 before, /device:TPU:0 now
where the time goes in v9:
time: 162 us; the launch traced here: 160 us
  waiting for transfers between devices  57.1 us (35%)
  Pallas kernels  56.8 us (35%)
  starting transfers between devices  34.8 us (21%)
  local copies, waits for them, and re-layouts  5.57 us (3%)
  other arithmetic  3.69 us (2%)
  between operations  1.67 us (1%)
    pallas_call x14, Pallas kernels, call(): pl.pallas_call(kernel, out_shape=out_shape, in_specs=in_specs, out_specs=...  56.8 us
    ppermute x20, waiting for transfers between devices, across(): lax.ppermute(values, 'col', [(place, place ^ bit) for place in range(shar...  54.8 us
    ppermute x20, starting transfers between devices, across(): lax.ppermute(values, 'col', [(place, place ^ bit) for place in range(shar...  23 us
    ppermute x2, starting transfers between devices, to_rows(): lax.ppermute(sent, 'row', [(place, place ^ 1) for place in range(4)])  7.21 us
    unnamed x37, local copies, waits for them, and re-layouts  3.32 us
  transfers between devices with their start and end apart: 27, of which 14 were waited for; matrix products, arithmetic and copies ran while one was open for 3% of the time, Pallas kernels for 32%

profile of v9, /device:TPU:0, one launch (start us, length us, event | category | flops | bytes accessed | tf_op | source)
XLA Modules:
  0.0 159.6 jit_solution(1463912422004204887)
XLA Ops:
  0.6 1.8 %copy.9 = bf16[27,8,32,128]{3,2,1,0:T(8,128)(2,1)S(1)} copy(bf16[27,8,32,128]{3,1,2,0:T(8,128)(2,1)} %bitcast.80) | data formatting | bytes 3538944
  2.5 0.5 collective-permute-start
  3.7 0.1 add_add_fusion
  3.8 1.4 copy-done
  5.2 4.1 %features_to_rows.1 = (bf16[48,64,128]{2,1,0:T(8,128)(2,1)S(1)}, bf16[48,64,128]{2,1,0:T(8,128)(2,1)S(1)}) custom-call(bf16[256,3072]{1,0:T(8,128)(2,1)S(1)} %copy-done, bf16[2,256,128]{2,1,0:T(8,128)(2,1)S(1)} %fusion.10.select_ref), custom_call_target="tpu_custom_call" | custom-call | tf_op jit(solution)/shard_map/features_to_rows/pallas_call | solution.py:50
  9.3 0.1 pad_add_fusion.facts_ref
  9.4 3.1 %forward.2 = (bf16[2,24,64,128]{3,2,1,0:T(8,128)(2,1)S(1)}, bf16[2,24,64,128]{3,2,1,0:T(8,128)(2,1)S(1)}, bf16[24,64,128]{2,1,0:T(8,128)(2,1)S(1)}, bf16[24,64,1...) custom-call(s32[3]{0:T(128)S(1)} %pad_add_fusion.facts_ref, ...), custom_call_target="tpu_custom_call" | custom-call | tf_op jit(solution)/shard_map/forward/pallas_call | solution.py:50
  12.6 5.3 %collective-permute-start.1 = (bf16[2,24,64,128]{3,2,1,0:T(8,128)(2,1)S(1)}, bf16[2,24,64,128]{3,2,1,0:T(8,128)(2,1)S(1)}, u32[]{:S(2)}, u32[]{:S(2)}) collective-permute-start(bf16[2,24,64,128]{3,2,1,0:T(8,128)(2,1)S(1)} %get-tuple-element.51), channel_id=1, source_target_pairs={{0,1},{1,0},{2,3},{3,2},{4,5},{5,4},{6,7},{7,6},{8,9},{9,8},{10,11... | collective-permute-start | bytes 2359304 | tf_op jit(solution)/shard_map/ppermute | solution.py:409
  17.8 1.0 collective-permute-start.3
  18.8 3.3 %forward.3 = (bf16[2,24,64,128]{3,2,1,0:T(8,128)(2,1)S(1)}, bf16[2,24,64,128]{3,2,1,0:T(8,128)(2,1)S(1)}, bf16[24,64,128]{2,1,0:T(8,128)(2,1)S(1)}, bf16[24,64,1...) custom-call(s32[3]{0:T(128)S(1)} %pad_add_fusion.facts_ref, ...), custom_call_target="tpu_custom_call" | custom-call | tf_op jit(solution)/shard_map/forward/pallas_call | solution.py:50
  22.1 2.8 %collective-permute-start.7 = (bf16[2,24,64,128]{3,2,1,0:T(8,128)(2,1)S(1)}, bf16[2,24,64,128]{3,2,1,0:T(8,128)(2,1)S(1)}, u32[]{:S(2)}, u32[]{:S(2)}) collective-permute-start(bf16[2,24,64,128]{3,2,1,0:T(8,128)(2,1)S(1)} %get-tuple-element.67), channel_id=1, source_target_pairs={{0,2},{1,3},{2,0},{3,1},{4,6},{5,7},{6,4},{7,5},{8,10},{9,11},{10,... | collective-permute-start | bytes 2359304 | tf_op jit(solution)/shard_map/ppermute | solution.py:409
  25.0 0.6 collective-permute-start.5
  25.6 4.1 %units_to_rows.1 = (bf16[48,64,128]{2,1,0:T(8,128)(2,1)S(1)}, bf16[48,64,128]{2,1,0:T(8,128)(2,1)S(1)}) custom-call(bf16[256,3072]{1,0:T(8,128)(2,1)S(1)} %copy-done.1, bf16[2,256,128]{2,1,0:T(8,128)(2,1)S(1)} %fusion.10.select_ref), custom_call_target="tpu_custom_call" | custom-call | tf_op jit(solution)/shard_map/units_to_rows/pallas_call | solution.py:50
  29.7 5.8 %transpose_tiles.1 = (bf16[216,32,128]{2,1,0:T(8,128)(2,1)S(1)}, bf16[216,32,128]{2,1,0:T(8,128)(2,1)S(1)}) custom-call(bf16[216,32,128]{2,1,0:T(8,128)(2,1)S(1)} %bitcast.57, bf16[216,32,128]{2,1,0:T(8,128)(2,1)S(1)} %collective-permute-done.other_ref), custom_call_target="tpu_custom_call" | custom-call | tf_op jit(solution)/shard_map/transpose_tiles/pallas_call | solution.py:50
  35.5 0.8 collective-permute-done.1.near_a
  36.3 1.1 collective-permute-start.2
  37.4 0.9 collective-permute-done.3.near_b
  38.3 1.1 collective-permute-start.4
  39.4 15.7 %collective-permute-done.7.near_b = bf16[2,24,64,128]{3,2,1,0:T(8,128)(2,1)S(1)} collective-permute-done((bf16[2,24,64,128]{3,2,1,0:T(8,128)(2,1)S(1)}, bf16[2,24,64,128]{3,2,1,0:T(8,128)(2,1)S(1)}, u32[]{:S(2)}, u32[]{:S(2)}) %collective-permute-start.7) | collective-permute-done | bytes 786464 | tf_op jit(solution)/shard_map/ppermute | solution.py:409
  55.1 0.1 collective-permute-start.8
  55.3 1.0 collective-permute-start.6
  56.3 7.2 %collective-permute-done.2.last_a = bf16[24,64,128]{2,1,0:T(8,128)(2,1)S(1)} collective-permute-done((bf16[24,64,128]{2,1,0:T(8,128)(2,1)S(1)}, bf16[24,64,128]{2,1,0:T(8,128)(2,1)S(1)}, u32[]{:S(2)}, u32[]{:S(2)}) %collective-permute-start.2) | collective-permute-done | bytes 393248 | tf_op jit(solution)/shard_map/ppermute | solution.py:409
  63.5 6.2 %collective-permute-done.8.last_b = bf16[24,64,128]{2,1,0:T(8,128)(2,1)S(1)} collective-permute-done((bf16[24,64,128]{2,1,0:T(8,128)(2,1)S(1)}, bf16[24,64,128]{2,1,0:T(8,128)(2,1)S(1)}, u32[]{:S(2)}, u32[]{:S(2)}) %collective-permute-start.8) | collective-permute-done | bytes 393248 | tf_op jit(solution)/shard_map/ppermute | solution.py:409
  69.8 1.5 collective-permute-done.6.last_a
  71.2 3.3 %gelu.2 = (bf16[24,64,128]{2,1,0:T(8,128)(2,1)}, bf16[24,64,128]{2,1,0:T(8,128)(2,1)}, bf16[48,64,128]{2,1,0:T(8,128)(2,1)S(1)}) custom-call(bf16[48,64,128]{2,1,0:T(8,128)(2,1)S(1)} %get-tuple-element.61.upstream_hbm, bf16[24,64,128]{2,1,0:T(8,128)(2,1)S(1)} %get-tuple-element.63.own_a, bf16[2,24,64,128]{3,2,1,0:T(8,128)(2,1)S(1)} %collective-permute-done.5.near_a, ...), custom_call_target="tpu_custom_call" | custom-call | tf_op jit(solution)/shard_map/gelu/pallas_call | solution.py:50
  74.6 1.0 collective-permute-start.12
  75.6 0.4 collective-permute-start.9
  76.0 1.1 collective-permute-start.11
  77.0 1.7 %collective-permute-start.10 = (bf16[24,64,128]{2,1,0:T(8,128)(2,1)}, bf16[24,64,128]{2,1,0:T(8,128)(2,1)}, u32[]{:S(2)}, u32[]{:S(2)}) collective-permute-start(bf16[24,64,128]{2,1,0:T(8,128)(2,1)} %get-tuple-element.73.refs_1_.refs_2_.refs_3_), channel_id=1, source_target_pairs={{0,1},{1,0},{2,3},{3,2},{4,5},{5,4},{6,7},{7,6},{8,9},{9,8},{10,11... | collective-permute-start | bytes 1179656 | tf_op jit(solution)/shard_map/ppermute | solution.py:409
  78.7 2.6 %gelu.3 = (bf16[24,64,128]{2,1,0:T(8,128)(2,1)S(1)}, bf16[24,64,128]{2,1,0:T(8,128)(2,1)S(1)}, bf16[48,64,128]{2,1,0:T(8,128)(2,1)S(1)}) custom-call(bf16[48,64,128]{2,1,0:T(8,128)(2,1)S(1)} %get-tuple-element.53.upstream_hbm, bf16[24,64,128]{2,1,0:T(8,128)(2,1)S(1)} %get-tuple-element.48.own_a, bf16[2,24,64,128]{3,2,1,0:T(8,128)(2,1)S(1)} %collective-permute-done.1.near_a, ...), custom_call_target="tpu_custom_call" | custom-call | tf_op jit(solution)/shard_map/gelu/pallas_call | solution.py:50
  81.3 5.7 %rows_to_units.1 = bf16[256,3072]{1,0:T(8,128)(2,1)} custom-call(bf16[2,256,128]{2,1,0:T(8,128)(2,1)S(1)} %fusion.10.select_ref, bf16[48,64,128]{2,1,0:T(8,128)(2,1)S(1)} %get-tuple-element.69.refs_0_, bf16[48,64,128]{2,1,0:T(8,128)(2,1)S(1)} %get-tuple-element.70.refs_1_), custom_call_target="tpu_custom_call" | custom-call | tf_op jit(solution)/shard_map/rows_to_units/pallas_call | solution.py:50
  87.0 0.4 collective-permute-start.14
  87.4 0.5 collective-permute-done.9.refs_2_.refs_3_.refs_4_
  88.0 1.1 collective-permute-start.13
  89.0 6.4 %collective-permute-done.11.refs_4_.refs_5_.refs_6_ = bf16[24,64,128]{2,1,0:T(8,128)(2,1)} collective-permute-done((bf16[24,64,128]{2,1,0:T(8,128)(2,1)}, bf16[24,64,128]{2,1,0:T(8,128)(2,1)}, u32[]{:S(2)}, u32[]{:S(2)}) %collective-permute-start.11) | collective-permute-done | bytes 393248 | tf_op jit(solution)/shard_map/ppermute | solution.py:409
  95.4 1.0 collective-permute-start.19
  96.4 1.1 collective-permute-start.18
  97.5 0.3 collective-permute-start.17
  97.8 7.0 %collective-permute-done.14.refs_7_.refs_8_.refs_9_ = bf16[24,64,128]{2,1,0:T(8,128)(2,1)} collective-permute-done((bf16[24,64,128]{2,1,0:T(8,128)(2,1)}, bf16[24,64,128]{2,1,0:T(8,128)(2,1)}, u32[]{:S(2)}, u32[]{:S(2)}) %collective-permute-start.14) | collective-permute-done | bytes 393248 | tf_op jit(solution)/shard_map/ppermute | solution.py:409
  104.8 0.4 collective-permute-start.16
  105.2 4.5 %backward.2 = bf16[128,3072]{1,0:T(8,128)(2,1)S(1)} custom-call(s32[3]{0:T(128)S(1)} %pad_add_fusion.facts_ref, s32[432]{0:T(512)S(1)} %bitcast.66, s32[432]{0:T(512)S(1)} %bitcast.74, bf16[216,32,128]{2,1,0:T(8,128)(2,1)S(1)} %copy-done.9, bf16[216,32,128]{2,1,0:T(8,128)(2,1)S(1)} %copy-done.11, ...), custom_call_target="tpu_custom_call" | custom-call | flops 8049999872 | bytes 7474572 | tf_op jit(solution)/shard_map/backward/pallas_call | solution.py:50
  109.8 3.9 %collective-permute-start.15 = (bf16[2,32,3072]{2,1,0:T(8,128)(2,1)S(1)}, bf16[2,32,3072]{2,1,0:T(8,128)(2,1)S(1)}, u32[]{:S(2)}, u32[]{:S(2)}) collective-permute-start(bf16[2,32,3072]{2,1,0:T(8,128)(2,1)S(1)} %dynamic-slice_bitcast_fusion.1), channel_id=1, source_target_pairs={{0,4},{4,0},{8,12},{12,8},{1,5},{5,1},{9,13},{13,9},{2,6},{6,2},{1... | collective-permute-start | bytes 1179656 | tf_op jit(solution)/shard_map/ppermute | solution.py:464
  113.7 5.3 %collective-permute-done.18.refs_4_.refs_5_.refs_7_ = bf16[24,64,128]{2,1,0:T(8,128)(2,1)S(1)} collective-permute-done((bf16[24,64,128]{2,1,0:T(8,128)(2,1)}, bf16[24,64,128]{2,1,0:T(8,128)(2,1)S(1)}, u32[]{:S(2)}, u32[]{:S(2)}) %collective-permute-start.18) | collective-permute-done | bytes 393248 | tf_op jit(solution)/shard_map/ppermute | solution.py:409
  119.0 0.7 collective-permute-done.16.refs_2_.refs_3_.refs_5_
  119.7 0.7 collective-permute-start.22
  120.4 1.0 collective-permute-start.21
  121.4 2.9 %outer_other.2 = bf16[216,32,128]{2,1,0:T(8,128)(2,1)S(1)} custom-call(s32[3]{0:T(128)S(1)} %pad_add_fusion.facts_ref, s32[432]{0:T(512)S(1)} %bitcast.67, s32[432]{0:T(512)S(1)} %bitcast.75, bf16[48,64,128]{2,1,0:T(8,128)(2,1)S(1)} %copy-done.5, bf16[24,64,128]{2,1,0:T(8,128)(2,1)} %get-tuple-element.72.refs_0_.refs_1_.refs_2_, ...), custom_call_target="tpu_custom_call" | custom-call | flops 5750000128 | bytes 5705100 | tf_op jit(solution)/shard_map/outer_other/pallas_call | solution.py:50
  124.3 0.4 collective-permute-start.24
  124.8 2.3 %collective-permute-start.20 = (bf16[32,3072]{1,0:T(8,128)(2,1)S(1)}, bf16[32,3072]{1,0:T(8,128)(2,1)S(1)}, u32[]{:S(2)}, u32[]{:S(2)}) collective-permute-start(bf16[32,3072]{1,0:T(8,128)(2,1)S(1)} %fusion.9), channel_id=1, source_target_pairs={{0,8},{4,12},{8,0},{12,4},{1,9},{5,13},{9,1},{13,5},{2,10},{6,14},... | collective-permute-start | bytes 589832 | tf_op jit(solution)/shard_map/ppermute | solution.py:469
  127.1 1.8 %collective-permute-done.22.refs_7_.refs_8_.refs_10_ = bf16[24,64,128]{2,1,0:T(8,128)(2,1)S(1)} collective-permute-done((bf16[24,64,128]{2,1,0:T(8,128)(2,1)S(1)}, bf16[24,64,128]{2,1,0:T(8,128)(2,1)S(1)}, u32[]{:S(2)}, u32[]{:S(2)}) %collective-permute-start.22) | collective-permute-done | bytes 393248 | tf_op jit(solution)/shard_map/ppermute | solution.py:409
  128.9 0.7 collective-permute-done.21.refs_6_.refs_7_.refs_9_
  129.6 4.4 %backward.3 = bf16[128,3072]{1,0:T(8,128)(2,1)S(1)} custom-call(s32[3]{0:T(128)S(1)} %pad_add_fusion.facts_ref, s32[432]{0:T(512)S(1)} %bitcast.68, s32[432]{0:T(512)S(1)} %bitcast.76, bf16[216,32,128]{2,1,0:T(8,128)(2,1)S(1)} %copy-done.9, bf16[216,32,128]{2,1,0:T(8,128)(2,1)S(1)} %copy-done.12, bf16[24,64,128]{2,1,0:T(8,128)(2,1)S(1)} %copy-done.14, ...), custom_call_target="tpu_custom_call" | custom-call | flops 8049999872 | bytes 7474572 | tf_op jit(solution)/shard_map/backward/pallas_call | solution.py:50
  134.1 3.3 %collective-permute-start.23 = (bf16[2,32,3072]{2,1,0:T(8,128)(2,1)S(1)}, bf16[2,32,3072]{2,1,0:T(8,128)(2,1)S(1)}, u32[]{:S(2)}, u32[]{:S(2)}) collective-permute-start(bf16[2,32,3072]{2,1,0:T(8,128)(2,1)S(1)} %dynamic-slice_bitcast_fusion), channel_id=1, source_target_pairs={{0,4},{4,0},{8,12},{12,8},{1,5},{5,1},{9,13},{13,9},{2,6},{6,2},{1... | collective-permute-start | bytes 1179656 | tf_op jit(solution)/shard_map/ppermute | solution.py:464
  137.4 2.6 %outer_other.3 = bf16[216,32,128]{2,1,0:T(8,128)(2,1)S(1)} custom-call(s32[3]{0:T(128)S(1)} %pad_add_fusion.facts_ref, s32[432]{0:T(512)S(1)} %bitcast.69, s32[432]{0:T(512)S(1)} %bitcast.77, bf16[48,64,128]{2,1,0:T(8,128)(2,1)S(1)} %copy-done.3, bf16[24,64,128]{2,1,0:T(8,128)(2,1)S(1)} %copy-done.14, bf16[24,64,128]{2,1,0:T(8,128)(2,1)S(1)} %copy-done.16, ...), custom_call_target="tpu_custom_call" | custom-call | flops 23000000512 | bytes 5705100 | tf_op jit(solution)/shard_map/outer_other/pallas_call | solution.py:50
  140.0 0.5 collective-permute-start.26
  140.6 0.8 fusion.8
  141.3 5.3 %outer_own.2.refs_0_ = bf16[216,32,128]{2,1,0:T(8,128)(2,1)S(1)} custom-call(s32[3]{0:T(128)S(1)} %pad_add_fusion.facts_ref, s32[432]{0:T(512)S(1)} %bitcast.70, s32[432]{0:T(512)S(1)} %bitcast.78, bf16[216,32,128]{2,1,0:T(8,128)(2,1)S(1)} %collective-permute-done.24.refs_0_, bf16[48,64,128]{2,1,0:T(8,128)(2,1)S(1)} %copy-done.5, ...), custom_call_target="tpu_custom_call" | custom-call | flops 23000000512 | bytes 7474572 | tf_op jit(solution)/shard_map/outer_own/pallas_call | solution.py:50
  146.7 0.7 fusion.6
  147.4 0.9 collective-permute-start.25
  148.3 5.1 %outer_own.3 = bf16[216,32,128]{2,1,0:T(8,128)(2,1)S(1)} custom-call(s32[3]{0:T(128)S(1)} %pad_add_fusion.facts_ref, s32[432]{0:T(512)S(1)} %bitcast.71, s32[432]{0:T(512)S(1)} %bitcast.79, bf16[216,32,128]{2,1,0:T(8,128)(2,1)S(1)} %outer_own.2.refs_0_, bf16[216,32,128]{2,1,0:T(8,128)(2,1)S(1)} %collective-permute-done.26.refs_1_, ...), custom_call_target="tpu_custom_call" | custom-call | flops 23000000512 | bytes 9244044 | tf_op jit(solution)/shard_map/outer_own/pallas_call | solution.py:50
  153.4 2.2 %reshape.154 = bf16[1,1,216,4096]{3,2,1,0:T(8,128)(2,1)} reshape(bf16[216,32,128]{2,1,0:T(8,128)(2,1)S(1)} %outer_own.3) | data formatting | bytes 3538944 | tf_op jit(solution)/shard_map/reshape | solution.py:499
  155.6 2.3 %collective-permute-done.25 = bf16[32,3072]{1,0:T(8,128)(2,1)} collective-permute-done((bf16[32,3072]{1,0:T(8,128)(2,1)}, bf16[32,3072]{1,0:T(8,128)(2,1)}, u32[]{:S(2)}, u32[]{:S(2)}) %collective-permute-start.25) | collective-permute-done | bytes 196640 | tf_op jit(solution)/shard_map/ppermute | solution.py:469
  157.9 1.0 fusion.5
  158.9 0.8 pad_maximum_fusion
  (60 shorter events, 0.5 us)
Async XLA Ops:
  2.5 6.9 %copy-start.6 = (s32[1,1,432]{2,1,0:T(1,128)S(1)}, s32[1,1,432]{2,1,0:T(1,128)}, u32[]{:S(2)}) copy-start(s32[1,1,432]{2,1,0:T(1,128)} %param.8) | copy-start | bytes 5188
  2.5 6.9 %copy-start.7 = (s32[1,1,432]{2,1,0:T(1,128)S(1)}, s32[1,1,432]{2,1,0:T(1,128)}, u32[]{:S(2)}) copy-start(s32[1,1,432]{2,1,0:T(1,128)} %param.9) | copy-start | bytes 5188
  2.5 6.9 %collective-permute-start = (bf16[216,32,128]{2,1,0:T(8,128)(2,1)S(1)}, bf16[216,32,128]{2,1,0:T(8,128)(2,1)S(1)}, u32[]{:S(2)}, u32[]{:S(2)}) collective-permute-start(bf16[216,32,128]{2,1,0:T(8,128)(2,1)S(1)} %bitcast.54), channel_id=1, source_target_pairs={{0,16},{16,0},{1,17},{17,1},{2,18},{18,2},{3,19},{19,3},{4,20},{20... | collective-permute-start | bytes 5308424 | tf_op jit(solution)/shard_map/ppermute | solution.py:412
  3.8 1.4 copy-start
  9.3 3.2 %copy-start.2 = (bf16[48,64,128]{2,1,0:T(8,128)(2,1)}, bf16[48,64,128]{2,1,0:T(8,128)(2,1)S(1)}, u32[]{:S(2)}) copy-start(bf16[48,64,128]{2,1,0:T(8,128)(2,1)S(1)} %get-tuple-element.89.table_ref.refs_0_.refs_2_) | copy-start | bytes 2359300
  9.3 9.5 %copy-start.4 = (bf16[48,64,128]{2,1,0:T(8,128)(2,1)}, bf16[48,64,128]{2,1,0:T(8,128)(2,1)S(1)}, u32[]{:S(2)}) copy-start(bf16[48,64,128]{2,1,0:T(8,128)(2,1)S(1)} %get-tuple-element.87.table_ref.refs_0_.refs_1_) | copy-start | bytes 2359300
  12.6 23.7 %collective-permute-start.1 = (bf16[2,24,64,128]{3,2,1,0:T(8,128)(2,1)S(1)}, bf16[2,24,64,128]{3,2,1,0:T(8,128)(2,1)S(1)}, u32[]{:S(2)}, u32[]{:S(2)}) collective-permute-start(bf16[2,24,64,128]{3,2,1,0:T(8,128)(2,1)S(1)} %get-tuple-element.51), channel_id=1, source_target_pairs={{0,1},{1,0},{2,3},{3,2},{4,5},{5,4},{6,7},{7,6},{8,9},{9,8},{10,11... | collective-permute-start | bytes 2359304 | tf_op jit(solution)/shard_map/ppermute | solution.py:409
  17.8 20.4 %collective-permute-start.3 = (bf16[2,24,64,128]{3,2,1,0:T(8,128)(2,1)S(1)}, bf16[2,24,64,128]{3,2,1,0:T(8,128)(2,1)S(1)}, u32[]{:S(2)}, u32[]{:S(2)}) collective-permute-start(bf16[2,24,64,128]{3,2,1,0:T(8,128)(2,1)S(1)} %get-tuple-element.59), channel_id=1, source_target_pairs={{0,2},{1,3},{2,0},{3,1},{4,6},{5,7},{6,4},{7,5},{8,10},{9,11},{10,... | collective-permute-start | bytes 2359304 | tf_op jit(solution)/shard_map/ppermute | solution.py:409
  18.8 6.8 %copy-start.1 = (bf16[256,3072]{1,0:T(8,128)(2,1)S(1)}, bf16[256,3072]{1,0:T(8,128)(2,1)}, u32[]{:S(2)}) copy-start(bf16[256,3072]{1,0:T(8,128)(2,1)} %values_ref.3) | copy-start | bytes 4718596
  22.1 33.0 %collective-permute-start.7 = (bf16[2,24,64,128]{3,2,1,0:T(8,128)(2,1)S(1)}, bf16[2,24,64,128]{3,2,1,0:T(8,128)(2,1)S(1)}, u32[]{:S(2)}, u32[]{:S(2)}) collective-permute-start(bf16[2,24,64,128]{3,2,1,0:T(8,128)(2,1)S(1)} %get-tuple-element.67), channel_id=1, source_target_pairs={{0,2},{1,3},{2,0},{3,1},{4,6},{5,7},{6,4},{7,5},{8,10},{9,11},{10,... | collective-permute-start | bytes 2359304 | tf_op jit(solution)/shard_map/ppermute | solution.py:409
  25.0 30.3 %collective-permute-start.5 = (bf16[2,24,64,128]{3,2,1,0:T(8,128)(2,1)S(1)}, bf16[2,24,64,128]{3,2,1,0:T(8,128)(2,1)S(1)}, u32[]{:S(2)}, u32[]{:S(2)}) collective-permute-start(bf16[2,24,64,128]{3,2,1,0:T(8,128)(2,1)S(1)} %get-tuple-element.64), channel_id=1, source_target_pairs={{0,1},{1,0},{2,3},{3,2},{4,5},{5,4},{6,7},{7,6},{8,9},{9,8},{10,11... | collective-permute-start | bytes 2359304 | tf_op jit(solution)/shard_map/ppermute | solution.py:409
  35.5 19.7 %copy-start.8 = (bf16[216,32,128]{2,1,0:T(8,128)(2,1)}, bf16[216,32,128]{2,1,0:T(8,128)(2,1)S(1)}, u32[]{:S(2)}) copy-start(bf16[216,32,128]{2,1,0:T(8,128)(2,1)S(1)} %get-tuple-element.56.own_ref) | copy-start | bytes 5308420
  35.5 19.7 %copy-start.10 = (bf16[216,32,128]{2,1,0:T(8,128)(2,1)}, bf16[216,32,128]{2,1,0:T(8,128)(2,1)S(1)}, u32[]{:S(2)}) copy-start(bf16[216,32,128]{2,1,0:T(8,128)(2,1)S(1)} %get-tuple-element.71.other_ref) | copy-start | bytes 5308420
  36.3 27.2 %collective-permute-start.2 = (bf16[24,64,128]{2,1,0:T(8,128)(2,1)S(1)}, bf16[24,64,128]{2,1,0:T(8,128)(2,1)S(1)}, u32[]{:S(2)}, u32[]{:S(2)}) collective-permute-start(bf16[24,64,128]{2,1,0:T(8,128)(2,1)S(1)} %fusion.3), channel_id=1, source_target_pairs={{0,2},{1,3},{2,0},{3,1},{4,6},{5,7},{6,4},{7,5},{8,10},{9,11},{10,... | collective-permute-start | bytes 1179656 | tf_op jit(solution)/shard_map/ppermute | solution.py:409
  38.3 25.2 %collective-permute-start.4 = (bf16[24,64,128]{2,1,0:T(8,128)(2,1)S(1)}, bf16[24,64,128]{2,1,0:T(8,128)(2,1)S(1)}, u32[]{:S(2)}, u32[]{:S(2)}) collective-permute-start(bf16[24,64,128]{2,1,0:T(8,128)(2,1)S(1)} %fusion.2), channel_id=1, source_target_pairs={{0,1},{1,0},{2,3},{3,2},{4,5},{5,4},{6,7},{7,6},{8,9},{9,8},{10,11... | collective-permute-start | bytes 1179656 | tf_op jit(solution)/shard_map/ppermute | solution.py:409
  55.1 14.6 %collective-permute-start.8 = (bf16[24,64,128]{2,1,0:T(8,128)(2,1)S(1)}, bf16[24,64,128]{2,1,0:T(8,128)(2,1)S(1)}, u32[]{:S(2)}, u32[]{:S(2)}) collective-permute-start(bf16[24,64,128]{2,1,0:T(8,128)(2,1)S(1)} %fusion), channel_id=1, source_target_pairs={{0,1},{1,0},{2,3},{3,2},{4,5},{5,4},{6,7},{7,6},{8,9},{9,8},{10,11... | collective-permute-start | bytes 1179656 | tf_op jit(solution)/shard_map/ppermute | solution.py:409
  55.3 15.9 %collective-permute-start.6 = (bf16[24,64,128]{2,1,0:T(8,128)(2,1)S(1)}, bf16[24,64,128]{2,1,0:T(8,128)(2,1)S(1)}, u32[]{:S(2)}, u32[]{:S(2)}) collective-permute-start(bf16[24,64,128]{2,1,0:T(8,128)(2,1)S(1)} %fusion.1), channel_id=1, source_target_pairs={{0,2},{1,3},{2,0},{3,1},{4,6},{5,7},{6,4},{7,5},{8,10},{9,11},{10,... | collective-permute-start | bytes 1179656 | tf_op jit(solution)/shard_map/ppermute | solution.py:409
  74.6 12.4 %collective-permute-start.12 = (bf16[24,64,128]{2,1,0:T(8,128)(2,1)}, bf16[24,64,128]{2,1,0:T(8,128)(2,1)}, u32[]{:S(2)}, u32[]{:S(2)}) collective-permute-start(bf16[24,64,128]{2,1,0:T(8,128)(2,1)} %get-tuple-element.73.refs_1_.refs_2_.refs_3_), channel_id=1, source_target_pairs={{0,2},{1,3},{2,0},{3,1},{4,6},{5,7},{6,4},{7,5},{8,10},{9,11},{10,... | collective-permute-start | bytes 1179656 | tf_op jit(solution)/shard_map/ppermute | solution.py:409
  75.6 12.4 %collective-permute-start.9 = (bf16[24,64,128]{2,1,0:T(8,128)(2,1)}, bf16[24,64,128]{2,1,0:T(8,128)(2,1)}, u32[]{:S(2)}, u32[]{:S(2)}) collective-permute-start(bf16[24,64,128]{2,1,0:T(8,128)(2,1)} %get-tuple-element.72.refs_0_.refs_1_.refs_2_), channel_id=1, source_target_pairs={{0,1},{1,0},{2,3},{3,2},{4,5},{5,4},{6,7},{7,6},{8,9},{9,8},{10,11... | collective-permute-start | bytes 1179656 | tf_op jit(solution)/shard_map/ppermute | solution.py:409
  76.0 19.5 %collective-permute-start.11 = (bf16[24,64,128]{2,1,0:T(8,128)(2,1)}, bf16[24,64,128]{2,1,0:T(8,128)(2,1)}, u32[]{:S(2)}, u32[]{:S(2)}) collective-permute-start(bf16[24,64,128]{2,1,0:T(8,128)(2,1)} %get-tuple-element.72.refs_0_.refs_1_.refs_2_), channel_id=1, source_target_pairs={{0,2},{1,3},{2,0},{3,1},{4,6},{5,7},{6,4},{7,5},{8,10},{9,11},{10,... | collective-permute-start | bytes 1179656 | tf_op jit(solution)/shard_map/ppermute | solution.py:409
  77.0 20.4 %collective-permute-start.10 = (bf16[24,64,128]{2,1,0:T(8,128)(2,1)}, bf16[24,64,128]{2,1,0:T(8,128)(2,1)}, u32[]{:S(2)}, u32[]{:S(2)}) collective-permute-start(bf16[24,64,128]{2,1,0:T(8,128)(2,1)} %get-tuple-element.73.refs_1_.refs_2_.refs_3_), channel_id=1, source_target_pairs={{0,1},{1,0},{2,3},{3,2},{4,5},{5,4},{6,7},{7,6},{8,9},{9,8},{10,11... | collective-permute-start | bytes 1179656 | tf_op jit(solution)/shard_map/ppermute | solution.py:409
  78.7 26.5 %copy-start.11 = (bf16[216,32,128]{2,1,0:T(8,128)(2,1)S(1)}, bf16[216,32,128]{2,1,0:T(8,128)(2,1)}, u32[]{:S(2)}) copy-start(bf16[216,32,128]{2,1,0:T(8,128)(2,1)} %copy-done.10) | copy-start | bytes 5308420
  81.3 5.7 %copy-start.13 = (bf16[24,64,128]{2,1,0:T(8,128)(2,1)}, bf16[24,64,128]{2,1,0:T(8,128)(2,1)S(1)}, u32[]{:S(2)}) copy-start(bf16[24,64,128]{2,1,0:T(8,128)(2,1)S(1)} %get-tuple-element.80.refs_0_.refs_1_.refs_3_) | copy-start | bytes 1179652
  81.3 5.7 %copy-start.15 = (bf16[24,64,128]{2,1,0:T(8,128)(2,1)}, bf16[24,64,128]{2,1,0:T(8,128)(2,1)S(1)}, u32[]{:S(2)}) copy-start(bf16[24,64,128]{2,1,0:T(8,128)(2,1)S(1)} %get-tuple-element.81.refs_1_.refs_2_.refs_4_) | copy-start | bytes 1179652
  81.3 23.9 %copy-start.9 = (bf16[216,32,128]{2,1,0:T(8,128)(2,1)S(1)}, bf16[216,32,128]{2,1,0:T(8,128)(2,1)}, u32[]{:S(2)}) copy-start(bf16[216,32,128]{2,1,0:T(8,128)(2,1)} %copy-done.8) | copy-start | bytes 5308420
  87.0 17.8 %collective-permute-start.14 = (bf16[24,64,128]{2,1,0:T(8,128)(2,1)}, bf16[24,64,128]{2,1,0:T(8,128)(2,1)}, u32[]{:S(2)}, u32[]{:S(2)}) collective-permute-start(bf16[24,64,128]{2,1,0:T(8,128)(2,1)} %collective-permute-done.12.refs_5_.refs_6_.refs_7_), channel_id=1, source_target_pairs={{0,1},{1,0},{2,3},{3,2},{4,5},{5,4},{6,7},{7,6},{8,9},{9,8},{10,11... | collective-permute-start | bytes 1179656 | tf_op jit(solution)/shard_map/ppermute | solution.py:409
  88.0 17.2 %collective-permute-start.13 = (bf16[24,64,128]{2,1,0:T(8,128)(2,1)}, bf16[24,64,128]{2,1,0:T(8,128)(2,1)}, u32[]{:S(2)}, u32[]{:S(2)}) collective-permute-start(bf16[24,64,128]{2,1,0:T(8,128)(2,1)} %collective-permute-done.9.refs_2_.refs_3_.refs_4_), channel_id=1, source_target_pairs={{0,2},{1,3},{2,0},{3,1},{4,6},{5,7},{6,4},{7,5},{8,10},{9,11},{10,... | collective-permute-start | bytes 1179656 | tf_op jit(solution)/shard_map/ppermute | solution.py:409
  95.4 18.3 %collective-permute-start.19 = (bf16[24,64,128]{2,1,0:T(8,128)(2,1)}, bf16[24,64,128]{2,1,0:T(8,128)(2,1)S(1)}, u32[]{:S(2)}, u32[]{:S(2)}) collective-permute-start(bf16[24,64,128]{2,1,0:T(8,128)(2,1)} %copy-done.15), channel_id=1, source_target_pairs={{0,2},{1,3},{2,0},{3,1},{4,6},{5,7},{6,4},{7,5},{8,10},{9,11},{10,... | collective-permute-start | bytes 1179656 | tf_op jit(solution)/shard_map/ppermute | solution.py:409
  96.4 22.6 %collective-permute-start.18 = (bf16[24,64,128]{2,1,0:T(8,128)(2,1)}, bf16[24,64,128]{2,1,0:T(8,128)(2,1)S(1)}, u32[]{:S(2)}, u32[]{:S(2)}) collective-permute-start(bf16[24,64,128]{2,1,0:T(8,128)(2,1)} %copy-done.13), channel_id=1, source_target_pairs={{0,2},{1,3},{2,0},{3,1},{4,6},{5,7},{6,4},{7,5},{8,10},{9,11},{10,... | collective-permute-start | bytes 1179656 | tf_op jit(solution)/shard_map/ppermute | solution.py:409
  97.5 21.5 %collective-permute-start.17 = (bf16[24,64,128]{2,1,0:T(8,128)(2,1)}, bf16[24,64,128]{2,1,0:T(8,128)(2,1)S(1)}, u32[]{:S(2)}, u32[]{:S(2)}) collective-permute-start(bf16[24,64,128]{2,1,0:T(8,128)(2,1)} %copy-done.15), channel_id=1, source_target_pairs={{0,1},{1,0},{2,3},{3,2},{4,5},{5,4},{6,7},{7,6},{8,9},{9,8},{10,11... | collective-permute-start | bytes 1179656 | tf_op jit(solution)/shard_map/ppermute | solution.py:409
  104.8 14.8 %collective-permute-start.16 = (bf16[24,64,128]{2,1,0:T(8,128)(2,1)}, bf16[24,64,128]{2,1,0:T(8,128)(2,1)S(1)}, u32[]{:S(2)}, u32[]{:S(2)}) collective-permute-start(bf16[24,64,128]{2,1,0:T(8,128)(2,1)} %copy-done.13), channel_id=1, source_target_pairs={{0,1},{1,0},{2,3},{3,2},{4,5},{5,4},{6,7},{7,6},{8,9},{9,8},{10,11... | collective-permute-start | bytes 1179656 | tf_op jit(solution)/shard_map/ppermute | solution.py:409
  105.2 16.2 %copy-start.5 = (bf16[48,64,128]{2,1,0:T(8,128)(2,1)S(1)}, bf16[48,64,128]{2,1,0:T(8,128)(2,1)}, u32[]{:S(2)}) copy-start(bf16[48,64,128]{2,1,0:T(8,128)(2,1)} %copy-done.4) | copy-start | bytes 2359300
  109.8 19.9 %copy-start.12 = (bf16[216,32,128]{2,1,0:T(8,128)(2,1)S(1)}, bf16[216,32,128]{2,1,0:T(8,128)(2,1)}, u32[]{:S(2)}) copy-start(bf16[216,32,128]{2,1,0:T(8,128)(2,1)} %copy-done.10) | copy-start | bytes 5308420
  109.8 19.9 %copy-start.14 = (bf16[24,64,128]{2,1,0:T(8,128)(2,1)S(1)}, bf16[24,64,128]{2,1,0:T(8,128)(2,1)}, u32[]{:S(2)}) copy-start(bf16[24,64,128]{2,1,0:T(8,128)(2,1)} %copy-done.13) | copy-start | bytes 1179652
  109.8 19.9 %copy-start.16 = (bf16[24,64,128]{2,1,0:T(8,128)(2,1)S(1)}, bf16[24,64,128]{2,1,0:T(8,128)(2,1)}, u32[]{:S(2)}) copy-start(bf16[24,64,128]{2,1,0:T(8,128)(2,1)} %copy-done.15) | copy-start | bytes 1179652
  109.8 14.9 %collective-permute-start.15 = (bf16[2,32,3072]{2,1,0:T(8,128)(2,1)S(1)}, bf16[2,32,3072]{2,1,0:T(8,128)(2,1)S(1)}, u32[]{:S(2)}, u32[]{:S(2)}) collective-permute-start(bf16[2,32,3072]{2,1,0:T(8,128)(2,1)S(1)} %dynamic-slice_bitcast_fusion.1), channel_id=1, source_target_pairs={{0,4},{4,0},{8,12},{12,8},{1,5},{5,1},{9,13},{13,9},{2,6},{6,2},{1... | collective-permute-start | bytes 1179656 | tf_op jit(solution)/shard_map/ppermute | solution.py:464
  119.7 9.2 %collective-permute-start.22 = (bf16[24,64,128]{2,1,0:T(8,128)(2,1)S(1)}, bf16[24,64,128]{2,1,0:T(8,128)(2,1)S(1)}, u32[]{:S(2)}, u32[]{:S(2)}) collective-permute-start(bf16[24,64,128]{2,1,0:T(8,128)(2,1)S(1)} %collective-permute-done.19.refs_5_.refs_6_.refs_8_), channel_id=1, source_target_pairs={{0,1},{1,0},{2,3},{3,2},{4,5},{5,4},{6,7},{7,6},{8,9},{9,8},{10,11... | collective-permute-start | bytes 1179656 | tf_op jit(solution)/shard_map/ppermute | solution.py:409
  120.4 9.3 %collective-permute-start.21 = (bf16[24,64,128]{2,1,0:T(8,128)(2,1)S(1)}, bf16[24,64,128]{2,1,0:T(8,128)(2,1)S(1)}, u32[]{:S(2)}, u32[]{:S(2)}) collective-permute-start(bf16[24,64,128]{2,1,0:T(8,128)(2,1)S(1)} %collective-permute-done.16.refs_2_.refs_3_.refs_5_), channel_id=1, source_target_pairs={{0,2},{1,3},{2,0},{3,1},{4,6},{5,7},{6,4},{7,5},{8,10},{9,11},{10,... | collective-permute-start | bytes 1179656 | tf_op jit(solution)/shard_map/ppermute | solution.py:409
  124.3 17.0 %collective-permute-start.24 = (bf16[216,32,128]{2,1,0:T(8,128)(2,1)S(1)}, bf16[216,32,128]{2,1,0:T(8,128)(2,1)S(1)}, u32[]{:S(2)}, u32[]{:S(2)}) collective-permute-start(bf16[216,32,128]{2,1,0:T(8,128)(2,1)S(1)} %outer_other.2), channel_id=1, source_target_pairs={{0,16},{16,0},{1,17},{17,1},{2,18},{18,2},{3,19},{19,3},{4,20},{20... | collective-permute-start | bytes 5308424 | tf_op jit(solution)/shard_map/ppermute | solution.py:412
  124.8 12.6 %copy-start.3 = (bf16[48,64,128]{2,1,0:T(8,128)(2,1)S(1)}, bf16[48,64,128]{2,1,0:T(8,128)(2,1)}, u32[]{:S(2)}) copy-start(bf16[48,64,128]{2,1,0:T(8,128)(2,1)} %copy-done.2) | copy-start | bytes 2359300
  124.8 15.8 %collective-permute-start.20 = (bf16[32,3072]{1,0:T(8,128)(2,1)S(1)}, bf16[32,3072]{1,0:T(8,128)(2,1)S(1)}, u32[]{:S(2)}, u32[]{:S(2)}) collective-permute-start(bf16[32,3072]{1,0:T(8,128)(2,1)S(1)} %fusion.9), channel_id=1, source_target_pairs={{0,8},{4,12},{8,0},{12,4},{1,9},{5,13},{9,1},{13,5},{2,10},{6,14},... | collective-permute-start | bytes 589832 | tf_op jit(solution)/shard_map/ppermute | solution.py:469
  134.1 12.6 %collective-permute-start.23 = (bf16[2,32,3072]{2,1,0:T(8,128)(2,1)S(1)}, bf16[2,32,3072]{2,1,0:T(8,128)(2,1)S(1)}, u32[]{:S(2)}, u32[]{:S(2)}) collective-permute-start(bf16[2,32,3072]{2,1,0:T(8,128)(2,1)S(1)} %dynamic-slice_bitcast_fusion), channel_id=1, source_target_pairs={{0,4},{4,0},{8,12},{12,8},{1,5},{5,1},{9,13},{13,9},{2,6},{6,2},{1... | collective-permute-start | bytes 1179656 | tf_op jit(solution)/shard_map/ppermute | solution.py:464
  140.0 8.3 %collective-permute-start.26 = (bf16[216,32,128]{2,1,0:T(8,128)(2,1)S(1)}, bf16[216,32,128]{2,1,0:T(8,128)(2,1)S(1)}, u32[]{:S(2)}, u32[]{:S(2)}) collective-permute-start(bf16[216,32,128]{2,1,0:T(8,128)(2,1)S(1)} %outer_other.3), channel_id=1, source_target_pairs={{0,16},{16,0},{1,17},{17,1},{2,18},{18,2},{3,19},{19,3},{4,20},{20... | collective-permute-start | bytes 5308424 | tf_op jit(solution)/shard_map/ppermute | solution.py:412
  147.4 10.4 %collective-permute-start.25 = (bf16[32,3072]{1,0:T(8,128)(2,1)}, bf16[32,3072]{1,0:T(8,128)(2,1)}, u32[]{:S(2)}, u32[]{:S(2)}) collective-permute-start(bf16[32,3072]{1,0:T(8,128)(2,1)} %fusion.6), channel_id=1, source_target_pairs={{0,8},{4,12},{8,0},{12,4},{1,9},{5,13},{9,1},{13,5},{2,10},{6,14},... | collective-permute-start | bytes 589832 | tf_op jit(solution)/shard_map/ppermute | solution.py:469
  153.4 5.5 %copy-start.17 = (bf16[32,3072]{1,0:T(8,128)(2,1)S(1)}, bf16[32,3072]{1,0:T(8,128)(2,1)}, u32[]{:S(2)}) copy-start(bf16[32,3072]{1,0:T(8,128)(2,1)} %fusion.8) | copy-start | bytes 589828
